TPU v7x, 128 devices: a whole 4x4x4 slice. The times are simulated.
128 devices in a mesh: ctx: 32 (over y_hi, x, z), fsdp: 4 (over y_lo, core).
Axes of the slice: x: 4, y: 4 (y_hi: 2, y_lo: 2; y = y_hi * 2 + y_lo), z: 4, core: 2. Of those that a mesh axis runs over, the one named last changes fastest.
Arguments:
- layer_input: bfloat16 [4, 4096, 1024], P('fsdp', 'ctx'), may hold values from -6 to 6
- cotangent: bfloat16 [4, 4096, 1024], P('fsdp', 'ctx'), may hold values from -6 to 6
- block_order: int32 [4, 64], P('fsdp'), may hold values from 0 to 63, as said below
- query_weight: bfloat16 [1024, 2048], P('fsdp'), may hold values from -0.1875 to 0.1875
- key_projection: bfloat16 [1024, 1024], P('fsdp'), may hold values from -0.1875 to 0.1875
- value_projection: bfloat16 [1024, 1024], P('fsdp'), may hold values from -0.1875 to 0.1875
- output_weight: bfloat16 [2048, 1024], P('fsdp'), may hold values from -0.75 to 0.75
- gate_weight: bfloat16 [1024, 3072], P('fsdp'), may hold values from -0.1875 to 0.1875
- up_weight: bfloat16 [1024, 3072], P('fsdp'), may hold values from -0.1875 to 0.1875
- down_weight: bfloat16 [3072, 1024], P('fsdp'), may hold values from -0.109375 to 0.109375
- first_gain: float32 [1024], replicated, may hold values from 0.5 to 1.5
- second_gain: float32 [1024], replicated, may hold values from 0.5 to 1.5
- query_gain: float32 [128], replicated, may hold values from 0.25 to 1.75
- key_norm_gain: float32 [128], replicated, may hold values from 0.25 to 1.75
Outputs:
- layer_output: bfloat16 [4, 4096, 1024], P('fsdp', 'ctx')
- input_gradient: float32 [4, 4096, 1024], P('fsdp', 'ctx')
- query_weight_gradient: float32 [1024, 2048], P('fsdp')
- key_weight_gradient: float32 [1024, 1024], P('fsdp')
- value_weight_gradient: float32 [1024, 1024], P('fsdp')
- output_weight_gradient: float32 [2048, 1024], P('fsdp')
- gate_weight_gradient: float32 [1024, 3072], P('fsdp')
- up_weight_gradient: float32 [1024, 3072], P('fsdp')
- down_weight_gradient: float32 [3072, 1024], P('fsdp')
- first_gain_gradient: float32 [1024], P('fsdp')
- second_gain_gradient: float32 [1024], P('fsdp')
- query_gain_gradient: float32 [128], P('fsdp')
- key_gain_gradient: float32 [128], P('fsdp')
Inputs may be any that keep to these rules, and one draw needn't show every extreme that they name: Each row of block_order names every block of 64 positions of its sequence exactly once; the two blocks of rows 2 c and 2 c + 1 are mirrored, block b together with block 2 * 32 - 1 - b, in either order.
All inputs are finite; a program needn't handle non-finite values.
Results may differ from a plain program's by a relative error of at most 0.034.
Values may be sent and summed in bfloat16 or wider, within the bound.
No kernel may reach another device: no remote copies, remote signals or barrier semaphores. Data moves between devices by JAX's collectives and lax.ppermute only.
A program may use at most 320 MiB of HBM per device.

v0:
```python
import math

import jax
import jax.numpy as jnp
from jax import lax
from jax.sharding import PartitionSpec as P

HQ = 16
KEY_VALUE_HEADS = 8
HEAD_SIZE = 128


EPSILON = 1e-06
THETA = 1000000.0
MASKED = -1e30


def rms_apply(values, norm_gain):
    row_scale = lax.rsqrt(jnp.mean(values * values, axis=-1, keepdims=True) + EPSILON)
    normed = values * row_scale
    return (normed * norm_gain, normed, row_scale)


def root_mean_square_backward(gradient, normed, row_scale, norm_gain):
    normed_grad = gradient * norm_gain
    return row_scale * (
        normed_grad - normed * jnp.mean(normed_grad * normed, axis=-1, keepdims=True)
    )


def rope_tables(positions, head_width):
    half_width = head_width // 2
    inverse_freq = jnp.power(THETA, -2.0 * jnp.arange(half_width, dtype=jnp.float32) / head_width)
    angles = positions.astype(jnp.float32)[:, None] * inverse_freq[None, :]
    return (jnp.cos(angles)[:, None, :], jnp.sin(angles)[:, None, :])


def rotary_apply(values, cosine_table, sine_values_table):
    half_width = values.shape[-1] // 2
    front_half = values[..., :half_width]
    back_half = values[..., half_width:]
    return jnp.concatenate(
        [
            front_half * cosine_table - back_half * sine_values_table,
            back_half * cosine_table + front_half * sine_values_table,
        ],
        axis=-1,
    )


def rotary_backward(gradient, cosine_table, sine_values_table):
    half_width = gradient.shape[-1] // 2
    front_half = gradient[..., :half_width]
    back_half = gradient[..., half_width:]
    return jnp.concatenate(
        [
            front_half * cosine_table + back_half * sine_values_table,
            back_half * cosine_table - front_half * sine_values_table,
        ],
        axis=-1,
    )


def left_dot(left_side, right_side):
    return lax.dot_general(
        left_side, right_side, (((0,), (0,)), ((), ())), preferred_element_type=jnp.float32
    )


def right_dot(left_side, right_side):
    return lax.dot_general(
        left_side, right_side, (((1,), (1,)), ((), ())), preferred_element_type=jnp.float32
    )


def on_device(
    layer_input,
    cotangent,
    block_order,
    query_weight,
    key_projection,
    value_projection,
    output_weight,
    gate_weight,
    up_weight,
    down_weight,
    first_gain,
    second_gain,
    query_gain,
    key_norm_gain,
):
    local_rows = layer_input.shape[1]
    block_rows = local_rows // 2
    block_count = 2 * lax.axis_size("ctx")
    slot_count = block_count + 1
    order_row = block_order[0]
    device_place = lax.axis_index("ctx")
    all_positions = (
        order_row[:, None] * block_rows + jnp.arange(block_rows, dtype=jnp.int32)[None, :]
    ).reshape(-1)
    own_positions = lax.dynamic_slice_in_dim(all_positions, device_place * local_rows, local_rows)
    cosine_table, sine_values_table = rope_tables(own_positions, HEAD_SIZE)
    paired_heads = KEY_VALUE_HEADS // 2
    pair_cols = 2 * HEAD_SIZE
    quad_cols = 4 * HEAD_SIZE
    scale_factor = 1.0 / math.sqrt(HEAD_SIZE)
    first_block = lax.dynamic_index_in_dim(order_row, 2 * device_place, 0, False)
    second_block = lax.dynamic_index_in_dim(order_row, 2 * device_place + 1, 0, False)
    low_first = first_block < second_block
    low_block = jnp.minimum(first_block, second_block)
    high_block = block_count - 1 - low_block
    low_offset = jnp.where(low_first, 0, block_rows).astype(jnp.int32)
    high_offset = block_rows - low_offset
    slot_numbers = jnp.arange(slot_count, dtype=jnp.int32)
    high_count = block_count - low_block
    is_high = slot_numbers < high_count
    key_block = jnp.where(is_high, slot_numbers, slot_numbers - high_count)
    query_block = jnp.where(is_high, high_block, low_block)
    block_numbers = jnp.arange(block_count, dtype=jnp.int32)
    inverse_order = jnp.sum(
        jnp.where(order_row[None, :] == block_numbers[:, None], block_numbers[None, :], 0), axis=1
    )
    row_block = jnp.sum(
        jnp.where(key_block[:, None] == block_numbers[None, :], inverse_order[None, :], 0), axis=1
    )
    slot_rows = (
        row_block[:, None] * block_rows + jnp.arange(block_rows, dtype=jnp.int32)[None, :]
    ).reshape(-1)
    offsets = jnp.arange(block_rows, dtype=jnp.int32)
    allowed = (key_block < query_block)[:, None, None] | (
        offsets[None, None, :] <= offsets[None, :, None]
    )
    allowed = allowed[:, None, None, :, :]
    slot_to_row = (row_block[:, None] == block_numbers[None, :]).astype(jnp.float32)
    high_mask = is_high[:, None, None, None, None]

    def split_rows(values):
        return (
            lax.dynamic_slice_in_dim(values, low_offset, block_rows, 0),
            lax.dynamic_slice_in_dim(values, high_offset, block_rows, 0),
        )

    def to_slots(values):
        low_part, high_part = split_rows(values)
        return jnp.where(high_mask, high_part[None], low_part[None])

    def from_slots(values):
        low_part = jnp.sum(jnp.where(high_mask, 0.0, values), axis=0)
        high_part = jnp.sum(jnp.where(high_mask, values, 0.0), axis=0)
        return jnp.where(
            low_first,
            jnp.concatenate([low_part, high_part], axis=0),
            jnp.concatenate([high_part, low_part], axis=0),
        )

    def slot_scores(query_slot, keys_slot):
        raw_scores = (
            jnp.einsum(
                "sqjed,skjd->sjeqk", query_slot, keys_slot, preferred_element_type=jnp.float32
            )
            * scale_factor
        )
        return jnp.where(allowed, raw_scores, MASKED)

    def slot_view(full_rows, head_pair):
        return full_rows[:, :, pair_cols * head_pair : pair_cols * (head_pair + 1)].reshape(
            slot_count, block_rows, 2, HEAD_SIZE
        )

    full_query, full_key, full_value, full_output, full_gate, full_up, full_down = (
        lax.all_gather(query_weight, "fsdp", axis=0, tiled=True),
        lax.all_gather(key_projection, "fsdp", axis=0, tiled=True),
        lax.all_gather(value_projection, "fsdp", axis=0, tiled=True),
        lax.all_gather(output_weight, "fsdp", axis=0, tiled=True),
        lax.all_gather(gate_weight, "fsdp", axis=0, tiled=True),
        lax.all_gather(up_weight, "fsdp", axis=0, tiled=True),
        lax.all_gather(down_weight, "fsdp", axis=0, tiled=True),
    )
    input_f32 = layer_input[0].astype(jnp.float32)
    gained, first_normed, first_scale = rms_apply(input_f32, first_gain)
    attention_input = gained.astype(jnp.bfloat16)
    query_pre = jnp.dot(attention_input, full_query, preferred_element_type=jnp.float32).reshape(
        local_rows, HQ, HEAD_SIZE
    )
    query_gained, query_normed, query_scale = rms_apply(query_pre, query_gain)
    query_rotated = rotary_apply(query_gained, cosine_table, sine_values_table).astype(jnp.bfloat16)
    key_before_norm = jnp.dot(
        attention_input, full_key, preferred_element_type=jnp.float32
    ).reshape(local_rows, KEY_VALUE_HEADS, HEAD_SIZE)
    key_after_gain, key_after_norm, key_norm_scale = rms_apply(key_before_norm, key_norm_gain)
    own_keys = (
        rotary_apply(key_after_gain, cosine_table, sine_values_table)
        .astype(jnp.bfloat16)
        .reshape(local_rows, KEY_VALUE_HEADS * HEAD_SIZE)
    )
    own_values = jnp.dot(attention_input, full_value, preferred_element_type=jnp.float32).astype(
        jnp.bfloat16
    )
    all_keys, all_values = (
        lax.all_gather(own_keys, "ctx", axis=0, tiled=True),
        lax.all_gather(own_values, "ctx", axis=0, tiled=True),
    )
    slot_keys = all_keys[slot_rows].reshape(slot_count, block_rows, KEY_VALUE_HEADS * HEAD_SIZE)
    slot_values = all_values[slot_rows].reshape(slot_count, block_rows, KEY_VALUE_HEADS * HEAD_SIZE)
    mixed_parts = []
    log_totals = []
    for head_pair in range(paired_heads):
        query_part = query_rotated[:, 4 * head_pair : 4 * head_pair + 4, :].reshape(
            local_rows, 2, 2, HEAD_SIZE
        )
        query_slot = to_slots(query_part)
        keys_slot = slot_view(slot_keys, head_pair)
        values_slot = slot_view(slot_values, head_pair)
        raw_scores = slot_scores(query_slot, keys_slot)
        slot_max = jnp.max(raw_scores, axis=-1, keepdims=True)
        low_max = jnp.max(jnp.where(high_mask, MASKED, slot_max), axis=0)
        high_max = jnp.max(jnp.where(high_mask, slot_max, MASKED), axis=0)
        slot_ref = jnp.where(high_mask, high_max[None], low_max[None])
        slot_sum = jnp.sum(jnp.exp(raw_scores - slot_ref), axis=-1, keepdims=True)
        low_total = low_max + jnp.log(jnp.sum(jnp.where(high_mask, 0.0, slot_sum), axis=0))
        high_total = high_max + jnp.log(jnp.sum(jnp.where(high_mask, slot_sum, 0.0), axis=0))
        slot_total = jnp.where(high_mask, high_total[None], low_total[None])
        weights_b = jnp.exp(raw_scores - slot_total).astype(jnp.bfloat16)
        mixture = jnp.einsum(
            "sjeqk,skjd->sqjed", weights_b, values_slot, preferred_element_type=jnp.float32
        )
        mixed_parts.append(from_slots(mixture).reshape(local_rows, quad_cols))
        log_totals.append(slot_total)
    mixed = jnp.concatenate(mixed_parts, axis=1)
    mixed_b = mixed.astype(jnp.bfloat16)
    residual_mid = input_f32 + jnp.dot(mixed_b, full_output, preferred_element_type=jnp.float32)
    gained_mid, second_normed, second_scale = rms_apply(residual_mid, second_gain)
    mlp_in = gained_mid.astype(jnp.bfloat16)
    gate_pre = jnp.dot(mlp_in, full_gate, preferred_element_type=jnp.float32)
    up_pre = jnp.dot(mlp_in, full_up, preferred_element_type=jnp.float32)
    sigmoid_gate = jax.nn.sigmoid(gate_pre)
    silu_gate = gate_pre * sigmoid_gate
    hidden = (silu_gate * up_pre).astype(jnp.bfloat16)
    layer_output = (
        residual_mid + jnp.dot(hidden, full_down, preferred_element_type=jnp.float32)
    ).astype(jnp.bfloat16)
    full_query, full_key, full_value, full_output, full_gate, full_up, full_down = (
        lax.all_gather(query_weight, "fsdp", axis=0, tiled=True),
        lax.all_gather(key_projection, "fsdp", axis=0, tiled=True),
        lax.all_gather(value_projection, "fsdp", axis=0, tiled=True),
        lax.all_gather(output_weight, "fsdp", axis=0, tiled=True),
        lax.all_gather(gate_weight, "fsdp", axis=0, tiled=True),
        lax.all_gather(up_weight, "fsdp", axis=0, tiled=True),
        lax.all_gather(down_weight, "fsdp", axis=0, tiled=True),
    )
    all_keys, all_values = (
        lax.all_gather(own_keys, "ctx", axis=0, tiled=True),
        lax.all_gather(own_values, "ctx", axis=0, tiled=True),
    )
    slot_keys = all_keys[slot_rows].reshape(slot_count, block_rows, KEY_VALUE_HEADS * HEAD_SIZE)
    slot_values = all_values[slot_rows].reshape(slot_count, block_rows, KEY_VALUE_HEADS * HEAD_SIZE)
    own_cotangent = cotangent[0]
    hidden_grad = right_dot(own_cotangent, full_down)
    gate_grad = (
        hidden_grad * up_pre * sigmoid_gate * (1.0 + gate_pre * (1.0 - sigmoid_gate))
    ).astype(jnp.bfloat16)
    up_grad = (hidden_grad * silu_gate).astype(jnp.bfloat16)
    mlp_in_grad = right_dot(gate_grad, full_gate) + right_dot(up_grad, full_up)
    second_gain_grad = jnp.sum(mlp_in_grad * second_normed, axis=0)
    mid_grad = own_cotangent.astype(jnp.float32) + root_mean_square_backward(
        mlp_in_grad, second_normed, second_scale, second_gain
    )
    mid_grad_b = mid_grad.astype(jnp.bfloat16)
    mixed_gradient = right_dot(mid_grad_b, full_output).astype(jnp.bfloat16)
    delta_rows = jnp.sum(
        mixed_gradient.astype(jnp.float32).reshape(local_rows, HQ, HEAD_SIZE)
        * mixed.reshape(local_rows, HQ, HEAD_SIZE),
        axis=-1,
    )
    query_grads = []
    key_grads = []
    value_grads = []
    for head_pair in range(paired_heads):
        query_part = query_rotated[:, 4 * head_pair : 4 * head_pair + 4, :].reshape(
            local_rows, 2, 2, HEAD_SIZE
        )
        query_slot = to_slots(query_part)
        keys_slot = slot_view(slot_keys, head_pair)
        values_slot = slot_view(slot_values, head_pair)
        out_slot = to_slots(
            mixed_gradient[:, quad_cols * head_pair : quad_cols * (head_pair + 1)].reshape(
                local_rows, 2, 2, HEAD_SIZE
            )
        )
        delta_local = jnp.transpose(
            delta_rows[:, 4 * head_pair : 4 * head_pair + 4].reshape(local_rows, 2, 2), (1, 2, 0)
        )
        delta_low = lax.dynamic_slice_in_dim(delta_local, low_offset, block_rows, 2)
        delta_high = lax.dynamic_slice_in_dim(delta_local, high_offset, block_rows, 2)
        delta_slot = jnp.where(high_mask, delta_high[None, ..., None], delta_low[None, ..., None])
        probabilities = jnp.exp(slot_scores(query_slot, keys_slot) - log_totals[head_pair])
        weights_b = probabilities.astype(jnp.bfloat16)
        value_slot_grad = jnp.einsum(
            "sjeqk,sqjed->skjd", weights_b, out_slot, preferred_element_type=jnp.float32
        ).reshape(slot_count, block_rows * pair_cols)
        prob_grad = jnp.einsum(
            "sqjed,skjd->sjeqk", out_slot, values_slot, preferred_element_type=jnp.float32
        )
        score_grad = (probabilities * (prob_grad - delta_slot)).astype(jnp.bfloat16)
        query_slot_grad = (
            jnp.einsum(
                "sjeqk,skjd->sqjed", score_grad, keys_slot, preferred_element_type=jnp.float32
            )
            * scale_factor
        )
        query_grads.append(from_slots(query_slot_grad).reshape(local_rows, 4, HEAD_SIZE))
        key_slot_grad = (
            jnp.einsum(
                "sjeqk,sqjed->skjd", score_grad, query_slot, preferred_element_type=jnp.float32
            )
            * scale_factor
        ).reshape(slot_count, block_rows * pair_cols)
        key_grads.append(
            jnp.dot(slot_to_row.T, key_slot_grad, precision=lax.Precision.HIGHEST).reshape(
                block_count * block_rows, pair_cols
            )
        )
        value_grads.append(
            jnp.dot(slot_to_row.T, value_slot_grad, precision=lax.Precision.HIGHEST).reshape(
                block_count * block_rows, pair_cols
            )
        )
    local_key_gradient, own_value_grad = (
        lax.psum_scatter(
            jnp.concatenate(key_grads, axis=1).astype(jnp.bfloat16),
            "ctx",
            scatter_dimension=0,
            tiled=True,
        ).astype(jnp.float32),
        lax.psum_scatter(
            jnp.concatenate(value_grads, axis=1).astype(jnp.bfloat16),
            "ctx",
            scatter_dimension=0,
            tiled=True,
        ).astype(jnp.float32),
    )
    query_back = rotary_backward(
        jnp.concatenate(query_grads, axis=1), cosine_table, sine_values_table
    )
    query_gain_grad = jnp.sum(query_back * query_normed, axis=(0, 1))
    query_pre_grad = (
        root_mean_square_backward(query_back, query_normed, query_scale, query_gain)
        .astype(jnp.bfloat16)
        .reshape(local_rows, HQ * HEAD_SIZE)
    )
    key_backward_pass = rotary_backward(
        local_key_gradient.reshape(local_rows, KEY_VALUE_HEADS, HEAD_SIZE),
        cosine_table,
        sine_values_table,
    )
    key_gain_grad = jnp.sum(key_backward_pass * key_after_norm, axis=(0, 1))
    key_before_norm_gradient = (
        root_mean_square_backward(key_backward_pass, key_after_norm, key_norm_scale, key_norm_gain)
        .astype(jnp.bfloat16)
        .reshape(local_rows, KEY_VALUE_HEADS * HEAD_SIZE)
    )
    value_gradient_second = own_value_grad.astype(jnp.bfloat16)
    attn_in_grad = (
        right_dot(query_pre_grad, full_query)
        + right_dot(key_before_norm_gradient, full_key)
        + right_dot(value_gradient_second, full_value)
    )
    first_gain_grad = jnp.sum(attn_in_grad * first_normed, axis=0)
    input_grad = mid_grad + root_mean_square_backward(
        attn_in_grad, first_normed, first_scale, first_gain
    )
    attn_cols, mixed_cols, mlp_cols, hidden_cols = (
        lax.all_to_all(attention_input, "fsdp", split_axis=1, concat_axis=0, tiled=True),
        lax.all_to_all(mixed_b, "fsdp", split_axis=1, concat_axis=0, tiled=True),
        lax.all_to_all(mlp_in, "fsdp", split_axis=1, concat_axis=0, tiled=True),
        lax.all_to_all(hidden, "fsdp", split_axis=1, concat_axis=0, tiled=True),
    )
    cot_rows, gate_rows, up_rows, mid_rows, query_rows, key_rows, value_row_block = (
        lax.all_gather(own_cotangent, "fsdp", axis=0, tiled=True),
        lax.all_gather(gate_grad, "fsdp", axis=0, tiled=True),
        lax.all_gather(up_grad, "fsdp", axis=0, tiled=True),
        lax.all_gather(mid_grad_b, "fsdp", axis=0, tiled=True),
        lax.all_gather(query_pre_grad, "fsdp", axis=0, tiled=True),
        lax.all_gather(key_before_norm_gradient, "fsdp", axis=0, tiled=True),
        lax.all_gather(value_gradient_second, "fsdp", axis=0, tiled=True),
    )
    query_shard = left_dot(attn_cols, query_rows)
    key_shard = left_dot(attn_cols, key_rows)
    value_shard = left_dot(attn_cols, value_row_block)
    output_shard = left_dot(mixed_cols, mid_rows)
    gate_shard = left_dot(mlp_cols, gate_rows)
    up_shard = left_dot(mlp_cols, up_rows)
    down_shard = left_dot(hidden_cols, cot_rows)
    first_shard, second_shard, query_gain_shard, key_gain_shard = (
        lax.psum_scatter(first_gain_grad, "fsdp", scatter_dimension=0, tiled=True),
        lax.psum_scatter(second_gain_grad, "fsdp", scatter_dimension=0, tiled=True),
        lax.psum_scatter(query_gain_grad, "fsdp", scatter_dimension=0, tiled=True),
        lax.psum_scatter(key_gain_grad, "fsdp", scatter_dimension=0, tiled=True),
    )
    (
        query_total,
        key_total,
        value_total,
        output_total,
        gate_total,
        up_total,
        down_total,
        first_total,
        second_total,
        query_gain_total,
        key_gain_total,
    ) = (
        lax.psum(query_shard.astype(jnp.bfloat16), "ctx").astype(jnp.float32),
        lax.psum(key_shard.astype(jnp.bfloat16), "ctx").astype(jnp.float32),
        lax.psum(value_shard.astype(jnp.bfloat16), "ctx").astype(jnp.float32),
        lax.psum(output_shard.astype(jnp.bfloat16), "ctx").astype(jnp.float32),
        lax.psum(gate_shard.astype(jnp.bfloat16), "ctx").astype(jnp.float32),
        lax.psum(up_shard.astype(jnp.bfloat16), "ctx").astype(jnp.float32),
        lax.psum(down_shard.astype(jnp.bfloat16), "ctx").astype(jnp.float32),
        lax.psum(first_shard.astype(jnp.bfloat16), "ctx").astype(jnp.float32),
        lax.psum(second_shard.astype(jnp.bfloat16), "ctx").astype(jnp.float32),
        lax.psum(query_gain_shard.astype(jnp.bfloat16), "ctx").astype(jnp.float32),
        lax.psum(key_gain_shard.astype(jnp.bfloat16), "ctx").astype(jnp.float32),
    )
    return (
        layer_output[None],
        input_grad[None],
        query_total,
        key_total,
        value_total,
        output_total,
        gate_total,
        up_total,
        down_total,
        first_total,
        second_total,
        query_gain_total,
        key_gain_total,
    )


def solution(mesh):
    in_specs = (
        P("fsdp", "ctx", None),
        P("fsdp", "ctx", None),
        P("fsdp", None),
        P("fsdp", None),
        P("fsdp", None),
        P("fsdp", None),
        P("fsdp", None),
        P("fsdp", None),
        P("fsdp", None),
        P("fsdp", None),
        P(),
        P(),
        P(),
        P(),
    )
    out_specs = (
        P("fsdp", "ctx", None),
        P("fsdp", "ctx", None),
        P("fsdp", None),
        P("fsdp", None),
        P("fsdp", None),
        P("fsdp", None),
        P("fsdp", None),
        P("fsdp", None),
        P("fsdp", None),
        P("fsdp"),
        P("fsdp"),
        P("fsdp"),
        P("fsdp"),
    )
    return jax.shard_map(
        on_device, mesh=mesh, in_specs=in_specs, out_specs=out_specs, check_vma=False
    )
```

profile of v0, /device:TPU:0, one launch (start us, length us, event | category | flops | bytes accessed | tf_op | source)
XLA Modules:
  0.0 1803.7 jit_solution(14802168267665761187)
XLA Ops:
  11.7 29.4 %all-gather.22.cloned.1.call-done = bf16[1024,1024]{1,0:T(8,128)(2,1)} async-done(((bf16[256,1024]{1,0:T(8,128)(2,1)}), bf16[1024,1024]{1,0:T(8,128)(2,1)}) %all-gather.22.cloned.1.call-update) | async-done | bytes 2097168 | tf_op jit(solution)/shard_map/all_gather | solution.py:172
  46.8 26.0 %all-gather.18.cloned.1.call-done = bf16[1024,1024]{1,0:T(8,128)(2,1)} async-done(((bf16[256,1024]{1,0:T(8,128)(2,1)}), bf16[1024,1024]{1,0:T(8,128)(2,1)}) %all-gather.18.cloned.1.call-update) | async-done | bytes 2097168 | tf_op jit(solution)/shard_map/all_gather | solution.py:173
  83.2 38.4 %all-gather.26.cloned.1.call-done = bf16[1024,2048]{1,0:T(8,128)(2,1)} async-done(((bf16[256,2048]{1,0:T(8,128)(2,1)}), bf16[1024,2048]{1,0:T(8,128)(2,1)}) %all-gather.26.cloned.1.call-update) | async-done | bytes 4194320 | tf_op jit(solution)/shard_map/all_gather | solution.py:171
  135.6 95.3 %all-gather.24.cloned.1.call-done = bf16[4096,1024]{1,0:T(8,128)(2,1)} async-done(((bf16[128,1024]{1,0:T(8,128)(2,1)}), bf16[4096,1024]{1,0:T(8,128)(2,1)}) %all-gather.24.cloned.1.call-update) | async-done | bytes 8388624 | tf_op jit(solution)/shard_map/all_gather | solution.py:200
  230.9 24.0 %gather_fusion.1 = bf16[4160,1024]{1,0:T(8,128)(2,1)} fusion(bf16[4096,1024]{1,0:T(8,128)(2,1)} %all-gather.24.cloned.1.call-done, s32[5120]{0:T(1024)S(1)} %pad_clamp_fusion), kind=kCustom, calls=%fused_computation.1 | custom fusion | bytes 17056000 | tf_op jit(solution)/shard_map/gather | solution.py:203
  265.7 9.3 fusion.44
  288.0 9.2 fusion.34
  297.3 7.5 fusion.30
  304.8 16.0 exponential_reduce_fusion.3
  321.6 14.0 exponential_reduce_fusion.2
  336.4 23.9 %gather_fusion = bf16[4160,1024]{1,0:T(8,128)(2,1)} fusion(bf16[4096,1024]{1,0:T(8,128)(2,1)} %all-gather.20.cloned.1.call-done, s32[5120]{0:T(1024)S(1)} %pad_clamp_fusion), kind=kCustom, calls=%fused_computation | custom fusion | bytes 17056000 | tf_op jit(solution)/shard_map/gather | solution.py:204
  387.2 9.9 fusion.144
  397.1 6.7 fusion.138
  410.5 17.1 select_reduce_fusion.15
  439.0 8.9 all-gather.30.cloned.1.call-done
  452.8 61.6 %all-gather.32.cloned.1.call-done = bf16[1024,3072]{1,0:T(8,128)(2,1)} async-done(((bf16[256,3072]{1,0:T(8,128)(2,1)}), bf16[1024,3072]{1,0:T(8,128)(2,1)}) %all-gather.32.cloned.1.call-update) | async-done | bytes 6291472 | tf_op jit(solution)/shard_map/all_gather | solution.py:176
  519.4 61.6 %all-gather.34.cloned.1.call-done = bf16[3072,1024]{1,0:T(8,128)(2,1)} async-done(((bf16[768,1024]{1,0:T(8,128)(2,1)}), bf16[3072,1024]{1,0:T(8,128)(2,1)}) %all-gather.34.cloned.1.call-update) | async-done | bytes 6291472 | tf_op jit(solution)/shard_map/all_gather | solution.py:177
  581.0 7.1 multiply_convert_fusion
  623.9 6.9 fusion.1
  640.4 6.8 reshape.974
  661.9 6.9 fusion.3
  678.4 6.8 reshape.972
  699.9 6.9 fusion.5
  716.4 7.1 reshape.970
  734.9 7.7 fusion.7
  750.5 6.8 reshape.968
  775.3 12.0 copy.447
  799.6 6.7 reshape.985
  825.1 6.7 reshape.983
  850.9 6.7 reshape.981
  876.3 6.7 reshape.979
  890.3 7.2 pad_maximum_fusion.1
  898.2 7.7 fusion.140
  905.9 7.0 fusion.134
  918.0 16.9 select_reduce_fusion.7
  939.9 51.9 %reduce-scatter.7.cloned.1.call-done = bf16[128,1024]{1,0:T(8,128)(2,1)} async-done(((bf16[4096,1024]{1,0:T(8,128)(2,1)}), bf16[128,1024]{1,0:T(8,128)(2,1)}) %reduce-scatter.7.cloned.1.call-update) | async-done | bytes 262160
  1000.4 10.0 all-to-all-done.3
  1015.5 177.2 %reduce-scatter.5.cloned.1.call-done = bf16[128,1024]{1,0:T(8,128)(2,1)} async-done(((bf16[4096,1024]{1,0:T(8,128)(2,1)}), bf16[128,1024]{1,0:T(8,128)(2,1)}) %reduce-scatter.5.cloned.1.call-update) | async-done | bytes 262160 | tf_op jit(solution)/shard_map/reduce_scatter | solution.py:335
  1192.7 16.9 all-gather.48.cloned.1.call-done
  1216.4 16.5 all-gather.42.cloned.1.call-done
  1239.6 24.5 %all-gather.36.cloned.1.call-done = bf16[512,2048]{0,1:T(8,128)(2,1)} async-done(((bf16[128,2048]{0,1:T(8,128)(2,1)}), bf16[512,2048]{0,1:T(8,128)(2,1)}) %all-gather.36.cloned.1.call-update) | async-done | bytes 2097168 | tf_op jit(solution)/shard_map/all_gather | solution.py:383
  1267.4 37.5 %all-gather.44.cloned.1.call-done = bf16[512,3072]{1,0:T(8,128)(2,1)} async-done(((bf16[128,3072]{1,0:T(8,128)(2,1)}), bf16[512,3072]{1,0:T(8,128)(2,1)}) %all-gather.44.cloned.1.call-update) | async-done | bytes 3145744 | tf_op jit(solution)/shard_map/all_gather | solution.py:380
  1309.0 36.2 %all-gather.46.cloned.1.call-done = bf16[512,3072]{1,0:T(8,128)(2,1)} async-done(((bf16[128,3072]{1,0:T(8,128)(2,1)}), bf16[512,3072]{1,0:T(8,128)(2,1)}) %all-gather.46.cloned.1.call-update) | async-done | bytes 3145744 | tf_op jit(solution)/shard_map/all_gather | solution.py:381
  1349.2 19.0 %all-gather.38.cloned.1.call-done = bf16[512,1024]{0,1:T(8,128)(2,1)} async-done(((bf16[128,1024]{0,1:T(8,128)(2,1)}), bf16[512,1024]{0,1:T(8,128)(2,1)}) %all-gather.38.cloned.1.call-update) | async-done | bytes 1048592 | tf_op jit(solution)/shard_map/all_gather | solution.py:384
  1370.7 21.6 %all-gather.40.cloned.1.call-done = bf16[512,1024]{1,0:T(8,128)(2,1)} async-done(((bf16[128,1024]{1,0:T(8,128)(2,1)}), bf16[512,1024]{1,0:T(8,128)(2,1)}) %all-gather.40.cloned.1.call-update) | async-done | bytes 1048592 | tf_op jit(solution)/shard_map/all_gather | solution.py:385
  1406.2 11.6 all-reduce.4
  1418.1 96.3 %all-reduce.5 = (bf16[256]{0:T(256)(128)(2,1)S(1)}, bf16[256]{0:T(256)(128)(2,1)S(1)}, bf16[32]{0:T(256)(128)(2,1)S(1)}, bf16[32]{0:T(256)(128)(2,1)S(1)}) all-reduce(bf16[256]{0:T(256)(128)(2,1)S(1)} %dynamic-slice.71, bf16[256]{0:T(256)(128)(2,1)S(1)} %dynamic-slice.70, ...), channel_id=1, replica_groups=mesh['ctx'=32,'fsdp'=4] {'ctx'}, use_global_device_ids=true, to_apply=%region_62.63 | all-reduce | flops 576 | bytes 2304 | tf_op jit(solution)/shard_map/psum | solution.py:420
  1517.7 265.4 %all-reduce.9.cloned.1.call-done = (bf16[256,2048]{1,0:T(8,128)(2,1)}, bf16[256,1024]{1,0:T(8,128)(2,1)}, bf16[256,1024]{1,0:T(8,128)(2,1)}, bf16[512,1024]{1,0:...) async-done(((bf16[256,2048]{1,0:T(8,128)(2,1)}, bf16[256,1024]{1,0:T(8,128)(2,1)}, bf16[256,1024]{1,0:T(8,128)(2,1)}, ...) | async-done | bytes 7864336 | tf_op jit(solution)/shard_map/psum | solution.py:413
  (556 shorter events, 399.2 us)
Async XLA Ops:
  7.2 36.8 %copy-start.8 = (bf16[1,128,1024]{2,1,0:T(8,128)(2,1)S(1)}, bf16[1,128,1024]{2,1,0:T(8,128)(2,1)}, u32[]{:S(2)}) copy-start(bf16[1,128,1024]{2,1,0:T(8,128)(2,1)} %param.14) | copy-start | bytes 786436
  7.2 36.8 %copy-start.78 = (f32[1024]{0:T(1024)S(1)}, f32[1024]{0:T(1024)}, u32[]{:S(2)}) copy-start(f32[1024]{0:T(1024)} %param.24) | copy-start | bytes 12292
  7.2 33.9 %all-gather.22.cloned.1.call-start = ((), (), s32[]{:S(2)}) async-start(), calls=%async_computation.8 | async-start | bytes 2621440 | tf_op jit(solution)/shard_map/all_gather | solution.py:172
  7.9 64.9 %all-gather.18.cloned.1.call-start = ((), (), s32[]{:S(2)}) async-start(), calls=%async_computation.6 | async-start | bytes 2621440 | tf_op jit(solution)/shard_map/all_gather | solution.py:173
  8.7 36.9 %copy-start.114 = (f32[128]{0:T(128)S(1)}, f32[128]{0:T(128)}, u32[]{:S(2)}) copy-start(f32[128]{0:T(128)} %param.27) | copy-start | bytes 1540
  8.7 112.9 %all-gather.26.cloned.1.call-start = ((), (), s32[]{:S(2)}) async-start(), calls=%async_computation.10 | async-start | bytes 5242880 | tf_op jit(solution)/shard_map/all_gather | solution.py:171
  9.4 221.4 %all-gather.24.cloned.1.call-start = ((), (), s32[]{:S(2)}) async-start(), calls=%async_computation.9 | async-start | bytes 8650752 | tf_op jit(solution)/shard_map/all_gather | solution.py:200
  11.5 116.5 %copy-start.109 = (f32[128]{0:T(128)}, f32[128]{0:T(128)S(1)}, u32[]{:S(2)}) copy-start(f32[128]{0:T(128)S(1)} %add_rsqrt_fusion.3) | copy-start | bytes 1540
  11.7 121.1 %copy-start.44 = (f32[128,64]{0,1:T(8,128)}, f32[128,64]{0,1:T(8,128)S(1)}, u32[]{:S(2)}) copy-start(f32[128,64]{0,1:T(8,128)S(1)} %get-tuple-element.152) | copy-start | bytes 98308
  11.7 121.1 %copy-start.46 = (f32[128,64]{0,1:T(8,128)}, f32[128,64]{0,1:T(8,128)S(1)}, u32[]{:S(2)}) copy-start(f32[128,64]{0,1:T(8,128)S(1)} %get-tuple-element.153) | copy-start | bytes 98308
  46.7 289.7 %all-gather.20.cloned.1.call-start = ((), (), s32[]{:S(2)}) async-start(), calls=%async_computation.7 | async-start | bytes 8650752 | tf_op jit(solution)/shard_map/all_gather | solution.py:201
  75.6 360.2 %all-gather.28.cloned.1.call-start = ((), (), s32[]{:S(2)}) async-start(), calls=%async_computation.11 | async-start | bytes 5242880 | tf_op jit(solution)/shard_map/all_gather | solution.py:174
  76.2 371.7 %all-gather.30.cloned.1.call-start = ((), (), s32[]{:S(2)}) async-start(), calls=%async_computation.12 | async-start | bytes 7864320 | tf_op jit(solution)/shard_map/all_gather | solution.py:175
  76.9 437.5 %all-gather.32.cloned.1.call-start = ((), (), s32[]{:S(2)}) async-start(), calls=%async_computation.13 | async-start | bytes 7864320 | tf_op jit(solution)/shard_map/all_gather | solution.py:176
  77.7 503.3 %all-gather.34.cloned.1.call-start = ((), (), s32[]{:S(2)}) async-start(), calls=%async_computation.14 | async-start | bytes 7864320 | tf_op jit(solution)/shard_map/all_gather | solution.py:177
  78.4 913.5 %reduce-scatter.7.cloned.1.call-start = ((), (), s32[]{:S(2)}) async-start(), calls=%async_computation.23 | async-start | bytes 8650752
  133.3 132.4 %copy-start.88 = (bf16[64,2,2,128]{3,0,2,1:T(8,128)(2,1)}, bf16[64,2,2,128]{3,0,2,1:T(8,128)(2,1)S(1)}, u32[]{:S(2)}) copy-start(bf16[64,2,2,128]{3,0,2,1:T(8,128)(2,1)S(1)} %copy.296) | copy-start | bytes 196612
  133.4 132.3 %copy-start.90 = (bf16[64,2,2,128]{3,0,2,1:T(8,128)(2,1)}, bf16[64,2,2,128]{3,0,2,1:T(8,128)(2,1)S(1)}, u32[]{:S(2)}) copy-start(bf16[64,2,2,128]{3,0,2,1:T(8,128)(2,1)S(1)} %copy.295) | copy-start | bytes 196612
  133.9 154.1 %copy-start.72 = (bf16[64,2,2,128]{3,0,2,1:T(8,128)(2,1)}, bf16[64,2,2,128]{3,0,2,1:T(8,128)(2,1)S(1)}, u32[]{:S(2)}) copy-start(bf16[64,2,2,128]{3,0,2,1:T(8,128)(2,1)S(1)} %copy.309) | copy-start | bytes 196612
  134.0 163.3 %copy-start.74 = (bf16[64,2,2,128]{3,0,2,1:T(8,128)(2,1)}, bf16[64,2,2,128]{3,0,2,1:T(8,128)(2,1)S(1)}, u32[]{:S(2)}) copy-start(bf16[64,2,2,128]{3,0,2,1:T(8,128)(2,1)S(1)} %copy.317) | copy-start | bytes 196612
  134.1 163.1 %copy-start.76 = (bf16[64,2,2,128]{3,0,2,1:T(8,128)(2,1)}, bf16[64,2,2,128]{3,0,2,1:T(8,128)(2,1)S(1)}, u32[]{:S(2)}) copy-start(bf16[64,2,2,128]{3,0,2,1:T(8,128)(2,1)S(1)} %copy.316) | copy-start | bytes 196612
  438.8 160.6 %copy-start.6 = (f32[128,1024]{1,0:T(8,128)}, f32[128,1024]{1,0:T(8,128)S(1)}, u32[]{:S(2)}) copy-start(f32[128,1024]{1,0:T(8,128)S(1)} %get-tuple-element.175) | copy-start | bytes 1572868
  438.8 160.6 %copy-start.112 = (f32[128]{0:T(128)}, f32[128]{0:T(128)S(1)}, u32[]{:S(2)}) copy-start(f32[128]{0:T(128)S(1)} %add_rsqrt_fusion.2) | copy-start | bytes 1540
  439.0 75.5 %copy-start.19 = (bf16[128,1024]{1,0:T(8,128)(2,1)}, bf16[128,1024]{1,0:T(8,128)(2,1)S(1)}, u32[]{:S(2)}) copy-start(bf16[128,1024]{1,0:T(8,128)(2,1)S(1)} %multiply_convert_fusion.5) | copy-start | bytes 786436
  452.8 128.2 %copy-start.31 = (bf16[1,128,1024]{2,1,0:T(8,128)(2,1)S(1)}, bf16[1,128,1024]{2,1,0:T(8,128)(2,1)}, u32[]{:S(2)}) copy-start(bf16[1,128,1024]{2,1,0:T(8,128)(2,1)} %param.15) | copy-start | bytes 786436
  787.3 405.4 %reduce-scatter.5.cloned.1.call-start = ((), (), s32[]{:S(2)}) async-start(), calls=%async_computation.15 | async-start | bytes 8650752 | tf_op jit(solution)/shard_map/reduce_scatter | solution.py:335
  897.6 312.1 %all-gather.48.cloned.1.call-start = ((), (), s32[]{:S(2)}) async-start(), calls=%async_computation.22 | async-start | bytes 1310720 | tf_op jit(solution)/shard_map/all_gather | solution.py:379
  898.2 334.8 %all-gather.42.cloned.1.call-start = ((), (), s32[]{:S(2)}) async-start(), calls=%async_computation.19 | async-start | bytes 1310720 | tf_op jit(solution)/shard_map/all_gather | solution.py:382
  917.7 346.4 %all-gather.36.cloned.1.call-start = ((), (), s32[]{:S(2)}) async-start(), calls=%async_computation.16 | async-start | bytes 2621440 | tf_op jit(solution)/shard_map/all_gather | solution.py:383
  937.1 56.1 %copy-start.15 = (f32[128,8,128]{0,2,1:T(8,128)S(1)}, f32[128,8,128]{0,2,1:T(8,128)}, u32[]{:S(2)}) copy-start(f32[128,8,128]{0,2,1:T(8,128)} %copy-done.14) | copy-start | bytes 1572868
  937.2 56.1 %copy-start.87 = (f32[128,8]{0,1:T(8,128)S(1)}, f32[128,8]{0,1:T(8,128)}, u32[]{:S(2)}) copy-start(f32[128,8]{0,1:T(8,128)} %copy-done.86) | copy-start | bytes 12292
  937.2 56.1 %copy-start.115 = (f32[128]{0:T(128)S(1)}, f32[128]{0:T(128)}, u32[]{:S(2)}) copy-start(f32[128]{0:T(128)} %param.27) | copy-start | bytes 1540
  937.6 56.7 %copy-start.29 = (bf16[128,3072]{1,0:T(8,128)(2,1)S(1)}, bf16[128,3072]{1,0:T(8,128)(2,1)}, u32[]{:S(2)}) copy-start(bf16[128,3072]{1,0:T(8,128)(2,1)} %get-tuple-element.107) | copy-start | bytes 2359300
  938.7 366.2 %all-gather.44.cloned.1.call-start = ((), (), s32[]{:S(2)}) async-start(), calls=%async_computation.20 | async-start | bytes 3932160 | tf_op jit(solution)/shard_map/all_gather | solution.py:380
  939.3 405.9 %all-gather.46.cloned.1.call-start = ((), (), s32[]{:S(2)}) async-start(), calls=%async_computation.21 | async-start | bytes 3932160 | tf_op jit(solution)/shard_map/all_gather | solution.py:381
  939.9 58.9 %copy-start.9 = (bf16[1,128,1024]{2,1,0:T(8,128)(2,1)S(1)}, bf16[1,128,1024]{2,1,0:T(8,128)(2,1)}, u32[]{:S(2)}) copy-start(bf16[1,128,1024]{2,1,0:T(8,128)(2,1)} %param.14) | copy-start | bytes 786436
  939.9 428.3 %all-gather.38.cloned.1.call-start = ((), (), s32[]{:S(2)}) async-start(), calls=%async_computation.17 | async-start | bytes 1310720 | tf_op jit(solution)/shard_map/all_gather | solution.py:384
  995.2 15.1 all-to-all-start.3
  1010.4 202.7 %all-to-all-start.1 = ((bf16[128,4,512]{2,0,1:T(8,128)(2,1)}), bf16[128,4,512]{2,0,1:T(8,128)(2,1)S(1)}, u32[]{:S(2)}, u32[]{:S(2)}) async-start(bf16[128,4,512]{2,0,1:T(8,128)(2,1)} %pad_maximum_fusion.5), calls=%async_computation.2 | async-start | bytes 1048576 | tf_op jit(solution)/shard_map/all_to_all | solution.py:374
  1013.8 378.5 %all-gather.40.cloned.1.call-start = ((), (), s32[]{:S(2)}) async-start(), calls=%async_computation.18 | async-start | bytes 1310720 | tf_op jit(solution)/shard_map/all_gather | solution.py:385
  1213.0 22.9 %all-to-all-start = ((bf16[128,4,256]{2,0,1:T(8,128)(2,1)}), bf16[128,4,256]{2,0,1:T(8,128)(2,1)S(1)}, u32[]{:S(2)}, u32[]{:S(2)}) async-start(bf16[128,4,256]{2,0,1:T(8,128)(2,1)} %fusion.167), calls=%async_computation.1 | async-start | bytes 524288 | tf_op jit(solution)/shard_map/all_to_all | solution.py:373
  1235.9 31.5 %all-to-all-start.2 = ((bf16[128,4,256]{2,0,1:T(8,128)(2,1)}), bf16[128,4,256]{2,0,1:T(8,128)(2,1)S(1)}, u32[]{:S(2)}, u32[]{:S(2)}) async-start(bf16[128,4,256]{2,0,1:T(8,128)(2,1)} %bitcast.339), calls=%async_computation.3 | async-start | bytes 524288 | tf_op jit(solution)/shard_map/all_to_all | solution.py:375
  1239.3 543.7 %all-reduce.9.cloned.1.call-start = ((), (), s32[]{:S(2)}) async-start(), calls=%async_computation.24 | async-start | bytes 15728640 | tf_op jit(solution)/shard_map/psum | solution.py:413
  1403.1 113.4 %copy-start.23 = (f32[128,1024]{1,0:T(8,128)S(1)}, f32[128,1024]{1,0:T(8,128)}, u32[]{:S(2)}) copy-start(f32[128,1024]{1,0:T(8,128)} %copy-done.22) | copy-start | bytes 1572868
  1403.1 113.4 %copy-start.32 = (bf16[1,128,1024]{2,1,0:T(8,128)(2,1)S(1)}, bf16[1,128,1024]{2,1,0:T(8,128)(2,1)}, u32[]{:S(2)}) copy-start(bf16[1,128,1024]{2,1,0:T(8,128)(2,1)} %param.15) | copy-start | bytes 786436
  1403.1 113.4 %copy-start.85 = (f32[1024]{0:T(1024)S(1)}, f32[1024]{0:T(1024)}, u32[]{:S(2)}) copy-start(f32[1024]{0:T(1024)} %param.25) | copy-start | bytes 12292
  1403.2 113.4 %copy-start.113 = (f32[128]{0:T(128)S(1)}, f32[128]{0:T(128)}, u32[]{:S(2)}) copy-start(f32[128]{0:T(128)} %copy-done.112) | copy-start | bytes 1540
  1403.2 113.4 %copy-start.119 = (f32[128]{0:T(128)S(1)}, f32[128]{0:T(128)}, u32[]{:S(2)}) copy-start(f32[128]{0:T(128)} %copy-done.118) | copy-start | bytes 1540
  (106 other events, 762.1 us)
Sparse Core Ops, SparseCore 0:
  9.7 31.3 all-gather.21
  42.8 29.9 all-gather.17
  74.5 47.0 all-gather.25
  125.1 105.6 all-gather.23
  234.4 101.9 all-gather.19
  337.9 43.7 all-gather.27
  383.4 64.4 all-gather.29
  449.6 64.8 all-gather.31
  516.1 64.8 all-gather.33
  787.5 204.3 reduce-scatter.6
  994.3 198.3 reduce-scatter.4
  1194.2 15.3 all-gather.47
  1211.3 21.6 all-gather.41
  1235.1 29.0 all-gather.35
  1265.6 39.2 all-gather.43
  1306.5 38.6 all-gather.45
  1346.7 21.4 all-gather.37
  1369.7 22.5 all-gather.39
  1396.6 386.4 all-reduce.8
where the time goes:
time: 1810 us; the launch traced here: 1800 us
  waiting for transfers between devices  1010 us (56%)
  local copies, waits for them, and re-layouts  302 us (17%)
  matrix products  291 us (16%)
  blocking collectives  108 us (6%)
  other arithmetic  61.9 us (3%)
  between operations  20.5 us (1%)
    psum x1, waiting for transfers between devices, on_device(): lax.psum(query_shard.astype(jnp.bfloat16), 'ctx').astype(jnp.float32)  265 us
    reduce_scatter x1, waiting for transfers between devices, on_device(): lax.psum_scatter(jnp.concatenate(value_grads, axis=1).astype(jnp.bfloat16...  177 us
    psum x1, blocking collectives, on_device(): lax.psum(first_shard.astype(jnp.bfloat16), 'ctx').astype(jnp.float32)  96.3 us
    all_gather x1, waiting for transfers between devices, on_device(): lax.all_gather(own_keys, 'ctx', axis=0, tiled=True)  95.3 us
    all_gather x1, waiting for transfers between devices, on_device(): lax.all_gather(down_weight, 'fsdp', axis=0, tiled=True)  61.6 us
    all_gather x1, waiting for transfers between devices, on_device(): lax.all_gather(up_weight, 'fsdp', axis=0, tiled=True)  61.6 us
    unnamed x20, waiting for transfers between devices  58.3 us
    dot_general x4, matrix products, slot_scores(): jnp.einsum('sqjed,skjd->sjeqk', query_slot, keys_slot, preferred_element_...  42.1 us
  transfers between devices with their start and end apart: 23, of which 19 were waited for; matrix products, arithmetic and copies ran while one was open for 24% of the time, Pallas kernels for 0%

commit v1 on v0

v1 whole, which is shorter than its diff:
```python
import math

import jax
import jax.numpy as jnp
from jax import lax
from jax.sharding import PartitionSpec as P

HQ = 16
KEY_VALUE_HEADS = 8
HEAD_SIZE = 128


EPSILON = 1e-06
THETA = 1000000.0
MASKED = -1e30


def rms_apply(values, norm_gain):
    row_scale = lax.rsqrt(jnp.mean(values * values, axis=-1, keepdims=True) + EPSILON)
    normed = values * row_scale
    return (normed * norm_gain, normed, row_scale)


def root_mean_square_backward(gradient, normed, row_scale, norm_gain):
    normed_grad = gradient * norm_gain
    return row_scale * (
        normed_grad - normed * jnp.mean(normed_grad * normed, axis=-1, keepdims=True)
    )


def rope_tables(positions, head_width):
    half_width = head_width // 2
    inverse_freq = jnp.power(THETA, -2.0 * jnp.arange(half_width, dtype=jnp.float32) / head_width)
    angles = positions.astype(jnp.float32)[:, None] * inverse_freq[None, :]
    return (jnp.cos(angles)[:, None, :], jnp.sin(angles)[:, None, :])


def rotary_apply(values, cosine_table, sine_values_table):
    half_width = values.shape[-1] // 2
    front_half = values[..., :half_width]
    back_half = values[..., half_width:]
    return jnp.concatenate(
        [
            front_half * cosine_table - back_half * sine_values_table,
            back_half * cosine_table + front_half * sine_values_table,
        ],
        axis=-1,
    )


def rotary_backward(gradient, cosine_table, sine_values_table):
    half_width = gradient.shape[-1] // 2
    front_half = gradient[..., :half_width]
    back_half = gradient[..., half_width:]
    return jnp.concatenate(
        [
            front_half * cosine_table + back_half * sine_values_table,
            back_half * cosine_table - front_half * sine_values_table,
        ],
        axis=-1,
    )


def left_dot(left_side, right_side):
    return lax.dot_general(
        left_side, right_side, (((0,), (0,)), ((), ())), preferred_element_type=jnp.float32
    )


def right_dot(left_side, right_side):
    return lax.dot_general(
        left_side, right_side, (((1,), (1,)), ((), ())), preferred_element_type=jnp.float32
    )


def on_device(
    layer_input,
    cotangent,
    block_order,
    query_weight,
    key_projection,
    value_projection,
    output_weight,
    gate_weight,
    up_weight,
    down_weight,
    first_gain,
    second_gain,
    query_gain,
    key_norm_gain,
):
    local_rows = layer_input.shape[1]
    block_rows = local_rows // 2
    ctx_size = lax.axis_size("ctx")
    halves = ctx_size // HQ
    half_devices = ctx_size // halves
    order_row = block_order[0]
    device_place = lax.axis_index("ctx")
    my_half = device_place // half_devices
    all_positions = (
        order_row[:, None] * block_rows + jnp.arange(block_rows, dtype=jnp.int32)[None, :]
    ).reshape(-1)
    own_positions = lax.dynamic_slice_in_dim(all_positions, device_place * local_rows, local_rows)
    cosine_table, sine_values_table = rope_tables(own_positions, HEAD_SIZE)
    scale_factor = 1.0 / math.sqrt(HEAD_SIZE)
    half_rows = half_devices * local_rows
    query_positions = lax.dynamic_slice_in_dim(all_positions, my_half * half_rows, half_rows)
    allowed = all_positions[None, :] <= query_positions[:, None]
    half_select = (jnp.arange(halves, dtype=jnp.int32) == my_half)[:, None, None, None]

    def to_heads(per_head):
        by_head = jnp.transpose(per_head, (1, 0, 2))
        return jnp.where(half_select, by_head[None], jnp.zeros_like(by_head)[None]).reshape(
            ctx_size, local_rows, per_head.shape[-1]
        )

    def gather_half(received):
        return lax.dynamic_slice_in_dim(received, my_half * half_devices, half_devices, 0).reshape(
            half_rows, received.shape[-1]
        )

    def from_heads(per_head):
        blocks = per_head.reshape(half_devices, local_rows, per_head.shape[-1])
        return jnp.where(half_select, blocks[None], jnp.zeros_like(blocks)[None]).reshape(
            ctx_size, local_rows, per_head.shape[-1]
        )

    def own_heads(received):
        mine = lax.dynamic_slice_in_dim(received, my_half * half_devices, half_devices, 0)
        return jnp.transpose(mine, (1, 0, 2))

    def exchange(values):
        return lax.all_to_all(values, "ctx", split_axis=0, concat_axis=0, tiled=True)

    full_query, full_key, full_value, full_output, full_gate, full_up, full_down = (
        lax.all_gather(query_weight, "fsdp", axis=0, tiled=True),
        lax.all_gather(key_projection, "fsdp", axis=0, tiled=True),
        lax.all_gather(value_projection, "fsdp", axis=0, tiled=True),
        lax.all_gather(output_weight, "fsdp", axis=0, tiled=True),
        lax.all_gather(gate_weight, "fsdp", axis=0, tiled=True),
        lax.all_gather(up_weight, "fsdp", axis=0, tiled=True),
        lax.all_gather(down_weight, "fsdp", axis=0, tiled=True),
    )
    input_f32 = layer_input[0].astype(jnp.float32)
    gained, first_normed, first_scale = rms_apply(input_f32, first_gain)
    attention_input = gained.astype(jnp.bfloat16)
    query_pre = jnp.dot(attention_input, full_query, preferred_element_type=jnp.float32).reshape(
        local_rows, HQ, HEAD_SIZE
    )
    query_gained, query_normed, query_scale = rms_apply(query_pre, query_gain)
    query_rotated = rotary_apply(query_gained, cosine_table, sine_values_table).astype(jnp.bfloat16)
    key_before_norm = jnp.dot(
        attention_input, full_key, preferred_element_type=jnp.float32
    ).reshape(local_rows, KEY_VALUE_HEADS, HEAD_SIZE)
    key_after_gain, key_after_norm, key_norm_scale = rms_apply(key_before_norm, key_norm_gain)
    own_keys = rotary_apply(key_after_gain, cosine_table, sine_values_table).astype(jnp.bfloat16)
    own_values = (
        jnp.dot(attention_input, full_value, preferred_element_type=jnp.float32)
        .astype(jnp.bfloat16)
        .reshape(local_rows, KEY_VALUE_HEADS, HEAD_SIZE)
    )
    group = HQ // KEY_VALUE_HEADS
    key_value = jnp.repeat(jnp.concatenate([own_keys, own_values], axis=-1), group, axis=1)
    sent = jnp.concatenate([to_heads(query_rotated), jnp.tile(
        jnp.transpose(key_value, (1, 0, 2)), (halves, 1, 1))], axis=-1)
    received = exchange(sent)
    head_query = gather_half(received[..., :HEAD_SIZE])
    head_key = received[..., HEAD_SIZE : 2 * HEAD_SIZE].reshape(-1, HEAD_SIZE)
    head_value = received[..., 2 * HEAD_SIZE :].reshape(-1, HEAD_SIZE)

    def head_scores():
        raw_scores = (
            jnp.einsum("qd,kd->qk", head_query, head_key, preferred_element_type=jnp.float32)
            * scale_factor
        )
        return jnp.where(allowed, raw_scores, MASKED)

    raw_scores = head_scores()
    row_max = jnp.max(raw_scores, axis=-1, keepdims=True)
    log_total = row_max + jnp.log(jnp.sum(jnp.exp(raw_scores - row_max), axis=-1, keepdims=True))
    weights_b = jnp.exp(raw_scores - log_total).astype(jnp.bfloat16)
    head_mixed = jnp.dot(weights_b, head_value, preferred_element_type=jnp.float32)
    mixed_b = own_heads(exchange(from_heads(head_mixed.astype(jnp.bfloat16)))).reshape(
        local_rows, HQ * HEAD_SIZE
    )
    residual_mid = input_f32 + jnp.dot(mixed_b, full_output, preferred_element_type=jnp.float32)
    gained_mid, second_normed, second_scale = rms_apply(residual_mid, second_gain)
    mlp_in = gained_mid.astype(jnp.bfloat16)
    gate_pre = jnp.dot(mlp_in, full_gate, preferred_element_type=jnp.float32)
    up_pre = jnp.dot(mlp_in, full_up, preferred_element_type=jnp.float32)
    sigmoid_gate = jax.nn.sigmoid(gate_pre)
    silu_gate = gate_pre * sigmoid_gate
    hidden = (silu_gate * up_pre).astype(jnp.bfloat16)
    layer_output = (
        residual_mid + jnp.dot(hidden, full_down, preferred_element_type=jnp.float32)
    ).astype(jnp.bfloat16)
    own_cotangent = cotangent[0]
    hidden_grad = right_dot(own_cotangent, full_down)
    gate_grad = (
        hidden_grad * up_pre * sigmoid_gate * (1.0 + gate_pre * (1.0 - sigmoid_gate))
    ).astype(jnp.bfloat16)
    up_grad = (hidden_grad * silu_gate).astype(jnp.bfloat16)
    mlp_in_grad = right_dot(gate_grad, full_gate) + right_dot(up_grad, full_up)
    second_gain_grad = jnp.sum(mlp_in_grad * second_normed, axis=0)
    mid_grad = own_cotangent.astype(jnp.float32) + root_mean_square_backward(
        mlp_in_grad, second_normed, second_scale, second_gain
    )
    mid_grad_b = mid_grad.astype(jnp.bfloat16)
    mixed_gradient = right_dot(mid_grad_b, full_output).astype(jnp.bfloat16)
    head_out_grad = gather_half(
        exchange(to_heads(mixed_gradient.reshape(local_rows, HQ, HEAD_SIZE)))
    )
    out_grad_f = head_out_grad.astype(jnp.float32)
    delta = jnp.sum(out_grad_f * head_mixed, axis=-1, keepdims=True)
    probabilities = jnp.exp(head_scores() - log_total)
    value_part = left_dot(probabilities.astype(jnp.bfloat16), head_out_grad)
    prob_grad = right_dot(head_out_grad, head_value)
    score_grad = (probabilities * (prob_grad - delta)).astype(jnp.bfloat16)
    query_part = jnp.dot(score_grad, head_key, preferred_element_type=jnp.float32) * scale_factor
    key_part = left_dot(score_grad, head_query) * scale_factor
    returned = exchange(jnp.concatenate([
        from_heads(query_part.astype(jnp.bfloat16)),
        jnp.concatenate([key_part, value_part], axis=-1).astype(jnp.bfloat16).reshape(
            ctx_size, local_rows, 2 * HEAD_SIZE),
    ], axis=-1))
    query_grad_rows = own_heads(returned[..., :HEAD_SIZE]).astype(jnp.float32)
    kv_parts = returned[..., HEAD_SIZE:].astype(jnp.float32).reshape(
        halves, KEY_VALUE_HEADS, group, local_rows, 2 * HEAD_SIZE)
    kv_grad = jnp.transpose(jnp.sum(kv_parts, axis=(0, 2)), (1, 0, 2))
    local_key_gradient = kv_grad[..., :HEAD_SIZE]
    own_value_grad = kv_grad[..., HEAD_SIZE:].reshape(local_rows, KEY_VALUE_HEADS * HEAD_SIZE)
    query_back = rotary_backward(query_grad_rows, cosine_table, sine_values_table)
    query_gain_grad = jnp.sum(query_back * query_normed, axis=(0, 1))
    query_pre_grad = (
        root_mean_square_backward(query_back, query_normed, query_scale, query_gain)
        .astype(jnp.bfloat16)
        .reshape(local_rows, HQ * HEAD_SIZE)
    )
    key_backward_pass = rotary_backward(
        local_key_gradient,
        cosine_table,
        sine_values_table,
    )
    key_gain_grad = jnp.sum(key_backward_pass * key_after_norm, axis=(0, 1))
    key_before_norm_gradient = (
        root_mean_square_backward(key_backward_pass, key_after_norm, key_norm_scale, key_norm_gain)
        .astype(jnp.bfloat16)
        .reshape(local_rows, KEY_VALUE_HEADS * HEAD_SIZE)
    )
    value_gradient_second = own_value_grad.astype(jnp.bfloat16)
    attn_in_grad = (
        right_dot(query_pre_grad, full_query)
        + right_dot(key_before_norm_gradient, full_key)
        + right_dot(value_gradient_second, full_value)
    )
    first_gain_grad = jnp.sum(attn_in_grad * first_normed, axis=0)
    input_grad = mid_grad + root_mean_square_backward(
        attn_in_grad, first_normed, first_scale, first_gain
    )
    attn_cols, mixed_cols, mlp_cols, hidden_cols = (
        lax.all_to_all(attention_input, "fsdp", split_axis=1, concat_axis=0, tiled=True),
        lax.all_to_all(mixed_b, "fsdp", split_axis=1, concat_axis=0, tiled=True),
        lax.all_to_all(mlp_in, "fsdp", split_axis=1, concat_axis=0, tiled=True),
        lax.all_to_all(hidden, "fsdp", split_axis=1, concat_axis=0, tiled=True),
    )
    cot_rows, gate_rows, up_rows, mid_rows, query_rows, key_rows, value_row_block = (
        lax.all_gather(own_cotangent, "fsdp", axis=0, tiled=True),
        lax.all_gather(gate_grad, "fsdp", axis=0, tiled=True),
        lax.all_gather(up_grad, "fsdp", axis=0, tiled=True),
        lax.all_gather(mid_grad_b, "fsdp", axis=0, tiled=True),
        lax.all_gather(query_pre_grad, "fsdp", axis=0, tiled=True),
        lax.all_gather(key_before_norm_gradient, "fsdp", axis=0, tiled=True),
        lax.all_gather(value_gradient_second, "fsdp", axis=0, tiled=True),
    )
    query_shard = left_dot(attn_cols, query_rows)
    key_shard = left_dot(attn_cols, key_rows)
    value_shard = left_dot(attn_cols, value_row_block)
    output_shard = left_dot(mixed_cols, mid_rows)
    gate_shard = left_dot(mlp_cols, gate_rows)
    up_shard = left_dot(mlp_cols, up_rows)
    down_shard = left_dot(hidden_cols, cot_rows)
    first_shard, second_shard, query_gain_shard, key_gain_shard = (
        lax.psum_scatter(first_gain_grad, "fsdp", scatter_dimension=0, tiled=True),
        lax.psum_scatter(second_gain_grad, "fsdp", scatter_dimension=0, tiled=True),
        lax.psum_scatter(query_gain_grad, "fsdp", scatter_dimension=0, tiled=True),
        lax.psum_scatter(key_gain_grad, "fsdp", scatter_dimension=0, tiled=True),
    )
    (
        query_total,
        key_total,
        value_total,
        output_total,
        gate_total,
        up_total,
        down_total,
        first_total,
        second_total,
        query_gain_total,
        key_gain_total,
    ) = (
        lax.psum(query_shard.astype(jnp.bfloat16), "ctx").astype(jnp.float32),
        lax.psum(key_shard.astype(jnp.bfloat16), "ctx").astype(jnp.float32),
        lax.psum(value_shard.astype(jnp.bfloat16), "ctx").astype(jnp.float32),
        lax.psum(output_shard.astype(jnp.bfloat16), "ctx").astype(jnp.float32),
        lax.psum(gate_shard.astype(jnp.bfloat16), "ctx").astype(jnp.float32),
        lax.psum(up_shard.astype(jnp.bfloat16), "ctx").astype(jnp.float32),
        lax.psum(down_shard.astype(jnp.bfloat16), "ctx").astype(jnp.float32),
        lax.psum(first_shard.astype(jnp.bfloat16), "ctx").astype(jnp.float32),
        lax.psum(second_shard.astype(jnp.bfloat16), "ctx").astype(jnp.float32),
        lax.psum(query_gain_shard.astype(jnp.bfloat16), "ctx").astype(jnp.float32),
        lax.psum(key_gain_shard.astype(jnp.bfloat16), "ctx").astype(jnp.float32),
    )
    return (
        layer_output[None],
        input_grad[None],
        query_total,
        key_total,
        value_total,
        output_total,
        gate_total,
        up_total,
        down_total,
        first_total,
        second_total,
        query_gain_total,
        key_gain_total,
    )


def solution(mesh):
    in_specs = (
        P("fsdp", "ctx", None),
        P("fsdp", "ctx", None),
        P("fsdp", None),
        P("fsdp", None),
        P("fsdp", None),
        P("fsdp", None),
        P("fsdp", None),
        P("fsdp", None),
        P("fsdp", None),
        P("fsdp", None),
        P(),
        P(),
        P(),
        P(),
    )
    out_specs = (
        P("fsdp", "ctx", None),
        P("fsdp", "ctx", None),
        P("fsdp", None),
        P("fsdp", None),
        P("fsdp", None),
        P("fsdp", None),
        P("fsdp", None),
        P("fsdp", None),
        P("fsdp", None),
        P("fsdp"),
        P("fsdp"),
        P("fsdp"),
        P("fsdp"),
    )
    return jax.shard_map(
        on_device, mesh=mesh, in_specs=in_specs, out_specs=out_specs, check_vma=False
    )
```

time: 1810 us -> 1120 us (0.62)
  waiting for transfers between devices: 1010 us -> 605 us
  local copies, waits for them, and re-layouts: 302 us -> 62.8 us
  matrix products: 291 us -> 149 us
  blocking collectives: 108 us -> 160 us
  starting transfers between devices: 15.2 us -> 46 us
    dot_general x32 -> x3, matrix products: 218 us -> 38.7 us  [the longest x1 15.6 us: on_device(): jnp.dot(weights_b, head_value, preferred_element_type=jnp.float32)]
    reduce_scatter x1 -> x0, waiting for transfers between devices: 177 us -> none  [on_device(): lax.psum_scatter(jnp.concatenate(value_grads, axis=1).astype(jnp.bfloat16...]
    reshape x33 -> x1, local copies, waits for them, and re-layouts: 136 us -> 1.22 us  [on_device(): jnp.repeat(jnp.concatenate([own_keys, own_values], axis=-1), group, axis=1)]
    all_gather x2 -> x0, waiting for transfers between devices: 96 us -> none  [the longest x1 95.3 us: on_device(): lax.all_gather(own_keys, 'ctx', axis=0, tiled=True)]
    all_to_all x0 -> x3, waiting for transfers between devices: none -> 65.8 us  [exchange(): lax.all_to_all(values, 'ctx', split_axis=0, concat_axis=0, tiled=True)]
    unnamed x20 -> x15, waiting for transfers between devices: 58.3 us -> 5.13 us
    all_to_all x0 -> x1, blocking collectives: none -> 50.9 us  [exchange(): lax.all_to_all(values, 'ctx', split_axis=0, concat_axis=0, tiled=True)]
    gather x2 -> x0, local copies, waits for them, and re-layouts: 47.9 us -> none  [the longest x1 24 us: on_device(): all_keys[slot_rows]]
  transfers between devices with their start and end apart: 23 -> 22, of which waited for: 19 -> 13; matrix products, arithmetic and copies ran while one was open for 24% -> 23% of each run, Pallas kernels for 0% -> 0%
where the time goes in v1:
time: 1120 us; the launch traced here: 1110 us
  waiting for transfers between devices  605 us (54%)
  blocking collectives  160 us (14%)
  matrix products  149 us (13%)
  other arithmetic  71.2 us (6%)
  local copies, waits for them, and re-layouts  62.8 us (6%)
  starting transfers between devices  46 us (4%)
  between operations  16.2 us (1%)
    psum x1, waiting for transfers between devices, on_device(): lax.psum(query_shard.astype(jnp.bfloat16), 'ctx').astype(jnp.float32)  264 us
    psum x1, blocking collectives, on_device(): lax.psum(first_shard.astype(jnp.bfloat16), 'ctx').astype(jnp.float32)  96.6 us
    all_to_all x3, waiting for transfers between devices, exchange(): lax.all_to_all(values, 'ctx', split_axis=0, concat_axis=0, tiled=True)  65.8 us
    all_gather x1, waiting for transfers between devices, on_device(): lax.all_gather(down_weight, 'fsdp', axis=0, tiled=True)  61.6 us
    all_gather x1, waiting for transfers between devices, on_device(): lax.all_gather(up_weight, 'fsdp', axis=0, tiled=True)  61.5 us
    all_to_all x1, blocking collectives, exchange(): lax.all_to_all(values, 'ctx', split_axis=0, concat_axis=0, tiled=True)  50.9 us
    dot_general x8, matrix products, right_dot(): lax.dot_general(left_side, right_side, (((1,), (1,)), ((), ())), preferre...  46.3 us
    all_gather x1, waiting for transfers between devices, on_device(): lax.all_gather(query_weight, 'fsdp', axis=0, tiled=True)  42.8 us
  transfers between devices with their start and end apart: 22, of which 13 were waited for; matrix products, arithmetic and copies ran while one was open for 23% of the time, Pallas kernels for 0%

profile of v1, /device:TPU:0, one launch (start us, length us, event | category | flops | bytes accessed | tf_op | source)
XLA Modules:
  0.0 1109.3 jit_solution(13082776294592990823)
XLA Ops:
  12.0 29.1 %all-gather.18.cloned.1.call-done = bf16[1024,1024]{1,0:T(8,128)(2,1)} async-done(((bf16[256,1024]{1,0:T(8,128)(2,1)}), bf16[1024,1024]{1,0:T(8,128)(2,1)}) %all-gather.18.cloned.1.call-update) | async-done | bytes 2097168 | tf_op jit(solution)/shard_map/all_gather | solution.py:137
  46.2 26.6 %all-gather.20.cloned.1.call-done = bf16[1024,1024]{1,0:T(8,128)(2,1)} async-done(((bf16[256,1024]{1,0:T(8,128)(2,1)}), bf16[1024,1024]{1,0:T(8,128)(2,1)}) %all-gather.20.cloned.1.call-update) | async-done | bytes 2097168 | tf_op jit(solution)/shard_map/all_gather | solution.py:138
  78.7 42.8 %all-gather.16.cloned.1.call-done = bf16[1024,2048]{1,0:T(8,128)(2,1)} async-done(((bf16[256,2048]{1,0:T(8,128)(2,1)}), bf16[1024,2048]{1,0:T(8,128)(2,1)}) %all-gather.16.cloned.1.call-update) | async-done | bytes 4194320 | tf_op jit(solution)/shard_map/all_gather | solution.py:136
  121.6 6.4 copy.55
  128.0 3.5 multiply_reduce_fusion.3
  135.7 3.5 pad_maximum_fusion
  139.2 9.6 all-to-all-start
  149.5 47.5 %all-to-all-done = bf16[32,128,384]{2,1,0:T(8,128)(2,1)} async-done(((bf16[32,128,384]{2,1,0:T(8,128)(2,1)}), bf16[32,128,384]{2,1,0:T(8,128)(2,1)}, u32[]{:S(2)}, u32[]{:S(2)}) %all-to-all-start) | async-done | bytes 3145760 | tf_op jit(solution)/shard_map/all_to_all | solution.py:133
  199.3 13.9 %fusion.43 = (f32[2048]{0:T(1024)S(1)}, f32[2048,4096]{1,0:T(8,128)}) fusion(s32[2048]{0:T(1024)S(1)} %dynamic_slice.18, s32[4096]{0:T(1024)S(1)} %add.152, bf16[2048,128]{1,0:T(8,128)(2,1)S(1)} %bitcast.220, bf16[4096,128]{1,0:T(8,128)(2,1)S(1)} %bitcast.212), kind=kOutput, calls=%fused_computation.130 | convolution fusion | flops 2181036032 | bytes 35160064 | tf_op jit(solution)/shard_map/qd,kd->qk/dot_general | solution.py:173
  213.2 15.9 %exponential_reduce_fusion = f32[2048]{0:T(1024)S(1)} fusion(f32[2048]{0:T(1024)S(1)} %get-tuple-element.56, f32[2048,4096]{1,0:T(8,128)} %get-tuple-element.57, s32[2048]{0:T(1024)S(1)} %dynamic_slice.18, s32[4096]{0:T(1024)S(1)} %add.152), kind=kLoop, calls=%fused_computation.6 | loop fusion | flops 41940992 | bytes 33595392 | tf_op jit(solution)/shard_map/reduce_sum | solution.py:180
  229.1 15.6 %fusion.45 = (bf16[2048,128]{1,0:T(8,128)(2,1)S(1)}, f32[2048,128]{1,0:T(8,128)}) fusion(bf16[4096,128]{1,0:T(8,128)(2,1)S(1)} %bitcast.214, f32[2048]{0:T(1024)S(1)} %log_add_fusion, f32[2048,4096]{1,0:T(8,128)} %get-tuple-element.57, s32[2048]{0:T(1024)S(1)} %dynamic_slice.18, s32[4096]{0:T(1024)S(1)} %add.152), kind=kOutput, calls=%fused_computation.132 | convolution fusion | flops 2189688832 | bytes 36208640 | tf_op jit(solution)/shard_map/dot_general | solution.py:182
  246.1 11.2 %all-to-all-start.1 = ((bf16[32,128,128]{1,2,0:T(8,128)(2,1)}), bf16[32,128,128]{1,2,0:T(8,128)(2,1)S(1)}, u32[]{:S(2)}, u32[]{:S(2)}) async-start(bf16[32,128,128]{1,2,0:T(8,128)(2,1)} %bitcast_select_fusion.3), calls=%async_computation.1 | async-start | bytes 2097152 | tf_op jit(solution)/shard_map/all_to_all | solution.py:133
  258.3 18.2 %all-to-all-done.1 = bf16[32,128,128]{1,2,0:T(8,128)(2,1)S(1)} async-done(((bf16[32,128,128]{1,2,0:T(8,128)(2,1)}), bf16[32,128,128]{1,2,0:T(8,128)(2,1)S(1)}, u32[]{:S(2)}, u32[]{:S(2)}) %all-to-all-start.1) | async-done | bytes 1048608 | tf_op jit(solution)/shard_map/all_to_all | solution.py:133
  276.6 3.2 multiply_reduce_fusion.8
  279.9 6.5 all-gather.24.cloned.1.call-done
  286.4 4.9 fusion.46
  291.4 61.5 %all-gather.26.cloned.1.call-done = bf16[1024,3072]{1,0:T(8,128)(2,1)} async-done(((bf16[256,3072]{1,0:T(8,128)(2,1)}), bf16[1024,3072]{1,0:T(8,128)(2,1)}) %all-gather.26.cloned.1.call-update) | async-done | bytes 6291472 | tf_op jit(solution)/shard_map/all_gather | solution.py:141
  352.8 4.9 fusion.47
  357.8 61.6 %all-gather.28.cloned.1.call-done = bf16[3072,1024]{1,0:T(8,128)(2,1)} async-done(((bf16[768,1024]{1,0:T(8,128)(2,1)}), bf16[3072,1024]{1,0:T(8,128)(2,1)}) %all-gather.28.cloned.1.call-update) | async-done | bytes 6291472 | tf_op jit(solution)/shard_map/all_gather | solution.py:142
  419.4 7.3 multiply_convert_fusion.1
  426.7 6.1 fusion.48
  432.7 5.4 multiply_reduce_fusion.5
  439.7 3.8 fusion.10
  447.1 9.5 all-to-all-start.2
  456.6 20.4 %fusion.2 = bf16[4096,2048]{0,1:T(8,128)(2,1)} fusion(f32[2048,4096]{1,0:T(8,128)} %get-tuple-element.57, f32[2048]{0:T(1024)S(1)} %log_add_fusion, s32[4096]{0:T(1024)S(1)} %add.152, s32[2048]{0:T(1024)S(1)} %dynamic_slice.18), kind=kLoop, calls=%fused_computation.3 | loop fusion | flops 41943040 | bytes 50364416 | tf_op jit(solution)/shard_map/convert_element_type | solution.py:181
  477.0 22.5 %copy.73 = bf16[4096,2048]{1,0:T(8,128)(2,1)} copy(bf16[4096,2048]{0,1:T(8,128)(2,1)} %fusion.2) | data formatting | bytes 33554432 | tf_op jit(solution)/shard_map/dot_general | solution.py:65
  503.5 20.3 %multiply_convert_fusion = bf16[2048,4096]{1,0:T(8,128)(2,1)} fusion(f32[2048]{0:T(1024)S(1)} %multiply_reduce_fusion.2, f32[2048]{0:T(1024)S(1)} %log_add_fusion, bf16[2048,128]{1,0:T(8,128)(2,1)S(1)} %bitcast.190, bf16[4096,128]{1,0:T(8,128)(2,1)} %bitcast.215, f32[2048,4096]{1,0:T(8,128)} %get-tuple-element.57, s32[2048]{0:T(1024)S(1)} %dynamic_slice.18, ...), kind=kOutput, calls=%fused_computation.4 | convolution fusion | flops 2206203904 | bytes 51945472 | tf_op jit(solution)/shard_map/dot_general | solution.py:71
  523.9 9.1 fusion.8
  535.5 5.8 fusion.7
  541.3 10.8 convolution_convert_fusion.6
  560.5 50.9 %all_to_all.93 = bf16[32,128,384]{1,2,0:T(8,128)(2,1)S(1)} all-to-all(bf16[32,128,384]{1,2,0:T(8,128)(2,1)S(1)} %pad_maximum_fusion.1), channel_id=1, replica_groups=mesh['ctx'=32,'fsdp'=4] {'ctx'}, dimensions={0} | all-to-all | bytes 6291456 | tf_op jit(solution)/shard_map/all_to_all | solution.py:133
  620.2 3.8 all-to-all-start.7
  625.3 16.3 %all-to-all-done.7 = bf16[128,4,768]{2,0,1:T(8,128)(2,1)S(1)} async-done(((bf16[128,4,768]{2,0,1:T(8,128)(2,1)}), bf16[128,4,768]{2,0,1:T(8,128)(2,1)S(1)}, u32[]{:S(2)}, u32[]{:S(2)}) %all-to-all-start.7) | async-done | bytes 786464 | tf_op jit(solution)/shard_map/all_to_all | solution.py:264
  641.6 3.5 all-to-all-start.5
  646.7 3.4 convolution_convert_fusion.4
  650.1 3.8 all-to-all-done.5
  653.9 3.4 all-to-all-start.6
  660.3 5.8 all-to-all-done.6
  666.1 3.4 all-to-all-start.4
  669.7 4.0 convolution_convert_fusion
  673.8 4.0 convolution_convert_fusion.1
  682.9 15.3 %all-gather.30.cloned.1.call-done = bf16[512,2048]{0,1:T(8,128)(2,1)} async-done(((bf16[128,2048]{0,1:T(8,128)(2,1)}), bf16[512,2048]{0,1:T(8,128)(2,1)}) %all-gather.30.cloned.1.call-update) | async-done | bytes 2097168 | tf_op jit(solution)/shard_map/all_gather | solution.py:271
  698.2 3.3 convolution_convert_fusion.2
  704.1 4.9 fusion.14
  712.9 12.1 %all-reduce.4 = (bf16[1024]{0:T(1024)(128)(2,1)S(1)}, bf16[1024]{0:T(1024)(128)(2,1)S(1)}, bf16[128]{0:T(256)(128)(2,1)S(1)}, bf16[128]{0:T(256)(128)(2,1)S(1)}) all-reduce(f32[1024]{0:T(1024)S(1)} %get-tuple-element.19, f32[1024]{0:T(1024)S(1)} %get-tuple-element.17, ...), channel_id=3, replica_groups=mesh['ctx'=32,'fsdp'=4] {'fsdp'}, use_global_device_ids=true, to_apply=%region_20.21.clone | all-reduce | flops 2304 | bytes 13824
  725.3 96.6 %all-reduce.5 = (bf16[256]{0:T(256)(128)(2,1)S(1)}, bf16[256]{0:T(256)(128)(2,1)S(1)}, bf16[32]{0:T(256)(128)(2,1)S(1)}, bf16[32]{0:T(256)(128)(2,1)S(1)}) all-reduce(bf16[256]{0:T(256)(128)(2,1)S(1)} %dynamic-slice.13, bf16[256]{0:T(256)(128)(2,1)S(1)} %dynamic-slice.12, ...), channel_id=1, replica_groups=mesh['ctx'=32,'fsdp'=4] {'ctx'}, use_global_device_ids=true, to_apply=%region_21.22 | all-reduce | flops 576 | bytes 2304 | tf_op jit(solution)/shard_map/psum | solution.py:308
  825.1 264.5 %all-reduce.9.cloned.1.call-done = (bf16[256,2048]{1,0:T(8,128)(2,1)}, bf16[256,1024]{1,0:T(8,128)(2,1)}, bf16[256,1024]{1,0:T(8,128)(2,1)}, bf16[512,1024]{1,0:...) async-done(((bf16[256,2048]{1,0:T(8,128)(2,1)}, bf16[256,1024]{1,0:T(8,128)(2,1)}, bf16[256,1024]{1,0:T(8,128)(2,1)}, ...) | async-done | bytes 7864336 | tf_op jit(solution)/shard_map/psum | solution.py:301
  1089.6 3.6 convert_element_type.203
  (218 shorter events, 82.9 us)
Async XLA Ops:
  7.2 4.4 copy-start
  7.2 33.9 %all-gather.18.cloned.1.call-start = ((), (), s32[]{:S(2)}) async-start(), calls=%async_computation.9 | async-start | bytes 2621440 | tf_op jit(solution)/shard_map/all_gather | solution.py:137
  7.9 64.9 %all-gather.20.cloned.1.call-start = ((), (), s32[]{:S(2)}) async-start(), calls=%async_computation.10 | async-start | bytes 2621440 | tf_op jit(solution)/shard_map/all_gather | solution.py:138
  8.7 112.9 %all-gather.16.cloned.1.call-start = ((), (), s32[]{:S(2)}) async-start(), calls=%async_computation.8 | async-start | bytes 5242880 | tf_op jit(solution)/shard_map/all_gather | solution.py:136
  9.4 34.6 %copy-start.29 = (f32[1024]{0:T(1024)S(1)}, f32[1024]{0:T(1024)}, u32[]{:S(2)}) copy-start(f32[1024]{0:T(1024)} %param.24) | copy-start | bytes 12292
  9.4 267.2 %all-gather.22.cloned.1.call-start = ((), (), s32[]{:S(2)}) async-start(), calls=%async_computation.11 | async-start | bytes 5242880 | tf_op jit(solution)/shard_map/all_gather | solution.py:139
  10.0 276.4 %all-gather.24.cloned.1.call-start = ((), (), s32[]{:S(2)}) async-start(), calls=%async_computation.12 | async-start | bytes 7864320 | tf_op jit(solution)/shard_map/all_gather | solution.py:140
  10.6 35.0 %copy-start.36 = (f32[128]{0:T(128)S(1)}, f32[128]{0:T(128)}, u32[]{:S(2)}) copy-start(f32[128]{0:T(128)} %param.27) | copy-start | bytes 1540
  10.6 342.2 %all-gather.26.cloned.1.call-start = ((), (), s32[]{:S(2)}) async-start(), calls=%async_computation.13 | async-start | bytes 7864320 | tf_op jit(solution)/shard_map/all_gather | solution.py:141
  11.8 116.2 %copy-start.34 = (f32[128]{0:T(128)}, f32[128]{0:T(128)S(1)}, u32[]{:S(2)}) copy-start(f32[128]{0:T(128)S(1)} %add_rsqrt_fusion.3) | copy-start | bytes 1540
  44.8 31.1 %copy-start.32 = (f32[128,8]{0,1:T(8,128)}, f32[128,8]{0,1:T(8,128)S(1)}, u32[]{:S(2)}) copy-start(f32[128,8]{0,1:T(8,128)S(1)} %add_rsqrt_fusion.1) | copy-start | bytes 12292
  139.2 57.9 %all-to-all-start = ((bf16[32,128,384]{2,1,0:T(8,128)(2,1)}), bf16[32,128,384]{2,1,0:T(8,128)(2,1)}, u32[]{:S(2)}, u32[]{:S(2)}) async-start(bf16[32,128,384]{2,1,0:T(8,128)(2,1)} %pad_maximum_fusion), calls=%async_computation | async-start | bytes 6291456 | tf_op jit(solution)/shard_map/all_to_all | solution.py:133
  148.7 270.6 %all-gather.28.cloned.1.call-start = ((), (), s32[]{:S(2)}) async-start(), calls=%async_computation.14 | async-start | bytes 7864320 | tf_op jit(solution)/shard_map/all_gather | solution.py:142
  199.2 14.0 %copy-start.22 = (bf16[32,128,128]{2,1,0:T(8,128)(2,1)}, bf16[32,128,128]{2,1,0:T(8,128)(2,1)S(1)}, u32[]{:S(2)}) copy-start(bf16[32,128,128]{2,1,0:T(8,128)(2,1)S(1)} %get-tuple-element.39) | copy-start | bytes 3145732
  199.2 29.9 %copy-start.24 = (bf16[32,128,128]{2,1,0:T(8,128)(2,1)}, bf16[32,128,128]{2,1,0:T(8,128)(2,1)S(1)}, u32[]{:S(2)}) copy-start(bf16[32,128,128]{2,1,0:T(8,128)(2,1)S(1)} %get-tuple-element.40) | copy-start | bytes 3145732
  199.3 13.9 %copy-start.27 = (bf16[16,128,128]{2,1,0:T(8,128)(2,1)}, bf16[16,128,128]{2,1,0:T(8,128)(2,1)S(1)}, u32[]{:S(2)}) copy-start(bf16[16,128,128]{2,1,0:T(8,128)(2,1)S(1)} %constant_dynamic-slice_fusion.2) | copy-start | bytes 1572868
  246.1 33.7 %copy-start.31 = (f32[1024]{0:T(1024)S(1)}, f32[1024]{0:T(1024)}, u32[]{:S(2)}) copy-start(f32[1024]{0:T(1024)} %param.25) | copy-start | bytes 12292
  246.1 30.4 %all-to-all-start.1 = ((bf16[32,128,128]{1,2,0:T(8,128)(2,1)}), bf16[32,128,128]{1,2,0:T(8,128)(2,1)S(1)}, u32[]{:S(2)}, u32[]{:S(2)}) async-start(bf16[32,128,128]{1,2,0:T(8,128)(2,1)} %bitcast_select_fusion.3), calls=%async_computation.1 | async-start | bytes 2097152 | tf_op jit(solution)/shard_map/all_to_all | solution.py:133
  257.3 389.4 %all-gather.42.cloned.1.call-start = ((), (), s32[]{:S(2)}) async-start(), calls=%async_computation.21 | async-start | bytes 1310720 | tf_op jit(solution)/shard_map/all_gather | solution.py:267
  258.1 399.2 %all-gather.36.cloned.1.call-start = ((), (), s32[]{:S(2)}) async-start(), calls=%async_computation.18 | async-start | bytes 1310720 | tf_op jit(solution)/shard_map/all_gather | solution.py:270
  276.6 14.8 %copy-start.7 = (bf16[16,128,128]{1,2,0:T(8,128)(2,1)}, bf16[16,128,128]{1,2,0:T(8,128)(2,1)S(1)}, u32[]{:S(2)}) copy-start(bf16[16,128,128]{1,2,0:T(8,128)(2,1)S(1)} %constant_dynamic-slice_fusion.1) | copy-start | bytes 1572868
  291.4 128.0 %copy-start.15 = (bf16[1,128,1024]{2,1,0:T(8,128)(2,1)S(1)}, bf16[1,128,1024]{2,1,0:T(8,128)(2,1)}, u32[]{:S(2)}) copy-start(bf16[1,128,1024]{2,1,0:T(8,128)(2,1)} %param.15) | copy-start | bytes 786436
  426.7 6.1 copy-start.14
  438.2 6.3 copy-start.10
  439.1 230.6 %all-gather.40.cloned.1.call-start = ((), (), s32[]{:S(2)}) async-start(), calls=%async_computation.20 | async-start | bytes 3932160 | tf_op jit(solution)/shard_map/all_gather | solution.py:269
  447.1 52.7 %all-to-all-start.2 = ((bf16[32,128,128]{1,2,0:T(8,128)(2,1)}), bf16[32,128,128]{1,2,0:T(8,128)(2,1)S(1)}, u32[]{:S(2)}, u32[]{:S(2)}) async-start(bf16[32,128,128]{1,2,0:T(8,128)(2,1)} %bitcast_select_fusion.2), calls=%async_computation.2 | async-start | bytes 2097152 | tf_op jit(solution)/shard_map/all_to_all | solution.py:133
  456.5 217.2 %all-gather.38.cloned.1.call-start = ((), (), s32[]{:S(2)}) async-start(), calls=%async_computation.19 | async-start | bytes 3932160 | tf_op jit(solution)/shard_map/all_gather | solution.py:268
  499.5 178.3 %all-gather.32.cloned.1.call-start = ((), (), s32[]{:S(2)}) async-start(), calls=%async_computation.16 | async-start | bytes 1310720 | tf_op jit(solution)/shard_map/all_gather | solution.py:272
  503.5 20.4 %copy-start.23 = (bf16[32,128,128]{2,1,0:T(8,128)(2,1)S(1)}, bf16[32,128,128]{2,1,0:T(8,128)(2,1)}, u32[]{:S(2)}) copy-start(bf16[32,128,128]{2,1,0:T(8,128)(2,1)} %copy-done.22) | copy-start | bytes 3145732
  523.9 9.2 copy-start.28
  523.9 11.6 %copy-start.41 = (bf16[2048,4096]{1,0:T(8,128)(2,1)S(1)}, bf16[2048,4096]{1,0:T(8,128)(2,1)}, u32[]{:S(2)}) copy-start(bf16[2048,4096]{1,0:T(8,128)(2,1)} %multiply_convert_fusion) | copy-start | bytes 50331652
  552.1 6.6 copy-start.12
  614.5 65.9 %all-gather.34.cloned.1.call-start = ((), (), s32[]{:S(2)}) async-start(), calls=%async_computation.17 | async-start | bytes 1310720 | tf_op jit(solution)/shard_map/all_gather | solution.py:273
  616.4 81.8 %all-gather.30.cloned.1.call-start = ((), (), s32[]{:S(2)}) async-start(), calls=%async_computation.15 | async-start | bytes 2621440 | tf_op jit(solution)/shard_map/all_gather | solution.py:271
  616.6 7.6 copy-start.30
  616.7 7.7 copy-start.8
  617.1 28.0 %copy-start.35 = (f32[128]{0:T(128)S(1)}, f32[128]{0:T(128)}, u32[]{:S(2)}) copy-start(f32[128]{0:T(128)} %copy-done.34) | copy-start | bytes 1540
  620.2 21.4 %all-to-all-start.7 = ((bf16[128,4,768]{2,0,1:T(8,128)(2,1)}), bf16[128,4,768]{2,0,1:T(8,128)(2,1)S(1)}, u32[]{:S(2)}, u32[]{:S(2)}) async-start(bf16[128,4,768]{2,0,1:T(8,128)(2,1)} %bitcast.180), calls=%async_computation.7 | async-start | bytes 1572864 | tf_op jit(solution)/shard_map/all_to_all | solution.py:264
  641.6 12.3 %all-to-all-start.5 = ((bf16[128,4,512]{2,0,1:T(8,128)(2,1)}), bf16[128,4,512]{2,0,1:T(8,128)(2,1)S(1)}, u32[]{:S(2)}, u32[]{:S(2)}) async-start(bf16[128,4,512]{2,0,1:T(8,128)(2,1)} %copy.69), calls=%async_computation.5 | async-start | bytes 1048576 | tf_op jit(solution)/shard_map/all_to_all | solution.py:262
  653.9 12.2 %all-to-all-start.6 = ((bf16[128,4,256]{2,0,1:T(8,128)(2,1)}), bf16[128,4,256]{2,0,1:T(8,128)(2,1)S(1)}, u32[]{:S(2)}, u32[]{:S(2)}) async-start(bf16[128,4,256]{2,0,1:T(8,128)(2,1)} %bitcast.181), calls=%async_computation.6 | async-start | bytes 524288 | tf_op jit(solution)/shard_map/all_to_all | solution.py:263
  666.1 11.7 %all-to-all-start.4 = ((bf16[128,4,256]{2,0,1:T(8,128)(2,1)}), bf16[128,4,256]{2,0,1:T(8,128)(2,1)S(1)}, u32[]{:S(2)}, u32[]{:S(2)}) async-start(bf16[128,4,256]{2,0,1:T(8,128)(2,1)} %fusion.18), calls=%async_computation.4 | async-start | bytes 524288 | tf_op jit(solution)/shard_map/all_to_all | solution.py:261
  669.5 420.1 %all-reduce.9.cloned.1.call-start = ((), (), s32[]{:S(2)}) async-start(), calls=%async_computation.22 | async-start | bytes 15728640 | tf_op jit(solution)/shard_map/psum | solution.py:301
  701.5 7.4 copy-start.5
  701.5 7.4 copy-start.16
  704.0 5.7 copy-start.6
  704.1 5.7 copy-start.17
  709.8 114.3 %copy-start.11 = (f32[128,1024]{1,0:T(8,128)S(1)}, f32[128,1024]{1,0:T(8,128)}, u32[]{:S(2)}) copy-start(f32[128,1024]{1,0:T(8,128)} %copy-done.10) | copy-start | bytes 1572868
  1089.6 5.6 copy-start.18
  (17 other events, 44.3 us)
Sparse Core Ops, SparseCore 0:
  9.7 31.3 all-gather.17
  42.8 29.9 all-gather.19
  74.5 47.0 all-gather.15
  123.1 81.4 all-gather.21
  206.1 80.3 all-gather.23
  288.0 64.8 all-gather.25
  354.5 64.8 all-gather.27
  421.0 22.4 all-gather.41
  445.8 32.6 all-gather.35
  480.5 39.7 all-gather.39
  522.0 38.6 all-gather.37
  614.6 24.0 all-gather.31
  640.3 25.8 all-gather.33
  668.4 29.7 all-gather.29
  702.3 387.2 all-reduce.8

commit v2 on v1

--- a/solution.py
+++ b/solution.py
@@ -8,6 +8,8 @@
 HQ = 16
 KEY_VALUE_HEADS = 8
 HEAD_SIZE = 128
+CTX = ("yh", "x", "z")
+FSDP = ("yl", "c")
 
 
 EPSILON = 1e-06
@@ -71,6 +73,31 @@
     return lax.dot_general(
         left_side, right_side, (((1,), (1,)), ((), ())), preferred_element_type=jnp.float32
     )
+
+
+def gather_fsdp(values):
+    across = lax.all_gather(values, "yl", axis=0, tiled=False)
+    both = lax.all_gather(across, "c", axis=1, tiled=False)
+    return both.reshape((-1,) + values.shape[1:])
+
+
+def reduce_ctx(shards):
+    flat = jnp.concatenate([s.astype(jnp.bfloat16).reshape(-1) for s in shards])
+    lanes = 128
+    step = 256 * lanes
+    padded = -(-flat.shape[0] // step) * step
+    flat = jnp.pad(flat, (0, padded - flat.shape[0])).reshape(padded // lanes, lanes)
+    part = lax.psum_scatter(flat, "z", scatter_dimension=0, tiled=True)
+    part = lax.psum_scatter(part, "x", scatter_dimension=0, tiled=True)
+    part = lax.psum(part, "yh")
+    part = lax.all_gather(part, "x", axis=0, tiled=True)
+    full = lax.all_gather(part, "z", axis=0, tiled=True).reshape(-1)
+    out = []
+    at = 0
+    for s in shards:
+        out.append(full[at : at + s.size].reshape(s.shape).astype(jnp.float32))
+        at += s.size
+    return tuple(out)
 
 
 def on_device(
@@ -91,11 +118,11 @@
 ):
     local_rows = layer_input.shape[1]
     block_rows = local_rows // 2
-    ctx_size = lax.axis_size("ctx")
+    ctx_size = lax.axis_size(CTX)
     halves = ctx_size // HQ
     half_devices = ctx_size // halves
     order_row = block_order[0]
-    device_place = lax.axis_index("ctx")
+    device_place = lax.axis_index(CTX)
     my_half = device_place // half_devices
     all_positions = (
         order_row[:, None] * block_rows + jnp.arange(block_rows, dtype=jnp.int32)[None, :]
@@ -130,16 +157,16 @@
         return jnp.transpose(mine, (1, 0, 2))
 
     def exchange(values):
-        return lax.all_to_all(values, "ctx", split_axis=0, concat_axis=0, tiled=True)
+        return lax.all_to_all(values, CTX, split_axis=0, concat_axis=0, tiled=True)
 
     full_query, full_key, full_value, full_output, full_gate, full_up, full_down = (
-        lax.all_gather(query_weight, "fsdp", axis=0, tiled=True),
-        lax.all_gather(key_projection, "fsdp", axis=0, tiled=True),
-        lax.all_gather(value_projection, "fsdp", axis=0, tiled=True),
-        lax.all_gather(output_weight, "fsdp", axis=0, tiled=True),
-        lax.all_gather(gate_weight, "fsdp", axis=0, tiled=True),
-        lax.all_gather(up_weight, "fsdp", axis=0, tiled=True),
-        lax.all_gather(down_weight, "fsdp", axis=0, tiled=True),
+        gather_fsdp(query_weight),
+        gather_fsdp(key_projection),
+        gather_fsdp(value_projection),
+        gather_fsdp(output_weight),
+        gather_fsdp(gate_weight),
+        gather_fsdp(up_weight),
+        gather_fsdp(down_weight),
     )
     input_f32 = layer_input[0].astype(jnp.float32)
     gained, first_normed, first_scale = rms_apply(input_f32, first_gain)
@@ -258,19 +285,19 @@
         attn_in_grad, first_normed, first_scale, first_gain
     )
     attn_cols, mixed_cols, mlp_cols, hidden_cols = (
-        lax.all_to_all(attention_input, "fsdp", split_axis=1, concat_axis=0, tiled=True),
-        lax.all_to_all(mixed_b, "fsdp", split_axis=1, concat_axis=0, tiled=True),
-        lax.all_to_all(mlp_in, "fsdp", split_axis=1, concat_axis=0, tiled=True),
-        lax.all_to_all(hidden, "fsdp", split_axis=1, concat_axis=0, tiled=True),
+        lax.all_to_all(attention_input, FSDP, split_axis=1, concat_axis=0, tiled=True),
+        lax.all_to_all(mixed_b, FSDP, split_axis=1, concat_axis=0, tiled=True),
+        lax.all_to_all(mlp_in, FSDP, split_axis=1, concat_axis=0, tiled=True),
+        lax.all_to_all(hidden, FSDP, split_axis=1, concat_axis=0, tiled=True),
     )
     cot_rows, gate_rows, up_rows, mid_rows, query_rows, key_rows, value_row_block = (
-        lax.all_gather(own_cotangent, "fsdp", axis=0, tiled=True),
-        lax.all_gather(gate_grad, "fsdp", axis=0, tiled=True),
-        lax.all_gather(up_grad, "fsdp", axis=0, tiled=True),
-        lax.all_gather(mid_grad_b, "fsdp", axis=0, tiled=True),
-        lax.all_gather(query_pre_grad, "fsdp", axis=0, tiled=True),
-        lax.all_gather(key_before_norm_gradient, "fsdp", axis=0, tiled=True),
-        lax.all_gather(value_gradient_second, "fsdp", axis=0, tiled=True),
+        gather_fsdp(own_cotangent),
+        gather_fsdp(gate_grad),
+        gather_fsdp(up_grad),
+        gather_fsdp(mid_grad_b),
+        gather_fsdp(query_pre_grad),
+        gather_fsdp(key_before_norm_gradient),
+        gather_fsdp(value_gradient_second),
     )
     query_shard = left_dot(attn_cols, query_rows)
     key_shard = left_dot(attn_cols, key_rows)
@@ -280,11 +307,14 @@
     up_shard = left_dot(mlp_cols, up_rows)
     down_shard = left_dot(hidden_cols, cot_rows)
     first_shard, second_shard, query_gain_shard, key_gain_shard = (
-        lax.psum_scatter(first_gain_grad, "fsdp", scatter_dimension=0, tiled=True),
-        lax.psum_scatter(second_gain_grad, "fsdp", scatter_dimension=0, tiled=True),
-        lax.psum_scatter(query_gain_grad, "fsdp", scatter_dimension=0, tiled=True),
-        lax.psum_scatter(key_gain_grad, "fsdp", scatter_dimension=0, tiled=True),
-    )
+        lax.psum_scatter(first_gain_grad, FSDP, scatter_dimension=0, tiled=True),
+        lax.psum_scatter(second_gain_grad, FSDP, scatter_dimension=0, tiled=True),
+        lax.psum_scatter(query_gain_grad, FSDP, scatter_dimension=0, tiled=True),
+        lax.psum_scatter(key_gain_grad, FSDP, scatter_dimension=0, tiled=True),
+    )
+    shards = (query_shard, key_shard, value_shard, output_shard, gate_shard, up_shard, down_shard,
+              first_shard, second_shard, query_gain_shard, key_gain_shard)
+    totals = reduce_ctx(shards)
     (
         query_total,
         key_total,
@@ -297,19 +327,7 @@
         second_total,
         query_gain_total,
         key_gain_total,
-    ) = (
-        lax.psum(query_shard.astype(jnp.bfloat16), "ctx").astype(jnp.float32),
-        lax.psum(key_shard.astype(jnp.bfloat16), "ctx").astype(jnp.float32),
-        lax.psum(value_shard.astype(jnp.bfloat16), "ctx").astype(jnp.float32),
-        lax.psum(output_shard.astype(jnp.bfloat16), "ctx").astype(jnp.float32),
-        lax.psum(gate_shard.astype(jnp.bfloat16), "ctx").astype(jnp.float32),
-        lax.psum(up_shard.astype(jnp.bfloat16), "ctx").astype(jnp.float32),
-        lax.psum(down_shard.astype(jnp.bfloat16), "ctx").astype(jnp.float32),
-        lax.psum(first_shard.astype(jnp.bfloat16), "ctx").astype(jnp.float32),
-        lax.psum(second_shard.astype(jnp.bfloat16), "ctx").astype(jnp.float32),
-        lax.psum(query_gain_shard.astype(jnp.bfloat16), "ctx").astype(jnp.float32),
-        lax.psum(key_gain_shard.astype(jnp.bfloat16), "ctx").astype(jnp.float32),
-    )
+    ) = totals
     return (
         layer_output[None],
         input_grad[None],
@@ -329,36 +347,37 @@
 
 def solution(mesh):
     in_specs = (
-        P("fsdp", "ctx", None),
-        P("fsdp", "ctx", None),
-        P("fsdp", None),
-        P("fsdp", None),
-        P("fsdp", None),
-        P("fsdp", None),
-        P("fsdp", None),
-        P("fsdp", None),
-        P("fsdp", None),
-        P("fsdp", None),
+        P(FSDP, CTX, None),
+        P(FSDP, CTX, None),
+        P(FSDP, None),
+        P(FSDP, None),
+        P(FSDP, None),
+        P(FSDP, None),
+        P(FSDP, None),
+        P(FSDP, None),
+        P(FSDP, None),
+        P(FSDP, None),
         P(),
         P(),
         P(),
         P(),
     )
     out_specs = (
-        P("fsdp", "ctx", None),
-        P("fsdp", "ctx", None),
-        P("fsdp", None),
-        P("fsdp", None),
-        P("fsdp", None),
-        P("fsdp", None),
-        P("fsdp", None),
-        P("fsdp", None),
-        P("fsdp", None),
-        P("fsdp"),
-        P("fsdp"),
-        P("fsdp"),
-        P("fsdp"),
-    )
+        P(FSDP, CTX, None),
+        P(FSDP, CTX, None),
+        P(FSDP, None),
+        P(FSDP, None),
+        P(FSDP, None),
+        P(FSDP, None),
+        P(FSDP, None),
+        P(FSDP, None),
+        P(FSDP, None),
+        P(FSDP),
+        P(FSDP),
+        P(FSDP),
+        P(FSDP),
+    )
+    torus_mesh = jax.sharding.Mesh(mesh.devices.reshape(2, 4, 4, 2, 2), ("yh", "x", "z", "yl", "c"))
     return jax.shard_map(
-        on_device, mesh=mesh, in_specs=in_specs, out_specs=out_specs, check_vma=False
-    )
+        on_device, mesh=torus_mesh, in_specs=in_specs, out_specs=out_specs, check_vma=False
+    )

time: 1120 us -> 1260 us (1.12)
  local copies, waits for them, and re-layouts: 62.8 us -> 204 us
  blocking collectives: 160 us -> 130 us
  waiting for transfers between devices: 605 us -> 632 us
    all_gather x14 -> x26, waiting for transfers between devices: 244 us -> 477 us  [the longest x10 283 us: gather_fsdp(): across = lax.all_gather(values, 'yl', axis=0, tiled=False)]
    psum x1, waiting for transfers between devices: 264 us -> 38 us  [reduce_ctx(): part = lax.psum(part, 'yh')]
    reduce_scatter x0 -> x2, waiting for transfers between devices: none -> 109 us  [the longest x1 78.5 us: reduce_ctx(): part = lax.psum_scatter(flat, 'z', scatter_dimension=0, tiled=True)]
    concatenate x0 -> x1, local copies, waits for them, and re-layouts: none -> 104 us  [reduce_ctx(): flat = jnp.concatenate([s.astype(jnp.bfloat16).reshape(-1) for s in shards])]
    psum x1 -> x0, blocking collectives: 96.6 us -> none  [on_device(): lax.psum(first_shard.astype(jnp.bfloat16), 'ctx').astype(jnp.float32)]
    all_to_all x7, waiting for transfers between devices: 91.7 us -> 1.26 us  [the longest x1 1.24 us: on_device(): lax.all_to_all(mixed_b, FSDP, split_axis=1, concat_axis=0, tiled=True)]
    all_gather x0 -> x4, blocking collectives: none -> 88.5 us  [gather_fsdp(): across = lax.all_gather(values, 'yl', axis=0, tiled=False)]
    all_to_all x1, blocking collectives: 50.9 us -> 30 us  [exchange(): return lax.all_to_all(values, CTX, split_axis=0, concat_axis=0, tiled=True)]
  transfers between devices with their start and end apart: 22 -> 36, of which waited for: 13 -> 21; matrix products, arithmetic and copies ran while one was open for 23% -> 20% of each run, Pallas kernels for 0% -> 0%
where the time goes in v2:
time: 1260 us; the launch traced here: 1240 us
  waiting for transfers between devices  632 us (50%)
  local copies, waits for them, and re-layouts  204 us (16%)
  matrix products  145 us (12%)
  blocking collectives  130 us (10%)
  other arithmetic  69.1 us (5%)
  starting transfers between devices  42.8 us (3%)
  between operations  16.7 us (1%)
    all_gather x10, waiting for transfers between devices, gather_fsdp(): across = lax.all_gather(values, 'yl', axis=0, tiled=False)  283 us
    concatenate x1, local copies, waits for them, and re-layouts, reduce_ctx(): flat = jnp.concatenate([s.astype(jnp.bfloat16).reshape(-1) for s in shards])  104 us
    all_gather x4, blocking collectives, gather_fsdp(): across = lax.all_gather(values, 'yl', axis=0, tiled=False)  88.5 us
    all_gather x14, waiting for transfers between devices, gather_fsdp(): both = lax.all_gather(across, 'c', axis=1, tiled=False)  87.6 us
    reduce_scatter x1, waiting for transfers between devices, reduce_ctx(): part = lax.psum_scatter(flat, 'z', scatter_dimension=0, tiled=True)  78.5 us
    all_gather x1, waiting for transfers between devices, reduce_ctx(): full = lax.all_gather(part, 'z', axis=0, tiled=True).reshape(-1)  75.6 us
    dot_general x8, matrix products, right_dot(): lax.dot_general(left_side, right_side, (((1,), (1,)), ((), ())), preferre...  45 us
    psum x1, waiting for transfers between devices, reduce_ctx(): part = lax.psum(part, 'yh')  38 us
  transfers between devices with their start and end apart: 36, of which 21 were waited for; matrix products, arithmetic and copies ran while one was open for 20% of the time, Pallas kernels for 0%

profile of v2, /device:TPU:0, one launch (start us, length us, event | category | flops | bytes accessed | tf_op | source)
XLA Modules:
  0.0 1239.8 jit_solution(9010868726562113697)
XLA Ops:
  11.2 24.8 %all-gather.61.cloned.1.call-done = bf16[512,1024]{1,0:T(8,128)(2,1)} async-done(((bf16[256,1024]{1,0:T(8,128)(2,1)}), bf16[512,1024]{1,0:T(8,128)(2,1)}) %all-gather.61.cloned.1.call-update) | async-done | bytes 1048592 | tf_op jit(solution)/shard_map/all_gather | solution.py:79
  36.1 26.4 %all-gather.65.cloned.1.call-done = bf16[512,1024]{1,0:T(8,128)(2,1)} async-done(((bf16[256,1024]{1,0:T(8,128)(2,1)}), bf16[512,1024]{1,0:T(8,128)(2,1)}) %all-gather.65.cloned.1.call-update) | async-done | bytes 1048592 | tf_op jit(solution)/shard_map/all_gather | solution.py:79
  62.6 38.2 %all-gather.57.cloned.1.call-done = bf16[512,2048]{1,0:T(8,128)(2,1)} async-done(((bf16[256,2048]{1,0:T(8,128)(2,1)}), bf16[512,2048]{1,0:T(8,128)(2,1)}) %all-gather.57.cloned.1.call-update) | async-done | bytes 2097168 | tf_op jit(solution)/shard_map/all_gather | solution.py:79
  101.5 37.5 %all-gather.69.cloned.1.call-done = bf16[1024,1024]{1,0:T(8,128)(2,1)} async-done(((bf16[512,1024]{1,0:T(8,128)(2,1)}), bf16[1024,1024]{1,0:T(8,128)(2,1)}) %all-gather.69.cloned.1.call-update) | async-done | bytes 2097168 | tf_op jit(solution)/shard_map/all_gather | solution.py:79
  139.0 49.9 %all-gather.73.cloned.1.call-done = bf16[512,3072]{1,0:T(8,128)(2,1)} async-done(((bf16[256,3072]{1,0:T(8,128)(2,1)}), bf16[512,3072]{1,0:T(8,128)(2,1)}) %all-gather.73.cloned.1.call-update) | async-done | bytes 3145744 | tf_op jit(solution)/shard_map/all_gather | solution.py:79
  189.6 49.3 %all-gather.77.cloned.1.call-done = bf16[512,3072]{1,0:T(8,128)(2,1)} async-done(((bf16[256,3072]{1,0:T(8,128)(2,1)}), bf16[512,3072]{1,0:T(8,128)(2,1)}) %all-gather.77.cloned.1.call-update) | async-done | bytes 3145744 | tf_op jit(solution)/shard_map/all_gather | solution.py:79
  239.2 15.6 %all-gather.63.cloned.1.call-done = bf16[2,512,1024]{2,1,0:T(8,128)(2,1)} async-done(((bf16[2,256,1024]{2,1,0:T(8,128)(2,1)}), bf16[2,512,1024]{2,1,0:T(8,128)(2,1)}) %all-gather.63.cloned.1.call-update) | async-done | bytes 2097168 | tf_op jit(solution)/shard_map/all_gather | solution.py:80
  259.9 11.2 all-gather.67.cloned.1.call-done
  277.0 13.5 %all-gather.59.cloned.1.call-done = bf16[2,512,2048]{2,1,0:T(8,128)(2,1)} async-done(((bf16[2,256,2048]{2,1,0:T(8,128)(2,1)}), bf16[2,512,2048]{2,1,0:T(8,128)(2,1)}) %all-gather.59.cloned.1.call-update) | async-done | bytes 4194320 | tf_op jit(solution)/shard_map/all_gather | solution.py:80
  290.5 6.4 copy.79
  308.1 9.9 all-to-all-start
  318.3 57.0 %all-gather.81.cloned.1.call-done = bf16[1536,1024]{1,0:T(8,128)(2,1)} async-done(((bf16[768,1024]{1,0:T(8,128)(2,1)}), bf16[1536,1024]{1,0:T(8,128)(2,1)}) %all-gather.81.cloned.1.call-update) | async-done | bytes 3145744 | tf_op jit(solution)/shard_map/all_gather | solution.py:79
  377.6 14.6 %fusion.49 = (f32[2048]{0:T(1024)S(1)}, f32[2048,4096]{1,0:T(8,128)}) fusion(s32[2048]{0:T(1024)S(1)} %dynamic_slice.18, s32[4096]{0:T(1024)S(1)} %add.146, bf16[2048,128]{1,0:T(8,128)(2,1)S(1)} %bitcast.313, bf16[4096,128]{1,0:T(8,128)(2,1)S(1)} %bitcast.307), kind=kOutput, calls=%fused_computation.148 | convolution fusion | flops 2181036032 | bytes 35160064 | tf_op jit(solution)/shard_map/qd,kd->qk/dot_general | solution.py:200
  392.2 16.1 %exponential_reduce_fusion = f32[2048]{0:T(1024)S(1)} fusion(f32[2048]{0:T(1024)S(1)} %get-tuple-element.56, f32[2048,4096]{1,0:T(8,128)} %get-tuple-element.57, s32[2048]{0:T(1024)S(1)} %dynamic_slice.18, s32[4096]{0:T(1024)S(1)} %add.146), kind=kLoop, calls=%fused_computation.6 | loop fusion | flops 41940992 | bytes 33595392 | tf_op jit(solution)/shard_map/reduce_sum | solution.py:207
  408.3 18.5 %fusion.51 = (bf16[2048,128]{1,0:T(8,128)(2,1)S(1)}, f32[2048,128]{1,0:T(8,128)}) fusion(bf16[4096,128]{1,0:T(8,128)(2,1)S(1)} %bitcast.309, f32[2048]{0:T(1024)S(1)} %log_add_fusion, f32[2048,4096]{1,0:T(8,128)} %get-tuple-element.57, s32[2048]{0:T(1024)S(1)} %dynamic_slice.18, s32[4096]{0:T(1024)S(1)} %add.146), kind=kOutput, calls=%fused_computation.150 | convolution fusion | flops 2189688832 | bytes 36208640 | tf_op jit(solution)/shard_map/dot_general | solution.py:209
  427.2 30.0 %all_to_all.93 = bf16[32,128,128]{1,2,0:T(8,128)(2,1)S(1)} all-to-all(bf16[32,128,128]{1,2,0:T(8,128)(2,1)S(1)} %bitcast_select_fusion.3), channel_id=1, replica_groups=mesh['yh'=2,'x'=4,'z'=4,'yl'=2,'c'=2] {'yh','x','z'}, dimensions={0} | all-to-all | bytes 2097152 | tf_op jit(solution)/shard_map/all_to_all | solution.py:160
  461.2 5.0 fusion.52
  466.2 5.0 fusion.53
  471.2 7.5 multiply_convert_fusion.1
  478.7 6.1 fusion.54
  484.8 5.6 multiply_reduce_fusion.5
  497.4 5.8 all-to-all-start.2
  503.7 20.3 %fusion.2 = bf16[4096,2048]{0,1:T(8,128)(2,1)} fusion(f32[2048,4096]{1,0:T(8,128)} %get-tuple-element.57, f32[2048]{0:T(1024)S(1)} %log_add_fusion, s32[4096]{0:T(1024)S(1)} %add.146, s32[2048]{0:T(1024)S(1)} %dynamic_slice.18), kind=kLoop, calls=%fused_computation.3 | loop fusion | flops 41943040 | bytes 50364416 | tf_op jit(solution)/shard_map/convert_element_type | solution.py:208
  524.0 22.6 %copy.81 = bf16[4096,2048]{1,0:T(8,128)(2,1)} copy(bf16[4096,2048]{0,1:T(8,128)(2,1)} %fusion.2) | data formatting | bytes 33554432 | tf_op jit(solution)/shard_map/dot_general | solution.py:67
  551.4 20.3 %multiply_convert_fusion = bf16[2048,4096]{1,0:T(8,128)(2,1)} fusion(f32[2048]{0:T(1024)S(1)} %multiply_reduce_fusion.2, f32[2048]{0:T(1024)S(1)} %log_add_fusion, bf16[2048,128]{1,0:T(8,128)(2,1)S(1)} %bitcast.265, bf16[4096,128]{1,0:T(8,128)(2,1)} %bitcast.310, f32[2048,4096]{1,0:T(8,128)} %get-tuple-element.57, s32[2048]{0:T(1024)S(1)} %dynamic_slice.18, ...), kind=kOutput, calls=%fused_computation.4 | convolution fusion | flops 2206203904 | bytes 51945472 | tf_op jit(solution)/shard_map/dot_general | solution.py:73
  571.7 9.3 fusion.8
  582.6 5.8 fusion.7
  594.9 10.3 convolution_convert_fusion.6
  608.4 9.9 all-to-all-start.3
  618.9 49.5 %all_gather.212 = bf16[2,128,1024]{2,1,0:T(8,128)(2,1)} all-gather(bf16[1,128,1024]{2,1,0:T(8,128)(2,1)S(1)} %copy-done.15), channel_id=1, replica_groups=mesh['yh'=2,'x'=4,'z'=4,'yl'=2,'c'=2] {'yl'}, dimensions={0}, use_global_device_ids=true | all-gather | bytes 786432 | tf_op jit(solution)/shard_map/all_gather | solution.py:79
  673.6 7.7 all-gather.17
  686.0 7.2 all_gather.194
  700.9 24.2 %all_gather.197 = bf16[2,128,1024]{2,1,0:T(8,128)(2,1)} all-gather(bf16[1,128,1024]{2,1,0:T(8,128)(2,1)S(1)} %copy.74), channel_id=1, replica_groups=mesh['yh'=2,'x'=4,'z'=4,'yl'=2,'c'=2] {'yl'}, dimensions={0}, use_global_device_ids=true | all-gather | bytes 786432 | tf_op jit(solution)/shard_map/all_gather | solution.py:79
  753.5 11.5 all-reduce.5
  773.1 8.3 all-gather.99.cloned.1.call-done
  785.8 10.4 all-gather.87.cloned.1.call-done
  798.8 12.2 all-gather.89.cloned.1.call-done
  813.8 13.3 %all-gather.85.cloned.1.call-done = bf16[2,256,2048]{2,1,0:T(8,128)(2,1)} async-done(((bf16[2,128,2048]{2,1,0:T(8,128)(2,1)}), bf16[2,256,2048]{2,1,0:T(8,128)(2,1)}) %all-gather.85.cloned.1.call-update) | async-done | bytes 2097168 | tf_op jit(solution)/shard_map/all_gather | solution.py:80
  830.8 103.5 %concatenate.38 = bf16[3932736]{0:T(1024)(128)(2,1)} concatenate(bf16[524288]{0:T(1024)(128)(2,1)} %bitcast.272, bf16[262144]{0:T(1024)(128)(2,1)} %bitcast.291, bf16[262144]{0:T(1024)(128)(2,1)} %bitcast.292, bf16[524288]{0:T(1024)(128)(2,1)S(1)} %bitcast.271, bf16[786432]{0:T(1024)(128)(2,1)} %bitcast.261, bf16[786432]{0:T(1024)(128)(2,1)} %bitcast.262, ...), dimensions={0} | concatenate | bytes 15730944 | tf_op jit(solution)/shard_map/concatenate | solution.py:85
  934.3 8.3 pad_bitcast_fusion
  942.7 78.5 %reduce-scatter.3.cloned.1.call-done = bf16[7744,128]{1,0:T(8,128)(2,1)} async-done(((bf16[30976,128]{1,0:T(8,128)(2,1)}), bf16[7744,128]{1,0:T(8,128)(2,1)}) %reduce-scatter.3.cloned.1.call-update) | async-done | bytes 1982480 | tf_op jit(solution)/shard_map/reduce_scatter | solution.py:90
  1021.2 30.6 %reduce-scatter.5.cloned.1.call-done = bf16[1936,128]{1,0:T(8,128)(2,1)} async-done(((bf16[7744,128]{1,0:T(8,128)(2,1)}), bf16[1936,128]{1,0:T(8,128)(2,1)}) %reduce-scatter.5.cloned.1.call-update) | async-done | bytes 495632 | tf_op jit(solution)/shard_map/reduce_scatter | solution.py:91
  1051.9 38.0 %all-reduce.8.cloned.1.call-done = bf16[1936,128]{1,0:T(8,128)(2,1)} async-done(((bf16[1936,128]{1,0:T(8,128)(2,1)}), bf16[1936,128]{1,0:T(8,128)(2,1)}) %all-reduce.8.cloned.1.call-update) | async-done | bytes 495632 | tf_op jit(solution)/shard_map/psum | solution.py:92
  1090.2 31.0 %all-gather.53.cloned.1.call-done = bf16[7744,128]{1,0:T(8,128)(2,1)} async-done(((bf16[1936,128]{1,0:T(8,128)(2,1)}), bf16[7744,128]{1,0:T(8,128)(2,1)}) %all-gather.53.cloned.1.call-update) | async-done | bytes 1982480 | tf_op jit(solution)/shard_map/all_gather | solution.py:93
  1121.3 4.6 fusion.21
  1127.0 75.6 %all-gather.55.cloned.1.call-done = bf16[30976,128]{1,0:T(8,128)(2,1)} async-done(((bf16[7744,128]{1,0:T(8,128)(2,1)}), bf16[30976,128]{1,0:T(8,128)(2,1)}) %all-gather.55.cloned.1.call-update) | async-done | bytes 7929872 | tf_op jit(solution)/shard_map/all_gather | solution.py:94
  1202.6 5.7 slice_convert_fusion
  1208.2 4.5 reshape.471
  (271 shorter events, 146.3 us)
Async XLA Ops:
  7.2 28.8 %all-gather.61.cloned.1.call-start = ((), (), s32[]{:S(2)}) async-start(), calls=%async_computation.18 | async-start | bytes 1572864 | tf_op jit(solution)/shard_map/all_gather | solution.py:79
  7.9 54.6 %all-gather.65.cloned.1.call-start = ((), (), s32[]{:S(2)}) async-start(), calls=%async_computation.20 | async-start | bytes 1572864 | tf_op jit(solution)/shard_map/all_gather | solution.py:79
  8.7 92.1 %all-gather.57.cloned.1.call-start = ((), (), s32[]{:S(2)}) async-start(), calls=%async_computation.16 | async-start | bytes 3145728 | tf_op jit(solution)/shard_map/all_gather | solution.py:79
  9.4 129.6 %all-gather.69.cloned.1.call-start = ((), (), s32[]{:S(2)}) async-start(), calls=%async_computation.22 | async-start | bytes 3145728 | tf_op jit(solution)/shard_map/all_gather | solution.py:79
  10.0 178.9 %all-gather.73.cloned.1.call-start = ((), (), s32[]{:S(2)}) async-start(), calls=%async_computation.24 | async-start | bytes 4718592 | tf_op jit(solution)/shard_map/all_gather | solution.py:79
  10.6 228.3 %all-gather.77.cloned.1.call-start = ((), (), s32[]{:S(2)}) async-start(), calls=%async_computation.26 | async-start | bytes 4718592 | tf_op jit(solution)/shard_map/all_gather | solution.py:79
  11.1 243.7 %all-gather.63.cloned.1.call-start = ((), (), s32[]{:S(2)}) async-start(), calls=%async_computation.19 | async-start | bytes 3145728 | tf_op jit(solution)/shard_map/all_gather | solution.py:80
  36.0 235.1 %all-gather.67.cloned.1.call-start = ((), (), s32[]{:S(2)}) async-start(), calls=%async_computation.21 | async-start | bytes 3145728 | tf_op jit(solution)/shard_map/all_gather | solution.py:80
  62.5 228.0 %all-gather.59.cloned.1.call-start = ((), (), s32[]{:S(2)}) async-start(), calls=%async_computation.17 | async-start | bytes 6291456 | tf_op jit(solution)/shard_map/all_gather | solution.py:80
  100.8 88.4 %copy-start.37 = (s32[1,64]{1,0:T(1,128)S(1)}, s32[1,64]{1,0:T(1,128)}, u32[]{:S(2)}) copy-start(s32[1,64]{1,0:T(1,128)} %param.16) | copy-start | bytes 772
  100.8 88.7 %copy-start = (bf16[1,128,1024]{2,1,0:T(8,128)(2,1)S(1)}, bf16[1,128,1024]{2,1,0:T(8,128)(2,1)}, u32[]{:S(2)}) copy-start(bf16[1,128,1024]{2,1,0:T(8,128)(2,1)} %param.14) | copy-start | bytes 786436
  100.8 274.5 %all-gather.81.cloned.1.call-start = ((), (), s32[]{:S(2)}) async-start(), calls=%async_computation.28 | async-start | bytes 4718592 | tf_op jit(solution)/shard_map/all_gather | solution.py:79
  101.4 355.9 %all-gather.71.cloned.1.call-start = ((), (), s32[]{:S(2)}) async-start(), calls=%async_computation.23 | async-start | bytes 6291456 | tf_op jit(solution)/shard_map/all_gather | solution.py:80
  139.0 322.3 %all-gather.75.cloned.1.call-start = ((), (), s32[]{:S(2)}) async-start(), calls=%async_computation.25 | async-start | bytes 9437184 | tf_op jit(solution)/shard_map/all_gather | solution.py:80
  188.9 68.7 %copy-start.27 = (f32[1024]{0:T(1024)S(1)}, f32[1024]{0:T(1024)}, u32[]{:S(2)}) copy-start(f32[1024]{0:T(1024)} %param.24) | copy-start | bytes 12292
  189.0 277.3 %all-gather.79.cloned.1.call-start = ((), (), s32[]{:S(2)}) async-start(), calls=%async_computation.27 | async-start | bytes 9437184 | tf_op jit(solution)/shard_map/all_gather | solution.py:80
  238.9 58.0 %copy-start.32 = (f32[128]{0:T(128)}, f32[128]{0:T(128)S(1)}, u32[]{:S(2)}) copy-start(f32[128]{0:T(128)S(1)} %add_rsqrt_fusion.3) | copy-start | bytes 1540
  308.1 67.2 %all-to-all-start = ((bf16[32,128,384]{2,1,0:T(8,128)(2,1)}), bf16[32,128,384]{2,1,0:T(8,128)(2,1)}, u32[]{:S(2)}, u32[]{:S(2)}) async-start(bf16[32,128,384]{2,1,0:T(8,128)(2,1)} %pad_maximum_fusion), calls=%async_computation | async-start | bytes 6291456 | tf_op jit(solution)/shard_map/all_to_all | solution.py:160
  318.0 153.2 %all-gather.83.cloned.1.call-start = ((), (), s32[]{:S(2)}) async-start(), calls=%async_computation.29 | async-start | bytes 9437184 | tf_op jit(solution)/shard_map/all_gather | solution.py:80
  377.5 30.8 %copy-start.24 = (bf16[32,128,128]{2,1,0:T(8,128)(2,1)}, bf16[32,128,128]{2,1,0:T(8,128)(2,1)S(1)}, u32[]{:S(2)}) copy-start(bf16[32,128,128]{2,1,0:T(8,128)(2,1)S(1)} %get-tuple-element.40) | copy-start | bytes 3145732
  427.2 33.9 %copy-start.29 = (f32[1024]{0:T(1024)S(1)}, f32[1024]{0:T(1024)}, u32[]{:S(2)}) copy-start(f32[1024]{0:T(1024)} %param.25) | copy-start | bytes 12292
  497.4 49.2 %all-to-all-start.2 = ((bf16[32,128,128]{1,2,0:T(8,128)(2,1)}), bf16[32,128,128]{1,2,0:T(8,128)(2,1)}, u32[]{:S(2)}, u32[]{:S(2)}) async-start(bf16[32,128,128]{1,2,0:T(8,128)(2,1)} %bitcast_select_fusion.2), calls=%async_computation.2 | async-start | bytes 2097152 | tf_op jit(solution)/shard_map/all_to_all | solution.py:160
  503.2 178.2 %all-gather.93.cloned.1.call-start = ((), (), s32[]{:S(2)}) async-start(), calls=%async_computation.34 | async-start | bytes 2359296 | tf_op jit(solution)/shard_map/all_gather | solution.py:79
  608.4 60.1 %all-to-all-start.3 = ((bf16[32,128,384]{1,2,0:T(8,128)(2,1)}), bf16[32,128,384]{1,2,0:T(8,128)(2,1)}, u32[]{:S(2)}, u32[]{:S(2)}) async-start(bf16[32,128,384]{1,2,0:T(8,128)(2,1)} %pad_maximum_fusion.1), calls=%async_computation.3 | async-start | bytes 6291456 | tf_op jit(solution)/shard_map/all_to_all | solution.py:160
  618.3 63.7 %all-gather.97.cloned.1.call-start = ((), (), s32[]{:S(2)}) async-start(), calls=%async_computation.36 | async-start | bytes 2359296 | tf_op jit(solution)/shard_map/all_gather | solution.py:79
  618.9 115.2 %all-gather.101.cloned.1.call-start = ((), (), s32[]{:S(2)}) async-start(), calls=%async_computation.38 | async-start | bytes 1572864 | tf_op jit(solution)/shard_map/all_gather | solution.py:80
  668.4 69.8 %all-gather.51.cloned.1.call-start = ((), (), s32[]{:S(2)}) async-start(), calls=%async_computation.10 | async-start | bytes 1572864 | tf_op jit(solution)/shard_map/all_gather | solution.py:79
  673.6 72.2 %all-gather.91.cloned.1.call-start = ((), (), s32[]{:S(2)}) async-start(), calls=%async_computation.33 | async-start | bytes 1572864 | tf_op jit(solution)/shard_map/all_gather | solution.py:80
  681.4 87.4 %all-gather.95.cloned.1.call-start = ((), (), s32[]{:S(2)}) async-start(), calls=%async_computation.35 | async-start | bytes 4718592 | tf_op jit(solution)/shard_map/all_gather | solution.py:80
  682.0 99.5 %all-gather.99.cloned.1.call-start = ((), (), s32[]{:S(2)}) async-start(), calls=%async_computation.37 | async-start | bytes 4718592 | tf_op jit(solution)/shard_map/all_gather | solution.py:80
  682.7 113.5 %all-gather.87.cloned.1.call-start = ((), (), s32[]{:S(2)}) async-start(), calls=%async_computation.31 | async-start | bytes 1572864 | tf_op jit(solution)/shard_map/all_gather | solution.py:80
  685.9 39.5 %copy-start.28 = (f32[1024]{0:T(1024)S(1)}, f32[1024]{0:T(1024)}, u32[]{:S(2)}) copy-start(f32[1024]{0:T(1024)} %param.24) | copy-start | bytes 12292
  693.2 37.4 %copy-start.33 = (f32[128]{0:T(128)S(1)}, f32[128]{0:T(128)}, u32[]{:S(2)}) copy-start(f32[128]{0:T(128)} %copy-done.32) | copy-start | bytes 1540
  695.3 36.2 %copy-start.38 = (u32[128]{0:T(128)S(1)}, u32[128]{0:T(128)}, u32[]{:S(2)}) copy-start(u32[128]{0:T(128)} %constant.90) | copy-start | bytes 1540
  695.3 31.1 %all-to-all-start.7 = ((bf16[128,4,768]{2,0,1:T(8,128)(2,1)}), bf16[128,4,768]{2,0,1:T(8,128)(2,1)}, u32[]{:S(2)}, u32[]{:S(2)}) async-start(bf16[128,4,768]{2,0,1:T(8,128)(2,1)} %bitcast.239), calls=%async_computation.7 | async-start | bytes 1572864 | tf_op jit(solution)/shard_map/all_to_all | solution.py:291
  699.6 111.4 %all-gather.89.cloned.1.call-start = ((), (), s32[]{:S(2)}) async-start(), calls=%async_computation.32 | async-start | bytes 1572864 | tf_op jit(solution)/shard_map/all_gather | solution.py:80
  700.7 33.4 %copy-start.19 = (bf16[128,8,128]{0,2,1:T(8,128)(2,1)}, bf16[128,8,128]{0,2,1:T(8,128)(2,1)S(1)}, u32[]{:S(2)}) copy-start(bf16[128,8,128]{0,2,1:T(8,128)(2,1)S(1)} %slice.169) | copy-start | bytes 786436
  726.4 13.1 %all-to-all-start.5 = ((bf16[128,4,512]{2,0,1:T(8,128)(2,1)}), bf16[128,4,512]{2,0,1:T(8,128)(2,1)}, u32[]{:S(2)}, u32[]{:S(2)}) async-start(bf16[128,4,512]{2,0,1:T(8,128)(2,1)} %copy.75), calls=%async_computation.5 | async-start | bytes 1048576 | tf_op jit(solution)/shard_map/all_to_all | solution.py:289
  730.5 96.6 %all-gather.85.cloned.1.call-start = ((), (), s32[]{:S(2)}) async-start(), calls=%async_computation.30 | async-start | bytes 3145728 | tf_op jit(solution)/shard_map/all_gather | solution.py:80
  739.5 25.8 %all-to-all-start.6 = ((bf16[128,4,256]{2,0,1:T(8,128)(2,1)}), bf16[128,4,256]{2,0,1:T(8,128)(2,1)S(1)}, u32[]{:S(2)}, u32[]{:S(2)}) async-start(bf16[128,4,256]{2,0,1:T(8,128)(2,1)} %bitcast.306), calls=%async_computation.6 | async-start | bytes 524288 | tf_op jit(solution)/shard_map/all_to_all | solution.py:290
  765.3 20.6 %all-to-all-start.4 = ((bf16[128,4,256]{2,0,1:T(8,128)(2,1)}), bf16[128,4,256]{2,0,1:T(8,128)(2,1)S(1)}, u32[]{:S(2)}, u32[]{:S(2)}) async-start(bf16[128,4,256]{2,0,1:T(8,128)(2,1)} %fusion.24), calls=%async_computation.4 | async-start | bytes 524288 | tf_op jit(solution)/shard_map/all_to_all | solution.py:288
  768.7 252.5 %reduce-scatter.3.cloned.1.call-start = ((), (), s32[]{:S(2)}) async-start(), calls=%async_computation.11 | async-start | bytes 9912320 | tf_op jit(solution)/shard_map/reduce_scatter | solution.py:90
  785.8 25.2 %copy-start.12 = (bf16[128,4,256]{2,0,1:T(8,128)(2,1)}, bf16[128,4,256]{2,0,1:T(8,128)(2,1)S(1)}, u32[]{:S(2)}) copy-start(bf16[128,4,256]{2,0,1:T(8,128)(2,1)S(1)} %all-to-all-done.4) | copy-start | bytes 786436
  942.6 178.6 %copy-start.14 = (bf16[128,3072]{1,0:T(8,128)(2,1)S(1)}, bf16[128,3072]{1,0:T(8,128)(2,1)}, u32[]{:S(2)}) copy-start(bf16[128,3072]{1,0:T(8,128)(2,1)} %get-tuple-element.38) | copy-start | bytes 2359300
  942.6 109.2 %reduce-scatter.5.cloned.1.call-start = ((), (), s32[]{:S(2)}) async-start(), calls=%async_computation.12 | async-start | bytes 2478080 | tf_op jit(solution)/shard_map/reduce_scatter | solution.py:91
  1021.2 68.7 %all-reduce.8.cloned.1.call-start = ((), (), s32[]{:S(2)}) async-start(), calls=%async_computation.13 | async-start | bytes 991232 | tf_op jit(solution)/shard_map/psum | solution.py:92
  1051.9 69.3 %all-gather.53.cloned.1.call-start = ((), (), s32[]{:S(2)}) async-start(), calls=%async_computation.14 | async-start | bytes 2478080 | tf_op jit(solution)/shard_map/all_gather | solution.py:93
  1089.9 112.7 %all-gather.55.cloned.1.call-start = ((), (), s32[]{:S(2)}) async-start(), calls=%async_computation.15 | async-start | bytes 9912320 | tf_op jit(solution)/shard_map/all_gather | solution.py:94
  (28 other events, 219.9 us)
Sparse Core Ops, SparseCore 0:
  9.7 26.2 all-gather.60
  37.6 24.7 all-gather.64
  64.1 36.6 all-gather.56
  102.3 36.6 all-gather.68
  140.5 48.4 all-gather.72
  190.4 48.4 all-gather.76
  240.5 14.2 all-gather.62
  256.5 14.6 all-gather.66
  272.8 17.6 all-gather.58
  292.0 83.2 all-gather.80
  377.0 21.1 all-gather.70
  399.6 20.8 all-gather.74
  422.2 20.7 all-gather.78
  444.5 20.7 all-gather.82
  546.7 31.0 all-gather.92
  621.0 55.6 all-gather.96
  678.2 14.9 all-gather.100
  695.3 32.9 all-gather.50
  730.0 15.8 all-gather.90
  747.3 16.2 all-gather.94
  765.3 16.1 all-gather.98
  783.1 13.0 all-gather.86
  797.9 13.0 all-gather.88
  812.5 14.6 all-gather.84
  942.7 78.3 reduce-scatter.2
  1023.4 28.3 reduce-scatter.4
  1054.3 35.5 all-reduce.7
  1091.6 29.5 all-gather.52
  1123.0 79.5 all-gather.54

commit v3 on v2

--- a/solution.py
+++ b/solution.py
@@ -81,23 +81,12 @@
     return both.reshape((-1,) + values.shape[1:])
 
 
-def reduce_ctx(shards):
-    flat = jnp.concatenate([s.astype(jnp.bfloat16).reshape(-1) for s in shards])
-    lanes = 128
-    step = 256 * lanes
-    padded = -(-flat.shape[0] // step) * step
-    flat = jnp.pad(flat, (0, padded - flat.shape[0])).reshape(padded // lanes, lanes)
-    part = lax.psum_scatter(flat, "z", scatter_dimension=0, tiled=True)
+def reduce_ctx(packed):
+    part = lax.psum_scatter(packed, "z", scatter_dimension=0, tiled=True)
     part = lax.psum_scatter(part, "x", scatter_dimension=0, tiled=True)
     part = lax.psum(part, "yh")
     part = lax.all_gather(part, "x", axis=0, tiled=True)
-    full = lax.all_gather(part, "z", axis=0, tiled=True).reshape(-1)
-    out = []
-    at = 0
-    for s in shards:
-        out.append(full[at : at + s.size].reshape(s.shape).astype(jnp.float32))
-        at += s.size
-    return tuple(out)
+    return lax.all_gather(part, "z", axis=0, tiled=True).astype(jnp.float32)
 
 
 def on_device(
@@ -159,30 +148,30 @@
     def exchange(values):
         return lax.all_to_all(values, CTX, split_axis=0, concat_axis=0, tiled=True)
 
-    full_query, full_key, full_value, full_output, full_gate, full_up, full_down = (
-        gather_fsdp(query_weight),
-        gather_fsdp(key_projection),
-        gather_fsdp(value_projection),
-        gather_fsdp(output_weight),
-        gather_fsdp(gate_weight),
-        gather_fsdp(up_weight),
-        gather_fsdp(down_weight),
-    )
+    qkv_cols = (query_weight.shape[1], key_projection.shape[1], value_projection.shape[1])
+    full_qkv = lax.all_gather(
+        jnp.concatenate([query_weight, key_projection, value_projection], axis=1), FSDP, axis=0, tiled=True
+    )
+    full_output = lax.all_gather(output_weight, FSDP, axis=0, tiled=True)
+    ff_cols = gate_weight.shape[1]
+    full_gate_up = lax.all_gather(
+        jnp.concatenate([gate_weight, up_weight], axis=1), FSDP, axis=0, tiled=True
+    )
+    full_down = lax.all_gather(down_weight, FSDP, axis=0, tiled=True)
     input_f32 = layer_input[0].astype(jnp.float32)
     gained, first_normed, first_scale = rms_apply(input_f32, first_gain)
     attention_input = gained.astype(jnp.bfloat16)
-    query_pre = jnp.dot(attention_input, full_query, preferred_element_type=jnp.float32).reshape(
-        local_rows, HQ, HEAD_SIZE
-    )
+    qkv_pre = jnp.dot(attention_input, full_qkv, preferred_element_type=jnp.float32)
+    query_pre = qkv_pre[:, : qkv_cols[0]].reshape(local_rows, HQ, HEAD_SIZE)
     query_gained, query_normed, query_scale = rms_apply(query_pre, query_gain)
     query_rotated = rotary_apply(query_gained, cosine_table, sine_values_table).astype(jnp.bfloat16)
-    key_before_norm = jnp.dot(
-        attention_input, full_key, preferred_element_type=jnp.float32
-    ).reshape(local_rows, KEY_VALUE_HEADS, HEAD_SIZE)
+    key_before_norm = qkv_pre[:, qkv_cols[0] : qkv_cols[0] + qkv_cols[1]].reshape(
+        local_rows, KEY_VALUE_HEADS, HEAD_SIZE
+    )
     key_after_gain, key_after_norm, key_norm_scale = rms_apply(key_before_norm, key_norm_gain)
     own_keys = rotary_apply(key_after_gain, cosine_table, sine_values_table).astype(jnp.bfloat16)
     own_values = (
-        jnp.dot(attention_input, full_value, preferred_element_type=jnp.float32)
+        qkv_pre[:, qkv_cols[0] + qkv_cols[1] :]
         .astype(jnp.bfloat16)
         .reshape(local_rows, KEY_VALUE_HEADS, HEAD_SIZE)
     )
@@ -213,8 +202,9 @@
     residual_mid = input_f32 + jnp.dot(mixed_b, full_output, preferred_element_type=jnp.float32)
     gained_mid, second_normed, second_scale = rms_apply(residual_mid, second_gain)
     mlp_in = gained_mid.astype(jnp.bfloat16)
-    gate_pre = jnp.dot(mlp_in, full_gate, preferred_element_type=jnp.float32)
-    up_pre = jnp.dot(mlp_in, full_up, preferred_element_type=jnp.float32)
+    gate_up_pre = jnp.dot(mlp_in, full_gate_up, preferred_element_type=jnp.float32)
+    gate_pre = gate_up_pre[:, :ff_cols]
+    up_pre = gate_up_pre[:, ff_cols:]
     sigmoid_gate = jax.nn.sigmoid(gate_pre)
     silu_gate = gate_pre * sigmoid_gate
     hidden = (silu_gate * up_pre).astype(jnp.bfloat16)
@@ -227,7 +217,8 @@
         hidden_grad * up_pre * sigmoid_gate * (1.0 + gate_pre * (1.0 - sigmoid_gate))
     ).astype(jnp.bfloat16)
     up_grad = (hidden_grad * silu_gate).astype(jnp.bfloat16)
-    mlp_in_grad = right_dot(gate_grad, full_gate) + right_dot(up_grad, full_up)
+    gate_up_grad = jnp.concatenate([gate_grad, up_grad], axis=1)
+    mlp_in_grad = right_dot(gate_up_grad, full_gate_up)
     second_gain_grad = jnp.sum(mlp_in_grad * second_normed, axis=0)
     mid_grad = own_cotangent.astype(jnp.float32) + root_mean_square_backward(
         mlp_in_grad, second_normed, second_scale, second_gain
@@ -275,59 +266,67 @@
         .reshape(local_rows, KEY_VALUE_HEADS * HEAD_SIZE)
     )
     value_gradient_second = own_value_grad.astype(jnp.bfloat16)
+    qkv_grad = jnp.concatenate([query_pre_grad, key_before_norm_gradient, value_gradient_second], axis=1)
     attn_in_grad = (
-        right_dot(query_pre_grad, full_query)
-        + right_dot(key_before_norm_gradient, full_key)
-        + right_dot(value_gradient_second, full_value)
+        right_dot(qkv_grad, full_qkv)
     )
     first_gain_grad = jnp.sum(attn_in_grad * first_normed, axis=0)
     input_grad = mid_grad + root_mean_square_backward(
         attn_in_grad, first_normed, first_scale, first_gain
     )
+    fsdp_size = lax.axis_size(FSDP)
+    col_parts = (attention_input, mixed_b, mlp_in, hidden)
+    widths = [p.shape[1] // fsdp_size for p in col_parts]
+    stacked = jnp.concatenate(
+        [p.reshape(local_rows, fsdp_size, w) for p, w in zip(col_parts, widths)], axis=2
+    )
+    cols = lax.all_to_all(stacked, FSDP, split_axis=1, concat_axis=0, tiled=True).reshape(
+        fsdp_size * local_rows, sum(widths)
+    )
+    bounds = [sum(widths[:i]) for i in range(5)]
     attn_cols, mixed_cols, mlp_cols, hidden_cols = (
-        lax.all_to_all(attention_input, FSDP, split_axis=1, concat_axis=0, tiled=True),
-        lax.all_to_all(mixed_b, FSDP, split_axis=1, concat_axis=0, tiled=True),
-        lax.all_to_all(mlp_in, FSDP, split_axis=1, concat_axis=0, tiled=True),
-        lax.all_to_all(hidden, FSDP, split_axis=1, concat_axis=0, tiled=True),
-    )
-    cot_rows, gate_rows, up_rows, mid_rows, query_rows, key_rows, value_row_block = (
-        gather_fsdp(own_cotangent),
-        gather_fsdp(gate_grad),
-        gather_fsdp(up_grad),
-        gather_fsdp(mid_grad_b),
-        gather_fsdp(query_pre_grad),
-        gather_fsdp(key_before_norm_gradient),
-        gather_fsdp(value_gradient_second),
-    )
-    query_shard = left_dot(attn_cols, query_rows)
-    key_shard = left_dot(attn_cols, key_rows)
-    value_shard = left_dot(attn_cols, value_row_block)
-    output_shard = left_dot(mixed_cols, mid_rows)
-    gate_shard = left_dot(mlp_cols, gate_rows)
-    up_shard = left_dot(mlp_cols, up_rows)
-    down_shard = left_dot(hidden_cols, cot_rows)
+        cols[:, bounds[i] : bounds[i + 1]] for i in range(4)
+    )
+    qkv_rows = lax.all_gather(qkv_grad, FSDP, axis=0, tiled=True)
+    gate_up_rows = lax.all_gather(gate_up_grad, FSDP, axis=0, tiled=True)
+    cot_mid_rows = lax.all_gather(
+        jnp.concatenate([own_cotangent, mid_grad_b], axis=1), FSDP, axis=0, tiled=True
+    )
+    model_width = own_cotangent.shape[1]
+    qkv_shard = left_dot(attn_cols, qkv_rows)
+    output_shard = left_dot(mixed_cols, cot_mid_rows[:, model_width:])
+    gate_up_shard = left_dot(mlp_cols, gate_up_rows)
+    down_shard = left_dot(hidden_cols, cot_mid_rows[:, :model_width])
+    shard_rows = qkv_shard.shape[0]
+    packed = jnp.concatenate(
+        [
+            qkv_shard,
+            output_shard.reshape(shard_rows, -1),
+            gate_up_shard,
+            down_shard.reshape(shard_rows, -1),
+        ],
+        axis=1,
+    ).astype(jnp.bfloat16)
+    reduced = reduce_ctx(packed)
+    pieces = []
+    at = 0
+    for width in (qkv_cols[0], qkv_cols[1], qkv_cols[2], output_shard.size // shard_rows, ff_cols, ff_cols,
+                  down_shard.size // shard_rows):
+        pieces.append(reduced[:, at : at + width])
+        at += width
+    query_total, key_total, value_total, output_total, gate_total, up_total, down_total = pieces
+    output_total = output_total.reshape(output_shard.shape)
+    down_total = down_total.reshape(down_shard.shape)
     first_shard, second_shard, query_gain_shard, key_gain_shard = (
         lax.psum_scatter(first_gain_grad, FSDP, scatter_dimension=0, tiled=True),
         lax.psum_scatter(second_gain_grad, FSDP, scatter_dimension=0, tiled=True),
         lax.psum_scatter(query_gain_grad, FSDP, scatter_dimension=0, tiled=True),
         lax.psum_scatter(key_gain_grad, FSDP, scatter_dimension=0, tiled=True),
     )
-    shards = (query_shard, key_shard, value_shard, output_shard, gate_shard, up_shard, down_shard,
-              first_shard, second_shard, query_gain_shard, key_gain_shard)
-    totals = reduce_ctx(shards)
-    (
-        query_total,
-        key_total,
-        value_total,
-        output_total,
-        gate_total,
-        up_total,
-        down_total,
-        first_total,
-        second_total,
-        query_gain_total,
-        key_gain_total,
-    ) = totals
+    first_total, second_total, query_gain_total, key_gain_total = (
+        lax.psum(g.astype(jnp.bfloat16), CTX).astype(jnp.float32)
+        for g in (first_shard, second_shard, query_gain_shard, key_gain_shard)
+    )
     return (
         layer_output[None],
         input_grad[None],

time: 1260 us -> 980 us (0.78)
  waiting for transfers between devices: 632 us -> 455 us
  local copies, waits for them, and re-layouts: 204 us -> 77.1 us
  blocking collectives: 130 us -> 179 us
    all_gather x25 -> x8, waiting for transfers between devices: 446 us -> 193 us  [the longest x1 78.7 us: on_device(): lax.all_gather(jnp.concatenate([query_weight, key_projection, value_proje...]
    concatenate x1 -> x2, local copies, waits for them, and re-layouts: 104 us -> 2.73 us  [rotary_backward(): jnp.concatenate([front_half * cosine_table + back_half * sine_values_tabl...]
    psum x0 -> x1, blocking collectives: none -> 95 us  [on_device(): lax.psum(g.astype(jnp.bfloat16), CTX).astype(jnp.float32)]
    all_gather x4 -> x0, blocking collectives: 88.5 us -> none  [gather_fsdp(): across = lax.all_gather(values, 'yl', axis=0, tiled=False)]
    all_to_all x3, waiting for transfers between devices: 0.01 us -> 85.9 us  [exchange(): return lax.all_to_all(values, CTX, split_axis=0, concat_axis=0, tiled=True)]
    all_to_all x0 -> x1, blocking collectives: none -> 41.4 us  [on_device(): lax.all_to_all(stacked, FSDP, split_axis=1, concat_axis=0, tiled=True)]
    convert_element_type x7 -> x0, local copies, waits for them, and re-layouts: 17.7 us -> none  [reduce_ctx(): out.append(full[at:at + s.size].reshape(s.shape).astype(jnp.float32))]
    all_to_all x4 -> x0, starting transfers between devices: 15.3 us -> none  [the longest x1 4.32 us: on_device(): lax.all_to_all(hidden, FSDP, split_axis=1, concat_axis=0, tiled=True)]
  transfers between devices with their start and end apart: 36 -> 15, of which waited for: 21 -> 10; matrix products, arithmetic and copies ran while one was open for 20% -> 24% of each run, Pallas kernels for 0% -> 0%
where the time goes in v3:
time: 980 us; the launch traced here: 972 us
  waiting for transfers between devices  455 us (46%)
  blocking collectives  179 us (18%)
  matrix products  139 us (14%)
  local copies, waits for them, and re-layouts  77.1 us (8%)
  other arithmetic  73.8 us (8%)
  starting transfers between devices  30.3 us (3%)
  between operations  16.9 us (2%)
    psum x1, blocking collectives, on_device(): lax.psum(g.astype(jnp.bfloat16), CTX).astype(jnp.float32)  95 us
    all_to_all x3, waiting for transfers between devices, exchange(): return lax.all_to_all(values, CTX, split_axis=0, concat_axis=0, tiled=True)  85.9 us
    all_gather x1, waiting for transfers between devices, on_device(): lax.all_gather(jnp.concatenate([query_weight, key_projection, value_proje...  78.7 us
    reduce_scatter x1, waiting for transfers between devices, reduce_ctx(): part = lax.psum_scatter(packed, 'z', scatter_dimension=0, tiled=True)  75.6 us
    all_gather x1, waiting for transfers between devices, on_device(): full_down = lax.all_gather(down_weight, FSDP, axis=0, tiled=True)  59.3 us
    all_gather x1, waiting for transfers between devices, on_device(): lax.all_gather(jnp.concatenate([gate_weight, up_weight], axis=1), FSDP, a...  51.7 us
    dot_general x5, matrix products, right_dot(): lax.dot_general(left_side, right_side, (((1,), (1,)), ((), ())), preferre...  46 us
    all_to_all x1, blocking collectives, on_device(): lax.all_to_all(stacked, FSDP, split_axis=1, concat_axis=0, tiled=True)  41.4 us
  transfers between devices with their start and end apart: 15, of which 10 were waited for; matrix products, arithmetic and copies ran while one was open for 24% of the time, Pallas kernels for 0%

profile of v3, /device:TPU:0, one launch (start us, length us, event | category | flops | bytes accessed | tf_op | source)
XLA Modules:
  0.0 971.5 jit_solution(5550237848268828728)
XLA Ops:
  7.2 3.2 pad_maximum_fusion.4
  14.6 78.7 %all-gather.10.cloned.1.call-done = bf16[1024,4096]{1,0:T(8,128)(2,1)} async-done(((bf16[256,4096]{1,0:T(8,128)(2,1)}), bf16[1024,4096]{1,0:T(8,128)(2,1)}) %all-gather.10.cloned.1.call-update) | async-done | bytes 8388624 | tf_op jit(solution)/shard_map/all_gather | solution.py:152
  93.3 4.7 fusion.26
  106.6 2.3 copy.175
  118.4 9.4 all-to-all-start
  128.4 47.6 %all-to-all-done = bf16[32,128,384]{2,1,0:T(8,128)(2,1)S(1)} async-done(((bf16[32,128,384]{2,1,0:T(8,128)(2,1)}), bf16[32,128,384]{2,1,0:T(8,128)(2,1)S(1)}, u32[]{:S(2)}, u32[]{:S(2)}) %all-to-all-start) | async-done | bytes 3145760 | tf_op jit(solution)/shard_map/all_to_all | solution.py:149
  176.7 14.0 %fusion.37 = (f32[2048]{0:T(1024)S(1)}, f32[2048,4096]{1,0:T(8,128)}) fusion(s32[2048]{0:T(1024)S(1)} %dynamic_slice.18, s32[4096]{0:T(1024)S(1)} %add.143, bf16[2048,128]{1,0:T(8,128)(2,1)S(1)} %bitcast.195, bf16[4096,128]{1,0:T(8,128)(2,1)S(1)} %bitcast.189), kind=kOutput, calls=%fused_computation.140 | convolution fusion | flops 2181036032 | bytes 35160064 | tf_op jit(solution)/shard_map/qd,kd->qk/dot_general | solution.py:189
  190.7 16.6 %exponential_reduce_fusion = f32[2048]{0:T(1024)S(1)} fusion(f32[2048]{0:T(1024)S(1)} %get-tuple-element.56, f32[2048,4096]{1,0:T(8,128)} %get-tuple-element.57, s32[2048]{0:T(1024)S(1)} %dynamic_slice.18, s32[4096]{0:T(1024)S(1)} %add.143), kind=kLoop, calls=%fused_computation.6 | loop fusion | flops 41940992 | bytes 33595392 | tf_op jit(solution)/shard_map/reduce_sum | solution.py:196
  207.3 15.6 %fusion.42 = (bf16[2048,128]{1,0:T(8,128)(2,1)S(1)}, f32[2048,128]{1,0:T(8,128)}) fusion(bf16[4096,128]{1,0:T(8,128)(2,1)S(1)} %bitcast.191, f32[2048]{0:T(1024)S(1)} %log_add_fusion, f32[2048,4096]{1,0:T(8,128)} %get-tuple-element.57, s32[2048]{0:T(1024)S(1)} %dynamic_slice.18, s32[4096]{0:T(1024)S(1)} %add.143), kind=kOutput, calls=%fused_computation.145 | convolution fusion | flops 2189688832 | bytes 36208640 | tf_op jit(solution)/shard_map/dot_general | solution.py:198
  223.4 31.4 %all_to_all.35 = bf16[32,128,128]{1,2,0:T(8,128)(2,1)S(1)} all-to-all(bf16[32,128,128]{1,2,0:T(8,128)(2,1)S(1)} %bitcast_select_fusion.3), channel_id=1, replica_groups=mesh['yh'=2,'x'=4,'z'=4,'yl'=2,'c'=2] {'yh','x','z'}, dimensions={0} | all-to-all | bytes 2097152 | tf_op jit(solution)/shard_map/all_to_all | solution.py:149
  254.9 3.2 multiply_reduce_fusion.10
  259.0 51.7 %all-gather.14.cloned.1.call-done = bf16[1024,6144]{1,0:T(8,128)(2,1)} async-done(((bf16[256,6144]{1,0:T(8,128)(2,1)}), bf16[1024,6144]{1,0:T(8,128)(2,1)}) %all-gather.14.cloned.1.call-update) | async-done | bytes 12582928 | tf_op jit(solution)/shard_map/all_gather | solution.py:157
  310.7 8.0 fusion.43
  318.8 59.3 %all-gather.16.cloned.1.call-done = bf16[3072,1024]{1,0:T(8,128)(2,1)} async-done(((bf16[768,1024]{1,0:T(8,128)(2,1)}), bf16[3072,1024]{1,0:T(8,128)(2,1)}) %all-gather.16.cloned.1.call-update) | async-done | bytes 6291472 | tf_op jit(solution)/shard_map/all_gather | solution.py:160
  378.1 7.7 multiply_convert_fusion.2
  385.9 7.2 multiply_reduce_fusion.5
  394.6 3.7 fusion.10
  400.1 9.4 all-to-all-start.2
  410.7 20.5 %fusion.2 = bf16[4096,2048]{0,1:T(8,128)(2,1)} fusion(f32[2048,4096]{1,0:T(8,128)} %get-tuple-element.57, f32[2048]{0:T(1024)S(1)} %log_add_fusion, s32[4096]{0:T(1024)S(1)} %add.143, s32[2048]{0:T(1024)S(1)} %dynamic_slice.18), kind=kLoop, calls=%fused_computation.3 | loop fusion | flops 41943040 | bytes 50364416 | tf_op jit(solution)/shard_map/convert_element_type | solution.py:197
  431.1 22.7 %copy.196 = bf16[4096,2048]{1,0:T(8,128)(2,1)} copy(bf16[4096,2048]{0,1:T(8,128)(2,1)} %fusion.2) | data formatting | bytes 33554432 | tf_op jit(solution)/shard_map/dot_general | solution.py:67
  456.7 20.9 %multiply_convert_fusion = bf16[2048,4096]{1,0:T(8,128)(2,1)} fusion(f32[2048]{0:T(1024)S(1)} %multiply_reduce_fusion.2, f32[2048]{0:T(1024)S(1)} %log_add_fusion, bf16[2048,128]{1,0:T(8,128)(2,1)S(1)} %bitcast.161, bf16[4096,128]{1,0:T(8,128)(2,1)} %bitcast.192, f32[2048,4096]{1,0:T(8,128)} %get-tuple-element.57, s32[2048]{0:T(1024)S(1)} %dynamic_slice.18, ...), kind=kOutput, calls=%fused_computation.4 | convolution fusion | flops 2206203904 | bytes 51945472 | tf_op jit(solution)/shard_map/dot_general | solution.py:73
  477.6 8.8 fusion.8
  486.9 10.6 %fusion.7 = bf16[4096,128]{1,0:T(8,128)(2,1)S(1)} fusion(bf16[2048,4096]{1,0:T(8,128)(2,1)} %multiply_convert_fusion, bf16[2048,128]{1,0:T(8,128)(2,1)} %bitcast.196), kind=kOutput, calls=%fused_computation.15 | convolution fusion | flops 2148532224 | bytes 18350080 | tf_op jit(solution)/shard_map/dot_general | solution.py:67
  498.8 9.5 convolution_convert_fusion.5
  508.3 2.8 pad_maximum_fusion.3
  511.1 9.9 %all-to-all-start.3 = ((bf16[32,128,384]{1,2,0:T(8,128)(2,1)}), bf16[32,128,384]{1,2,0:T(8,128)(2,1)S(1)}, u32[]{:S(2)}, u32[]{:S(2)}) async-start(bf16[32,128,384]{1,2,0:T(8,128)(2,1)} %pad_maximum_fusion.3), calls=%async_computation.3 | async-start | bytes 6291456 | tf_op jit(solution)/shard_map/all_to_all | solution.py:149
  522.9 2.5 copy.195
  528.3 38.3 %all-to-all-done.3 = bf16[32,128,384]{1,2,0:T(8,128)(2,1)S(1)} async-done(((bf16[32,128,384]{1,2,0:T(8,128)(2,1)}), bf16[32,128,384]{1,2,0:T(8,128)(2,1)S(1)}, u32[]{:S(2)}, u32[]{:S(2)}) %all-to-all-start.3) | async-done | bytes 3145760 | tf_op jit(solution)/shard_map/all_to_all | solution.py:149
  569.1 2.5 copy.198
  582.4 41.4 %all_to_all.36 = bf16[128,4,1792]{2,0,1:T(8,128)(2,1)S(1)} all-to-all(bf16[128,4,1792]{2,0,1:T(8,128)(2,1)S(1)} %pad_maximum_fusion.5), channel_id=1, replica_groups=mesh['yh'=2,'x'=4,'z'=4,'yl'=2,'c'=2] {'yl','c'}, dimensions={1} | all-to-all | bytes 3670016 | tf_op jit(solution)/shard_map/all_to_all | solution.py:283
  623.8 2.6 convolution_convert_fusion.4
  627.6 3.4 convolution_convert_fusion.3
  631.0 3.7 reshape.309
  634.7 4.7 convolution_convert_fusion
  639.4 3.4 all-gather.18.cloned.1.call-done
  642.7 3.7 convolution_convert_fusion.1
  646.4 3.5 pad_maximum_fusion
  650.1 75.6 %reduce-scatter.3.cloned.1.call-done = bf16[64,15360]{1,0:T(8,128)(2,1)} async-done(((bf16[256,15360]{1,0:T(8,128)(2,1)}), bf16[64,15360]{1,0:T(8,128)(2,1)}) %reduce-scatter.3.cloned.1.call-update) | async-done | bytes 1966096 | tf_op jit(solution)/shard_map/reduce_scatter | solution.py:85
  725.8 30.5 %reduce-scatter.5.cloned.1.call-done = bf16[16,15360]{1,0:T(8,128)(2,1)} async-done(((bf16[64,15360]{1,0:T(8,128)(2,1)}), bf16[16,15360]{1,0:T(8,128)(2,1)}) %reduce-scatter.5.cloned.1.call-update) | async-done | bytes 491536 | tf_op jit(solution)/shard_map/reduce_scatter | solution.py:86
  756.4 38.0 %all-reduce.8.cloned.1.call-done = bf16[16,15360]{1,0:T(8,128)(2,1)} async-done(((bf16[16,15360]{1,0:T(8,128)(2,1)}), bf16[16,15360]{1,0:T(8,128)(2,1)}) %all-reduce.8.cloned.1.call-update) | async-done | bytes 491536 | tf_op jit(solution)/shard_map/psum | solution.py:87
  794.6 30.5 %all-gather.24.cloned.1.call-done = bf16[64,15360]{1,0:T(8,128)(2,1)} async-done(((bf16[16,15360]{1,0:T(8,128)(2,1)}), bf16[64,15360]{1,0:T(8,128)(2,1)}) %all-gather.24.cloned.1.call-update) | async-done | bytes 1966096 | tf_op jit(solution)/shard_map/all_gather | solution.py:88
  827.2 4.5 fusion.12
  831.8 6.4 multiply_reduce_fusion.6
  838.2 11.7 %all-reduce.4 = (bf16[1024]{0:T(1024)(128)(2,1)S(1)}, bf16[1024]{0:T(1024)(128)(2,1)S(1)}, bf16[128]{0:T(256)(128)(2,1)S(1)}, bf16[128]{0:T(256)(128)(2,1)S(1)}) all-reduce(f32[1024]{0:T(1024)S(1)} %get-tuple-element.15, f32[1024]{0:T(1024)S(1)} %copy-done.46, ...), channel_id=4, replica_groups=mesh['yh'=2,'x'=4,'z'=4,'yl'=2,'c'=2] {'yl','c'}, use_global_device_ids=true, to_apply=%region_16.17.clone | all-reduce | flops 2304 | bytes 13824
  850.2 95.0 %all-reduce.5 = (bf16[256]{0:T(256)(128)(2,1)S(1)}, bf16[256]{0:T(256)(128)(2,1)S(1)}, bf16[32]{0:T(256)(128)(2,1)S(1)}, bf16[32]{0:T(256)(128)(2,1)S(1)}) all-reduce(bf16[256]{0:T(256)(128)(2,1)S(1)} %dynamic-slice.13, bf16[256]{0:T(256)(128)(2,1)S(1)} %dynamic-slice.12, ...), channel_id=1, replica_groups=mesh['yh'=2,'x'=4,'z'=4,'yl'=2,'c'=2] {'yh','x','z'}, use_global_device_ids=true, to_apply=%region_17.18 | all-reduce | flops 576 | bytes 2304 | tf_op jit(solution)/shard_map/psum | solution.py:327
  948.5 6.3 fusion.38
  956.9 3.4 fusion.39
  961.7 2.8 fusion.40
  (261 shorter events, 60.5 us)
Async XLA Ops:
  7.2 86.1 %all-gather.10.cloned.1.call-start = ((), (), s32[]{:S(2)}) async-start(), calls=%async_computation.7 | async-start | bytes 10485760 | tf_op jit(solution)/shard_map/all_gather | solution.py:152
  10.5 244.4 %all-gather.12.cloned.1.call-start = ((), (), s32[]{:S(2)}) async-start(), calls=%async_computation.8 | async-start | bytes 5242880 | tf_op jit(solution)/shard_map/all_gather | solution.py:155
  11.3 82.0 %copy-start.38 = (f32[1024]{0:T(1024)S(1)}, f32[1024]{0:T(1024)}, u32[]{:S(2)}) copy-start(f32[1024]{0:T(1024)} %param.24) | copy-start | bytes 12292
  11.3 299.5 %all-gather.14.cloned.1.call-start = ((), (), s32[]{:S(2)}) async-start(), calls=%async_computation.9 | async-start | bytes 15728640 | tf_op jit(solution)/shard_map/all_gather | solution.py:157
  14.4 83.6 %copy-start.52 = (f32[128]{0:T(128)}, f32[128]{0:T(128)S(1)}, u32[]{:S(2)}) copy-start(f32[128]{0:T(128)S(1)} %add_rsqrt_fusion.3) | copy-start | bytes 1540
  98.0 15.4 %copy-start.3 = (f32[128,4096]{1,0:T(8,128)}, f32[128,4096]{1,0:T(8,128)S(1)}, u32[]{:S(2)}) copy-start(f32[128,4096]{1,0:T(8,128)S(1)} %fusion.26) | copy-start | bytes 6291460
  101.1 7.9 copy-start.5
  109.7 415.8 %copy-start.44 = (f32[128,8]{0,1:T(8,128)}, f32[128,8]{0,1:T(8,128)S(1)}, u32[]{:S(2)}) copy-start(f32[128,8]{0,1:T(8,128)S(1)} %add_rsqrt_fusion.1) | copy-start | bytes 12292
  118.4 57.6 %all-to-all-start = ((bf16[32,128,384]{2,1,0:T(8,128)(2,1)}), bf16[32,128,384]{2,1,0:T(8,128)(2,1)S(1)}, u32[]{:S(2)}, u32[]{:S(2)}) async-start(bf16[32,128,384]{2,1,0:T(8,128)(2,1)} %pad_maximum_fusion.1), calls=%async_computation | async-start | bytes 6291456 | tf_op jit(solution)/shard_map/all_to_all | solution.py:149
  127.8 250.3 %all-gather.16.cloned.1.call-start = ((), (), s32[]{:S(2)}) async-start(), calls=%async_computation.10 | async-start | bytes 7864320 | tf_op jit(solution)/shard_map/all_gather | solution.py:160
  176.6 14.1 %copy-start.30 = (bf16[32,128,128]{2,1,0:T(8,128)(2,1)}, bf16[32,128,128]{2,1,0:T(8,128)(2,1)S(1)}, u32[]{:S(2)}) copy-start(bf16[32,128,128]{2,1,0:T(8,128)(2,1)S(1)} %get-tuple-element.39) | copy-start | bytes 3145732
  176.6 30.7 %copy-start.32 = (bf16[32,128,128]{2,1,0:T(8,128)(2,1)}, bf16[32,128,128]{2,1,0:T(8,128)(2,1)S(1)}, u32[]{:S(2)}) copy-start(bf16[32,128,128]{2,1,0:T(8,128)(2,1)S(1)} %get-tuple-element.40) | copy-start | bytes 3145732
  176.7 14.0 %copy-start.37 = (bf16[16,128,128]{2,1,0:T(8,128)(2,1)}, bf16[16,128,128]{2,1,0:T(8,128)(2,1)S(1)}, u32[]{:S(2)}) copy-start(bf16[16,128,128]{2,1,0:T(8,128)(2,1)S(1)} %constant_dynamic-slice_fusion.2) | copy-start | bytes 1572868
  207.3 15.9 %copy-start.51 = (pred[32]{0:T(512)(128)(4,1)S(1)}, pred[32]{0:T(512)(128)(4,1)}, u32[]{:S(2)}) copy-start(pred[32]{0:T(512)(128)(4,1)} %broadcast_in_dim.118) | copy-start | bytes 100
  223.4 35.5 %copy-start.42 = (f32[1024]{0:T(1024)S(1)}, f32[1024]{0:T(1024)}, u32[]{:S(2)}) copy-start(f32[1024]{0:T(1024)} %param.25) | copy-start | bytes 12292
  254.8 64.0 %copy-start.12 = (bf16[16,128,128]{1,2,0:T(8,128)(2,1)}, bf16[16,128,128]{1,2,0:T(8,128)(2,1)S(1)}, u32[]{:S(2)}) copy-start(bf16[16,128,128]{1,2,0:T(8,128)(2,1)S(1)} %constant_dynamic-slice_fusion.1) | copy-start | bytes 1572868
  258.1 135.0 %copy-start.48 = (f32[128]{0:T(128)}, f32[128]{0:T(128)S(1)}, u32[]{:S(2)}) copy-start(f32[128]{0:T(128)S(1)} %add_rsqrt_fusion.2) | copy-start | bytes 1540
  259.0 59.8 %copy-start.21 = (bf16[128,1024]{1,0:T(8,128)(2,1)}, bf16[128,1024]{1,0:T(8,128)(2,1)S(1)}, u32[]{:S(2)}) copy-start(bf16[128,1024]{1,0:T(8,128)(2,1)S(1)} %multiply_convert_fusion.4) | copy-start | bytes 786436
  378.1 7.7 copy-start
  394.6 14.9 %copy-start.23 = (bf16[1,128,1024]{2,1,0:T(8,128)(2,1)S(1)}, bf16[1,128,1024]{2,1,0:T(8,128)(2,1)}, u32[]{:S(2)}) copy-start(bf16[1,128,1024]{2,1,0:T(8,128)(2,1)} %param.15) | copy-start | bytes 786436
  400.1 55.0 %all-to-all-start.2 = ((bf16[32,128,128]{1,2,0:T(8,128)(2,1)}), bf16[32,128,128]{1,2,0:T(8,128)(2,1)S(1)}, u32[]{:S(2)}, u32[]{:S(2)}) async-start(bf16[32,128,128]{1,2,0:T(8,128)(2,1)} %bitcast_select_fusion.2), calls=%async_computation.2 | async-start | bytes 2097152 | tf_op jit(solution)/shard_map/all_to_all | solution.py:149
  409.5 214.3 %all-gather.20.cloned.1.call-start = ((), (), s32[]{:S(2)}) async-start(), calls=%async_computation.12 | async-start | bytes 2621440 | tf_op jit(solution)/shard_map/all_gather | solution.py:292
  410.4 224.3 %all-gather.22.cloned.1.call-start = ((), (), s32[]{:S(2)}) async-start(), calls=%async_computation.13 | async-start | bytes 7864320 | tf_op jit(solution)/shard_map/all_gather | solution.py:291
  431.1 22.7 %copy-start.16 = (bf16[128,3072]{1,0:T(8,128)(2,1)S(1)}, bf16[128,3072]{1,0:T(8,128)(2,1)}, u32[]{:S(2)}) copy-start(bf16[128,3072]{1,0:T(8,128)(2,1)} %get-tuple-element.32) | copy-start | bytes 2359300
  431.1 22.7 %copy-start.17 = (bf16[128,3072]{1,0:T(8,128)(2,1)S(1)}, bf16[128,3072]{1,0:T(8,128)(2,1)}, u32[]{:S(2)}) copy-start(bf16[128,3072]{1,0:T(8,128)(2,1)} %get-tuple-element.33) | copy-start | bytes 2359300
  456.7 20.9 %copy-start.31 = (bf16[32,128,128]{2,1,0:T(8,128)(2,1)S(1)}, bf16[32,128,128]{2,1,0:T(8,128)(2,1)}, u32[]{:S(2)}) copy-start(bf16[32,128,128]{2,1,0:T(8,128)(2,1)} %copy-done.30) | copy-start | bytes 3145732
  511.1 10.1 %copy-start.54 = (f32[128]{0:T(128)S(1)}, f32[128]{0:T(128)}, u32[]{:S(2)}) copy-start(f32[128]{0:T(128)} %param.27) | copy-start | bytes 1540
  511.1 10.7 %copy-start.56 = (f32[128]{0:T(128)S(1)}, f32[128]{0:T(128)}, u32[]{:S(2)}) copy-start(f32[128]{0:T(128)} %param.26) | copy-start | bytes 1540
  511.1 10.7 %copy-start.41 = (f32[128,16]{0,1:T(8,128)S(1)}, f32[128,16]{0,1:T(8,128)}, u32[]{:S(2)}) copy-start(f32[128,16]{0,1:T(8,128)} %copy-done.40) | copy-start | bytes 24580
  511.1 55.5 %all-to-all-start.3 = ((bf16[32,128,384]{1,2,0:T(8,128)(2,1)}), bf16[32,128,384]{1,2,0:T(8,128)(2,1)S(1)}, u32[]{:S(2)}, u32[]{:S(2)}) async-start(bf16[32,128,384]{1,2,0:T(8,128)(2,1)} %pad_maximum_fusion.3), calls=%async_computation.3 | async-start | bytes 6291456 | tf_op jit(solution)/shard_map/all_to_all | solution.py:149
  521.0 121.7 %all-gather.18.cloned.1.call-start = ((), (), s32[]{:S(2)}) async-start(), calls=%async_computation.11 | async-start | bytes 5242880 | tf_op jit(solution)/shard_map/all_gather | solution.py:290
  581.4 144.3 %reduce-scatter.3.cloned.1.call-start = ((), (), s32[]{:S(2)}) async-start(), calls=%async_computation.14 | async-start | bytes 9830400 | tf_op jit(solution)/shard_map/reduce_scatter | solution.py:85
  623.8 7.2 copy-start.20
  650.0 175.3 %copy-start.60 = (u32[128]{0:T(128)S(1)}, u32[128]{0:T(128)}, u32[]{:S(2)}) copy-start(u32[128]{0:T(128)} %constant.87) | copy-start | bytes 1540
  650.0 177.2 %copy-start.2 = (f32[128,1024]{1,0:T(8,128)S(1)}, f32[128,1024]{1,0:T(8,128)}, u32[]{:S(2)}) copy-start(f32[128,1024]{1,0:T(8,128)} %copy-done.1) | copy-start | bytes 1572868
  650.0 177.2 %copy-start.19 = (bf16[128,3072]{1,0:T(8,128)(2,1)S(1)}, bf16[128,3072]{1,0:T(8,128)(2,1)}, u32[]{:S(2)}) copy-start(bf16[128,3072]{1,0:T(8,128)(2,1)} %get-tuple-element.38) | copy-start | bytes 2359300
  650.0 106.3 %reduce-scatter.5.cloned.1.call-start = ((), (), s32[]{:S(2)}) async-start(), calls=%async_computation.15 | async-start | bytes 2457600 | tf_op jit(solution)/shard_map/reduce_scatter | solution.py:86
  725.7 68.6 %all-reduce.8.cloned.1.call-start = ((), (), s32[]{:S(2)}) async-start(), calls=%async_computation.16 | async-start | bytes 983040 | tf_op jit(solution)/shard_map/psum | solution.py:87
  756.3 68.9 %all-gather.24.cloned.1.call-start = ((), (), s32[]{:S(2)}) async-start(), calls=%async_computation.17 | async-start | bytes 2457600 | tf_op jit(solution)/shard_map/all_gather | solution.py:88
  794.4 154.1 %all-gather.26.cloned.1.call-start = ((), (), s32[]{:S(2)}) async-start(), calls=%async_computation.18 | async-start | bytes 9830400 | tf_op jit(solution)/shard_map/all_gather | solution.py:89
  825.2 6.5 copy-start.26
  825.2 6.5 copy-start.34
  831.7 6.5 copy-start.46
  831.7 115.7 %copy-start.9 = (f32[128,1024]{1,0:T(8,128)S(1)}, f32[128,1024]{1,0:T(8,128)}, u32[]{:S(2)}) copy-start(f32[128,1024]{1,0:T(8,128)} %get-tuple-element.62) | copy-start | bytes 1572868
  831.7 115.7 %copy-start.24 = (bf16[1,128,1024]{2,1,0:T(8,128)(2,1)S(1)}, bf16[1,128,1024]{2,1,0:T(8,128)(2,1)}, u32[]{:S(2)}) copy-start(bf16[1,128,1024]{2,1,0:T(8,128)(2,1)} %param.15) | copy-start | bytes 786436
  831.7 115.7 %copy-start.43 = (f32[1024]{0:T(1024)S(1)}, f32[1024]{0:T(1024)}, u32[]{:S(2)}) copy-start(f32[1024]{0:T(1024)} %param.25) | copy-start | bytes 12292
  831.7 115.7 %copy-start.49 = (f32[128]{0:T(128)S(1)}, f32[128]{0:T(128)}, u32[]{:S(2)}) copy-start(f32[128]{0:T(128)} %copy-done.48) | copy-start | bytes 1540
  831.8 115.7 %copy-start.58 = (f32[128]{0:T(128)S(1)}, f32[128]{0:T(128)}, u32[]{:S(2)}) copy-start(f32[128]{0:T(128)} %copy-done.57) | copy-start | bytes 1540
  (28 other events, 91.0 us)
Sparse Core Ops, SparseCore 0:
  10.6 82.6 all-gather.9
  94.9 82.6 all-gather.11
  179.9 130.7 all-gather.13
  312.3 65.8 all-gather.15
  411.7 30.5 all-gather.19
  455.2 64.7 all-gather.21
  581.5 61.1 all-gather.17
  650.1 75.5 reduce-scatter.2
  728.1 28.1 reduce-scatter.4
  758.6 35.7 all-reduce.7
  796.0 29.1 all-gather.23
  826.7 79.8 all-gather.25

commit v4 on v3

--- a/solution.py
+++ b/solution.py
@@ -79,6 +79,18 @@
     across = lax.all_gather(values, "yl", axis=0, tiled=False)
     both = lax.all_gather(across, "c", axis=1, tiled=False)
     return both.reshape((-1,) + values.shape[1:])
+
+
+def permute_gather(values):
+    size = lax.axis_size(FSDP)
+    me = lax.axis_index(FSDP)
+    received = [values]
+    for s in range(1, size):
+        pairs = [(i, i ^ s) for i in range(size)]
+        received.append(lax.ppermute(values, FSDP, pairs))
+    stacked = jnp.stack(received)
+    ordered = [lax.dynamic_index_in_dim(stacked, me ^ j, 0, False) for j in range(size)]
+    return jnp.concatenate(ordered, axis=0)
 
 
 def reduce_ctx(packed):
@@ -152,12 +164,12 @@
     full_qkv = lax.all_gather(
         jnp.concatenate([query_weight, key_projection, value_projection], axis=1), FSDP, axis=0, tiled=True
     )
-    full_output = lax.all_gather(output_weight, FSDP, axis=0, tiled=True)
+    full_output = permute_gather(output_weight)
     ff_cols = gate_weight.shape[1]
     full_gate_up = lax.all_gather(
         jnp.concatenate([gate_weight, up_weight], axis=1), FSDP, axis=0, tiled=True
     )
-    full_down = lax.all_gather(down_weight, FSDP, axis=0, tiled=True)
+    full_down = permute_gather(down_weight)
     input_f32 = layer_input[0].astype(jnp.float32)
     gained, first_normed, first_scale = rms_apply(input_f32, first_gain)
     attention_input = gained.astype(jnp.bfloat16)
@@ -292,18 +304,29 @@
     cot_mid_rows = lax.all_gather(
         jnp.concatenate([own_cotangent, mid_grad_b], axis=1), FSDP, axis=0, tiled=True
     )
+    first_shard, second_shard, query_gain_shard, key_gain_shard = (
+        lax.psum_scatter(first_gain_grad, FSDP, scatter_dimension=0, tiled=True),
+        lax.psum_scatter(second_gain_grad, FSDP, scatter_dimension=0, tiled=True),
+        lax.psum_scatter(query_gain_grad, FSDP, scatter_dimension=0, tiled=True),
+        lax.psum_scatter(key_gain_grad, FSDP, scatter_dimension=0, tiled=True),
+    )
     model_width = own_cotangent.shape[1]
     qkv_shard = left_dot(attn_cols, qkv_rows)
     output_shard = left_dot(mixed_cols, cot_mid_rows[:, model_width:])
     gate_up_shard = left_dot(mlp_cols, gate_up_rows)
     down_shard = left_dot(hidden_cols, cot_mid_rows[:, :model_width])
     shard_rows = qkv_shard.shape[0]
+    gain_parts = (first_shard, second_shard, query_gain_shard, key_gain_shard)
+    gain_block = jnp.zeros((shard_rows, 128), jnp.float32)
+    for column, g in enumerate(gain_parts):
+        gain_block = gain_block.at[: g.shape[0], column].set(g)
     packed = jnp.concatenate(
         [
             qkv_shard,
             output_shard.reshape(shard_rows, -1),
             gate_up_shard,
             down_shard.reshape(shard_rows, -1),
+            gain_block,
         ],
         axis=1,
     ).astype(jnp.bfloat16)
@@ -317,15 +340,8 @@
     query_total, key_total, value_total, output_total, gate_total, up_total, down_total = pieces
     output_total = output_total.reshape(output_shard.shape)
     down_total = down_total.reshape(down_shard.shape)
-    first_shard, second_shard, query_gain_shard, key_gain_shard = (
-        lax.psum_scatter(first_gain_grad, FSDP, scatter_dimension=0, tiled=True),
-        lax.psum_scatter(second_gain_grad, FSDP, scatter_dimension=0, tiled=True),
-        lax.psum_scatter(query_gain_grad, FSDP, scatter_dimension=0, tiled=True),
-        lax.psum_scatter(key_gain_grad, FSDP, scatter_dimension=0, tiled=True),
-    )
     first_total, second_total, query_gain_total, key_gain_total = (
-        lax.psum(g.astype(jnp.bfloat16), CTX).astype(jnp.float32)
-        for g in (first_shard, second_shard, query_gain_shard, key_gain_shard)
+        reduced[: g.shape[0], at + column] for column, g in enumerate(gain_parts)
     )
     return (
         layer_output[None],

time: 980 us -> 1040 us (1.061)
  blocking collectives: 179 us -> 10.2 us
  waiting for transfers between devices: 455 us -> 613 us
  starting transfers between devices: 30.3 us -> 57.8 us
  local copies, waits for them, and re-layouts: 77.1 us -> 100 us
  other arithmetic: 73.8 us -> 94.7 us
    ppermute x0 -> x6, waiting for transfers between devices: none -> 167 us  [permute_gather(): received.append(lax.ppermute(values, FSDP, pairs))]
    psum x1 -> x0, blocking collectives: 95 us -> none  [on_device(): lax.psum(g.astype(jnp.bfloat16), CTX).astype(jnp.float32)]
    all_gather x1, waiting for transfers between devices: 0.01 us -> 76 us  [reduce_ctx(): return lax.all_gather(part, 'z', axis=0, tiled=True).astype(jnp.float32)]
    all_to_all x2 -> x0, blocking collectives: 72.7 us -> none  [the longest x1 41.4 us: on_device(): lax.all_to_all(stacked, FSDP, split_axis=1, concat_axis=0, tiled=True)]
    all_gather x2 -> x0, waiting for transfers between devices: 59.4 us -> none  [the longest x1 59.3 us: on_device(): full_down = lax.all_gather(down_weight, FSDP, axis=0, tiled=True)]
    all_gather x1, waiting for transfers between devices: 51.7 us -> 0.02 us  [on_device(): lax.all_gather(jnp.concatenate([gate_weight, up_weight], axis=1), FSDP, a...]
    all_to_all x3 -> x4, waiting for transfers between devices: 85.9 us -> 36.6 us  [exchange(): return lax.all_to_all(values, CTX, split_axis=0, concat_axis=0, tiled=True)]
    all_gather x1, waiting for transfers between devices: 0.01 us -> 39.7 us  [on_device(): gate_up_rows = lax.all_gather(gate_up_grad, FSDP, axis=0, tiled=True)]
  transfers between devices with their start and end apart: 15 -> 21, of which waited for: 10 -> 14; matrix products, arithmetic and copies ran while one was open for 24% -> 20% of each run, Pallas kernels for 0% -> 0%
where the time goes in v4:
time: 1040 us; the launch traced here: 1030 us
  waiting for transfers between devices  613 us (59%)
  matrix products  136 us (13%)
  local copies, waits for them, and re-layouts  100 us (10%)
  other arithmetic  94.7 us (9%)
  starting transfers between devices  57.8 us (6%)
  between operations  17 us (2%)
    ppermute x6, waiting for transfers between devices, permute_gather(): received.append(lax.ppermute(values, FSDP, pairs))  167 us
    all_gather x1, waiting for transfers between devices, on_device(): lax.all_gather(jnp.concatenate([query_weight, key_projection, value_proje...  79.4 us
    reduce_scatter x1, waiting for transfers between devices, reduce_ctx(): part = lax.psum_scatter(packed, 'z', scatter_dimension=0, tiled=True)  78.9 us
    all_gather x1, waiting for transfers between devices, reduce_ctx(): return lax.all_gather(part, 'z', axis=0, tiled=True).astype(jnp.float32)  76 us
    dot_general x5, matrix products, right_dot(): lax.dot_general(left_side, right_side, (((1,), (1,)), ((), ())), preferre...  48.6 us
    all_to_all x4, starting transfers between devices, exchange(): return lax.all_to_all(values, CTX, split_axis=0, concat_axis=0, tiled=True)  47.1 us
    all_gather x1, waiting for transfers between devices, on_device(): gate_up_rows = lax.all_gather(gate_up_grad, FSDP, axis=0, tiled=True)  39.7 us
    psum x1, waiting for transfers between devices, reduce_ctx(): part = lax.psum(part, 'yh')  38.1 us
  transfers between devices with their start and end apart: 21, of which 14 were waited for; matrix products, arithmetic and copies ran while one was open for 20% of the time, Pallas kernels for 0%

profile of v4, /device:TPU:0, one launch (start us, length us, event | category | flops | bytes accessed | tf_op | source)
XLA Modules:
  0.0 1028.6 jit_solution(15148480890038066246)
XLA Ops:
  7.2 3.2 pad_maximum_fusion.7
  13.9 79.4 %all-gather.8.cloned.1.call-done = bf16[1024,4096]{1,0:T(8,128)(2,1)} async-done(((bf16[256,4096]{1,0:T(8,128)(2,1)}), bf16[1024,4096]{1,0:T(8,128)(2,1)}) %all-gather.8.cloned.1.call-update) | async-done | bytes 8388624 | tf_op jit(solution)/shard_map/all_gather | solution.py:164
  93.3 4.7 fusion.28
  118.5 9.4 all-to-all-start
  132.9 84.9 %collective-permute-done.1 = bf16[512,1024]{1,0:T(8,128)(2,1)} collective-permute-done((bf16[512,1024]{1,0:T(8,128)(2,1)}, bf16[512,1024]{1,0:T(8,128)(2,1)}, u32[]{:S(2)}, u32[]{:S(2)}) %collective-permute-start.1) | collective-permute-done | bytes 1048608 | tf_op jit(solution)/shard_map/ppermute | solution.py:90
  217.8 44.9 %collective-permute-done.2 = bf16[512,1024]{1,0:T(8,128)(2,1)} collective-permute-done((bf16[512,1024]{1,0:T(8,128)(2,1)}, bf16[512,1024]{1,0:T(8,128)(2,1)}, u32[]{:S(2)}, u32[]{:S(2)}) %collective-permute-start.2) | collective-permute-done | bytes 1048608 | tf_op jit(solution)/shard_map/ppermute | solution.py:90
  262.7 3.7 pad_maximum_fusion.2
  267.1 14.0 %fusion.42 = (f32[2048]{0:T(1024)S(1)}, f32[2048,4096]{1,0:T(8,128)}) fusion(s32[2048]{0:T(1024)S(1)} %dynamic_slice.44, s32[4096]{0:T(1024)S(1)} %add.167, bf16[2048,128]{1,0:T(8,128)(2,1)S(1)} %bitcast.231, bf16[4096,128]{1,0:T(8,128)(2,1)S(1)} %bitcast.223), kind=kOutput, calls=%fused_computation.173 | convolution fusion | flops 2181036032 | bytes 35160064 | tf_op jit(solution)/shard_map/qd,kd->qk/dot_general | solution.py:201
  281.0 15.1 %exponential_reduce_fusion = f32[2048]{0:T(1024)S(1)} fusion(f32[2048]{0:T(1024)S(1)} %get-tuple-element.118, f32[2048,4096]{1,0:T(8,128)} %get-tuple-element.119, s32[2048]{0:T(1024)S(1)} %dynamic_slice.44, s32[4096]{0:T(1024)S(1)} %add.167), kind=kLoop, calls=%fused_computation.6 | loop fusion | flops 41940992 | bytes 33595392 | tf_op jit(solution)/shard_map/reduce_sum | solution.py:208
  296.1 15.1 %fusion.49 = (bf16[2048,128]{1,0:T(8,128)(2,1)S(1)}, f32[2048,128]{1,0:T(8,128)}) fusion(bf16[4096,128]{1,0:T(8,128)(2,1)S(1)} %bitcast.225, f32[2048]{0:T(1024)S(1)} %log_add_fusion, f32[2048,4096]{1,0:T(8,128)} %get-tuple-element.119, s32[2048]{0:T(1024)S(1)} %dynamic_slice.44, s32[4096]{0:T(1024)S(1)} %add.167), kind=kOutput, calls=%fused_computation.180 | convolution fusion | flops 2189688832 | bytes 36208640 | tf_op jit(solution)/shard_map/dot_general | solution.py:210
  312.7 14.8 %all-to-all-start.1 = ((bf16[32,128,128]{1,2,0:T(8,128)(2,1)}), bf16[32,128,128]{1,2,0:T(8,128)(2,1)S(1)}, u32[]{:S(2)}, u32[]{:S(2)}) async-start(bf16[32,128,128]{1,2,0:T(8,128)(2,1)} %bitcast_select_fusion.3), calls=%async_computation.1 | async-start | bytes 2097152 | tf_op jit(solution)/shard_map/all_to_all | solution.py:161
  327.5 4.5 dynamic-slice_bitcast_fusion.7
  331.9 36.8 %collective-permute-done.5 = bf16[768,1024]{1,0:T(8,128)(2,1)} collective-permute-done((bf16[768,1024]{1,0:T(8,128)(2,1)}, bf16[768,1024]{1,0:T(8,128)(2,1)}, u32[]{:S(2)}, u32[]{:S(2)}) %collective-permute-start.5) | collective-permute-done | bytes 1572896 | tf_op jit(solution)/shard_map/ppermute | solution.py:90
  368.7 3.3 pad_maximum_fusion
  372.0 2.9 dynamic-slice_bitcast_fusion.3
  379.6 6.5 fusion.50
  386.2 10.4 %multiply_convert_fusion.2 = (bf16[128,3072]{1,0:T(8,128)(2,1)}, bf16[128,3072]{1,0:T(8,128)(2,1)}, bf16[128,3072]{1,0:T(8,128)(2,1)}) fusion(f32[128,6144]{1,0:T(8,128)S(1)} %fusion.50, bf16[1,128,1024]{2,1,0:T(8,128)(2,1)S(1)} %copy-done.17, bf16[768,1024]{1,0:T(8,128)(2,1)S(1)} %copy-done.28, bf16[768,1024]{1,0:T(8,128)(2,1)S(1)} %copy-done.29, ...), kind=kOutput, calls=%fused_computation.34 | convolution fusion | flops 836370432 | bytes 12058624 | tf_op jit(solution)/shard_map/dot_general | solution.py:73
  396.7 7.3 multiply_reduce_fusion.5
  405.4 3.4 fusion.12
  410.6 13.1 %all-to-all-start.2 = ((bf16[32,128,128]{1,2,0:T(8,128)(2,1)}), bf16[32,128,128]{1,2,0:T(8,128)(2,1)S(1)}, u32[]{:S(2)}, u32[]{:S(2)}) async-start(bf16[32,128,128]{1,2,0:T(8,128)(2,1)} %bitcast_select_fusion.2), calls=%async_computation.2 | async-start | bytes 2097152 | tf_op jit(solution)/shard_map/all_to_all | solution.py:161
  423.7 20.3 %fusion.2 = bf16[4096,2048]{0,1:T(8,128)(2,1)} fusion(f32[2048,4096]{1,0:T(8,128)} %get-tuple-element.119, f32[2048]{0:T(1024)S(1)} %log_add_fusion, s32[4096]{0:T(1024)S(1)} %add.167, s32[2048]{0:T(1024)S(1)} %dynamic_slice.44), kind=kLoop, calls=%fused_computation.3 | loop fusion | flops 41943040 | bytes 50364416 | tf_op jit(solution)/shard_map/convert_element_type | solution.py:209
  444.0 22.6 %copy.230 = bf16[4096,2048]{1,0:T(8,128)(2,1)} copy(bf16[4096,2048]{0,1:T(8,128)(2,1)} %fusion.2) | data formatting | bytes 33554432 | tf_op jit(solution)/shard_map/dot_general | solution.py:67
  467.3 20.2 %multiply_convert_fusion = bf16[2048,4096]{1,0:T(8,128)(2,1)} fusion(f32[2048]{0:T(1024)S(1)} %multiply_reduce_fusion.2, f32[2048]{0:T(1024)S(1)} %log_add_fusion, bf16[2048,128]{1,0:T(8,128)(2,1)S(1)} %bitcast.195, bf16[4096,128]{1,0:T(8,128)(2,1)} %bitcast.226, f32[2048,4096]{1,0:T(8,128)} %get-tuple-element.119, s32[2048]{0:T(1024)S(1)} %dynamic_slice.44, ...), kind=kOutput, calls=%fused_computation.4 | convolution fusion | flops 2206203904 | bytes 51945472 | tf_op jit(solution)/shard_map/dot_general | solution.py:73
  487.5 8.6 fusion.10
  498.3 4.9 fusion.9
  504.9 9.3 convolution_convert_fusion.5
  514.2 2.8 pad_maximum_fusion.6
  517.1 10.0 all-to-all-start.3
  535.8 35.6 %all-to-all-done.3 = bf16[32,128,384]{1,2,0:T(8,128)(2,1)S(1)} async-done(((bf16[32,128,384]{1,2,0:T(8,128)(2,1)}), bf16[32,128,384]{1,2,0:T(8,128)(2,1)S(1)}, u32[]{:S(2)}, u32[]{:S(2)}) %all-to-all-start.3) | async-done | bytes 3145760 | tf_op jit(solution)/shard_map/all_to_all | solution.py:161
  593.7 5.3 all-to-all-start.4
  603.4 34.8 %all-to-all-done.4 = bf16[128,4,1792]{2,0,1:T(8,128)(2,1)S(1)} async-done(((bf16[128,4,1792]{2,0,1:T(8,128)(2,1)}), bf16[128,4,1792]{2,0,1:T(8,128)(2,1)S(1)}, u32[]{:S(2)}, u32[]{:S(2)}) %all-to-all-start.4) | async-done | bytes 1835040 | tf_op jit(solution)/shard_map/all_to_all | solution.py:295
  639.5 3.4 convolution_convert_fusion.3
  645.5 3.1 convolution_convert_fusion.4
  650.1 7.3 multiply_reduce_fusion.6
  657.4 10.2 all-reduce.5
  677.5 5.0 fusion.8
  683.5 39.7 %all-gather.16.cloned.1.call-done = bf16[512,6144]{1,0:T(8,128)(2,1)} async-done(((bf16[128,6144]{1,0:T(8,128)(2,1)}), bf16[512,6144]{1,0:T(8,128)(2,1)}) %all-gather.16.cloned.1.call-update) | async-done | bytes 6291472 | tf_op jit(solution)/shard_map/all_gather | solution.py:303
  723.2 6.4 fusion.7
  731.7 78.9 %reduce-scatter.3.cloned.1.call-done = bf16[64,15488]{1,0:T(8,128)(2,1)} async-done(((bf16[256,15488]{1,0:T(8,128)(2,1)}), bf16[64,15488]{1,0:T(8,128)(2,1)}) %reduce-scatter.3.cloned.1.call-update) | async-done | bytes 1982480 | tf_op jit(solution)/shard_map/reduce_scatter | solution.py:97
  810.6 30.8 %reduce-scatter.5.cloned.1.call-done = bf16[16,15488]{1,0:T(8,128)(2,1)} async-done(((bf16[64,15488]{1,0:T(8,128)(2,1)}), bf16[16,15488]{1,0:T(8,128)(2,1)}) %reduce-scatter.5.cloned.1.call-update) | async-done | bytes 495632 | tf_op jit(solution)/shard_map/reduce_scatter | solution.py:98
  841.4 38.1 %all-reduce.8.cloned.1.call-done = bf16[16,15488]{1,0:T(8,128)(2,1)} async-done(((bf16[16,15488]{1,0:T(8,128)(2,1)}), bf16[16,15488]{1,0:T(8,128)(2,1)}) %all-reduce.8.cloned.1.call-update) | async-done | bytes 495632 | tf_op jit(solution)/shard_map/psum | solution.py:99
  879.6 31.3 %all-gather.18.cloned.1.call-done = bf16[64,15488]{1,0:T(8,128)(2,1)} async-done(((bf16[16,15488]{1,0:T(8,128)(2,1)}), bf16[64,15488]{1,0:T(8,128)(2,1)}) %all-gather.18.cloned.1.call-update) | async-done | bytes 1982480 | tf_op jit(solution)/shard_map/all_gather | solution.py:100
  911.0 3.9 fusion.14
  916.1 76.0 %all-gather.20.cloned.1.call-done = bf16[256,15488]{1,0:T(8,128)(2,1)} async-done(((bf16[64,15488]{1,0:T(8,128)(2,1)}), bf16[256,15488]{1,0:T(8,128)(2,1)}) %all-gather.20.cloned.1.call-update) | async-done | bytes 7929872 | tf_op jit(solution)/shard_map/all_gather | solution.py:101
  992.1 9.9 convert_element_type.118
  1005.2 4.1 fusion.43
  1009.4 4.6 reshape.438
  1014.0 3.4 fusion.44
  (315 shorter events, 104.0 us)
Async XLA Ops:
  7.2 86.1 %all-gather.8.cloned.1.call-start = ((), (), s32[]{:S(2)}) async-start(), calls=%async_computation.7 | async-start | bytes 10485760 | tf_op jit(solution)/shard_map/all_gather | solution.py:164
  10.5 82.8 %copy-start.47 = (f32[1024]{0:T(1024)S(1)}, f32[1024]{0:T(1024)}, u32[]{:S(2)}) copy-start(f32[1024]{0:T(1024)} %param.32) | copy-start | bytes 12292
  10.5 369.0 %all-gather.10.cloned.1.call-start = ((), (), s32[]{:S(2)}) async-start(), calls=%async_computation.8 | async-start | bytes 15728640 | tf_op jit(solution)/shard_map/all_gather | solution.py:169
  13.7 84.3 %copy-start.60 = (f32[128]{0:T(128)}, f32[128]{0:T(128)S(1)}, u32[]{:S(2)}) copy-start(f32[128]{0:T(128)S(1)} %add_rsqrt_fusion.3) | copy-start | bytes 1540
  13.9 96.6 %copy-start.39 = (f32[128,64]{0,1:T(8,128)}, f32[128,64]{0,1:T(8,128)S(1)}, u32[]{:S(2)}) copy-start(f32[128,64]{0,1:T(8,128)S(1)} %get-tuple-element.112) | copy-start | bytes 98308
  13.9 96.6 %copy-start.41 = (f32[128,64]{0,1:T(8,128)}, f32[128,64]{0,1:T(8,128)S(1)}, u32[]{:S(2)}) copy-start(f32[128,64]{0,1:T(8,128)S(1)} %get-tuple-element.113) | copy-start | bytes 98308
  98.0 15.5 %copy-start.1 = (f32[128,4096]{1,0:T(8,128)}, f32[128,4096]{1,0:T(8,128)S(1)}, u32[]{:S(2)}) copy-start(f32[128,4096]{1,0:T(8,128)S(1)} %fusion.28) | copy-start | bytes 6291460
  118.5 147.9 %all-to-all-start = ((bf16[32,128,384]{2,1,0:T(8,128)(2,1)}), bf16[32,128,384]{2,1,0:T(8,128)(2,1)S(1)}, u32[]{:S(2)}, u32[]{:S(2)}) async-start(bf16[32,128,384]{2,1,0:T(8,128)(2,1)} %pad_maximum_fusion.4), calls=%async_computation | async-start | bytes 6291456 | tf_op jit(solution)/shard_map/all_to_all | solution.py:161
  127.9 3.9 collective-permute-start
  129.2 88.6 %collective-permute-start.1 = (bf16[512,1024]{1,0:T(8,128)(2,1)}, bf16[512,1024]{1,0:T(8,128)(2,1)}, u32[]{:S(2)}, u32[]{:S(2)}) collective-permute-start(bf16[512,1024]{1,0:T(8,128)(2,1)} %param.28), channel_id=1, source_target_pairs={{0,2},{1,3},{2,0},{3,1},{4,6},{5,7},{6,4},{7,5},{8,10},{9,11},{10,... | collective-permute-start | bytes 3145736 | tf_op jit(solution)/shard_map/ppermute | solution.py:90
  129.4 133.4 %collective-permute-start.2 = (bf16[512,1024]{1,0:T(8,128)(2,1)}, bf16[512,1024]{1,0:T(8,128)(2,1)}, u32[]{:S(2)}, u32[]{:S(2)}) collective-permute-start(bf16[512,1024]{1,0:T(8,128)(2,1)} %param.28), channel_id=1, source_target_pairs={{0,3},{1,2},{2,1},{3,0},{4,7},{5,6},{6,5},{7,4},{8,11},{9,10},{10,... | collective-permute-start | bytes 3145736 | tf_op jit(solution)/shard_map/ppermute | solution.py:90
  130.6 201.3 %collective-permute-start.3 = (bf16[768,1024]{1,0:T(8,128)(2,1)}, bf16[768,1024]{1,0:T(8,128)(2,1)}, u32[]{:S(2)}, u32[]{:S(2)}) collective-permute-start(bf16[768,1024]{1,0:T(8,128)(2,1)} %param.31), channel_id=1, source_target_pairs={{0,1},{1,0},{2,3},{3,2},{4,5},{5,4},{6,7},{7,6},{8,9},{9,8},{10,11... | collective-permute-start | bytes 4718600 | tf_op jit(solution)/shard_map/ppermute | solution.py:90
  131.3 200.6 %collective-permute-start.4 = (bf16[768,1024]{1,0:T(8,128)(2,1)}, bf16[768,1024]{1,0:T(8,128)(2,1)}, u32[]{:S(2)}, u32[]{:S(2)}) collective-permute-start(bf16[768,1024]{1,0:T(8,128)(2,1)} %param.31), channel_id=1, source_target_pairs={{0,2},{1,3},{2,0},{3,1},{4,6},{5,7},{6,4},{7,5},{8,10},{9,11},{10,... | collective-permute-start | bytes 4718600 | tf_op jit(solution)/shard_map/ppermute | solution.py:90
  131.8 236.9 %collective-permute-start.5 = (bf16[768,1024]{1,0:T(8,128)(2,1)}, bf16[768,1024]{1,0:T(8,128)(2,1)}, u32[]{:S(2)}, u32[]{:S(2)}) collective-permute-start(bf16[768,1024]{1,0:T(8,128)(2,1)} %param.31), channel_id=1, source_target_pairs={{0,3},{1,2},{2,1},{3,0},{4,7},{5,6},{6,5},{7,4},{8,11},{9,10},{10,... | collective-permute-start | bytes 4718600 | tf_op jit(solution)/shard_map/ppermute | solution.py:90
  267.0 14.0 %copy-start.33 = (bf16[32,128,128]{2,1,0:T(8,128)(2,1)}, bf16[32,128,128]{2,1,0:T(8,128)(2,1)S(1)}, u32[]{:S(2)}) copy-start(bf16[32,128,128]{2,1,0:T(8,128)(2,1)S(1)} %get-tuple-element.97) | copy-start | bytes 3145732
  267.0 29.1 %copy-start.35 = (bf16[32,128,128]{2,1,0:T(8,128)(2,1)}, bf16[32,128,128]{2,1,0:T(8,128)(2,1)S(1)}, u32[]{:S(2)}) copy-start(bf16[32,128,128]{2,1,0:T(8,128)(2,1)S(1)} %get-tuple-element.98) | copy-start | bytes 3145732
  267.1 14.0 %copy-start.44 = (bf16[16,128,128]{2,1,0:T(8,128)(2,1)}, bf16[16,128,128]{2,1,0:T(8,128)(2,1)S(1)}, u32[]{:S(2)}) copy-start(bf16[16,128,128]{2,1,0:T(8,128)(2,1)S(1)} %constant_dynamic-slice_fusion.2) | copy-start | bytes 1572868
  296.1 15.4 %copy-start.59 = (pred[32]{0:T(512)(128)(4,1)S(1)}, pred[32]{0:T(512)(128)(4,1)}, u32[]{:S(2)}) copy-start(pred[32]{0:T(512)(128)(4,1)} %broadcast_in_dim.119) | copy-start | bytes 100
  312.7 63.2 %all-to-all-start.1 = ((bf16[32,128,128]{1,2,0:T(8,128)(2,1)}), bf16[32,128,128]{1,2,0:T(8,128)(2,1)S(1)}, u32[]{:S(2)}, u32[]{:S(2)}) async-start(bf16[32,128,128]{1,2,0:T(8,128)(2,1)} %bitcast_select_fusion.3), calls=%async_computation.1 | async-start | bytes 2097152 | tf_op jit(solution)/shard_map/all_to_all | solution.py:161
  327.5 41.3 %copy-start.23 = (bf16[768,1024]{1,0:T(8,128)(2,1)S(1)}, bf16[768,1024]{1,0:T(8,128)(2,1)}, u32[]{:S(2)}) copy-start(bf16[768,1024]{1,0:T(8,128)(2,1)} %param.31) | copy-start | bytes 4718596
  378.6 25.3 %copy-start.56 = (f32[128]{0:T(128)}, f32[128]{0:T(128)S(1)}, u32[]{:S(2)}) copy-start(f32[128]{0:T(128)S(1)} %add_rsqrt_fusion.2) | copy-start | bytes 1540
  379.6 17.0 %slice-start = ((s8[12582912]{0:T(1024)(128)(4,1)}), s8[4194304]{0:T(1024)(128)(4,1)S(1)}, s32[]{:S(2)}) async-start(s8[12582912]{0:T(1024)(128)(4,1)} %bitcast.189), calls=%async_computation.17 | async-start | bytes 8388608
  379.6 17.0 %slice-start.1 = ((s8[12582912]{0:T(1024)(128)(4,1)}), s8[4194304]{0:T(1024)(128)(4,1)S(1)}, s32[]{:S(2)}) async-start(s8[12582912]{0:T(1024)(128)(4,1)} %bitcast.189), calls=%async_computation.18 | async-start | bytes 8388608
  386.2 10.4 %slice-start.2 = ((s8[12582912]{0:T(1024)(128)(4,1)}), s8[4194304]{0:T(1024)(128)(4,1)S(1)}, s32[]{:S(2)}) async-start(s8[12582912]{0:T(1024)(128)(4,1)} %bitcast.189), calls=%async_computation.19 | async-start | bytes 8388608
  410.6 56.0 %all-to-all-start.2 = ((bf16[32,128,128]{1,2,0:T(8,128)(2,1)}), bf16[32,128,128]{1,2,0:T(8,128)(2,1)S(1)}, u32[]{:S(2)}, u32[]{:S(2)}) async-start(bf16[32,128,128]{1,2,0:T(8,128)(2,1)} %bitcast_select_fusion.2), calls=%async_computation.2 | async-start | bytes 2097152 | tf_op jit(solution)/shard_map/all_to_all | solution.py:161
  444.0 23.0 %copy-start.32 = (f32[2048,128]{1,0:T(8,128)S(1)}, f32[2048,128]{1,0:T(8,128)}, u32[]{:S(2)}) copy-start(f32[2048,128]{1,0:T(8,128)} %get-tuple-element.121) | copy-start | bytes 3145732
  467.3 20.2 %copy-start.34 = (bf16[32,128,128]{2,1,0:T(8,128)(2,1)S(1)}, bf16[32,128,128]{2,1,0:T(8,128)(2,1)}, u32[]{:S(2)}) copy-start(bf16[32,128,128]{2,1,0:T(8,128)(2,1)} %copy-done.33) | copy-start | bytes 3145732
  487.5 10.7 %copy-start.70 = (bf16[2048,4096]{1,0:T(8,128)(2,1)S(1)}, bf16[2048,4096]{1,0:T(8,128)(2,1)}, u32[]{:S(2)}) copy-start(bf16[2048,4096]{1,0:T(8,128)(2,1)} %multiply_convert_fusion) | copy-start | bytes 50331652
  517.1 10.0 copy-start.64
  517.1 12.2 %copy-start.62 = (f32[128]{0:T(128)S(1)}, f32[128]{0:T(128)}, u32[]{:S(2)}) copy-start(f32[128]{0:T(128)} %param.35) | copy-start | bytes 1540
  517.1 12.3 %copy-start.50 = (f32[128,16]{0,1:T(8,128)S(1)}, f32[128,16]{0,1:T(8,128)}, u32[]{:S(2)}) copy-start(f32[128,16]{0,1:T(8,128)} %copy-done.49) | copy-start | bytes 24580
  517.1 15.9 %copy-start.54 = (f32[128,8]{0,1:T(8,128)S(1)}, f32[128,8]{0,1:T(8,128)}, u32[]{:S(2)}) copy-start(f32[128,8]{0,1:T(8,128)} %copy-done.53) | copy-start | bytes 12292
  517.1 54.3 %all-to-all-start.3 = ((bf16[32,128,384]{1,2,0:T(8,128)(2,1)}), bf16[32,128,384]{1,2,0:T(8,128)(2,1)S(1)}, u32[]{:S(2)}, u32[]{:S(2)}) async-start(bf16[32,128,384]{1,2,0:T(8,128)(2,1)} %pad_maximum_fusion.6), calls=%async_computation.3 | async-start | bytes 6291456 | tf_op jit(solution)/shard_map/all_to_all | solution.py:161
  527.1 111.2 %all-gather.14.cloned.1.call-start = ((), (), s32[]{:S(2)}) async-start(), calls=%async_computation.10 | async-start | bytes 2621440 | tf_op jit(solution)/shard_map/all_gather | solution.py:304
  529.0 148.4 %all-gather.12.cloned.1.call-start = ((), (), s32[]{:S(2)}) async-start(), calls=%async_computation.9 | async-start | bytes 5242880 | tf_op jit(solution)/shard_map/all_gather | solution.py:302
  529.4 42.3 %copy-start.40 = (f32[128,64]{0,1:T(8,128)S(1)}, f32[128,64]{0,1:T(8,128)}, u32[]{:S(2)}) copy-start(f32[128,64]{0,1:T(8,128)} %copy-done.39) | copy-start | bytes 98308
  529.4 42.3 %copy-start.42 = (f32[128,64]{0,1:T(8,128)S(1)}, f32[128,64]{0,1:T(8,128)}, u32[]{:S(2)}) copy-start(f32[128,64]{0,1:T(8,128)} %copy-done.41) | copy-start | bytes 98308
  588.7 134.5 %all-gather.16.cloned.1.call-start = ((), (), s32[]{:S(2)}) async-start(), calls=%async_computation.11 | async-start | bytes 7864320 | tf_op jit(solution)/shard_map/all_gather | solution.py:303
  592.3 10.5 %copy-start.67 = (s32[2]{0:T(128)S(1)}, s32[2]{0:T(128)}, u32[]{:S(2)}) copy-start(s32[2]{0:T(128)} %constant.204.clone.1) | copy-start | bytes 28
  593.7 44.5 %all-to-all-start.4 = ((bf16[128,4,1792]{2,0,1:T(8,128)(2,1)}), bf16[128,4,1792]{2,0,1:T(8,128)(2,1)S(1)}, u32[]{:S(2)}, u32[]{:S(2)}) async-start(bf16[128,4,1792]{2,0,1:T(8,128)(2,1)} %pad_maximum_fusion.8), calls=%async_computation.4 | async-start | bytes 3670016 | tf_op jit(solution)/shard_map/all_to_all | solution.py:295
  599.0 211.6 %reduce-scatter.3.cloned.1.call-start = ((), (), s32[]{:S(2)}) async-start(), calls=%async_computation.12 | async-start | bytes 9912320 | tf_op jit(solution)/shard_map/reduce_scatter | solution.py:97
  731.6 179.3 %copy-start.6 = (f32[128,1024]{1,0:T(8,128)S(1)}, f32[128,1024]{1,0:T(8,128)}, u32[]{:S(2)}) copy-start(f32[128,1024]{1,0:T(8,128)} %copy-done.5) | copy-start | bytes 1572868
  731.6 179.3 %copy-start.27 = (bf16[768,1024]{1,0:T(8,128)(2,1)S(1)}, bf16[768,1024]{1,0:T(8,128)(2,1)}, u32[]{:S(2)}) copy-start(bf16[768,1024]{1,0:T(8,128)(2,1)} %get-tuple-element.82) | copy-start | bytes 4718596
  731.6 109.8 %reduce-scatter.5.cloned.1.call-start = ((), (), s32[]{:S(2)}) async-start(), calls=%async_computation.13 | async-start | bytes 2478080 | tf_op jit(solution)/shard_map/reduce_scatter | solution.py:98
  810.6 69.0 %all-reduce.8.cloned.1.call-start = ((), (), s32[]{:S(2)}) async-start(), calls=%async_computation.14 | async-start | bytes 991232 | tf_op jit(solution)/shard_map/psum | solution.py:99
  841.4 69.5 %all-gather.18.cloned.1.call-start = ((), (), s32[]{:S(2)}) async-start(), calls=%async_computation.15 | async-start | bytes 2478080 | tf_op jit(solution)/shard_map/all_gather | solution.py:100
  879.6 112.5 %all-gather.20.cloned.1.call-start = ((), (), s32[]{:S(2)}) async-start(), calls=%async_computation.16 | async-start | bytes 9912320 | tf_op jit(solution)/shard_map/all_gather | solution.py:101
  992.1 13.1 %copy-start = (bf16[256,15488]{1,0:T(8,128)(2,1)S(1)}, bf16[256,15488]{1,0:T(8,128)(2,1)}, u32[]{:S(2)}) copy-start(bf16[256,15488]{1,0:T(8,128)(2,1)} %all-gather.20.cloned.1.call-done) | copy-start | bytes 23789572
  (47 other events, 196.2 us)
Sparse Core Ops, SparseCore 0:
  10.6 82.6 all-gather.7
  95.5 228.6 all-gather.9
  529.6 48.7 all-gather.13
  588.8 66.8 all-gather.11
  657.7 65.4 all-gather.15
  731.7 78.7 reduce-scatter.2
  813.0 28.3 reduce-scatter.4
  844.0 35.5 all-reduce.7
  881.4 29.5 all-gather.17
  912.5 79.5 all-gather.19

commit v5 on v4

--- a/solution.py
+++ b/solution.py
@@ -79,18 +79,6 @@
     across = lax.all_gather(values, "yl", axis=0, tiled=False)
     both = lax.all_gather(across, "c", axis=1, tiled=False)
     return both.reshape((-1,) + values.shape[1:])
-
-
-def permute_gather(values):
-    size = lax.axis_size(FSDP)
-    me = lax.axis_index(FSDP)
-    received = [values]
-    for s in range(1, size):
-        pairs = [(i, i ^ s) for i in range(size)]
-        received.append(lax.ppermute(values, FSDP, pairs))
-    stacked = jnp.stack(received)
-    ordered = [lax.dynamic_index_in_dim(stacked, me ^ j, 0, False) for j in range(size)]
-    return jnp.concatenate(ordered, axis=0)
 
 
 def reduce_ctx(packed):
@@ -164,12 +152,12 @@
     full_qkv = lax.all_gather(
         jnp.concatenate([query_weight, key_projection, value_projection], axis=1), FSDP, axis=0, tiled=True
     )
-    full_output = permute_gather(output_weight)
+    full_output = lax.all_gather(output_weight, FSDP, axis=0, tiled=True)
     ff_cols = gate_weight.shape[1]
     full_gate_up = lax.all_gather(
         jnp.concatenate([gate_weight, up_weight], axis=1), FSDP, axis=0, tiled=True
     )
-    full_down = permute_gather(down_weight)
+    full_down = lax.all_gather(down_weight, FSDP, axis=0, tiled=True)
     input_f32 = layer_input[0].astype(jnp.float32)
     gained, first_normed, first_scale = rms_apply(input_f32, first_gain)
     attention_input = gained.astype(jnp.bfloat16)

time: 1040 us -> 1020 us (0.981)
  blocking collectives: 10.2 us -> 41.6 us
  starting transfers between devices: 57.8 us -> 36.8 us
  waiting for transfers between devices: 613 us -> 600 us
    ppermute x6 -> x0, waiting for transfers between devices: 167 us -> none  [permute_gather(): received.append(lax.ppermute(values, FSDP, pairs))]
    all_gather x0 -> x2, waiting for transfers between devices: none -> 59.4 us  [the longest x1 59.4 us: on_device(): full_down = lax.all_gather(down_weight, FSDP, axis=0, tiled=True)]
    all_gather x1, waiting for transfers between devices: 0.02 us -> 51.7 us  [on_device(): lax.all_gather(jnp.concatenate([gate_weight, up_weight], axis=1), FSDP, a...]
    all_to_all x4 -> x3, waiting for transfers between devices: 36.6 us -> 83.7 us  [exchange(): return lax.all_to_all(values, CTX, split_axis=0, concat_axis=0, tiled=True)]
    all_to_all x0 -> x1, blocking collectives: none -> 31.4 us  [exchange(): return lax.all_to_all(values, CTX, split_axis=0, concat_axis=0, tiled=True)]
    all_to_all x4 -> x3, starting transfers between devices: 47.1 us -> 29.1 us  [exchange(): return lax.all_to_all(values, CTX, split_axis=0, concat_axis=0, tiled=True)]
  transfers between devices with their start and end apart: 21 -> 16, of which waited for: 14 -> 12; matrix products, arithmetic and copies ran while one was open for 20% -> 20% of each run, Pallas kernels for 0% -> 0%
where the time goes in v5:
time: 1020 us; the launch traced here: 1010 us
  waiting for transfers between devices  600 us (59%)
  matrix products  137 us (13%)
  local copies, waits for them, and re-layouts  92.9 us (9%)
  other arithmetic  87.8 us (9%)
  blocking collectives  41.6 us (4%)
  starting transfers between devices  36.8 us (4%)
  between operations  16.9 us (2%)
    all_to_all x3, waiting for transfers between devices, exchange(): return lax.all_to_all(values, CTX, split_axis=0, concat_axis=0, tiled=True)  83.7 us
    reduce_scatter x1, waiting for transfers between devices, reduce_ctx(): part = lax.psum_scatter(packed, 'z', scatter_dimension=0, tiled=True)  78.8 us
    all_gather x1, waiting for transfers between devices, on_device(): lax.all_gather(jnp.concatenate([query_weight, key_projection, value_proje...  78.7 us
    all_gather x1, waiting for transfers between devices, reduce_ctx(): return lax.all_gather(part, 'z', axis=0, tiled=True).astype(jnp.float32)  75.4 us
    all_gather x1, waiting for transfers between devices, on_device(): full_down = lax.all_gather(down_weight, FSDP, axis=0, tiled=True)  59.4 us
    all_gather x1, waiting for transfers between devices, on_device(): lax.all_gather(jnp.concatenate([gate_weight, up_weight], axis=1), FSDP, a...  51.7 us
    dot_general x5, matrix products, right_dot(): lax.dot_general(left_side, right_side, (((1,), (1,)), ((), ())), preferre...  46.2 us
    psum x1, waiting for transfers between devices, reduce_ctx(): part = lax.psum(part, 'yh')  38 us
  transfers between devices with their start and end apart: 16, of which 12 were waited for; matrix products, arithmetic and copies ran while one was open for 20% of the time, Pallas kernels for 0%

profile of v5, /device:TPU:0, one launch (start us, length us, event | category | flops | bytes accessed | tf_op | source)
XLA Modules:
  0.0 1013.5 jit_solution(7612472668852740691)
XLA Ops:
  7.2 3.2 pad_maximum_fusion.3
  14.6 78.7 %all-gather.10.cloned.1.call-done = bf16[1024,4096]{1,0:T(8,128)(2,1)} async-done(((bf16[256,4096]{1,0:T(8,128)(2,1)}), bf16[1024,4096]{1,0:T(8,128)(2,1)}) %all-gather.10.cloned.1.call-update) | async-done | bytes 8388624 | tf_op jit(solution)/shard_map/all_gather | solution.py:152
  93.3 4.7 fusion.28
  118.4 9.4 all-to-all-start
  128.3 47.6 %all-to-all-done = bf16[32,128,384]{2,1,0:T(8,128)(2,1)S(1)} async-done(((bf16[32,128,384]{2,1,0:T(8,128)(2,1)}), bf16[32,128,384]{2,1,0:T(8,128)(2,1)S(1)}, u32[]{:S(2)}, u32[]{:S(2)}) %all-to-all-start) | async-done | bytes 3145760 | tf_op jit(solution)/shard_map/all_to_all | solution.py:149
  176.6 13.9 %fusion.39 = (f32[2048]{0:T(1024)S(1)}, f32[2048,4096]{1,0:T(8,128)}) fusion(s32[2048]{0:T(1024)S(1)} %dynamic_slice.18, s32[4096]{0:T(1024)S(1)} %add.145, bf16[2048,128]{1,0:T(8,128)(2,1)S(1)} %bitcast.205, bf16[4096,128]{1,0:T(8,128)(2,1)S(1)} %bitcast.199), kind=kOutput, calls=%fused_computation.157 | convolution fusion | flops 2181036032 | bytes 35160064 | tf_op jit(solution)/shard_map/qd,kd->qk/dot_general | solution.py:189
  190.5 16.6 %exponential_reduce_fusion = f32[2048]{0:T(1024)S(1)} fusion(f32[2048]{0:T(1024)S(1)} %get-tuple-element.110, f32[2048,4096]{1,0:T(8,128)} %get-tuple-element.111, s32[2048]{0:T(1024)S(1)} %dynamic_slice.18, s32[4096]{0:T(1024)S(1)} %add.145), kind=kLoop, calls=%fused_computation.6 | loop fusion | flops 41940992 | bytes 33595392 | tf_op jit(solution)/shard_map/reduce_sum | solution.py:196
  207.2 15.6 %fusion.46 = (bf16[2048,128]{1,0:T(8,128)(2,1)S(1)}, f32[2048,128]{1,0:T(8,128)}) fusion(bf16[4096,128]{1,0:T(8,128)(2,1)S(1)} %bitcast.201, f32[2048]{0:T(1024)S(1)} %log_add_fusion, f32[2048,4096]{1,0:T(8,128)} %get-tuple-element.111, s32[2048]{0:T(1024)S(1)} %dynamic_slice.18, s32[4096]{0:T(1024)S(1)} %add.145), kind=kOutput, calls=%fused_computation.164 | convolution fusion | flops 2189688832 | bytes 36208640 | tf_op jit(solution)/shard_map/dot_general | solution.py:198
  223.3 31.4 %all_to_all.35 = bf16[32,128,128]{1,2,0:T(8,128)(2,1)S(1)} all-to-all(bf16[32,128,128]{1,2,0:T(8,128)(2,1)S(1)} %bitcast_select_fusion.3), channel_id=1, replica_groups=mesh['yh'=2,'x'=4,'z'=4,'yl'=2,'c'=2] {'yh','x','z'}, dimensions={0} | all-to-all | bytes 2097152 | tf_op jit(solution)/shard_map/all_to_all | solution.py:149
  254.8 3.2 multiply_reduce_fusion.10
  258.9 51.7 %all-gather.14.cloned.1.call-done = bf16[1024,6144]{1,0:T(8,128)(2,1)} async-done(((bf16[256,6144]{1,0:T(8,128)(2,1)}), bf16[1024,6144]{1,0:T(8,128)(2,1)}) %all-gather.14.cloned.1.call-update) | async-done | bytes 12582928 | tf_op jit(solution)/shard_map/all_gather | solution.py:157
  310.6 8.0 fusion.47
  318.7 59.4 %all-gather.16.cloned.1.call-done = bf16[3072,1024]{1,0:T(8,128)(2,1)} async-done(((bf16[768,1024]{1,0:T(8,128)(2,1)}), bf16[3072,1024]{1,0:T(8,128)(2,1)}) %all-gather.16.cloned.1.call-update) | async-done | bytes 6291472 | tf_op jit(solution)/shard_map/all_gather | solution.py:160
  378.1 7.7 multiply_convert_fusion.2
  385.8 7.3 multiply_reduce_fusion.5
  395.3 3.7 fusion.12
  400.7 9.6 all-to-all-start.2
  410.4 20.3 %fusion.2 = bf16[4096,2048]{0,1:T(8,128)(2,1)} fusion(f32[2048,4096]{1,0:T(8,128)} %get-tuple-element.111, f32[2048]{0:T(1024)S(1)} %log_add_fusion, s32[4096]{0:T(1024)S(1)} %add.145, s32[2048]{0:T(1024)S(1)} %dynamic_slice.18), kind=kLoop, calls=%fused_computation.3 | loop fusion | flops 41943040 | bytes 50364416 | tf_op jit(solution)/shard_map/convert_element_type | solution.py:197
  430.7 22.7 %copy.222 = bf16[4096,2048]{1,0:T(8,128)(2,1)} copy(bf16[4096,2048]{0,1:T(8,128)(2,1)} %fusion.2) | data formatting | bytes 33554432 | tf_op jit(solution)/shard_map/dot_general | solution.py:67
  454.1 20.3 %multiply_convert_fusion = bf16[2048,4096]{1,0:T(8,128)(2,1)} fusion(f32[2048]{0:T(1024)S(1)} %multiply_reduce_fusion.2, f32[2048]{0:T(1024)S(1)} %log_add_fusion, bf16[2048,128]{1,0:T(8,128)(2,1)S(1)} %bitcast.171, bf16[4096,128]{1,0:T(8,128)(2,1)} %bitcast.202, f32[2048,4096]{1,0:T(8,128)} %get-tuple-element.111, s32[2048]{0:T(1024)S(1)} %dynamic_slice.18, ...), kind=kOutput, calls=%fused_computation.4 | convolution fusion | flops 2206203904 | bytes 51945472 | tf_op jit(solution)/shard_map/dot_general | solution.py:73
  474.3 8.8 fusion.10
  485.1 4.9 fusion.9
  491.7 9.3 convolution_convert_fusion.5
  501.0 2.8 pad_maximum_fusion.2
  503.9 10.1 all-to-all-start.3
  523.2 36.1 %all-to-all-done.3 = bf16[32,128,384]{1,2,0:T(8,128)(2,1)S(1)} async-done(((bf16[32,128,384]{1,2,0:T(8,128)(2,1)}), bf16[32,128,384]{1,2,0:T(8,128)(2,1)S(1)}, u32[]{:S(2)}, u32[]{:S(2)}) %all-to-all-start.3) | async-done | bytes 3145760 | tf_op jit(solution)/shard_map/all_to_all | solution.py:149
  575.4 2.7 pad_maximum_fusion.5
  580.4 6.9 all-to-all-start.4
  591.7 37.8 %all-to-all-done.4 = bf16[128,4,1792]{2,0,1:T(8,128)(2,1)S(1)} async-done(((bf16[128,4,1792]{2,0,1:T(8,128)(2,1)}), bf16[128,4,1792]{2,0,1:T(8,128)(2,1)S(1)}, u32[]{:S(2)}, u32[]{:S(2)}) %all-to-all-start.4) | async-done | bytes 1835040 | tf_op jit(solution)/shard_map/all_to_all | solution.py:283
  630.8 3.4 convolution_convert_fusion.3
  634.2 2.6 reshape.428
  636.8 3.1 convolution_convert_fusion.4
  641.4 7.3 multiply_reduce_fusion.6
  648.7 10.2 %all-reduce.5 = (f32[1024]{0:T(1024)S(1)}, f32[1024]{0:T(1024)S(1)}, bf16[128]{0:T(256)(128)(2,1)S(1)}, bf16[128]{0:T(256)(128)(2,1)S(1)}) all-reduce(f32[1024]{0:T(1024)S(1)} %get-tuple-element.67, f32[1024]{0:T(1024)S(1)} %copy-done.45, ...), channel_id=2, replica_groups=mesh['yh'=2,'x'=4,'z'=4,'yl'=2,'c'=2] {'yl','c'}, use_global_device_ids=true, to_apply=%region_14.15.clone | all-reduce | flops 2304 | bytes 17920
  668.6 4.9 fusion.8
  674.6 33.8 %all-gather.22.cloned.1.call-done = bf16[512,6144]{1,0:T(8,128)(2,1)} async-done(((bf16[128,6144]{1,0:T(8,128)(2,1)}), bf16[512,6144]{1,0:T(8,128)(2,1)}) %all-gather.22.cloned.1.call-update) | async-done | bytes 6291472 | tf_op jit(solution)/shard_map/all_gather | solution.py:291
  708.4 6.4 fusion.7
  716.7 78.8 %reduce-scatter.3.cloned.1.call-done = bf16[64,15488]{1,0:T(8,128)(2,1)} async-done(((bf16[256,15488]{1,0:T(8,128)(2,1)}), bf16[64,15488]{1,0:T(8,128)(2,1)}) %reduce-scatter.3.cloned.1.call-update) | async-done | bytes 1982480 | tf_op jit(solution)/shard_map/reduce_scatter | solution.py:85
  795.6 30.7 %reduce-scatter.5.cloned.1.call-done = bf16[16,15488]{1,0:T(8,128)(2,1)} async-done(((bf16[64,15488]{1,0:T(8,128)(2,1)}), bf16[16,15488]{1,0:T(8,128)(2,1)}) %reduce-scatter.5.cloned.1.call-update) | async-done | bytes 495632 | tf_op jit(solution)/shard_map/reduce_scatter | solution.py:86
  826.4 38.0 %all-reduce.8.cloned.1.call-done = bf16[16,15488]{1,0:T(8,128)(2,1)} async-done(((bf16[16,15488]{1,0:T(8,128)(2,1)}), bf16[16,15488]{1,0:T(8,128)(2,1)}) %all-reduce.8.cloned.1.call-update) | async-done | bytes 495632 | tf_op jit(solution)/shard_map/psum | solution.py:87
  864.5 31.3 %all-gather.24.cloned.1.call-done = bf16[64,15488]{1,0:T(8,128)(2,1)} async-done(((bf16[16,15488]{1,0:T(8,128)(2,1)}), bf16[64,15488]{1,0:T(8,128)(2,1)}) %all-gather.24.cloned.1.call-update) | async-done | bytes 1982480 | tf_op jit(solution)/shard_map/all_gather | solution.py:88
  895.8 4.6 fusion.14
  901.5 75.4 %all-gather.26.cloned.1.call-done = bf16[256,15488]{1,0:T(8,128)(2,1)} async-done(((bf16[64,15488]{1,0:T(8,128)(2,1)}), bf16[256,15488]{1,0:T(8,128)(2,1)}) %all-gather.26.cloned.1.call-update) | async-done | bytes 7929872 | tf_op jit(solution)/shard_map/all_gather | solution.py:89
  976.9 9.9 convert_element_type.118
  990.1 4.1 fusion.40
  994.2 4.6 reshape.438
  998.8 3.4 fusion.41
  1003.6 2.8 fusion.42
  (279 shorter events, 86.9 us)
Async XLA Ops:
  7.2 86.1 %all-gather.10.cloned.1.call-start = ((), (), s32[]{:S(2)}) async-start(), calls=%async_computation.7 | async-start | bytes 10485760 | tf_op jit(solution)/shard_map/all_gather | solution.py:152
  10.5 244.3 %all-gather.12.cloned.1.call-start = ((), (), s32[]{:S(2)}) async-start(), calls=%async_computation.8 | async-start | bytes 5242880 | tf_op jit(solution)/shard_map/all_gather | solution.py:155
  11.3 82.0 %copy-start.37 = (f32[1024]{0:T(1024)S(1)}, f32[1024]{0:T(1024)}, u32[]{:S(2)}) copy-start(f32[1024]{0:T(1024)} %param.32) | copy-start | bytes 12292
  11.3 299.4 %all-gather.14.cloned.1.call-start = ((), (), s32[]{:S(2)}) async-start(), calls=%async_computation.9 | async-start | bytes 15728640 | tf_op jit(solution)/shard_map/all_gather | solution.py:157
  14.4 83.6 %copy-start.51 = (f32[128]{0:T(128)}, f32[128]{0:T(128)S(1)}, u32[]{:S(2)}) copy-start(f32[128]{0:T(128)S(1)} %add_rsqrt_fusion.3) | copy-start | bytes 1540
  98.0 15.4 %copy-start.4 = (f32[128,4096]{1,0:T(8,128)}, f32[128,4096]{1,0:T(8,128)S(1)}, u32[]{:S(2)}) copy-start(f32[128,4096]{1,0:T(8,128)S(1)} %fusion.28) | copy-start | bytes 6291460
  101.0 7.9 copy-start.6
  109.6 410.8 %copy-start.43 = (f32[128,8]{0,1:T(8,128)}, f32[128,8]{0,1:T(8,128)S(1)}, u32[]{:S(2)}) copy-start(f32[128,8]{0,1:T(8,128)S(1)} %add_rsqrt_fusion.1) | copy-start | bytes 12292
  118.4 57.6 %all-to-all-start = ((bf16[32,128,384]{2,1,0:T(8,128)(2,1)}), bf16[32,128,384]{2,1,0:T(8,128)(2,1)S(1)}, u32[]{:S(2)}, u32[]{:S(2)}) async-start(bf16[32,128,384]{2,1,0:T(8,128)(2,1)} %pad_maximum_fusion), calls=%async_computation | async-start | bytes 6291456 | tf_op jit(solution)/shard_map/all_to_all | solution.py:149
  127.7 250.3 %all-gather.16.cloned.1.call-start = ((), (), s32[]{:S(2)}) async-start(), calls=%async_computation.10 | async-start | bytes 7864320 | tf_op jit(solution)/shard_map/all_gather | solution.py:160
  176.5 14.0 %copy-start.29 = (bf16[32,128,128]{2,1,0:T(8,128)(2,1)}, bf16[32,128,128]{2,1,0:T(8,128)(2,1)S(1)}, u32[]{:S(2)}) copy-start(bf16[32,128,128]{2,1,0:T(8,128)(2,1)S(1)} %get-tuple-element.89) | copy-start | bytes 3145732
  176.5 30.7 %copy-start.31 = (bf16[32,128,128]{2,1,0:T(8,128)(2,1)}, bf16[32,128,128]{2,1,0:T(8,128)(2,1)S(1)}, u32[]{:S(2)}) copy-start(bf16[32,128,128]{2,1,0:T(8,128)(2,1)S(1)} %get-tuple-element.90) | copy-start | bytes 3145732
  176.6 14.0 %copy-start.34 = (bf16[16,128,128]{2,1,0:T(8,128)(2,1)}, bf16[16,128,128]{2,1,0:T(8,128)(2,1)S(1)}, u32[]{:S(2)}) copy-start(bf16[16,128,128]{2,1,0:T(8,128)(2,1)S(1)} %constant_dynamic-slice_fusion.2) | copy-start | bytes 1572868
  207.2 15.9 %copy-start.50 = (pred[32]{0:T(512)(128)(4,1)S(1)}, pred[32]{0:T(512)(128)(4,1)}, u32[]{:S(2)}) copy-start(pred[32]{0:T(512)(128)(4,1)} %broadcast_in_dim.119) | copy-start | bytes 100
  223.3 35.5 %copy-start.41 = (f32[1024]{0:T(1024)S(1)}, f32[1024]{0:T(1024)}, u32[]{:S(2)}) copy-start(f32[1024]{0:T(1024)} %param.33) | copy-start | bytes 12292
  254.8 63.9 %copy-start.12 = (bf16[16,128,128]{1,2,0:T(8,128)(2,1)}, bf16[16,128,128]{1,2,0:T(8,128)(2,1)S(1)}, u32[]{:S(2)}) copy-start(bf16[16,128,128]{1,2,0:T(8,128)(2,1)S(1)} %constant_dynamic-slice_fusion.1) | copy-start | bytes 1572868
  258.0 135.1 %copy-start.47 = (f32[128]{0:T(128)}, f32[128]{0:T(128)S(1)}, u32[]{:S(2)}) copy-start(f32[128]{0:T(128)S(1)} %add_rsqrt_fusion.2) | copy-start | bytes 1540
  258.9 59.8 %copy-start.19 = (bf16[128,1024]{1,0:T(8,128)(2,1)}, bf16[128,1024]{1,0:T(8,128)(2,1)S(1)}, u32[]{:S(2)}) copy-start(bf16[128,1024]{1,0:T(8,128)(2,1)S(1)} %multiply_convert_fusion.4) | copy-start | bytes 786436
  378.1 7.7 copy-start.1
  393.1 6.5 copy-start.56
  400.7 52.7 %all-to-all-start.2 = ((bf16[32,128,128]{1,2,0:T(8,128)(2,1)}), bf16[32,128,128]{1,2,0:T(8,128)(2,1)S(1)}, u32[]{:S(2)}, u32[]{:S(2)}) async-start(bf16[32,128,128]{1,2,0:T(8,128)(2,1)} %bitcast_select_fusion.2), calls=%async_computation.2 | async-start | bytes 2097152 | tf_op jit(solution)/shard_map/all_to_all | solution.py:149
  430.7 23.0 %copy-start.28 = (f32[2048,128]{1,0:T(8,128)S(1)}, f32[2048,128]{1,0:T(8,128)}, u32[]{:S(2)}) copy-start(f32[2048,128]{1,0:T(8,128)} %get-tuple-element.113) | copy-start | bytes 3145732
  454.1 20.3 %copy-start.30 = (bf16[32,128,128]{2,1,0:T(8,128)(2,1)S(1)}, bf16[32,128,128]{2,1,0:T(8,128)(2,1)}, u32[]{:S(2)}) copy-start(bf16[32,128,128]{2,1,0:T(8,128)(2,1)} %copy-done.29) | copy-start | bytes 3145732
  474.3 8.8 copy-start.35
  474.3 10.7 %copy-start.61 = (bf16[2048,4096]{1,0:T(8,128)(2,1)S(1)}, bf16[2048,4096]{1,0:T(8,128)(2,1)}, u32[]{:S(2)}) copy-start(bf16[2048,4096]{1,0:T(8,128)(2,1)} %multiply_convert_fusion) | copy-start | bytes 50331652
  503.9 10.1 %copy-start.55 = (f32[128]{0:T(128)S(1)}, f32[128]{0:T(128)}, u32[]{:S(2)}) copy-start(f32[128]{0:T(128)} %param.34) | copy-start | bytes 1540
  503.9 12.3 %copy-start.53 = (f32[128]{0:T(128)S(1)}, f32[128]{0:T(128)}, u32[]{:S(2)}) copy-start(f32[128]{0:T(128)} %param.35) | copy-start | bytes 1540
  503.9 12.9 %copy-start.40 = (f32[128,16]{0,1:T(8,128)S(1)}, f32[128,16]{0,1:T(8,128)}, u32[]{:S(2)}) copy-start(f32[128,16]{0,1:T(8,128)} %copy-done.39) | copy-start | bytes 24580
  503.9 55.4 %all-to-all-start.3 = ((bf16[32,128,384]{1,2,0:T(8,128)(2,1)}), bf16[32,128,384]{1,2,0:T(8,128)(2,1)S(1)}, u32[]{:S(2)}, u32[]{:S(2)}) async-start(bf16[32,128,384]{1,2,0:T(8,128)(2,1)} %pad_maximum_fusion.2), calls=%async_computation.3 | async-start | bytes 6291456 | tf_op jit(solution)/shard_map/all_to_all | solution.py:149
  514.0 115.6 %all-gather.20.cloned.1.call-start = ((), (), s32[]{:S(2)}) async-start(), calls=%async_computation.12 | async-start | bytes 2621440 | tf_op jit(solution)/shard_map/all_gather | solution.py:292
  515.9 152.7 %all-gather.18.cloned.1.call-start = ((), (), s32[]{:S(2)}) async-start(), calls=%async_computation.11 | async-start | bytes 5242880 | tf_op jit(solution)/shard_map/all_gather | solution.py:290
  564.5 6.2 copy-start.5
  564.6 6.2 copy-start.46
  565.6 7.1 copy-start.14
  575.4 133.0 %all-gather.22.cloned.1.call-start = ((), (), s32[]{:S(2)}) async-start(), calls=%async_computation.13 | async-start | bytes 7864320 | tf_op jit(solution)/shard_map/all_gather | solution.py:291
  578.9 8.3 copy-start.60
  578.9 12.1 %copy-start.58 = (s32[2]{0:T(128)S(1)}, s32[2]{0:T(128)}, u32[]{:S(2)}) copy-start(s32[2]{0:T(128)} %constant.176.clone.1) | copy-start | bytes 28
  580.4 49.2 %all-to-all-start.4 = ((bf16[128,4,1792]{2,0,1:T(8,128)(2,1)}), bf16[128,4,1792]{2,0,1:T(8,128)(2,1)S(1)}, u32[]{:S(2)}, u32[]{:S(2)}) async-start(bf16[128,4,1792]{2,0,1:T(8,128)(2,1)} %pad_maximum_fusion.4), calls=%async_computation.4 | async-start | bytes 3670016 | tf_op jit(solution)/shard_map/all_to_all | solution.py:283
  587.2 208.3 %reduce-scatter.3.cloned.1.call-start = ((), (), s32[]{:S(2)}) async-start(), calls=%async_computation.14 | async-start | bytes 9912320 | tf_op jit(solution)/shard_map/reduce_scatter | solution.py:85
  634.2 7.2 copy-start.25
  641.4 7.3 copy-start.45
  716.7 179.1 %copy-start.3 = (f32[128,1024]{1,0:T(8,128)S(1)}, f32[128,1024]{1,0:T(8,128)}, u32[]{:S(2)}) copy-start(f32[128,1024]{1,0:T(8,128)} %copy-done.2) | copy-start | bytes 1572868
  716.7 179.1 %copy-start.18 = (bf16[128,3072]{1,0:T(8,128)(2,1)S(1)}, bf16[128,3072]{1,0:T(8,128)(2,1)}, u32[]{:S(2)}) copy-start(bf16[128,3072]{1,0:T(8,128)(2,1)} %get-tuple-element.88) | copy-start | bytes 2359300
  716.7 109.7 %reduce-scatter.5.cloned.1.call-start = ((), (), s32[]{:S(2)}) async-start(), calls=%async_computation.15 | async-start | bytes 2478080 | tf_op jit(solution)/shard_map/reduce_scatter | solution.py:86
  795.6 68.8 %all-reduce.8.cloned.1.call-start = ((), (), s32[]{:S(2)}) async-start(), calls=%async_computation.16 | async-start | bytes 991232 | tf_op jit(solution)/shard_map/psum | solution.py:87
  826.4 69.4 %all-gather.24.cloned.1.call-start = ((), (), s32[]{:S(2)}) async-start(), calls=%async_computation.17 | async-start | bytes 2478080 | tf_op jit(solution)/shard_map/all_gather | solution.py:88
  864.4 112.5 %all-gather.26.cloned.1.call-start = ((), (), s32[]{:S(2)}) async-start(), calls=%async_computation.18 | async-start | bytes 9912320 | tf_op jit(solution)/shard_map/all_gather | solution.py:89
  976.9 13.2 %copy-start = (bf16[256,15488]{1,0:T(8,128)(2,1)S(1)}, bf16[256,15488]{1,0:T(8,128)(2,1)}, u32[]{:S(2)}) copy-start(bf16[256,15488]{1,0:T(8,128)(2,1)} %all-gather.26.cloned.1.call-done) | copy-start | bytes 23789572
  (30 other events, 89.1 us)
Sparse Core Ops, SparseCore 0:
  10.6 82.6 all-gather.9
  94.9 82.7 all-gather.11
  180.0 130.6 all-gather.13
  312.2 65.8 all-gather.15
  516.2 51.6 all-gather.19
  575.5 68.3 all-gather.17
  646.1 62.2 all-gather.21
  716.8 78.7 reduce-scatter.2
  798.0 28.3 reduce-scatter.4
  828.8 35.5 all-reduce.7
  866.2 29.5 all-gather.23
  897.3 79.5 all-gather.25

commit v6 on v5

--- a/solution.py
+++ b/solution.py
@@ -84,7 +84,9 @@
 def reduce_ctx(packed):
     part = lax.psum_scatter(packed, "z", scatter_dimension=0, tiled=True)
     part = lax.psum_scatter(part, "x", scatter_dimension=0, tiled=True)
-    part = lax.psum(part, "yh")
+    part = (part.astype(jnp.float32) + lax.ppermute(part, "yh", [(0, 1), (1, 0)]).astype(jnp.float32)).astype(
+        part.dtype
+    )
     part = lax.all_gather(part, "x", axis=0, tiled=True)
     return lax.all_gather(part, "z", axis=0, tiled=True).astype(jnp.float32)
 
@@ -225,6 +227,34 @@
     )
     mid_grad_b = mid_grad.astype(jnp.bfloat16)
     mixed_gradient = right_dot(mid_grad_b, full_output).astype(jnp.bfloat16)
+    fsdp_size = lax.axis_size(FSDP)
+    col_parts = (attention_input, mixed_b, mlp_in, hidden)
+    widths = [p.shape[1] // fsdp_size for p in col_parts]
+    stacked = jnp.concatenate(
+        [p.reshape(local_rows, fsdp_size, w) for p, w in zip(col_parts, widths)], axis=2
+    )
+    cols = lax.all_to_all(stacked, FSDP, split_axis=1, concat_axis=0, tiled=True).reshape(
+        fsdp_size * local_rows, sum(widths)
+    )
+    bounds = [sum(widths[:i]) for i in range(5)]
+    attn_cols, mixed_cols, mlp_cols, hidden_cols = (
+        cols[:, bounds[i] : bounds[i + 1]] for i in range(4)
+    )
+    gate_up_rows = lax.all_gather(gate_up_grad, FSDP, axis=0, tiled=True)
+    cot_mid_rows = lax.all_gather(
+        jnp.concatenate([own_cotangent, mid_grad_b], axis=1), FSDP, axis=0, tiled=True
+    )
+    model_width = own_cotangent.shape[1]
+    output_shard = left_dot(mixed_cols, cot_mid_rows[:, model_width:])
+    gate_up_shard = left_dot(mlp_cols, gate_up_rows)
+    down_shard = left_dot(hidden_cols, cot_mid_rows[:, :model_width])
+    mlp_rows = gate_up_shard.shape[0]
+    mlp_packed = jnp.concatenate(
+        [output_shard.reshape(mlp_rows, -1), gate_up_shard, down_shard.reshape(mlp_rows, -1)],
+        axis=1,
+    ).astype(jnp.bfloat16)
+    mlp_packed, mixed_gradient = lax.optimization_barrier((mlp_packed, mixed_gradient))
+    mlp_reduced = reduce_ctx(mlp_packed)
     head_out_grad = gather_half(
         exchange(to_heads(mixed_gradient.reshape(local_rows, HQ, HEAD_SIZE)))
     )
@@ -274,60 +304,30 @@
     input_grad = mid_grad + root_mean_square_backward(
         attn_in_grad, first_normed, first_scale, first_gain
     )
-    fsdp_size = lax.axis_size(FSDP)
-    col_parts = (attention_input, mixed_b, mlp_in, hidden)
-    widths = [p.shape[1] // fsdp_size for p in col_parts]
-    stacked = jnp.concatenate(
-        [p.reshape(local_rows, fsdp_size, w) for p, w in zip(col_parts, widths)], axis=2
-    )
-    cols = lax.all_to_all(stacked, FSDP, split_axis=1, concat_axis=0, tiled=True).reshape(
-        fsdp_size * local_rows, sum(widths)
-    )
-    bounds = [sum(widths[:i]) for i in range(5)]
-    attn_cols, mixed_cols, mlp_cols, hidden_cols = (
-        cols[:, bounds[i] : bounds[i + 1]] for i in range(4)
-    )
     qkv_rows = lax.all_gather(qkv_grad, FSDP, axis=0, tiled=True)
-    gate_up_rows = lax.all_gather(gate_up_grad, FSDP, axis=0, tiled=True)
-    cot_mid_rows = lax.all_gather(
-        jnp.concatenate([own_cotangent, mid_grad_b], axis=1), FSDP, axis=0, tiled=True
-    )
     first_shard, second_shard, query_gain_shard, key_gain_shard = (
         lax.psum_scatter(first_gain_grad, FSDP, scatter_dimension=0, tiled=True),
         lax.psum_scatter(second_gain_grad, FSDP, scatter_dimension=0, tiled=True),
         lax.psum_scatter(query_gain_grad, FSDP, scatter_dimension=0, tiled=True),
         lax.psum_scatter(key_gain_grad, FSDP, scatter_dimension=0, tiled=True),
     )
-    model_width = own_cotangent.shape[1]
     qkv_shard = left_dot(attn_cols, qkv_rows)
-    output_shard = left_dot(mixed_cols, cot_mid_rows[:, model_width:])
-    gate_up_shard = left_dot(mlp_cols, gate_up_rows)
-    down_shard = left_dot(hidden_cols, cot_mid_rows[:, :model_width])
     shard_rows = qkv_shard.shape[0]
     gain_parts = (first_shard, second_shard, query_gain_shard, key_gain_shard)
     gain_block = jnp.zeros((shard_rows, 128), jnp.float32)
     for column, g in enumerate(gain_parts):
         gain_block = gain_block.at[: g.shape[0], column].set(g)
-    packed = jnp.concatenate(
-        [
-            qkv_shard,
-            output_shard.reshape(shard_rows, -1),
-            gate_up_shard,
-            down_shard.reshape(shard_rows, -1),
-            gain_block,
-        ],
-        axis=1,
-    ).astype(jnp.bfloat16)
-    reduced = reduce_ctx(packed)
-    pieces = []
-    at = 0
-    for width in (qkv_cols[0], qkv_cols[1], qkv_cols[2], output_shard.size // shard_rows, ff_cols, ff_cols,
-                  down_shard.size // shard_rows):
-        pieces.append(reduced[:, at : at + width])
-        at += width
-    query_total, key_total, value_total, output_total, gate_total, up_total, down_total = pieces
-    output_total = output_total.reshape(output_shard.shape)
-    down_total = down_total.reshape(down_shard.shape)
+    attn_reduced = reduce_ctx(jnp.concatenate([qkv_shard, gain_block], axis=1).astype(jnp.bfloat16))
+    output_width = output_shard.size // shard_rows
+    output_total = mlp_reduced[:, :output_width].reshape(output_shard.shape)
+    gate_total = mlp_reduced[:, output_width : output_width + ff_cols]
+    up_total = mlp_reduced[:, output_width + ff_cols : output_width + 2 * ff_cols]
+    down_total = mlp_reduced[:, output_width + 2 * ff_cols :].reshape(down_shard.shape)
+    query_total = attn_reduced[:, : qkv_cols[0]]
+    key_total = attn_reduced[:, qkv_cols[0] : qkv_cols[0] + qkv_cols[1]]
+    value_total = attn_reduced[:, qkv_cols[0] + qkv_cols[1] : sum(qkv_cols)]
+    at = sum(qkv_cols)
+    reduced = attn_reduced
     first_total, second_total, query_gain_total, key_gain_total = (
         reduced[: g.shape[0], at + column] for column, g in enumerate(gain_parts)
     )

time: 1020 us -> 986 us (0.967)
  waiting for transfers between devices: 600 us -> 549 us
  blocking collectives: 41.6 us -> 59 us
    reduce_scatter x1 -> x2, waiting for transfers between devices: 78.8 us -> 30 us  [reduce_ctx(): part = lax.psum_scatter(packed, 'z', scatter_dimension=0, tiled=True)]
    psum x1 -> x0, waiting for transfers between devices: 38 us -> none  [reduce_ctx(): part = lax.psum(part, 'yh')]
    all_gather x1, waiting for transfers between devices: 31.3 us -> 5.86 us  [reduce_ctx(): part = lax.all_gather(part, 'x', axis=0, tiled=True)]
    all_gather x1, waiting for transfers between devices: 33.8 us -> 54 us  [on_device(): gate_up_rows = lax.all_gather(gate_up_grad, FSDP, axis=0, tiled=True)]
    all_gather x0 -> x1, blocking collectives: none -> 15.3 us  [reduce_ctx(): part = lax.all_gather(part, 'x', axis=0, tiled=True)]
    reduce_scatter x1 -> x2, waiting for transfers between devices: 30.7 us -> 45.4 us  [reduce_ctx(): part = lax.psum_scatter(part, 'x', scatter_dimension=0, tiled=True)]
    all_gather x1, waiting for transfers between devices: 0.02 us -> 13.3 us  [on_device(): qkv_rows = lax.all_gather(qkv_grad, FSDP, axis=0, tiled=True)]
    all_gather x1 -> x2, waiting for transfers between devices: 75.4 us -> 83.6 us  [reduce_ctx(): return lax.all_gather(part, 'z', axis=0, tiled=True).astype(jnp.float32)]
  transfers between devices with their start and end apart: 16 -> 20, of which waited for: 12 -> 15; matrix products, arithmetic and copies ran while one was open for 20% -> 27% of each run, Pallas kernels for 0% -> 0%
where the time goes in v6:
time: 986 us; the launch traced here: 977 us
  waiting for transfers between devices  549 us (56%)
  matrix products  140 us (14%)
  other arithmetic  88.1 us (9%)
  local copies, waits for them, and re-layouts  84.3 us (9%)
  blocking collectives  59 us (6%)
  starting transfers between devices  40.2 us (4%)
  between operations  17 us (2%)
    all_to_all x3, waiting for transfers between devices, exchange(): return lax.all_to_all(values, CTX, split_axis=0, concat_axis=0, tiled=True)  85.7 us
    all_gather x2, waiting for transfers between devices, reduce_ctx(): return lax.all_gather(part, 'z', axis=0, tiled=True).astype(jnp.float32)  83.6 us
    all_gather x1, waiting for transfers between devices, on_device(): lax.all_gather(jnp.concatenate([query_weight, key_projection, value_proje...  78.6 us
    all_gather x1, waiting for transfers between devices, on_device(): full_down = lax.all_gather(down_weight, FSDP, axis=0, tiled=True)  59.3 us
    all_gather x1, waiting for transfers between devices, on_device(): gate_up_rows = lax.all_gather(gate_up_grad, FSDP, axis=0, tiled=True)  54 us
    all_gather x1, waiting for transfers between devices, on_device(): lax.all_gather(jnp.concatenate([gate_weight, up_weight], axis=1), FSDP, a...  51.7 us
    dot_general x5, matrix products, right_dot(): lax.dot_general(left_side, right_side, (((1,), (1,)), ((), ())), preferre...  46.1 us
    reduce_scatter x2, waiting for transfers between devices, reduce_ctx(): part = lax.psum_scatter(part, 'x', scatter_dimension=0, tiled=True)  45.4 us
  transfers between devices with their start and end apart: 20, of which 15 were waited for; matrix products, arithmetic and copies ran while one was open for 27% of the time, Pallas kernels for 0%

profile of v6, /device:TPU:0, one launch (start us, length us, event | category | flops | bytes accessed | tf_op | source)
XLA Modules:
  0.0 976.8 jit_solution(8809402792879629912)
XLA Ops:
  7.2 3.2 pad_maximum_fusion.5
  14.6 78.6 %all-gather.11.cloned.1.call-done = bf16[1024,4096]{1,0:T(8,128)(2,1)} async-done(((bf16[256,4096]{1,0:T(8,128)(2,1)}), bf16[1024,4096]{1,0:T(8,128)(2,1)}) %all-gather.11.cloned.1.call-update) | async-done | bytes 8388624 | tf_op jit(solution)/shard_map/all_gather | solution.py:154
  93.3 4.7 fusion.25
  118.5 9.4 all-to-all-start
  128.7 47.3 %all-to-all-done = bf16[32,128,384]{2,1,0:T(8,128)(2,1)S(1)} async-done(((bf16[32,128,384]{2,1,0:T(8,128)(2,1)}), bf16[32,128,384]{2,1,0:T(8,128)(2,1)S(1)}, u32[]{:S(2)}, u32[]{:S(2)}) %all-to-all-start) | async-done | bytes 3145760 | tf_op jit(solution)/shard_map/all_to_all | solution.py:151
  176.7 13.9 %fusion.36 = (f32[2048]{0:T(1024)S(1)}, f32[2048,4096]{1,0:T(8,128)}) fusion(s32[2048]{0:T(1024)S(1)} %dynamic_slice.18, s32[4096]{0:T(1024)S(1)} %add.153, bf16[2048,128]{1,0:T(8,128)(2,1)S(1)} %bitcast.205, bf16[4096,128]{1,0:T(8,128)(2,1)S(1)} %bitcast.199), kind=kOutput, calls=%fused_computation.155 | convolution fusion | flops 2181036032 | bytes 35160064 | tf_op jit(solution)/shard_map/qd,kd->qk/dot_general | solution.py:191
  190.6 16.6 %exponential_reduce_fusion = f32[2048]{0:T(1024)S(1)} fusion(f32[2048]{0:T(1024)S(1)} %get-tuple-element.112, f32[2048,4096]{1,0:T(8,128)} %get-tuple-element.113, s32[2048]{0:T(1024)S(1)} %dynamic_slice.18, s32[4096]{0:T(1024)S(1)} %add.153), kind=kLoop, calls=%fused_computation.6 | loop fusion | flops 41940992 | bytes 33595392 | tf_op jit(solution)/shard_map/reduce_sum | solution.py:198
  207.3 15.6 %fusion.42 = (bf16[2048,128]{1,0:T(8,128)(2,1)S(1)}, f32[2048,128]{1,0:T(8,128)}) fusion(bf16[4096,128]{1,0:T(8,128)(2,1)S(1)} %bitcast.201, f32[2048]{0:T(1024)S(1)} %log_add_fusion, f32[2048,4096]{1,0:T(8,128)} %get-tuple-element.113, s32[2048]{0:T(1024)S(1)} %dynamic_slice.18, s32[4096]{0:T(1024)S(1)} %add.153), kind=kOutput, calls=%fused_computation.161 | convolution fusion | flops 2189688832 | bytes 36208640 | tf_op jit(solution)/shard_map/dot_general | solution.py:200
  223.4 31.4 %all_to_all.35 = bf16[32,128,128]{1,2,0:T(8,128)(2,1)S(1)} all-to-all(bf16[32,128,128]{1,2,0:T(8,128)(2,1)S(1)} %bitcast_select_fusion.3), channel_id=1, replica_groups=mesh['yh'=2,'x'=4,'z'=4,'yl'=2,'c'=2] {'yh','x','z'}, dimensions={0} | all-to-all | bytes 2097152 | tf_op jit(solution)/shard_map/all_to_all | solution.py:151
  254.9 3.2 multiply_reduce_fusion.10
  259.0 51.7 %all-gather.15.cloned.1.call-done = bf16[1024,6144]{1,0:T(8,128)(2,1)} async-done(((bf16[256,6144]{1,0:T(8,128)(2,1)}), bf16[1024,6144]{1,0:T(8,128)(2,1)}) %all-gather.15.cloned.1.call-update) | async-done | bytes 12582928 | tf_op jit(solution)/shard_map/all_gather | solution.py:159
  310.8 8.0 fusion.43
  318.8 59.3 %all-gather.17.cloned.1.call-done = bf16[3072,1024]{1,0:T(8,128)(2,1)} async-done(((bf16[768,1024]{1,0:T(8,128)(2,1)}), bf16[3072,1024]{1,0:T(8,128)(2,1)}) %all-gather.17.cloned.1.call-update) | async-done | bytes 6291472 | tf_op jit(solution)/shard_map/all_gather | solution.py:162
  378.1 7.7 multiply_convert_fusion.2
  385.9 7.3 multiply_reduce_fusion.5
  401.5 4.1 all-to-all-start.2
  405.5 3.8 convolution_convert_fusion.2
  409.4 35.9 %all-to-all-done.2 = bf16[128,4,1792]{2,0,1:T(8,128)(2,1)S(1)} async-done(((bf16[128,4,1792]{2,0,1:T(8,128)(2,1)}), bf16[128,4,1792]{2,0,1:T(8,128)(2,1)S(1)}, u32[]{:S(2)}, u32[]{:S(2)}) %all-to-all-start.2) | async-done | bytes 1835040 | tf_op jit(solution)/shard_map/all_to_all | solution.py:236
  446.5 2.9 convolution_convert_fusion.4
  450.8 3.6 convolution_convert_fusion.3
  457.1 54.0 %all-gather.21.cloned.1.call-done = bf16[512,6144]{1,0:T(8,128)(2,1)} async-done(((bf16[128,6144]{1,0:T(8,128)(2,1)}), bf16[512,6144]{1,0:T(8,128)(2,1)}) %all-gather.21.cloned.1.call-update) | async-done | bytes 6291472 | tf_op jit(solution)/shard_map/all_gather | solution.py:243
  511.1 4.7 convolution_convert_fusion
  515.8 3.5 pad_maximum_fusion
  521.0 9.4 all-to-all-start.3
  530.6 20.3 %fusion.2 = bf16[4096,2048]{0,1:T(8,128)(2,1)} fusion(f32[2048,4096]{1,0:T(8,128)} %get-tuple-element.113, f32[2048]{0:T(1024)S(1)} %log_add_fusion, s32[4096]{0:T(1024)S(1)} %add.153, s32[2048]{0:T(1024)S(1)} %dynamic_slice.18), kind=kLoop, calls=%fused_computation.3 | loop fusion | flops 41943040 | bytes 50364416 | tf_op jit(solution)/shard_map/convert_element_type | solution.py:199
  550.9 22.5 %copy.222 = bf16[4096,2048]{1,0:T(8,128)(2,1)} copy(bf16[4096,2048]{0,1:T(8,128)(2,1)} %fusion.2) | data formatting | bytes 33554432 | tf_op jit(solution)/shard_map/dot_general | solution.py:67
  575.0 20.6 %multiply_convert_fusion = bf16[2048,4096]{1,0:T(8,128)(2,1)} fusion(f32[2048]{0:T(1024)S(1)} %multiply_reduce_fusion.2, f32[2048]{0:T(1024)S(1)} %log_add_fusion, bf16[2048,128]{1,0:T(8,128)(2,1)S(1)} %bitcast.170, bf16[4096,128]{1,0:T(8,128)(2,1)} %bitcast.202, f32[2048,4096]{1,0:T(8,128)} %get-tuple-element.113, s32[2048]{0:T(1024)S(1)} %dynamic_slice.18, ...), kind=kOutput, calls=%fused_computation.4 | convolution fusion | flops 2206203904 | bytes 51945472 | tf_op jit(solution)/shard_map/dot_general | solution.py:73
  595.7 8.7 fusion.8
  604.8 10.6 %fusion.7 = bf16[4096,128]{1,0:T(8,128)(2,1)S(1)} fusion(bf16[2048,4096]{1,0:T(8,128)(2,1)} %multiply_convert_fusion, bf16[2048,128]{1,0:T(8,128)(2,1)} %bitcast.206), kind=kOutput, calls=%fused_computation.15 | convolution fusion | flops 2148532224 | bytes 18350080 | tf_op jit(solution)/shard_map/dot_general | solution.py:67
  616.7 9.4 convolution_convert_fusion.5
  628.9 9.8 %all-to-all-start.4 = ((bf16[32,128,384]{1,2,0:T(8,128)(2,1)}), bf16[32,128,384]{1,2,0:T(8,128)(2,1)S(1)}, u32[]{:S(2)}, u32[]{:S(2)}) async-start(bf16[32,128,384]{1,2,0:T(8,128)(2,1)} %pad_maximum_fusion.3), calls=%async_computation.4 | async-start | bytes 6291456 | tf_op jit(solution)/shard_map/all_to_all | solution.py:151
  645.5 38.4 %all-to-all-done.4 = bf16[32,128,384]{1,2,0:T(8,128)(2,1)S(1)} async-done(((bf16[32,128,384]{1,2,0:T(8,128)(2,1)}), bf16[32,128,384]{1,2,0:T(8,128)(2,1)S(1)}, u32[]{:S(2)}, u32[]{:S(2)}) %all-to-all-start.4) | async-done | bytes 3145760 | tf_op jit(solution)/shard_map/all_to_all | solution.py:151
  705.8 6.6 multiply_reduce_fusion.6
  712.5 12.3 %all-reduce.5 = (f32[1024]{0:T(1024)S(1)}, f32[1024]{0:T(1024)S(1)}, bf16[128]{0:T(256)(128)(2,1)S(1)}, bf16[128]{0:T(256)(128)(2,1)S(1)}) all-reduce(f32[1024]{0:T(1024)S(1)} %get-tuple-element.71, f32[1024]{0:T(1024)S(1)} %copy-done.47, ...), channel_id=2, replica_groups=mesh['yh'=2,'x'=4,'z'=4,'yl'=2,'c'=2] {'yl','c'}, use_global_device_ids=true, to_apply=%region_14.15.clone | all-reduce | flops 2304 | bytes 17920
  734.2 13.3 %all-gather.23.cloned.1.call-done = bf16[512,4096]{1,0:T(8,128)(2,1)} async-done(((bf16[128,4096]{1,0:T(8,128)(2,1)}), bf16[512,4096]{1,0:T(8,128)(2,1)}) %all-gather.23.cloned.1.call-update) | async-done | bytes 4194320 | tf_op jit(solution)/shard_map/all_gather | solution.py:307
  747.5 3.6 convolution_convert_fusion.1
  752.6 23.8 %reduce-scatter.11.cloned.1.call-done = bf16[16,11264]{1,0:T(8,128)(2,1)} async-done(((bf16[64,11264]{1,0:T(8,128)(2,1)}), bf16[16,11264]{1,0:T(8,128)(2,1)}) %reduce-scatter.11.cloned.1.call-update) | async-done | bytes 360464 | tf_op jit(solution)/shard_map/reduce_scatter | solution.py:86
  776.4 3.0 collective-permute-start.1
  779.4 30.0 %reduce-scatter.5.cloned.1.call-done = bf16[64,4224]{1,0:T(8,128)(2,1)} async-done(((bf16[256,4224]{1,0:T(8,128)(2,1)}), bf16[64,4224]{1,0:T(8,128)(2,1)}) %reduce-scatter.5.cloned.1.call-update) | async-done | bytes 540688 | tf_op jit(solution)/shard_map/reduce_scatter | solution.py:85
  811.3 21.7 %reduce-scatter.7.cloned.1.call-done = bf16[16,4224]{1,0:T(8,128)(2,1)} async-done(((bf16[64,4224]{1,0:T(8,128)(2,1)}), bf16[16,4224]{1,0:T(8,128)(2,1)}) %reduce-scatter.7.cloned.1.call-update) | async-done | bytes 135184 | tf_op jit(solution)/shard_map/reduce_scatter | solution.py:86
  833.0 3.0 collective-permute-start
  836.0 3.7 collective-permute-done
  840.7 15.3 %all_gather.40 = bf16[64,4224]{1,0:T(8,128)(2,1)} all-gather(bf16[16,4224]{1,0:T(8,128)(2,1)S(1)} %add_convert_fusion.2), channel_id=1, replica_groups=mesh['yh'=2,'x'=4,'z'=4,'yl'=2,'c'=2] {'x'}, dimensions={0}, use_global_device_ids=true | all-gather | bytes 675840 | tf_op jit(solution)/shard_map/all_gather | solution.py:90
  856.4 5.9 all-gather.27.cloned.1.call-done
  862.3 4.5 fusion.11
  868.0 27.5 %all-gather.25.cloned.1.call-done = bf16[256,4224]{1,0:T(8,128)(2,1)} async-done(((bf16[64,4224]{1,0:T(8,128)(2,1)}), bf16[256,4224]{1,0:T(8,128)(2,1)}) %all-gather.25.cloned.1.call-update) | async-done | bytes 2162704 | tf_op jit(solution)/shard_map/all_gather | solution.py:91
  902.4 56.1 %all-gather.29.cloned.1.call-done = bf16[256,11264]{1,0:T(8,128)(2,1)} async-done(((bf16[64,11264]{1,0:T(8,128)(2,1)}), bf16[256,11264]{1,0:T(8,128)(2,1)}) %all-gather.29.cloned.1.call-update) | async-done | bytes 5767184 | tf_op jit(solution)/shard_map/all_gather | solution.py:91
  958.5 6.3 fusion.37
  (294 shorter events, 102.9 us)
Async XLA Ops:
  7.2 86.1 %all-gather.11.cloned.1.call-start = ((), (), s32[]{:S(2)}) async-start(), calls=%async_computation.9 | async-start | bytes 10485760 | tf_op jit(solution)/shard_map/all_gather | solution.py:154
  10.5 244.4 %all-gather.13.cloned.1.call-start = ((), (), s32[]{:S(2)}) async-start(), calls=%async_computation.10 | async-start | bytes 5242880 | tf_op jit(solution)/shard_map/all_gather | solution.py:157
  11.3 82.0 %copy-start.38 = (f32[1024]{0:T(1024)S(1)}, f32[1024]{0:T(1024)}, u32[]{:S(2)}) copy-start(f32[1024]{0:T(1024)} %param.32) | copy-start | bytes 12292
  11.3 299.5 %all-gather.15.cloned.1.call-start = ((), (), s32[]{:S(2)}) async-start(), calls=%async_computation.11 | async-start | bytes 15728640 | tf_op jit(solution)/shard_map/all_gather | solution.py:159
  14.4 83.6 %copy-start.52 = (f32[128]{0:T(128)}, f32[128]{0:T(128)S(1)}, u32[]{:S(2)}) copy-start(f32[128]{0:T(128)S(1)} %add_rsqrt_fusion.3) | copy-start | bytes 1540
  14.6 95.8 %copy-start.33 = (f32[128,64]{0,1:T(8,128)}, f32[128,64]{0,1:T(8,128)S(1)}, u32[]{:S(2)}) copy-start(f32[128,64]{0,1:T(8,128)S(1)} %get-tuple-element.106) | copy-start | bytes 98308
  14.6 95.8 %copy-start.35 = (f32[128,64]{0,1:T(8,128)}, f32[128,64]{0,1:T(8,128)S(1)}, u32[]{:S(2)}) copy-start(f32[128,64]{0,1:T(8,128)S(1)} %get-tuple-element.107) | copy-start | bytes 98308
  98.0 15.5 %copy-start.4 = (f32[128,4096]{1,0:T(8,128)}, f32[128,4096]{1,0:T(8,128)S(1)}, u32[]{:S(2)}) copy-start(f32[128,4096]{1,0:T(8,128)S(1)} %fusion.25) | copy-start | bytes 6291460
  101.1 7.9 copy-start.6
  118.5 57.6 %all-to-all-start = ((bf16[32,128,384]{2,1,0:T(8,128)(2,1)}), bf16[32,128,384]{2,1,0:T(8,128)(2,1)S(1)}, u32[]{:S(2)}, u32[]{:S(2)}) async-start(bf16[32,128,384]{2,1,0:T(8,128)(2,1)} %pad_maximum_fusion.1), calls=%async_computation | async-start | bytes 6291456 | tf_op jit(solution)/shard_map/all_to_all | solution.py:151
  127.8 250.3 %all-gather.17.cloned.1.call-start = ((), (), s32[]{:S(2)}) async-start(), calls=%async_computation.12 | async-start | bytes 7864320 | tf_op jit(solution)/shard_map/all_gather | solution.py:162
  128.4 316.8 %all-gather.19.cloned.1.call-start = ((), (), s32[]{:S(2)}) async-start(), calls=%async_computation.13 | async-start | bytes 2621440 | tf_op jit(solution)/shard_map/all_gather | solution.py:244
  176.6 14.0 %copy-start.27 = (bf16[32,128,128]{2,1,0:T(8,128)(2,1)}, bf16[32,128,128]{2,1,0:T(8,128)(2,1)S(1)}, u32[]{:S(2)}) copy-start(bf16[32,128,128]{2,1,0:T(8,128)(2,1)S(1)} %get-tuple-element.89) | copy-start | bytes 3145732
  176.6 30.7 %copy-start.29 = (bf16[32,128,128]{2,1,0:T(8,128)(2,1)}, bf16[32,128,128]{2,1,0:T(8,128)(2,1)S(1)}, u32[]{:S(2)}) copy-start(bf16[32,128,128]{2,1,0:T(8,128)(2,1)S(1)} %get-tuple-element.90) | copy-start | bytes 3145732
  176.7 13.9 %copy-start.37 = (bf16[16,128,128]{2,1,0:T(8,128)(2,1)}, bf16[16,128,128]{2,1,0:T(8,128)(2,1)S(1)}, u32[]{:S(2)}) copy-start(bf16[16,128,128]{2,1,0:T(8,128)(2,1)S(1)} %constant_dynamic-slice_fusion.2) | copy-start | bytes 1572868
  207.3 15.9 %copy-start.51 = (pred[32]{0:T(512)(128)(4,1)S(1)}, pred[32]{0:T(512)(128)(4,1)}, u32[]{:S(2)}) copy-start(pred[32]{0:T(512)(128)(4,1)} %broadcast_in_dim.119) | copy-start | bytes 100
  223.4 35.5 %copy-start.43 = (f32[1024]{0:T(1024)S(1)}, f32[1024]{0:T(1024)}, u32[]{:S(2)}) copy-start(f32[1024]{0:T(1024)} %param.33) | copy-start | bytes 12292
  254.8 64.0 %copy-start.12 = (bf16[16,128,128]{1,2,0:T(8,128)(2,1)}, bf16[16,128,128]{1,2,0:T(8,128)(2,1)S(1)}, u32[]{:S(2)}) copy-start(bf16[16,128,128]{1,2,0:T(8,128)(2,1)S(1)} %constant_dynamic-slice_fusion.1) | copy-start | bytes 1572868
  258.1 135.1 %copy-start.48 = (f32[128]{0:T(128)}, f32[128]{0:T(128)S(1)}, u32[]{:S(2)}) copy-start(f32[128]{0:T(128)S(1)} %add_rsqrt_fusion.2) | copy-start | bytes 1540
  259.0 59.8 %copy-start.20 = (bf16[128,1024]{1,0:T(8,128)(2,1)}, bf16[128,1024]{1,0:T(8,128)(2,1)S(1)}, u32[]{:S(2)}) copy-start(bf16[128,1024]{1,0:T(8,128)(2,1)S(1)} %multiply_convert_fusion.4) | copy-start | bytes 786436
  378.1 7.7 copy-start
  396.6 114.5 %all-gather.21.cloned.1.call-start = ((), (), s32[]{:S(2)}) async-start(), calls=%async_computation.14 | async-start | bytes 7864320 | tf_op jit(solution)/shard_map/all_gather | solution.py:243
  401.5 43.8 %all-to-all-start.2 = ((bf16[128,4,1792]{2,0,1:T(8,128)(2,1)}), bf16[128,4,1792]{2,0,1:T(8,128)(2,1)S(1)}, u32[]{:S(2)}, u32[]{:S(2)}) async-start(bf16[128,4,1792]{2,0,1:T(8,128)(2,1)} %pad_maximum_fusion.6), calls=%async_computation.2 | async-start | bytes 3670016 | tf_op jit(solution)/shard_map/all_to_all | solution.py:236
  521.0 52.5 %all-to-all-start.3 = ((bf16[32,128,128]{1,2,0:T(8,128)(2,1)}), bf16[32,128,128]{1,2,0:T(8,128)(2,1)S(1)}, u32[]{:S(2)}, u32[]{:S(2)}) async-start(bf16[32,128,128]{1,2,0:T(8,128)(2,1)} %bitcast_select_fusion.2), calls=%async_computation.3 | async-start | bytes 2097152 | tf_op jit(solution)/shard_map/all_to_all | solution.py:151
  530.4 171.4 %reduce-scatter.9.cloned.1.call-start = ((), (), s32[]{:S(2)}) async-start(), calls=%async_computation.19 | async-start | bytes 7208960 | tf_op jit(solution)/shard_map/reduce_scatter | solution.py:85
  575.0 20.6 %copy-start.28 = (bf16[32,128,128]{2,1,0:T(8,128)(2,1)S(1)}, bf16[32,128,128]{2,1,0:T(8,128)(2,1)}, u32[]{:S(2)}) copy-start(bf16[32,128,128]{2,1,0:T(8,128)(2,1)} %copy-done.27) | copy-start | bytes 3145732
  628.9 10.2 %copy-start.55 = (f32[128]{0:T(128)S(1)}, f32[128]{0:T(128)}, u32[]{:S(2)}) copy-start(f32[128]{0:T(128)} %param.35) | copy-start | bytes 1540
  628.9 10.2 %copy-start.57 = (f32[128]{0:T(128)S(1)}, f32[128]{0:T(128)}, u32[]{:S(2)}) copy-start(f32[128]{0:T(128)} %param.34) | copy-start | bytes 1540
  628.9 10.2 %copy-start.42 = (f32[128,16]{0,1:T(8,128)S(1)}, f32[128,16]{0,1:T(8,128)}, u32[]{:S(2)}) copy-start(f32[128,16]{0,1:T(8,128)} %copy-done.41) | copy-start | bytes 24580
  628.9 13.8 %copy-start.46 = (f32[128,8]{0,1:T(8,128)S(1)}, f32[128,8]{0,1:T(8,128)}, u32[]{:S(2)}) copy-start(f32[128,8]{0,1:T(8,128)} %copy-done.45) | copy-start | bytes 12292
  628.9 55.0 %all-to-all-start.4 = ((bf16[32,128,384]{1,2,0:T(8,128)(2,1)}), bf16[32,128,384]{1,2,0:T(8,128)(2,1)S(1)}, u32[]{:S(2)}, u32[]{:S(2)}) async-start(bf16[32,128,384]{1,2,0:T(8,128)(2,1)} %pad_maximum_fusion.3), calls=%async_computation.4 | async-start | bytes 6291456 | tf_op jit(solution)/shard_map/all_to_all | solution.py:151
  638.7 108.7 %all-gather.23.cloned.1.call-start = ((), (), s32[]{:S(2)}) async-start(), calls=%async_computation.15 | async-start | bytes 5242880 | tf_op jit(solution)/shard_map/all_gather | solution.py:307
  639.1 45.0 %copy-start.34 = (f32[128,64]{0,1:T(8,128)S(1)}, f32[128,64]{0,1:T(8,128)}, u32[]{:S(2)}) copy-start(f32[128,64]{0,1:T(8,128)} %copy-done.33) | copy-start | bytes 98308
  639.1 45.0 %copy-start.36 = (f32[128,64]{0,1:T(8,128)S(1)}, f32[128,64]{0,1:T(8,128)}, u32[]{:S(2)}) copy-start(f32[128,64]{0,1:T(8,128)} %copy-done.35) | copy-start | bytes 98308
  691.5 7.1 copy-start.14
  698.6 7.2 copy-start.40
  698.6 7.2 copy-start.54
  701.1 75.2 %reduce-scatter.11.cloned.1.call-start = ((), (), s32[]{:S(2)}) async-start(), calls=%async_computation.20 | async-start | bytes 1802240 | tf_op jit(solution)/shard_map/reduce_scatter | solution.py:86
  701.9 107.5 %reduce-scatter.5.cloned.1.call-start = ((), (), s32[]{:S(2)}) async-start(), calls=%async_computation.16 | async-start | bytes 2703360 | tf_op jit(solution)/shard_map/reduce_scatter | solution.py:85
  705.8 6.7 copy-start.47
  752.5 109.7 %copy-start.2 = (f32[128,1024]{1,0:T(8,128)S(1)}, f32[128,1024]{1,0:T(8,128)}, u32[]{:S(2)}) copy-start(f32[128,1024]{1,0:T(8,128)} %copy-done.1) | copy-start | bytes 1572868
  752.5 109.7 %copy-start.18 = (bf16[128,3072]{1,0:T(8,128)(2,1)S(1)}, bf16[128,3072]{1,0:T(8,128)(2,1)}, u32[]{:S(2)}) copy-start(bf16[128,3072]{1,0:T(8,128)(2,1)} %get-tuple-element.88) | copy-start | bytes 2359300
  752.6 80.4 %reduce-scatter.7.cloned.1.call-start = ((), (), s32[]{:S(2)}) async-start(), calls=%async_computation.17 | async-start | bytes 675840 | tf_op jit(solution)/shard_map/reduce_scatter | solution.py:86
  776.4 33.1 %collective-permute-start.1 = (bf16[16,11264]{1,0:T(8,128)(2,1)}, bf16[16,11264]{1,0:T(8,128)(2,1)S(1)}, u32[]{:S(2)}, u32[]{:S(2)}) collective-permute-start(bf16[16,11264]{1,0:T(8,128)(2,1)} %reduce-scatter.11.cloned.1.call-done), channel_id=1, source_target_pairs={{0,64},{64,0},{1,65},{65,1},{2,66},{66,2},{3,67},{67,3},{4,68},{68... | collective-permute-start | bytes 1081352 | tf_op jit(solution)/shard_map/ppermute | solution.py:87
  809.4 52.8 %all-gather.27.cloned.1.call-start = ((), (), s32[]{:S(2)}) async-start(), calls=%async_computation.21 | async-start | bytes 1802240 | tf_op jit(solution)/shard_map/all_gather | solution.py:90
  811.3 84.2 %all-gather.25.cloned.1.call-start = ((), (), s32[]{:S(2)}) async-start(), calls=%async_computation.18 | async-start | bytes 2703360 | tf_op jit(solution)/shard_map/all_gather | solution.py:91
  833.0 6.7 collective-permute-start
  856.0 102.5 %all-gather.29.cloned.1.call-start = ((), (), s32[]{:S(2)}) async-start(), calls=%async_computation.22 | async-start | bytes 7208960 | tf_op jit(solution)/shard_map/all_gather | solution.py:91
  (35 other events, 128.0 us)
Sparse Core Ops, SparseCore 0:
  10.6 82.6 all-gather.10
  94.9 82.8 all-gather.12
  180.1 130.6 all-gather.14
  312.3 65.8 all-gather.16
  396.7 48.1 all-gather.18
  447.0 64.0 all-gather.20
  573.6 61.5 reduce-scatter.8
  701.3 46.1 all-gather.22
  749.9 26.4 reduce-scatter.10
  779.2 30.1 reduce-scatter.4
  811.9 21.0 reduce-scatter.6
  835.1 27.0 all-gather.26
  863.9 31.6 all-gather.24
  897.0 61.4 all-gather.28

commit v7 on v6

--- a/solution.py
+++ b/solution.py
@@ -77,7 +77,9 @@
 
 def gather_fsdp(values):
     across = lax.all_gather(values, "yl", axis=0, tiled=False)
-    both = lax.all_gather(across, "c", axis=1, tiled=False)
+    other = lax.ppermute(across, "c", [(0, 1), (1, 0)])
+    first_core = lax.axis_index("c") == 0
+    both = jnp.stack([jnp.where(first_core, across, other), jnp.where(first_core, other, across)], axis=1)
     return both.reshape((-1,) + values.shape[1:])
 
 
@@ -151,15 +153,11 @@
         return lax.all_to_all(values, CTX, split_axis=0, concat_axis=0, tiled=True)
 
     qkv_cols = (query_weight.shape[1], key_projection.shape[1], value_projection.shape[1])
-    full_qkv = lax.all_gather(
-        jnp.concatenate([query_weight, key_projection, value_projection], axis=1), FSDP, axis=0, tiled=True
-    )
-    full_output = lax.all_gather(output_weight, FSDP, axis=0, tiled=True)
+    full_qkv = gather_fsdp(jnp.concatenate([query_weight, key_projection, value_projection], axis=1))
+    full_output = gather_fsdp(output_weight)
     ff_cols = gate_weight.shape[1]
-    full_gate_up = lax.all_gather(
-        jnp.concatenate([gate_weight, up_weight], axis=1), FSDP, axis=0, tiled=True
-    )
-    full_down = lax.all_gather(down_weight, FSDP, axis=0, tiled=True)
+    full_gate_up = gather_fsdp(jnp.concatenate([gate_weight, up_weight], axis=1))
+    full_down = gather_fsdp(down_weight)
     input_f32 = layer_input[0].astype(jnp.float32)
     gained, first_normed, first_scale = rms_apply(input_f32, first_gain)
     attention_input = gained.astype(jnp.bfloat16)

time: 986 us -> 972 us (0.986)
  other arithmetic: 88.1 us -> 120 us
  blocking collectives: 59 us -> 27.6 us
  waiting for transfers between devices: 549 us -> 533 us
  matrix products: 140 us -> 129 us
  starting transfers between devices: 40.2 us -> 50.3 us
    all_to_all x3 -> x4, waiting for transfers between devices: 85.7 us -> 46.5 us  [exchange(): return lax.all_to_all(values, CTX, split_axis=0, concat_axis=0, tiled=True)]
    another operation x10 -> x18, other arithmetic: 7.59 us -> 40.3 us  [the longest x8 32.6 us: gather_fsdp(): jnp.stack([jnp.where(first_core, across, other), jnp.where(first_core, ot...]
    all_to_all x1 -> x0, blocking collectives: 31.4 us -> none  [exchange(): return lax.all_to_all(values, CTX, split_axis=0, concat_axis=0, tiled=True)]
    all_gather x4, waiting for transfers between devices: 190 us -> 214 us  [gather_fsdp(): across = lax.all_gather(values, 'yl', axis=0, tiled=False)]
    all_to_all x3 -> x4, starting transfers between devices: 28.6 us -> 38 us  [exchange(): return lax.all_to_all(values, CTX, split_axis=0, concat_axis=0, tiled=True)]
  transfers between devices with their start and end apart: 20 -> 25, of which waited for: 15 -> 16; matrix products, arithmetic and copies ran while one was open for 27% -> 29% of each run, Pallas kernels for 0% -> 0%
where the time goes in v7:
time: 972 us; the launch traced here: 961 us
  waiting for transfers between devices  533 us (55%)
  matrix products  129 us (13%)
  other arithmetic  120 us (12%)
  local copies, waits for them, and re-layouts  84.1 us (9%)
  starting transfers between devices  50.3 us (5%)
  blocking collectives  27.6 us (3%)
  between operations  16.8 us (2%)
    all_gather x4, waiting for transfers between devices, gather_fsdp(): across = lax.all_gather(values, 'yl', axis=0, tiled=False)  214 us
    all_gather x2, waiting for transfers between devices, reduce_ctx(): return lax.all_gather(part, 'z', axis=0, tiled=True).astype(jnp.float32)  83.6 us
    all_gather x1, waiting for transfers between devices, on_device(): gate_up_rows = lax.all_gather(gate_up_grad, FSDP, axis=0, tiled=True)  51.8 us
    all_to_all x4, waiting for transfers between devices, exchange(): return lax.all_to_all(values, CTX, split_axis=0, concat_axis=0, tiled=True)  46.5 us
    reduce_scatter x2, waiting for transfers between devices, reduce_ctx(): part = lax.psum_scatter(part, 'x', scatter_dimension=0, tiled=True)  45.4 us
    dot_general x5, matrix products, right_dot(): lax.dot_general(left_side, right_side, (((1,), (1,)), ((), ())), preferre...  42.2 us
    all_to_all x4, starting transfers between devices, exchange(): return lax.all_to_all(values, CTX, split_axis=0, concat_axis=0, tiled=True)  38 us
    dot_general x6, matrix products, left_dot(): lax.dot_general(left_side, right_side, (((0,), (0,)), ((), ())), preferre...  34.7 us
  transfers between devices with their start and end apart: 25, of which 16 were waited for; matrix products, arithmetic and copies ran while one was open for 29% of the time, Pallas kernels for 0%

profile of v7, /device:TPU:0, one launch (start us, length us, event | category | flops | bytes accessed | tf_op | source)
XLA Modules:
  0.0 960.9 jit_solution(7043047428078517606)
XLA Ops:
  12.0 60.4 %all-gather.27.cloned.1.call-done = bf16[512,4096]{1,0:T(8,128)(2,1)} async-done(((bf16[256,4096]{1,0:T(8,128)(2,1)}), bf16[512,4096]{1,0:T(8,128)(2,1)}) %all-gather.27.cloned.1.call-update) | async-done | bytes 4194320 | tf_op jit(solution)/shard_map/all_gather | solution.py:79
  75.7 4.2 collective-permute-done
  79.9 5.2 select_bitcast_fusion.3
  85.1 6.6 pad_maximum_fusion.1
  91.6 4.7 fusion.37
  116.6 9.4 all-to-all-start
  126.2 68.4 %all-gather.33.cloned.1.call-done = bf16[1536,1024]{1,0:T(8,128)(2,1)} async-done(((bf16[768,1024]{1,0:T(8,128)(2,1)}), bf16[1536,1024]{1,0:T(8,128)(2,1)}) %all-gather.33.cloned.1.call-update) | async-done | bytes 3145744 | tf_op jit(solution)/shard_map/all_gather | solution.py:79
  194.6 4.5 select_bitcast_fusion.7
  199.1 85.3 %all-gather.31.cloned.1.call-done = bf16[512,6144]{1,0:T(8,128)(2,1)} async-done(((bf16[256,6144]{1,0:T(8,128)(2,1)}), bf16[512,6144]{1,0:T(8,128)(2,1)}) %all-gather.31.cloned.1.call-update) | async-done | bytes 6291472 | tf_op jit(solution)/shard_map/all_gather | solution.py:79
  285.3 14.0 %fusion.48 = (f32[2048]{0:T(1024)S(1)}, f32[2048,4096]{1,0:T(8,128)}) fusion(s32[2048]{0:T(1024)S(1)} %dynamic_slice.18, s32[4096]{0:T(1024)S(1)} %add.153, bf16[2048,128]{1,0:T(8,128)(2,1)S(1)} %bitcast.269, bf16[4096,128]{1,0:T(8,128)(2,1)S(1)} %bitcast.263), kind=kOutput, calls=%fused_computation.176 | convolution fusion | flops 2181036032 | bytes 35160064 | tf_op jit(solution)/shard_map/qd,kd->qk/dot_general | solution.py:189
  299.3 15.1 %exponential_reduce_fusion = f32[2048]{0:T(1024)S(1)} fusion(f32[2048]{0:T(1024)S(1)} %get-tuple-element.120, f32[2048,4096]{1,0:T(8,128)} %get-tuple-element.121, s32[2048]{0:T(1024)S(1)} %dynamic_slice.18, s32[4096]{0:T(1024)S(1)} %add.153), kind=kLoop, calls=%fused_computation.6 | loop fusion | flops 41940992 | bytes 33595392 | tf_op jit(solution)/shard_map/reduce_sum | solution.py:196
  314.4 15.1 %fusion.54 = (bf16[2048,128]{1,0:T(8,128)(2,1)S(1)}, f32[2048,128]{1,0:T(8,128)}) fusion(bf16[4096,128]{1,0:T(8,128)(2,1)S(1)} %bitcast.265, f32[2048]{0:T(1024)S(1)} %log_add_fusion, f32[2048,4096]{1,0:T(8,128)} %get-tuple-element.121, s32[2048]{0:T(1024)S(1)} %dynamic_slice.18, s32[4096]{0:T(1024)S(1)} %add.153), kind=kOutput, calls=%fused_computation.182 | convolution fusion | flops 2189688832 | bytes 36208640 | tf_op jit(solution)/shard_map/dot_general | solution.py:198
  330.9 9.4 all-to-all-start.1
  340.8 4.1 pad_maximum_fusion.4
  350.6 8.2 all-to-all-done.1
  362.9 5.4 select_bitcast_fusion.1
  371.4 4.0 multiply_convert_fusion.2
  375.4 7.3 multiply_reduce_fusion.5
  391.0 3.8 all-to-all-start.2
  394.8 3.7 convolution_convert_fusion.2
  398.5 33.3 %all-to-all-done.2 = bf16[128,4,1792]{2,0,1:T(8,128)(2,1)S(1)} async-done(((bf16[128,4,1792]{2,0,1:T(8,128)(2,1)}), bf16[128,4,1792]{2,0,1:T(8,128)(2,1)S(1)}, u32[]{:S(2)}, u32[]{:S(2)}) %all-to-all-start.2) | async-done | bytes 1835040 | tf_op jit(solution)/shard_map/all_to_all | solution.py:234
  437.4 3.6 convolution_convert_fusion.3
  443.7 51.8 %all-gather.17.cloned.1.call-done = bf16[512,6144]{1,0:T(8,128)(2,1)} async-done(((bf16[128,6144]{1,0:T(8,128)(2,1)}), bf16[512,6144]{1,0:T(8,128)(2,1)}) %all-gather.17.cloned.1.call-update) | async-done | bytes 6291472 | tf_op jit(solution)/shard_map/all_gather | solution.py:241
  495.5 4.7 convolution_convert_fusion
  500.2 3.4 pad_maximum_fusion.3
  505.4 9.4 all-to-all-start.3
  515.0 20.3 %fusion.2 = bf16[4096,2048]{0,1:T(8,128)(2,1)} fusion(f32[2048,4096]{1,0:T(8,128)} %get-tuple-element.121, f32[2048]{0:T(1024)S(1)} %log_add_fusion, s32[4096]{0:T(1024)S(1)} %add.153, s32[2048]{0:T(1024)S(1)} %dynamic_slice.18), kind=kLoop, calls=%fused_computation.3 | loop fusion | flops 41943040 | bytes 50364416 | tf_op jit(solution)/shard_map/convert_element_type | solution.py:197
  535.3 22.5 %copy.254 = bf16[4096,2048]{1,0:T(8,128)(2,1)} copy(bf16[4096,2048]{0,1:T(8,128)(2,1)} %fusion.2) | data formatting | bytes 33554432 | tf_op jit(solution)/shard_map/dot_general | solution.py:67
  559.4 20.6 %multiply_convert_fusion = bf16[2048,4096]{1,0:T(8,128)(2,1)} fusion(f32[2048]{0:T(1024)S(1)} %multiply_reduce_fusion.2, f32[2048]{0:T(1024)S(1)} %log_add_fusion, bf16[2048,128]{1,0:T(8,128)(2,1)S(1)} %bitcast.228, bf16[4096,128]{1,0:T(8,128)(2,1)} %bitcast.266, f32[2048,4096]{1,0:T(8,128)} %get-tuple-element.121, s32[2048]{0:T(1024)S(1)} %dynamic_slice.18, ...), kind=kOutput, calls=%fused_computation.4 | convolution fusion | flops 2206203904 | bytes 51945472 | tf_op jit(solution)/shard_map/dot_general | solution.py:73
  580.0 8.7 fusion.8
  589.2 10.6 %fusion.7 = bf16[4096,128]{1,0:T(8,128)(2,1)S(1)} fusion(bf16[2048,4096]{1,0:T(8,128)(2,1)} %multiply_convert_fusion, bf16[2048,128]{1,0:T(8,128)(2,1)} %bitcast.270), kind=kOutput, calls=%fused_computation.20 | convolution fusion | flops 2148532224 | bytes 18350080 | tf_op jit(solution)/shard_map/dot_general | solution.py:67
  601.1 9.4 convolution_convert_fusion.5
  613.3 9.8 %all-to-all-start.4 = ((bf16[32,128,384]{1,2,0:T(8,128)(2,1)}), bf16[32,128,384]{1,2,0:T(8,128)(2,1)S(1)}, u32[]{:S(2)}, u32[]{:S(2)}) async-start(bf16[32,128,384]{1,2,0:T(8,128)(2,1)} %pad_maximum_fusion.7), calls=%async_computation.4 | async-start | bytes 6291456 | tf_op jit(solution)/shard_map/all_to_all | solution.py:153
  630.0 38.3 %all-to-all-done.4 = bf16[32,128,384]{1,2,0:T(8,128)(2,1)S(1)} async-done(((bf16[32,128,384]{1,2,0:T(8,128)(2,1)}), bf16[32,128,384]{1,2,0:T(8,128)(2,1)S(1)}, u32[]{:S(2)}, u32[]{:S(2)}) %all-to-all-start.4) | async-done | bytes 3145760 | tf_op jit(solution)/shard_map/all_to_all | solution.py:153
  690.2 6.6 fusion.33
  696.8 12.3 %all-reduce.5 = (f32[1024]{0:T(1024)S(1)}, f32[1024]{0:T(1024)S(1)}, bf16[128]{0:T(256)(128)(2,1)S(1)}, bf16[128]{0:T(256)(128)(2,1)S(1)}) all-reduce(f32[1024]{0:T(1024)S(1)} %get-tuple-element.71, f32[1024]{0:T(1024)S(1)} %copy-done.49, ...), channel_id=6, replica_groups=mesh['yh'=2,'x'=4,'z'=4,'yl'=2,'c'=2] {'yl','c'}, use_global_device_ids=true, to_apply=%region_14.15.clone | all-reduce | flops 2304 | bytes 17920
  718.7 13.1 %all-gather.19.cloned.1.call-done = bf16[512,4096]{1,0:T(8,128)(2,1)} async-done(((bf16[128,4096]{1,0:T(8,128)(2,1)}), bf16[512,4096]{1,0:T(8,128)(2,1)}) %all-gather.19.cloned.1.call-update) | async-done | bytes 4194320 | tf_op jit(solution)/shard_map/all_gather | solution.py:305
  731.8 3.6 convolution_convert_fusion.1
  737.0 23.8 %reduce-scatter.11.cloned.1.call-done = bf16[16,11264]{1,0:T(8,128)(2,1)} async-done(((bf16[64,11264]{1,0:T(8,128)(2,1)}), bf16[16,11264]{1,0:T(8,128)(2,1)}) %reduce-scatter.11.cloned.1.call-update) | async-done | bytes 360464 | tf_op jit(solution)/shard_map/reduce_scatter | solution.py:88
  763.8 30.0 %reduce-scatter.5.cloned.1.call-done = bf16[64,4224]{1,0:T(8,128)(2,1)} async-done(((bf16[256,4224]{1,0:T(8,128)(2,1)}), bf16[64,4224]{1,0:T(8,128)(2,1)}) %reduce-scatter.5.cloned.1.call-update) | async-done | bytes 540688 | tf_op jit(solution)/shard_map/reduce_scatter | solution.py:87
  795.8 21.7 %reduce-scatter.7.cloned.1.call-done = bf16[16,4224]{1,0:T(8,128)(2,1)} async-done(((bf16[64,4224]{1,0:T(8,128)(2,1)}), bf16[16,4224]{1,0:T(8,128)(2,1)}) %reduce-scatter.7.cloned.1.call-update) | async-done | bytes 135184 | tf_op jit(solution)/shard_map/reduce_scatter | solution.py:88
  820.4 3.7 collective-permute-done.4
  825.1 15.3 %all_gather.56 = bf16[64,4224]{1,0:T(8,128)(2,1)} all-gather(bf16[16,4224]{1,0:T(8,128)(2,1)S(1)} %add_convert_fusion.2), channel_id=1, replica_groups=mesh['yh'=2,'x'=4,'z'=4,'yl'=2,'c'=2] {'x'}, dimensions={0}, use_global_device_ids=true | all-gather | bytes 675840 | tf_op jit(solution)/shard_map/all_gather | solution.py:92
  841.0 5.6 all-gather.23.cloned.1.call-done
  846.7 4.5 fusion.11
  852.4 27.5 %all-gather.21.cloned.1.call-done = bf16[256,4224]{1,0:T(8,128)(2,1)} async-done(((bf16[64,4224]{1,0:T(8,128)(2,1)}), bf16[256,4224]{1,0:T(8,128)(2,1)}) %all-gather.21.cloned.1.call-update) | async-done | bytes 2162704 | tf_op jit(solution)/shard_map/all_gather | solution.py:93
  886.8 56.1 %all-gather.25.cloned.1.call-done = bf16[256,11264]{1,0:T(8,128)(2,1)} async-done(((bf16[64,11264]{1,0:T(8,128)(2,1)}), bf16[256,11264]{1,0:T(8,128)(2,1)}) %all-gather.25.cloned.1.call-update) | async-done | bytes 5767184 | tf_op jit(solution)/shard_map/all_gather | solution.py:93
  942.9 6.3 fusion.49
  (320 shorter events, 128.9 us)
Async XLA Ops:
  7.2 65.2 %copy-start.27 = (bf16[256,3072]{1,0:T(8,128)(2,1)S(1)}, bf16[256,3072]{1,0:T(8,128)(2,1)}, u32[]{:S(2)}) copy-start(bf16[256,3072]{1,0:T(8,128)(2,1)} %param.29) | copy-start | bytes 4718596
  7.2 65.2 %copy-start.26 = (bf16[256,3072]{1,0:T(8,128)(2,1)S(1)}, bf16[256,3072]{1,0:T(8,128)(2,1)}, u32[]{:S(2)}) copy-start(bf16[256,3072]{1,0:T(8,128)(2,1)} %param.30) | copy-start | bytes 4718596
  7.2 65.2 %all-gather.27.cloned.1.call-start = ((), (), s32[]{:S(2)}) async-start(), calls=%async_computation.19 | async-start | bytes 6291456 | tf_op jit(solution)/shard_map/all_gather | solution.py:79
  10.5 115.5 %all-gather.29.cloned.1.call-start = ((), (), s32[]{:S(2)}) async-start(), calls=%async_computation.20 | async-start | bytes 3145728 | tf_op jit(solution)/shard_map/all_gather | solution.py:79
  11.2 183.3 %all-gather.33.cloned.1.call-start = ((), (), s32[]{:S(2)}) async-start(), calls=%async_computation.22 | async-start | bytes 4718592 | tf_op jit(solution)/shard_map/all_gather | solution.py:79
  12.0 272.4 %all-gather.31.cloned.1.call-start = ((), (), s32[]{:S(2)}) async-start(), calls=%async_computation.21 | async-start | bytes 9437184 | tf_op jit(solution)/shard_map/all_gather | solution.py:79
  72.4 7.5 collective-permute-start
  75.5 16.2 %copy-start.54 = (f32[128]{0:T(128)}, f32[128]{0:T(128)S(1)}, u32[]{:S(2)}) copy-start(f32[128]{0:T(128)S(1)} %add_rsqrt_fusion.3) | copy-start | bytes 1540
  75.7 33.0 %copy-start.35 = (f32[128,64]{0,1:T(8,128)}, f32[128,64]{0,1:T(8,128)S(1)}, u32[]{:S(2)}) copy-start(f32[128,64]{0,1:T(8,128)S(1)} %get-tuple-element.114) | copy-start | bytes 98308
  75.7 33.0 %copy-start.37 = (f32[128,64]{0,1:T(8,128)}, f32[128,64]{0,1:T(8,128)S(1)}, u32[]{:S(2)}) copy-start(f32[128,64]{0,1:T(8,128)S(1)} %get-tuple-element.115) | copy-start | bytes 98308
  96.3 15.3 %copy-start.3 = (f32[128,4096]{1,0:T(8,128)}, f32[128,4096]{1,0:T(8,128)S(1)}, u32[]{:S(2)}) copy-start(f32[128,4096]{1,0:T(8,128)S(1)} %fusion.37) | copy-start | bytes 6291460
  116.6 168.1 %all-to-all-start = ((bf16[32,128,384]{2,1,0:T(8,128)(2,1)}), bf16[32,128,384]{2,1,0:T(8,128)(2,1)S(1)}, u32[]{:S(2)}, u32[]{:S(2)}) async-start(bf16[32,128,384]{2,1,0:T(8,128)(2,1)} %pad_maximum_fusion.5), calls=%async_computation | async-start | bytes 6291456 | tf_op jit(solution)/shard_map/all_to_all | solution.py:153
  126.0 68.5 %collective-permute-start.1 = (bf16[2,512,1024]{2,1,0:T(8,128)(2,1)}, bf16[2,512,1024]{2,1,0:T(8,128)(2,1)}, u32[]{:S(2)}, u32[]{:S(2)}) collective-permute-start(bf16[2,512,1024]{2,1,0:T(8,128)(2,1)} %bitcast.257), channel_id=1, source_target_pairs={{0,1},{1,0},{2,3},{3,2},{4,5},{5,4},{6,7},{7,6},{8,9},{9,8},{10,11... | collective-permute-start | bytes 6291464 | tf_op jit(solution)/shard_map/ppermute | solution.py:80
  194.5 150.4 %collective-permute-start.3 = (bf16[2,768,1024]{2,1,0:T(8,128)(2,1)}, bf16[2,768,1024]{2,1,0:T(8,128)(2,1)}, u32[]{:S(2)}, u32[]{:S(2)}) collective-permute-start(bf16[2,768,1024]{2,1,0:T(8,128)(2,1)} %bitcast.243), channel_id=1, source_target_pairs={{0,1},{1,0},{2,3},{3,2},{4,5},{5,4},{6,7},{7,6},{8,9},{9,8},{10,11... | collective-permute-start | bytes 9437192 | tf_op jit(solution)/shard_map/ppermute | solution.py:80
  284.4 78.4 %collective-permute-start.2 = (bf16[2,256,6144]{2,1,0:T(8,128)(2,1)}, bf16[2,256,6144]{2,1,0:T(8,128)(2,1)}, u32[]{:S(2)}, u32[]{:S(2)}) collective-permute-start(bf16[2,256,6144]{2,1,0:T(8,128)(2,1)} %bitcast.226), channel_id=1, source_target_pairs={{0,1},{1,0},{2,3},{3,2},{4,5},{5,4},{6,7},{7,6},{8,9},{9,8},{10,11... | collective-permute-start | bytes 18874376 | tf_op jit(solution)/shard_map/ppermute | solution.py:80
  285.2 14.0 %copy-start.29 = (bf16[32,128,128]{2,1,0:T(8,128)(2,1)}, bf16[32,128,128]{2,1,0:T(8,128)(2,1)S(1)}, u32[]{:S(2)}) copy-start(bf16[32,128,128]{2,1,0:T(8,128)(2,1)S(1)} %get-tuple-element.97) | copy-start | bytes 3145732
  285.2 29.1 %copy-start.31 = (bf16[32,128,128]{2,1,0:T(8,128)(2,1)}, bf16[32,128,128]{2,1,0:T(8,128)(2,1)S(1)}, u32[]{:S(2)}) copy-start(bf16[32,128,128]{2,1,0:T(8,128)(2,1)S(1)} %get-tuple-element.98) | copy-start | bytes 3145732
  285.3 14.0 %copy-start.39 = (bf16[16,128,128]{2,1,0:T(8,128)(2,1)}, bf16[16,128,128]{2,1,0:T(8,128)(2,1)S(1)}, u32[]{:S(2)}) copy-start(bf16[16,128,128]{2,1,0:T(8,128)(2,1)S(1)} %constant_dynamic-slice_fusion.2) | copy-start | bytes 1572868
  314.4 15.4 %copy-start.53 = (pred[32]{0:T(512)(128)(4,1)S(1)}, pred[32]{0:T(512)(128)(4,1)}, u32[]{:S(2)}) copy-start(pred[32]{0:T(512)(128)(4,1)} %broadcast_in_dim.119) | copy-start | bytes 100
  329.5 11.3 %copy-start.7 = (bf16[2,1,512,1024]{3,2,1,0:T(8,128)(2,1)S(1)}, bf16[2,1,512,1024]{3,2,1,0:T(8,128)(2,1)}, u32[]{:S(2)}) copy-start(bf16[2,1,512,1024]{3,2,1,0:T(8,128)(2,1)} %get-tuple-element.92) | copy-start | bytes 6291460
  330.9 27.9 %all-to-all-start.1 = ((bf16[32,128,128]{1,2,0:T(8,128)(2,1)}), bf16[32,128,128]{1,2,0:T(8,128)(2,1)S(1)}, u32[]{:S(2)}, u32[]{:S(2)}) async-start(bf16[32,128,128]{1,2,0:T(8,128)(2,1)} %bitcast_select_fusion.3), calls=%async_computation.1 | async-start | bytes 2097152 | tf_op jit(solution)/shard_map/all_to_all | solution.py:153
  340.3 91.5 %all-gather.15.cloned.1.call-start = ((), (), s32[]{:S(2)}) async-start(), calls=%async_computation.9 | async-start | bytes 2621440 | tf_op jit(solution)/shard_map/all_gather | solution.py:242
  350.6 11.5 %copy-start.45 = (f32[1024]{0:T(1024)S(1)}, f32[1024]{0:T(1024)}, u32[]{:S(2)}) copy-start(f32[1024]{0:T(1024)} %param.33) | copy-start | bytes 12292
  362.1 20.6 %copy-start.50 = (f32[128]{0:T(128)}, f32[128]{0:T(128)S(1)}, u32[]{:S(2)}) copy-start(f32[128]{0:T(128)S(1)} %add_rsqrt_fusion.2) | copy-start | bytes 1540
  362.9 8.5 slice-start
  386.1 109.4 %all-gather.17.cloned.1.call-start = ((), (), s32[]{:S(2)}) async-start(), calls=%async_computation.10 | async-start | bytes 7864320 | tf_op jit(solution)/shard_map/all_gather | solution.py:241
  391.0 40.8 %all-to-all-start.2 = ((bf16[128,4,1792]{2,0,1:T(8,128)(2,1)}), bf16[128,4,1792]{2,0,1:T(8,128)(2,1)S(1)}, u32[]{:S(2)}, u32[]{:S(2)}) async-start(bf16[128,4,1792]{2,0,1:T(8,128)(2,1)} %pad_maximum_fusion.10), calls=%async_computation.2 | async-start | bytes 3670016 | tf_op jit(solution)/shard_map/all_to_all | solution.py:234
  505.4 52.5 %all-to-all-start.3 = ((bf16[32,128,128]{1,2,0:T(8,128)(2,1)}), bf16[32,128,128]{1,2,0:T(8,128)(2,1)S(1)}, u32[]{:S(2)}, u32[]{:S(2)}) async-start(bf16[32,128,128]{1,2,0:T(8,128)(2,1)} %bitcast_select_fusion.2), calls=%async_computation.3 | async-start | bytes 2097152 | tf_op jit(solution)/shard_map/all_to_all | solution.py:153
  514.8 171.4 %reduce-scatter.9.cloned.1.call-start = ((), (), s32[]{:S(2)}) async-start(), calls=%async_computation.15 | async-start | bytes 7208960 | tf_op jit(solution)/shard_map/reduce_scatter | solution.py:87
  559.4 20.6 %copy-start.30 = (bf16[32,128,128]{2,1,0:T(8,128)(2,1)S(1)}, bf16[32,128,128]{2,1,0:T(8,128)(2,1)}, u32[]{:S(2)}) copy-start(bf16[32,128,128]{2,1,0:T(8,128)(2,1)} %copy-done.29) | copy-start | bytes 3145732
  613.3 10.2 %copy-start.57 = (f32[128]{0:T(128)S(1)}, f32[128]{0:T(128)}, u32[]{:S(2)}) copy-start(f32[128]{0:T(128)} %param.35) | copy-start | bytes 1540
  613.3 10.2 %copy-start.59 = (f32[128]{0:T(128)S(1)}, f32[128]{0:T(128)}, u32[]{:S(2)}) copy-start(f32[128]{0:T(128)} %param.34) | copy-start | bytes 1540
  613.3 10.2 %copy-start.44 = (f32[128,16]{0,1:T(8,128)S(1)}, f32[128,16]{0,1:T(8,128)}, u32[]{:S(2)}) copy-start(f32[128,16]{0,1:T(8,128)} %copy-done.43) | copy-start | bytes 24580
  613.3 13.8 %copy-start.48 = (f32[128,8]{0,1:T(8,128)S(1)}, f32[128,8]{0,1:T(8,128)}, u32[]{:S(2)}) copy-start(f32[128,8]{0,1:T(8,128)} %copy-done.47) | copy-start | bytes 12292
  613.3 55.0 %all-to-all-start.4 = ((bf16[32,128,384]{1,2,0:T(8,128)(2,1)}), bf16[32,128,384]{1,2,0:T(8,128)(2,1)S(1)}, u32[]{:S(2)}, u32[]{:S(2)}) async-start(bf16[32,128,384]{1,2,0:T(8,128)(2,1)} %pad_maximum_fusion.7), calls=%async_computation.4 | async-start | bytes 6291456 | tf_op jit(solution)/shard_map/all_to_all | solution.py:153
  623.1 108.7 %all-gather.19.cloned.1.call-start = ((), (), s32[]{:S(2)}) async-start(), calls=%async_computation.11 | async-start | bytes 5242880 | tf_op jit(solution)/shard_map/all_gather | solution.py:305
  623.5 45.0 %copy-start.36 = (f32[128,64]{0,1:T(8,128)S(1)}, f32[128,64]{0,1:T(8,128)}, u32[]{:S(2)}) copy-start(f32[128,64]{0,1:T(8,128)} %copy-done.35) | copy-start | bytes 98308
  623.5 45.0 %copy-start.38 = (f32[128,64]{0,1:T(8,128)S(1)}, f32[128,64]{0,1:T(8,128)}, u32[]{:S(2)}) copy-start(f32[128,64]{0,1:T(8,128)} %copy-done.37) | copy-start | bytes 98308
  685.5 75.2 %reduce-scatter.11.cloned.1.call-start = ((), (), s32[]{:S(2)}) async-start(), calls=%async_computation.16 | async-start | bytes 1802240 | tf_op jit(solution)/shard_map/reduce_scatter | solution.py:88
  686.3 107.5 %reduce-scatter.5.cloned.1.call-start = ((), (), s32[]{:S(2)}) async-start(), calls=%async_computation.12 | async-start | bytes 2703360 | tf_op jit(solution)/shard_map/reduce_scatter | solution.py:87
  736.9 109.7 %copy-start.1 = (f32[128,1024]{1,0:T(8,128)S(1)}, f32[128,1024]{1,0:T(8,128)}, u32[]{:S(2)}) copy-start(f32[128,1024]{1,0:T(8,128)} %copy-done) | copy-start | bytes 1572868
  736.9 109.7 %copy-start.19 = (bf16[128,3072]{1,0:T(8,128)(2,1)S(1)}, bf16[128,3072]{1,0:T(8,128)(2,1)}, u32[]{:S(2)}) copy-start(bf16[128,3072]{1,0:T(8,128)(2,1)} %get-tuple-element.96) | copy-start | bytes 2359300
  737.0 80.5 %reduce-scatter.7.cloned.1.call-start = ((), (), s32[]{:S(2)}) async-start(), calls=%async_computation.13 | async-start | bytes 675840 | tf_op jit(solution)/shard_map/reduce_scatter | solution.py:88
  760.8 33.1 %collective-permute-start.5 = (bf16[16,11264]{1,0:T(8,128)(2,1)}, bf16[16,11264]{1,0:T(8,128)(2,1)S(1)}, u32[]{:S(2)}, u32[]{:S(2)}) collective-permute-start(bf16[16,11264]{1,0:T(8,128)(2,1)} %reduce-scatter.11.cloned.1.call-done), channel_id=1, source_target_pairs={{0,64},{64,0},{1,65},{65,1},{2,66},{66,2},{3,67},{67,3},{4,68},{68... | collective-permute-start | bytes 1081352 | tf_op jit(solution)/shard_map/ppermute | solution.py:89
  793.8 52.8 %all-gather.23.cloned.1.call-start = ((), (), s32[]{:S(2)}) async-start(), calls=%async_computation.17 | async-start | bytes 1802240 | tf_op jit(solution)/shard_map/all_gather | solution.py:92
  795.7 84.2 %all-gather.21.cloned.1.call-start = ((), (), s32[]{:S(2)}) async-start(), calls=%async_computation.14 | async-start | bytes 2703360 | tf_op jit(solution)/shard_map/all_gather | solution.py:93
  817.4 6.7 collective-permute-start.4
  840.4 102.5 %all-gather.25.cloned.1.call-start = ((), (), s32[]{:S(2)}) async-start(), calls=%async_computation.18 | async-start | bytes 7208960 | tf_op jit(solution)/shard_map/all_gather | solution.py:93
  (44 other events, 180.6 us)
Sparse Core Ops, SparseCore 0:
  10.6 61.7 all-gather.26
  74.0 36.6 all-gather.28
  112.3 82.1 all-gather.32
  196.6 87.7 all-gather.30
  386.2 39.0 all-gather.14
  427.3 68.0 all-gather.16
  558.0 61.5 reduce-scatter.8
  685.7 46.1 all-gather.18
  734.3 26.4 reduce-scatter.10
  763.6 30.1 reduce-scatter.4
  796.3 21.0 reduce-scatter.6
  819.5 27.0 all-gather.22
  848.3 31.6 all-gather.20
  881.4 61.4 all-gather.24

commit v8 on v7

--- a/solution.py
+++ b/solution.py
@@ -75,12 +75,19 @@
     )
 
 
-def gather_fsdp(values):
-    across = lax.all_gather(values, "yl", axis=0, tiled=False)
+def gather_across(values):
+    return lax.all_gather(values, "yl", axis=0, tiled=False)
+
+
+def gather_cores(across, shard_shape):
     other = lax.ppermute(across, "c", [(0, 1), (1, 0)])
     first_core = lax.axis_index("c") == 0
     both = jnp.stack([jnp.where(first_core, across, other), jnp.where(first_core, other, across)], axis=1)
-    return both.reshape((-1,) + values.shape[1:])
+    return both.reshape((-1,) + shard_shape[1:])
+
+
+def gather_fsdp(values):
+    return gather_cores(gather_across(values), values.shape)
 
 
 def reduce_ctx(packed):
@@ -154,10 +161,11 @@
 
     qkv_cols = (query_weight.shape[1], key_projection.shape[1], value_projection.shape[1])
     full_qkv = gather_fsdp(jnp.concatenate([query_weight, key_projection, value_projection], axis=1))
-    full_output = gather_fsdp(output_weight)
+    across_output = gather_across(output_weight)
     ff_cols = gate_weight.shape[1]
-    full_gate_up = gather_fsdp(jnp.concatenate([gate_weight, up_weight], axis=1))
-    full_down = gather_fsdp(down_weight)
+    gate_up_weight = jnp.concatenate([gate_weight, up_weight], axis=1)
+    across_gate_up = gather_across(gate_up_weight)
+    across_down = gather_across(down_weight)
     input_f32 = layer_input[0].astype(jnp.float32)
     gained, first_normed, first_scale = rms_apply(input_f32, first_gain)
     attention_input = gained.astype(jnp.bfloat16)
@@ -196,6 +204,12 @@
     log_total = row_max + jnp.log(jnp.sum(jnp.exp(raw_scores - row_max), axis=-1, keepdims=True))
     weights_b = jnp.exp(raw_scores - log_total).astype(jnp.bfloat16)
     head_mixed = jnp.dot(weights_b, head_value, preferred_element_type=jnp.float32)
+    head_mixed, across_output, across_gate_up, across_down = lax.optimization_barrier(
+        (head_mixed, across_output, across_gate_up, across_down)
+    )
+    full_output = gather_cores(across_output, output_weight.shape)
+    full_gate_up = gather_cores(across_gate_up, gate_up_weight.shape)
+    full_down = gather_cores(across_down, down_weight.shape)
     mixed_b = own_heads(exchange(from_heads(head_mixed.astype(jnp.bfloat16)))).reshape(
         local_rows, HQ * HEAD_SIZE
     )

time: 972 us -> 933 us (0.960)
  waiting for transfers between devices: 533 us -> 483 us
  blocking collectives: 27.6 us -> 55.6 us
  other arithmetic: 120 us -> 109 us
    all_gather x4, waiting for transfers between devices: 214 us -> 128 us  [gather_across(): return lax.all_gather(values, 'yl', axis=0, tiled=False)]
    all_to_all x4 -> x3, waiting for transfers between devices: 46.5 us -> 81.1 us  [exchange(): return lax.all_to_all(values, CTX, split_axis=0, concat_axis=0, tiled=True)]
    all_to_all x0 -> x1, blocking collectives: none -> 28.3 us  [exchange(): return lax.all_to_all(values, CTX, split_axis=0, concat_axis=0, tiled=True)]
    another operation x18, other arithmetic: 40.3 us -> 29.3 us  [the longest x8 22.4 us: gather_cores(): jnp.stack([jnp.where(first_core, across, other), jnp.where(first_core, ot...]
    all_to_all x4 -> x3, starting transfers between devices: 38 us -> 28.6 us  [exchange(): return lax.all_to_all(values, CTX, split_axis=0, concat_axis=0, tiled=True)]
  transfers between devices with their start and end apart: 25 -> 24, of which waited for: 16 -> 15; matrix products, arithmetic and copies ran while one was open for 29% -> 29% of each run, Pallas kernels for 0% -> 0%
where the time goes in v8:
time: 933 us; the launch traced here: 923 us
  waiting for transfers between devices  483 us (52%)
  matrix products  127 us (14%)
  other arithmetic  109 us (12%)
  local copies, waits for them, and re-layouts  91.5 us (10%)
  blocking collectives  55.6 us (6%)
  starting transfers between devices  40.9 us (4%)
  between operations  16.8 us (2%)
    all_gather x4, waiting for transfers between devices, gather_across(): return lax.all_gather(values, 'yl', axis=0, tiled=False)  128 us
    all_gather x2, waiting for transfers between devices, reduce_ctx(): return lax.all_gather(part, 'z', axis=0, tiled=True).astype(jnp.float32)  83.6 us
    all_to_all x3, waiting for transfers between devices, exchange(): return lax.all_to_all(values, CTX, split_axis=0, concat_axis=0, tiled=True)  81.1 us
    all_gather x1, waiting for transfers between devices, on_device(): gate_up_rows = lax.all_gather(gate_up_grad, FSDP, axis=0, tiled=True)  51.8 us
    reduce_scatter x2, waiting for transfers between devices, reduce_ctx(): part = lax.psum_scatter(part, 'x', scatter_dimension=0, tiled=True)  45.4 us
    dot_general x5, matrix products, right_dot(): lax.dot_general(left_side, right_side, (((1,), (1,)), ((), ())), preferre...  42.2 us
    dot_general x6, matrix products, left_dot(): lax.dot_general(left_side, right_side, (((0,), (0,)), ((), ())), preferre...  34.7 us
    all_to_all x1, waiting for transfers between devices, on_device(): lax.all_to_all(stacked, FSDP, split_axis=1, concat_axis=0, tiled=True)  33.2 us
  transfers between devices with their start and end apart: 24, of which 15 were waited for; matrix products, arithmetic and copies ran while one was open for 29% of the time, Pallas kernels for 0%

profile of v8, /device:TPU:0, one launch (start us, length us, event | category | flops | bytes accessed | tf_op | source)
XLA Modules:
  0.0 923.0 jit_solution(16245383733965457491)
XLA Ops:
  7.2 3.1 pad_maximum_fusion.9
  10.4 61.8 %all-gather.27.cloned.1.call-done = bf16[512,4096]{1,0:T(8,128)(2,1)} async-done(((bf16[256,4096]{1,0:T(8,128)(2,1)}), bf16[512,4096]{1,0:T(8,128)(2,1)}) %all-gather.27.cloned.1.call-update) | async-done | bytes 4194320 | tf_op jit(solution)/shard_map/all_gather | solution.py:79
  74.4 5.4 collective-permute-done
  79.8 5.2 select_bitcast_fusion.3
  84.9 6.5 pad_maximum_fusion.1
  91.5 4.7 fusion.37
  113.9 9.4 %all-to-all-start = ((bf16[32,128,384]{2,1,0:T(8,128)(2,1)}), bf16[32,128,384]{2,1,0:T(8,128)(2,1)S(1)}, u32[]{:S(2)}, u32[]{:S(2)}) async-start(bf16[32,128,384]{2,1,0:T(8,128)(2,1)} %pad_maximum_fusion.5), calls=%async_computation | async-start | bytes 6291456 | tf_op jit(solution)/shard_map/all_to_all | solution.py:160
  123.4 4.2 pad_maximum_fusion.6
  127.9 42.6 %all-to-all-done = bf16[32,128,384]{2,1,0:T(8,128)(2,1)S(1)} async-done(((bf16[32,128,384]{2,1,0:T(8,128)(2,1)}), bf16[32,128,384]{2,1,0:T(8,128)(2,1)S(1)}, u32[]{:S(2)}, u32[]{:S(2)}) %all-to-all-start) | async-done | bytes 3145760 | tf_op jit(solution)/shard_map/all_to_all | solution.py:160
  171.1 14.0 %fusion.48 = (f32[2048]{0:T(1024)S(1)}, f32[2048,4096]{1,0:T(8,128)}) fusion(s32[2048]{0:T(1024)S(1)} %dynamic_slice.18, s32[4096]{0:T(1024)S(1)} %add.153, bf16[2048,128]{1,0:T(8,128)(2,1)S(1)} %bitcast.269, bf16[4096,128]{1,0:T(8,128)(2,1)S(1)} %bitcast.264), kind=kOutput, calls=%fused_computation.176 | convolution fusion | flops 2181036032 | bytes 35160064 | tf_op jit(solution)/shard_map/qd,kd->qk/dot_general | solution.py:197
  185.1 15.1 %exponential_reduce_fusion = f32[2048]{0:T(1024)S(1)} fusion(f32[2048]{0:T(1024)S(1)} %get-tuple-element.128, f32[2048,4096]{1,0:T(8,128)} %get-tuple-element.129, s32[2048]{0:T(1024)S(1)} %dynamic_slice.18, s32[4096]{0:T(1024)S(1)} %add.153), kind=kLoop, calls=%fused_computation.6 | loop fusion | flops 41940992 | bytes 33595392 | tf_op jit(solution)/shard_map/reduce_sum | solution.py:204
  200.2 15.6 %fusion.4 = f32[2048,128]{1,0:T(8,128)S(1)} fusion(bf16[4096,128]{1,0:T(8,128)(2,1)S(1)} %bitcast.266, f32[2048]{0:T(1024)S(1)} %log_add_fusion, f32[2048,4096]{1,0:T(8,128)} %get-tuple-element.129, s32[4096]{0:T(1024)S(1)} %add.153, s32[2048]{0:T(1024)S(1)} %dynamic_slice.18), kind=kOutput, calls=%fused_computation.9 | convolution fusion | flops 2189426688 | bytes 35684352 | tf_op jit(solution)/shard_map/dot_general | solution.py:206
  215.9 66.5 %all-gather.31.cloned.1.call-done = bf16[512,6144]{1,0:T(8,128)(2,1)} async-done(((bf16[256,6144]{1,0:T(8,128)(2,1)}), bf16[512,6144]{1,0:T(8,128)(2,1)}) %all-gather.31.cloned.1.call-update) | async-done | bytes 6291472 | tf_op jit(solution)/shard_map/all_gather | solution.py:79
  283.4 28.3 %all_to_all.35 = bf16[32,128,128]{1,2,0:T(8,128)(2,1)S(1)} all-to-all(bf16[32,128,128]{1,2,0:T(8,128)(2,1)S(1)} %bitcast_select_fusion.3), channel_id=1, replica_groups=mesh['yh'=2,'x'=4,'z'=4,'yl'=2,'c'=2] {'yh','x','z'}, dimensions={0} | all-to-all | bytes 2097152 | tf_op jit(solution)/shard_map/all_to_all | solution.py:160
  322.0 3.2 slice-done
  326.5 3.8 select_bitcast_fusion.1
  333.5 4.0 multiply_convert_fusion.2
  337.5 7.2 multiply_reduce_fusion.5
  353.1 3.8 all-to-all-start.2
  356.9 3.7 convolution_convert_fusion.2
  360.6 33.2 %all-to-all-done.2 = bf16[128,4,1792]{2,0,1:T(8,128)(2,1)S(1)} async-done(((bf16[128,4,1792]{2,0,1:T(8,128)(2,1)}), bf16[128,4,1792]{2,0,1:T(8,128)(2,1)S(1)}, u32[]{:S(2)}, u32[]{:S(2)}) %all-to-all-start.2) | async-done | bytes 1835040 | tf_op jit(solution)/shard_map/all_to_all | solution.py:248
  399.5 3.6 convolution_convert_fusion.3
  405.8 51.8 %all-gather.17.cloned.1.call-done = bf16[512,6144]{1,0:T(8,128)(2,1)} async-done(((bf16[128,6144]{1,0:T(8,128)(2,1)}), bf16[512,6144]{1,0:T(8,128)(2,1)}) %all-gather.17.cloned.1.call-update) | async-done | bytes 6291472 | tf_op jit(solution)/shard_map/all_gather | solution.py:255
  457.6 4.7 convolution_convert_fusion
  462.3 3.4 pad_maximum_fusion.3
  467.5 9.4 %all-to-all-start.3 = ((bf16[32,128,128]{1,2,0:T(8,128)(2,1)}), bf16[32,128,128]{1,2,0:T(8,128)(2,1)S(1)}, u32[]{:S(2)}, u32[]{:S(2)}) async-start(bf16[32,128,128]{1,2,0:T(8,128)(2,1)} %bitcast_select_fusion.2), calls=%async_computation.3 | async-start | bytes 2097152 | tf_op jit(solution)/shard_map/all_to_all | solution.py:160
  477.1 20.3 %fusion.2 = bf16[4096,2048]{0,1:T(8,128)(2,1)} fusion(f32[2048,4096]{1,0:T(8,128)} %get-tuple-element.129, f32[2048]{0:T(1024)S(1)} %log_add_fusion, s32[4096]{0:T(1024)S(1)} %add.153, s32[2048]{0:T(1024)S(1)} %dynamic_slice.18), kind=kLoop, calls=%fused_computation.3 | loop fusion | flops 41943040 | bytes 50364416 | tf_op jit(solution)/shard_map/convert_element_type | solution.py:205
  497.4 22.5 %copy.254 = bf16[4096,2048]{1,0:T(8,128)(2,1)} copy(bf16[4096,2048]{0,1:T(8,128)(2,1)} %fusion.2) | data formatting | bytes 33554432 | tf_op jit(solution)/shard_map/dot_general | solution.py:67
  521.5 20.6 %multiply_convert_fusion = bf16[2048,4096]{1,0:T(8,128)(2,1)} fusion(f32[2048]{0:T(1024)S(1)} %multiply_reduce_fusion.2, f32[2048]{0:T(1024)S(1)} %log_add_fusion, bf16[2048,128]{1,0:T(8,128)(2,1)S(1)} %bitcast.228, bf16[4096,128]{1,0:T(8,128)(2,1)} %bitcast.267, f32[2048,4096]{1,0:T(8,128)} %get-tuple-element.129, s32[2048]{0:T(1024)S(1)} %dynamic_slice.18, ...), kind=kOutput, calls=%fused_computation.4 | convolution fusion | flops 2206203904 | bytes 51945472 | tf_op jit(solution)/shard_map/dot_general | solution.py:73
  542.1 8.7 fusion.8
  551.3 10.6 %fusion.7 = bf16[4096,128]{1,0:T(8,128)(2,1)S(1)} fusion(bf16[2048,4096]{1,0:T(8,128)(2,1)} %multiply_convert_fusion, bf16[2048,128]{1,0:T(8,128)(2,1)} %bitcast.270), kind=kOutput, calls=%fused_computation.20 | convolution fusion | flops 2148532224 | bytes 18350080 | tf_op jit(solution)/shard_map/dot_general | solution.py:67
  563.1 9.4 %convolution_convert_fusion.5 = bf16[32,128,128]{1,2,0:T(8,128)(2,1)S(1)} fusion(bf16[32,128,2048]{2,1,0:T(8,128)(2,1)} %bitcast.213, bf16[2048,128,1]{1,0,2:T(8,128)(2,1)S(1)} %bitcast.229), kind=kOutput, calls=%fused_computation.47 | convolution fusion | flops 2148007936 | bytes 18350080 | tf_op jit(solution)/shard_map/dot_general | solution.py:67
  575.3 9.8 %all-to-all-start.4 = ((bf16[32,128,384]{1,2,0:T(8,128)(2,1)}), bf16[32,128,384]{1,2,0:T(8,128)(2,1)S(1)}, u32[]{:S(2)}, u32[]{:S(2)}) async-start(bf16[32,128,384]{1,2,0:T(8,128)(2,1)} %pad_maximum_fusion.7), calls=%async_computation.4 | async-start | bytes 6291456 | tf_op jit(solution)/shard_map/all_to_all | solution.py:160
  592.1 38.5 %all-to-all-done.4 = bf16[32,128,384]{1,2,0:T(8,128)(2,1)S(1)} async-done(((bf16[32,128,384]{1,2,0:T(8,128)(2,1)}), bf16[32,128,384]{1,2,0:T(8,128)(2,1)S(1)}, u32[]{:S(2)}, u32[]{:S(2)}) %all-to-all-start.4) | async-done | bytes 3145760 | tf_op jit(solution)/shard_map/all_to_all | solution.py:160
  652.5 6.6 fusion.33
  659.2 12.0 %all-reduce.5 = (f32[1024]{0:T(1024)S(1)}, f32[1024]{0:T(1024)S(1)}, bf16[128]{0:T(256)(128)(2,1)S(1)}, bf16[128]{0:T(256)(128)(2,1)S(1)}) all-reduce(f32[1024]{0:T(1024)S(1)} %get-tuple-element.79, f32[1024]{0:T(1024)S(1)} %copy-done.51, ...), channel_id=6, replica_groups=mesh['yh'=2,'x'=4,'z'=4,'yl'=2,'c'=2] {'yl','c'}, use_global_device_ids=true, to_apply=%region_14.15.clone | all-reduce | flops 2304 | bytes 17920
  680.6 13.4 %all-gather.19.cloned.1.call-done = bf16[512,4096]{1,0:T(8,128)(2,1)} async-done(((bf16[128,4096]{1,0:T(8,128)(2,1)}), bf16[512,4096]{1,0:T(8,128)(2,1)}) %all-gather.19.cloned.1.call-update) | async-done | bytes 4194320 | tf_op jit(solution)/shard_map/all_gather | solution.py:319
  694.0 3.6 convolution_convert_fusion.1
  699.2 23.7 %reduce-scatter.11.cloned.1.call-done = bf16[16,11264]{1,0:T(8,128)(2,1)} async-done(((bf16[64,11264]{1,0:T(8,128)(2,1)}), bf16[16,11264]{1,0:T(8,128)(2,1)}) %reduce-scatter.11.cloned.1.call-update) | async-done | bytes 360464 | tf_op jit(solution)/shard_map/reduce_scatter | solution.py:95
  725.9 30.0 %reduce-scatter.5.cloned.1.call-done = bf16[64,4224]{1,0:T(8,128)(2,1)} async-done(((bf16[256,4224]{1,0:T(8,128)(2,1)}), bf16[64,4224]{1,0:T(8,128)(2,1)}) %reduce-scatter.5.cloned.1.call-update) | async-done | bytes 540688 | tf_op jit(solution)/shard_map/reduce_scatter | solution.py:94
  757.9 21.6 %reduce-scatter.7.cloned.1.call-done = bf16[16,4224]{1,0:T(8,128)(2,1)} async-done(((bf16[64,4224]{1,0:T(8,128)(2,1)}), bf16[16,4224]{1,0:T(8,128)(2,1)}) %reduce-scatter.7.cloned.1.call-update) | async-done | bytes 135184 | tf_op jit(solution)/shard_map/reduce_scatter | solution.py:95
  782.6 3.7 collective-permute-done.4
  787.2 15.3 %all_gather.56 = bf16[64,4224]{1,0:T(8,128)(2,1)} all-gather(bf16[16,4224]{1,0:T(8,128)(2,1)S(1)} %add_convert_fusion.2), channel_id=1, replica_groups=mesh['yh'=2,'x'=4,'z'=4,'yl'=2,'c'=2] {'x'}, dimensions={0}, use_global_device_ids=true | all-gather | bytes 675840 | tf_op jit(solution)/shard_map/all_gather | solution.py:99
  803.1 5.6 all-gather.23.cloned.1.call-done
  808.9 4.5 fusion.11
  814.5 27.5 %all-gather.21.cloned.1.call-done = bf16[256,4224]{1,0:T(8,128)(2,1)} async-done(((bf16[64,4224]{1,0:T(8,128)(2,1)}), bf16[256,4224]{1,0:T(8,128)(2,1)}) %all-gather.21.cloned.1.call-update) | async-done | bytes 2162704 | tf_op jit(solution)/shard_map/all_gather | solution.py:100
  849.0 56.1 %all-gather.25.cloned.1.call-done = bf16[256,11264]{1,0:T(8,128)(2,1)} async-done(((bf16[64,11264]{1,0:T(8,128)(2,1)}), bf16[256,11264]{1,0:T(8,128)(2,1)}) %all-gather.25.cloned.1.call-update) | async-done | bytes 5767184 | tf_op jit(solution)/shard_map/all_gather | solution.py:100
  905.1 6.3 fusion.49
  (324 shorter events, 121.4 us)
Async XLA Ops:
  7.2 65.9 %copy-start.65 = (s32[1,64]{1,0:T(1,128)S(1)}, s32[1,64]{1,0:T(1,128)}, u32[]{:S(2)}) copy-start(s32[1,64]{1,0:T(1,128)} %param.24) | copy-start | bytes 772
  7.2 66.8 %copy-start.10 = (bf16[1,128,1024]{2,1,0:T(8,128)(2,1)S(1)}, bf16[1,128,1024]{2,1,0:T(8,128)(2,1)}, u32[]{:S(2)}) copy-start(bf16[1,128,1024]{2,1,0:T(8,128)(2,1)} %param.22) | copy-start | bytes 786436
  7.2 65.1 %all-gather.27.cloned.1.call-start = ((), (), s32[]{:S(2)}) async-start(), calls=%async_computation.19 | async-start | bytes 6291456 | tf_op jit(solution)/shard_map/all_gather | solution.py:79
  10.4 205.5 %all-gather.29.cloned.1.call-start = ((), (), s32[]{:S(2)}) async-start(), calls=%async_computation.20 | async-start | bytes 3145728 | tf_op jit(solution)/shard_map/all_gather | solution.py:79
  72.3 7.5 collective-permute-start
  72.3 143.6 %all-gather.33.cloned.1.call-start = ((), (), s32[]{:S(2)}) async-start(), calls=%async_computation.22 | async-start | bytes 4718592 | tf_op jit(solution)/shard_map/all_gather | solution.py:79
  74.1 17.4 %copy-start.56 = (f32[128]{0:T(128)}, f32[128]{0:T(128)S(1)}, u32[]{:S(2)}) copy-start(f32[128]{0:T(128)S(1)} %add_rsqrt_fusion.3) | copy-start | bytes 1540
  74.3 33.8 %copy-start.37 = (f32[128,64]{0,1:T(8,128)}, f32[128,64]{0,1:T(8,128)S(1)}, u32[]{:S(2)}) copy-start(f32[128,64]{0,1:T(8,128)S(1)} %get-tuple-element.122) | copy-start | bytes 98308
  74.4 33.8 %copy-start.39 = (f32[128,64]{0,1:T(8,128)}, f32[128,64]{0,1:T(8,128)S(1)}, u32[]{:S(2)}) copy-start(f32[128,64]{0,1:T(8,128)S(1)} %get-tuple-element.123) | copy-start | bytes 98308
  96.2 7.4 copy-start.5
  113.9 56.6 %all-to-all-start = ((bf16[32,128,384]{2,1,0:T(8,128)(2,1)}), bf16[32,128,384]{2,1,0:T(8,128)(2,1)S(1)}, u32[]{:S(2)}, u32[]{:S(2)}) async-start(bf16[32,128,384]{2,1,0:T(8,128)(2,1)} %pad_maximum_fusion.5), calls=%async_computation | async-start | bytes 6291456 | tf_op jit(solution)/shard_map/all_to_all | solution.py:160
  123.3 159.0 %all-gather.31.cloned.1.call-start = ((), (), s32[]{:S(2)}) async-start(), calls=%async_computation.21 | async-start | bytes 9437184 | tf_op jit(solution)/shard_map/all_gather | solution.py:79
  127.6 266.3 %all-gather.15.cloned.1.call-start = ((), (), s32[]{:S(2)}) async-start(), calls=%async_computation.9 | async-start | bytes 2621440 | tf_op jit(solution)/shard_map/all_gather | solution.py:256
  171.1 14.0 %copy-start.31 = (bf16[32,128,128]{2,1,0:T(8,128)(2,1)}, bf16[32,128,128]{2,1,0:T(8,128)(2,1)S(1)}, u32[]{:S(2)}) copy-start(bf16[32,128,128]{2,1,0:T(8,128)(2,1)S(1)} %get-tuple-element.105) | copy-start | bytes 3145732
  171.1 29.1 %copy-start.33 = (bf16[32,128,128]{2,1,0:T(8,128)(2,1)}, bf16[32,128,128]{2,1,0:T(8,128)(2,1)S(1)}, u32[]{:S(2)}) copy-start(bf16[32,128,128]{2,1,0:T(8,128)(2,1)S(1)} %get-tuple-element.106) | copy-start | bytes 3145732
  171.1 14.0 %copy-start.41 = (bf16[16,128,128]{2,1,0:T(8,128)(2,1)}, bf16[16,128,128]{2,1,0:T(8,128)(2,1)S(1)}, u32[]{:S(2)}) copy-start(bf16[16,128,128]{2,1,0:T(8,128)(2,1)S(1)} %constant_dynamic-slice_fusion.2) | copy-start | bytes 1572868
  200.2 83.0 %copy-start.55 = (pred[32]{0:T(512)(128)(4,1)S(1)}, pred[32]{0:T(512)(128)(4,1)}, u32[]{:S(2)}) copy-start(pred[32]{0:T(512)(128)(4,1)} %broadcast_in_dim.119) | copy-start | bytes 100
  215.8 98.3 %copy-start.17 = (f32[2048,128]{1,0:T(8,128)}, f32[2048,128]{1,0:T(8,128)S(1)}, u32[]{:S(2)}) copy-start(f32[2048,128]{1,0:T(8,128)S(1)} %fusion.4) | copy-start | bytes 3145732
  282.3 39.6 %collective-permute-start.2 = (bf16[2,256,6144]{2,1,0:T(8,128)(2,1)}, bf16[2,256,6144]{2,1,0:T(8,128)(2,1)}, u32[]{:S(2)}, u32[]{:S(2)}) collective-permute-start(bf16[2,256,6144]{2,1,0:T(8,128)(2,1)} %bitcast.224), channel_id=1, source_target_pairs={{0,1},{1,0},{2,3},{3,2},{4,5},{5,4},{6,7},{7,6},{8,9},{9,8},{10,11... | collective-permute-start | bytes 18874376 | tf_op jit(solution)/shard_map/ppermute | solution.py:83
  282.3 29.4 %collective-permute-start.1 = (bf16[2,512,1024]{2,1,0:T(8,128)(2,1)}, bf16[2,512,1024]{2,1,0:T(8,128)(2,1)}, u32[]{:S(2)}, u32[]{:S(2)}) collective-permute-start(bf16[2,512,1024]{2,1,0:T(8,128)(2,1)} %bitcast.258), channel_id=1, source_target_pairs={{0,1},{1,0},{2,3},{3,2},{4,5},{5,4},{6,7},{7,6},{8,9},{9,8},{10,11... | collective-permute-start | bytes 6291464 | tf_op jit(solution)/shard_map/ppermute | solution.py:83
  282.8 36.2 %collective-permute-start.3 = (bf16[2,768,1024]{2,1,0:T(8,128)(2,1)}, bf16[2,768,1024]{2,1,0:T(8,128)(2,1)}, u32[]{:S(2)}, u32[]{:S(2)}) collective-permute-start(bf16[2,768,1024]{2,1,0:T(8,128)(2,1)} %bitcast.243), channel_id=1, source_target_pairs={{0,1},{1,0},{2,3},{3,2},{4,5},{5,4},{6,7},{7,6},{8,9},{9,8},{10,11... | collective-permute-start | bytes 9437192 | tf_op jit(solution)/shard_map/ppermute | solution.py:83
  283.2 28.5 %copy-start.30 = (bf16[1024,1024]{1,0:T(8,128)(2,1)S(1)}, bf16[1024,1024]{1,0:T(8,128)(2,1)}, u32[]{:S(2)}) copy-start(bf16[1024,1024]{1,0:T(8,128)(2,1)} %all-gather.29.cloned.1.call-done) | copy-start | bytes 6291460
  317.4 27.3 %copy-start.52 = (f32[128]{0:T(128)}, f32[128]{0:T(128)S(1)}, u32[]{:S(2)}) copy-start(f32[128]{0:T(128)S(1)} %add_rsqrt_fusion.2) | copy-start | bytes 1540
  322.0 11.5 %copy-start.1 = (bf16[2,2,768,1024]{3,2,1,0:T(8,128)(2,1)}, bf16[2,2,768,1024]{3,2,1,0:T(8,128)(2,1)S(1)}, u32[]{:S(2)}) copy-start(bf16[2,2,768,1024]{3,2,1,0:T(8,128)(2,1)S(1)} %pad_maximum_fusion.2) | copy-start | bytes 18874372
  348.1 109.4 %all-gather.17.cloned.1.call-start = ((), (), s32[]{:S(2)}) async-start(), calls=%async_computation.10 | async-start | bytes 7864320 | tf_op jit(solution)/shard_map/all_gather | solution.py:255
  353.1 40.8 %all-to-all-start.2 = ((bf16[128,4,1792]{2,0,1:T(8,128)(2,1)}), bf16[128,4,1792]{2,0,1:T(8,128)(2,1)S(1)}, u32[]{:S(2)}, u32[]{:S(2)}) async-start(bf16[128,4,1792]{2,0,1:T(8,128)(2,1)} %pad_maximum_fusion.10), calls=%async_computation.2 | async-start | bytes 3670016 | tf_op jit(solution)/shard_map/all_to_all | solution.py:248
  467.5 52.5 %all-to-all-start.3 = ((bf16[32,128,128]{1,2,0:T(8,128)(2,1)}), bf16[32,128,128]{1,2,0:T(8,128)(2,1)S(1)}, u32[]{:S(2)}, u32[]{:S(2)}) async-start(bf16[32,128,128]{1,2,0:T(8,128)(2,1)} %bitcast_select_fusion.2), calls=%async_computation.3 | async-start | bytes 2097152 | tf_op jit(solution)/shard_map/all_to_all | solution.py:160
  476.8 171.6 %reduce-scatter.9.cloned.1.call-start = ((), (), s32[]{:S(2)}) async-start(), calls=%async_computation.15 | async-start | bytes 7208960 | tf_op jit(solution)/shard_map/reduce_scatter | solution.py:94
  521.5 20.6 %copy-start.32 = (bf16[32,128,128]{2,1,0:T(8,128)(2,1)S(1)}, bf16[32,128,128]{2,1,0:T(8,128)(2,1)}, u32[]{:S(2)}) copy-start(bf16[32,128,128]{2,1,0:T(8,128)(2,1)} %copy-done.31) | copy-start | bytes 3145732
  575.3 10.2 %copy-start.59 = (f32[128]{0:T(128)S(1)}, f32[128]{0:T(128)}, u32[]{:S(2)}) copy-start(f32[128]{0:T(128)} %param.35) | copy-start | bytes 1540
  575.3 10.2 %copy-start.61 = (f32[128]{0:T(128)S(1)}, f32[128]{0:T(128)}, u32[]{:S(2)}) copy-start(f32[128]{0:T(128)} %param.34) | copy-start | bytes 1540
  575.3 10.3 %copy-start.46 = (f32[128,16]{0,1:T(8,128)S(1)}, f32[128,16]{0,1:T(8,128)}, u32[]{:S(2)}) copy-start(f32[128,16]{0,1:T(8,128)} %copy-done.45) | copy-start | bytes 24580
  575.3 13.8 %copy-start.50 = (f32[128,8]{0,1:T(8,128)S(1)}, f32[128,8]{0,1:T(8,128)}, u32[]{:S(2)}) copy-start(f32[128,8]{0,1:T(8,128)} %copy-done.49) | copy-start | bytes 12292
  575.3 55.2 %all-to-all-start.4 = ((bf16[32,128,384]{1,2,0:T(8,128)(2,1)}), bf16[32,128,384]{1,2,0:T(8,128)(2,1)S(1)}, u32[]{:S(2)}, u32[]{:S(2)}) async-start(bf16[32,128,384]{1,2,0:T(8,128)(2,1)} %pad_maximum_fusion.7), calls=%async_computation.4 | async-start | bytes 6291456 | tf_op jit(solution)/shard_map/all_to_all | solution.py:160
  585.2 108.8 %all-gather.19.cloned.1.call-start = ((), (), s32[]{:S(2)}) async-start(), calls=%async_computation.11 | async-start | bytes 5242880 | tf_op jit(solution)/shard_map/all_gather | solution.py:319
  585.6 45.2 %copy-start.38 = (f32[128,64]{0,1:T(8,128)S(1)}, f32[128,64]{0,1:T(8,128)}, u32[]{:S(2)}) copy-start(f32[128,64]{0,1:T(8,128)} %copy-done.37) | copy-start | bytes 98308
  585.6 45.2 %copy-start.40 = (f32[128,64]{0,1:T(8,128)S(1)}, f32[128,64]{0,1:T(8,128)}, u32[]{:S(2)}) copy-start(f32[128,64]{0,1:T(8,128)} %copy-done.39) | copy-start | bytes 98308
  645.2 7.3 copy-start.44
  647.8 75.1 %reduce-scatter.11.cloned.1.call-start = ((), (), s32[]{:S(2)}) async-start(), calls=%async_computation.16 | async-start | bytes 1802240 | tf_op jit(solution)/shard_map/reduce_scatter | solution.py:95
  648.5 107.4 %reduce-scatter.5.cloned.1.call-start = ((), (), s32[]{:S(2)}) async-start(), calls=%async_computation.12 | async-start | bytes 2703360 | tf_op jit(solution)/shard_map/reduce_scatter | solution.py:94
  699.1 109.7 %copy-start.3 = (f32[128,1024]{1,0:T(8,128)S(1)}, f32[128,1024]{1,0:T(8,128)}, u32[]{:S(2)}) copy-start(f32[128,1024]{1,0:T(8,128)} %copy-done.2) | copy-start | bytes 1572868
  699.1 109.7 %copy-start.23 = (bf16[128,3072]{1,0:T(8,128)(2,1)S(1)}, bf16[128,3072]{1,0:T(8,128)(2,1)}, u32[]{:S(2)}) copy-start(bf16[128,3072]{1,0:T(8,128)(2,1)} %get-tuple-element.104) | copy-start | bytes 2359300
  699.1 80.4 %reduce-scatter.7.cloned.1.call-start = ((), (), s32[]{:S(2)}) async-start(), calls=%async_computation.13 | async-start | bytes 675840 | tf_op jit(solution)/shard_map/reduce_scatter | solution.py:95
  722.9 33.1 %collective-permute-start.5 = (bf16[16,11264]{1,0:T(8,128)(2,1)}, bf16[16,11264]{1,0:T(8,128)(2,1)S(1)}, u32[]{:S(2)}, u32[]{:S(2)}) collective-permute-start(bf16[16,11264]{1,0:T(8,128)(2,1)} %reduce-scatter.11.cloned.1.call-done), channel_id=1, source_target_pairs={{0,64},{64,0},{1,65},{65,1},{2,66},{66,2},{3,67},{67,3},{4,68},{68... | collective-permute-start | bytes 1081352 | tf_op jit(solution)/shard_map/ppermute | solution.py:96
  756.0 52.8 %all-gather.23.cloned.1.call-start = ((), (), s32[]{:S(2)}) async-start(), calls=%async_computation.17 | async-start | bytes 1802240 | tf_op jit(solution)/shard_map/all_gather | solution.py:99
  757.9 84.2 %all-gather.21.cloned.1.call-start = ((), (), s32[]{:S(2)}) async-start(), calls=%async_computation.14 | async-start | bytes 2703360 | tf_op jit(solution)/shard_map/all_gather | solution.py:100
  779.6 6.7 collective-permute-start.4
  802.6 102.5 %all-gather.25.cloned.1.call-start = ((), (), s32[]{:S(2)}) async-start(), calls=%async_computation.18 | async-start | bytes 7208960 | tf_op jit(solution)/shard_map/all_gather | solution.py:100
  (45 other events, 163.5 us)
Sparse Core Ops, SparseCore 0:
  10.5 61.7 all-gather.26
  73.9 36.6 all-gather.28
  112.2 79.6 all-gather.32
  194.0 88.2 all-gather.30
  348.3 39.0 all-gather.14
  389.4 68.1 all-gather.16
  520.0 61.5 reduce-scatter.8
  647.9 46.0 all-gather.18
  696.4 26.4 reduce-scatter.10
  725.8 30.1 reduce-scatter.4
  758.5 21.0 reduce-scatter.6
  781.6 27.0 all-gather.22
  810.4 31.6 all-gather.20
  843.6 61.4 all-gather.24

commit v9 on v8

--- a/solution.py
+++ b/solution.py
@@ -265,11 +265,11 @@
         [output_shard.reshape(mlp_rows, -1), gate_up_shard, down_shard.reshape(mlp_rows, -1)],
         axis=1,
     ).astype(jnp.bfloat16)
-    mlp_packed, mixed_gradient = lax.optimization_barrier((mlp_packed, mixed_gradient))
-    mlp_reduced = reduce_ctx(mlp_packed)
     head_out_grad = gather_half(
         exchange(to_heads(mixed_gradient.reshape(local_rows, HQ, HEAD_SIZE)))
     )
+    mlp_packed, head_out_grad = lax.optimization_barrier((mlp_packed, head_out_grad))
+    mlp_reduced = reduce_ctx(mlp_packed)
     out_grad_f = head_out_grad.astype(jnp.float32)
     delta = jnp.sum(out_grad_f * head_mixed, axis=-1, keepdims=True)
     probabilities = jnp.exp(head_scores() - log_total)

time: 933 us -> 871 us (0.934)
  local copies, waits for them, and re-layouts: 91.5 us -> 68.8 us
  other arithmetic: 109 us -> 96.6 us
  waiting for transfers between devices: 483 us -> 471 us
    dot_general x1 -> x0, local copies, waits for them, and re-layouts: 22.5 us -> none  [left_dot(): lax.dot_general(left_side, right_side, (((0,), (0,)), ((), ())), preferre...]
    all_to_all x3, waiting for transfers between devices: 81.1 us -> 97.4 us  [exchange(): return lax.all_to_all(values, CTX, split_axis=0, concat_axis=0, tiled=True)]
    all_gather x1, waiting for transfers between devices: 51.8 us -> 38.2 us  [on_device(): gate_up_rows = lax.all_gather(gate_up_grad, FSDP, axis=0, tiled=True)]
    convert_element_type x1, other arithmetic: 20.3 us -> 8.82 us  [on_device(): weights_b = jnp.exp(raw_scores - log_total).astype(jnp.bfloat16)]
    all_to_all x1, waiting for transfers between devices: 33.2 us -> 23.8 us  [on_device(): lax.all_to_all(stacked, FSDP, split_axis=1, concat_axis=0, tiled=True)]
  transfers between devices with their start and end apart: 24 -> 24, of which waited for: 15 -> 16; matrix products, arithmetic and copies ran while one was open for 29% -> 26% of each run, Pallas kernels for 0% -> 0%
where the time goes in v9:
time: 871 us; the launch traced here: 861 us
  waiting for transfers between devices  471 us (54%)
  matrix products  119 us (14%)
  other arithmetic  96.6 us (11%)
  local copies, waits for them, and re-layouts  68.8 us (8%)
  blocking collectives  54.8 us (6%)
  starting transfers between devices  33.8 us (4%)
  between operations  17.1 us (2%)
    all_gather x4, waiting for transfers between devices, gather_across(): return lax.all_gather(values, 'yl', axis=0, tiled=False)  123 us
    all_to_all x3, waiting for transfers between devices, exchange(): return lax.all_to_all(values, CTX, split_axis=0, concat_axis=0, tiled=True)  97.4 us
    all_gather x2, waiting for transfers between devices, reduce_ctx(): return lax.all_gather(part, 'z', axis=0, tiled=True).astype(jnp.float32)  84.2 us
    reduce_scatter x2, waiting for transfers between devices, reduce_ctx(): part = lax.psum_scatter(part, 'x', scatter_dimension=0, tiled=True)  45.3 us
    dot_general x5, matrix products, right_dot(): lax.dot_general(left_side, right_side, (((1,), (1,)), ((), ())), preferre...  41.8 us
    all_gather x1, waiting for transfers between devices, on_device(): gate_up_rows = lax.all_gather(gate_up_grad, FSDP, axis=0, tiled=True)  38.2 us
    dot_general x6, matrix products, left_dot(): lax.dot_general(left_side, right_side, (((0,), (0,)), ((), ())), preferre...  32.9 us
    reduce_scatter x2, waiting for transfers between devices, reduce_ctx(): part = lax.psum_scatter(packed, 'z', scatter_dimension=0, tiled=True)  30.1 us
  transfers between devices with their start and end apart: 24, of which 16 were waited for; matrix products, arithmetic and copies ran while one was open for 26% of the time, Pallas kernels for 0%

profile of v9, /device:TPU:0, one launch (start us, length us, event | category | flops | bytes accessed | tf_op | source)
XLA Modules:
  0.0 861.5 jit_solution(4952340063503465388)
XLA Ops:
  10.4 61.8 %all-gather.27.cloned.1.call-done = bf16[512,4096]{1,0:T(8,128)(2,1)} async-done(((bf16[256,4096]{1,0:T(8,128)(2,1)}), bf16[512,4096]{1,0:T(8,128)(2,1)}) %all-gather.27.cloned.1.call-update) | async-done | bytes 4194320 | tf_op jit(solution)/shard_map/all_gather | solution.py:79
  74.0 5.8 collective-permute-done
  79.7 5.2 select_bitcast_fusion.3
  84.9 6.5 pad_maximum_fusion.1
  91.4 4.7 fusion.32
  107.1 9.4 %all-to-all-start = ((bf16[32,128,384]{2,1,0:T(8,128)(2,1)}), bf16[32,128,384]{2,1,0:T(8,128)(2,1)S(1)}, u32[]{:S(2)}, u32[]{:S(2)}) async-start(bf16[32,128,384]{2,1,0:T(8,128)(2,1)} %pad_maximum_fusion.5), calls=%async_computation | async-start | bytes 6291456 | tf_op jit(solution)/shard_map/all_to_all | solution.py:160
  116.5 3.8 pad_maximum_fusion.6
  120.7 41.7 %all-to-all-done = bf16[32,128,384]{2,1,0:T(8,128)(2,1)S(1)} async-done(((bf16[32,128,384]{2,1,0:T(8,128)(2,1)}), bf16[32,128,384]{2,1,0:T(8,128)(2,1)S(1)}, u32[]{:S(2)}, u32[]{:S(2)}) %all-to-all-start) | async-done | bytes 3145760 | tf_op jit(solution)/shard_map/all_to_all | solution.py:160
  163.2 13.7 %fusion.48 = (f32[2048]{0:T(1024)S(1)}, f32[2048,4096]{1,0:T(8,128)}) fusion(bf16[2048,128]{1,0:T(8,128)(2,1)S(1)} %bitcast.256, bf16[4096,128]{1,0:T(8,128)(2,1)S(1)} %bitcast.253, s32[2048]{0:T(1024)S(1)} %dynamic-slice-done, s32[4096]{0:T(1024)S(1)} %copy-done.54), kind=kOutput, calls=%fused_computation.176 | convolution fusion | flops 2181036032 | bytes 35160064 | tf_op jit(solution)/shard_map/qd,kd->qk/dot_general | solution.py:197
  176.8 14.9 %exponential_reduce_fusion = f32[2048]{0:T(1024)S(1)} fusion(f32[2048,4096]{1,0:T(8,128)} %get-tuple-element.129, f32[2048]{0:T(1024)S(1)} %get-tuple-element.128), kind=kLoop, calls=%fused_computation.2 | loop fusion | flops 16775168 | bytes 33570816 | tf_op jit(solution)/shard_map/reduce_sum | solution.py:204
  191.8 5.3 copy-done
  197.1 8.8 %fusion = bf16[2048,4096]{1,0:T(8,128)(2,1)} fusion(f32[2048,4096]{1,0:T(8,128)S(1)} %copy-done, f32[2048]{0:T(1024)S(1)} %log_add_fusion), kind=kLoop, calls=%fused_computation.4 | loop fusion | flops 16777216 | bytes 50339840 | tf_op jit(solution)/shard_map/convert_element_type | solution.py:205
  205.9 9.6 %fusion.49 = f32[2048,128]{1,0:T(8,128)S(1)} fusion(bf16[2048,4096]{1,0:T(8,128)(2,1)} %fusion, bf16[4096,128]{1,0:T(8,128)(2,1)S(1)} %bitcast.225), kind=kOutput, calls=%fused_computation.177 | convolution fusion | flops 2147483648 | bytes 18874368 | tf_op jit(solution)/shard_map/dot_general | solution.py:206
  215.5 60.9 %all-gather.31.cloned.1.call-done = bf16[512,6144]{1,0:T(8,128)(2,1)} async-done(((bf16[256,6144]{1,0:T(8,128)(2,1)}), bf16[512,6144]{1,0:T(8,128)(2,1)}) %all-gather.31.cloned.1.call-update) | async-done | bytes 6291472 | tf_op jit(solution)/shard_map/all_gather | solution.py:79
  277.4 28.2 %all_to_all.35 = bf16[32,128,128]{1,2,0:T(8,128)(2,1)S(1)} all-to-all(bf16[32,128,128]{1,2,0:T(8,128)(2,1)S(1)} %bitcast_select_fusion.2), channel_id=1, replica_groups=mesh['yh'=2,'x'=4,'z'=4,'yl'=2,'c'=2] {'yh','x','z'}, dimensions={0} | all-to-all | bytes 2097152 | tf_op jit(solution)/shard_map/all_to_all | solution.py:160
  316.4 4.9 select_bitcast_fusion.1
  324.4 4.0 multiply_convert_fusion.2
  328.4 7.2 multiply_reduce_fusion.5
  340.4 3.7 fusion.4
  345.9 5.1 all-to-all-start.3
  354.8 15.4 %all-to-all-done.3 = bf16[32,128,128]{1,2,0:T(8,128)(2,1)S(1)} async-done(((bf16[32,128,128]{1,2,0:T(8,128)(2,1)}), bf16[32,128,128]{1,2,0:T(8,128)(2,1)S(1)}, u32[]{:S(2)}, u32[]{:S(2)}) %all-to-all-start.3) | async-done | bytes 1048608 | tf_op jit(solution)/shard_map/all_to_all | solution.py:160
  370.2 4.4 all-to-all-start.2
  375.0 23.8 %all-to-all-done.2 = bf16[128,4,1792]{2,0,1:T(8,128)(2,1)} async-done(((bf16[128,4,1792]{2,0,1:T(8,128)(2,1)}), bf16[128,4,1792]{2,0,1:T(8,128)(2,1)}, u32[]{:S(2)}, u32[]{:S(2)}) %all-to-all-start.2) | async-done | bytes 1835040 | tf_op jit(solution)/shard_map/all_to_all | solution.py:248
  398.8 3.6 convolution_convert_fusion.4
  405.2 3.1 convolution_convert_fusion.5
  409.7 38.2 %all-gather.17.cloned.1.call-done = bf16[512,6144]{1,0:T(8,128)(2,1)} async-done(((bf16[128,6144]{1,0:T(8,128)(2,1)}), bf16[512,6144]{1,0:T(8,128)(2,1)}) %all-gather.17.cloned.1.call-update) | async-done | bytes 6291472 | tf_op jit(solution)/shard_map/all_gather | solution.py:255
  447.9 4.7 convolution_convert_fusion
  452.7 3.5 pad_maximum_fusion.3
  456.1 9.3 %convolution_convert_fusion.2 = bf16[4096,128]{1,0:T(8,128)(2,1)} fusion(bf16[2048,4096]{1,0:T(8,128)(2,1)} %fusion, bf16[2048,128]{1,0:T(8,128)(2,1)S(1)} %bitcast.218), kind=kOutput, calls=%fused_computation.15 | convolution fusion | flops 2148007936 | bytes 18350080 | tf_op jit(solution)/shard_map/dot_general | solution.py:67
  468.2 20.0 %multiply_convert_fusion = bf16[2048,4096]{1,0:T(8,128)(2,1)} fusion(f32[2048,4096]{1,0:T(8,128)} %get-tuple-element.129, f32[2048]{0:T(1024)S(1)} %multiply_reduce_fusion.2, f32[2048]{0:T(1024)S(1)} %log_add_fusion, bf16[2048,128]{1,0:T(8,128)(2,1)S(1)} %bitcast.220, bf16[4096,128]{1,0:T(8,128)(2,1)S(1)} %bitcast.226), kind=kOutput, calls=%fused_computation | convolution fusion | flops 2181038080 | bytes 51920896 | tf_op jit(solution)/shard_map/dot_general | solution.py:73
  488.2 8.6 fusion.1
  497.5 9.2 %fusion.2 = bf16[2048,128]{1,0:T(8,128)(2,1)} fusion(bf16[2048,4096]{1,0:T(8,128)(2,1)} %multiply_convert_fusion, bf16[4096,128]{1,0:T(8,128)(2,1)S(1)} %bitcast.254), kind=kOutput, calls=%fused_computation.27 | convolution fusion | flops 2148007936 | bytes 18350080 | tf_op jit(solution)/shard_map/dot_general | solution.py:279
  511.9 7.5 all-to-all-start.4
  527.1 40.2 %all-to-all-done.4 = bf16[32,128,384]{1,2,0:T(8,128)(2,1)S(1)} async-done(((bf16[32,128,384]{1,2,0:T(8,128)(2,1)}), bf16[32,128,384]{1,2,0:T(8,128)(2,1)S(1)}, u32[]{:S(2)}, u32[]{:S(2)}) %all-to-all-start.4) | async-done | bytes 3145760 | tf_op jit(solution)/shard_map/all_to_all | solution.py:160
  591.5 6.8 fusion.28
  598.3 11.2 %all-reduce.5 = (f32[1024]{0:T(1024)S(1)}, f32[1024]{0:T(1024)S(1)}, bf16[128]{0:T(256)(128)(2,1)S(1)}, bf16[128]{0:T(256)(128)(2,1)S(1)}) all-reduce(f32[1024]{0:T(1024)S(1)} %get-tuple-element.79, f32[1024]{0:T(1024)S(1)} %copy-done.56, ...), channel_id=6, replica_groups=mesh['yh'=2,'x'=4,'z'=4,'yl'=2,'c'=2] {'yl','c'}, use_global_device_ids=true, to_apply=%region_14.15.clone | all-reduce | flops 2304 | bytes 17920
  619.2 13.1 %all-gather.19.cloned.1.call-done = bf16[512,4096]{1,0:T(8,128)(2,1)} async-done(((bf16[128,4096]{1,0:T(8,128)(2,1)}), bf16[512,4096]{1,0:T(8,128)(2,1)}) %all-gather.19.cloned.1.call-update) | async-done | bytes 4194320 | tf_op jit(solution)/shard_map/all_gather | solution.py:319
  632.2 3.6 convolution_convert_fusion.1
  637.4 23.6 %reduce-scatter.11.cloned.1.call-done = bf16[16,11264]{1,0:T(8,128)(2,1)} async-done(((bf16[64,11264]{1,0:T(8,128)(2,1)}), bf16[16,11264]{1,0:T(8,128)(2,1)}) %reduce-scatter.11.cloned.1.call-update) | async-done | bytes 360464 | tf_op jit(solution)/shard_map/reduce_scatter | solution.py:95
  664.1 30.1 %reduce-scatter.5.cloned.1.call-done = bf16[64,4224]{1,0:T(8,128)(2,1)} async-done(((bf16[256,4224]{1,0:T(8,128)(2,1)}), bf16[64,4224]{1,0:T(8,128)(2,1)}) %reduce-scatter.5.cloned.1.call-update) | async-done | bytes 540688 | tf_op jit(solution)/shard_map/reduce_scatter | solution.py:94
  696.1 21.7 %reduce-scatter.7.cloned.1.call-done = bf16[16,4224]{1,0:T(8,128)(2,1)} async-done(((bf16[64,4224]{1,0:T(8,128)(2,1)}), bf16[16,4224]{1,0:T(8,128)(2,1)}) %reduce-scatter.7.cloned.1.call-update) | async-done | bytes 135184 | tf_op jit(solution)/shard_map/reduce_scatter | solution.py:95
  720.8 3.7 collective-permute-done.4
  725.4 15.3 %all_gather.56 = bf16[64,4224]{1,0:T(8,128)(2,1)} all-gather(bf16[16,4224]{1,0:T(8,128)(2,1)S(1)} %add_convert_fusion.2), channel_id=1, replica_groups=mesh['yh'=2,'x'=4,'z'=4,'yl'=2,'c'=2] {'x'}, dimensions={0}, use_global_device_ids=true | all-gather | bytes 675840 | tf_op jit(solution)/shard_map/all_gather | solution.py:99
  740.8 6.2 all-gather.23.cloned.1.call-done
  747.0 4.5 fusion.6
  752.7 27.5 %all-gather.21.cloned.1.call-done = bf16[256,4224]{1,0:T(8,128)(2,1)} async-done(((bf16[64,4224]{1,0:T(8,128)(2,1)}), bf16[256,4224]{1,0:T(8,128)(2,1)}) %all-gather.21.cloned.1.call-update) | async-done | bytes 2162704 | tf_op jit(solution)/shard_map/all_gather | solution.py:100
  786.5 56.7 %all-gather.25.cloned.1.call-done = bf16[256,11264]{1,0:T(8,128)(2,1)} async-done(((bf16[64,11264]{1,0:T(8,128)(2,1)}), bf16[256,11264]{1,0:T(8,128)(2,1)}) %all-gather.25.cloned.1.call-update) | async-done | bytes 5767184 | tf_op jit(solution)/shard_map/all_gather | solution.py:100
  846.2 6.3 fusion.43
  (335 shorter events, 117.2 us)
Async XLA Ops:
  7.2 65.0 %all-gather.27.cloned.1.call-start = ((), (), s32[]{:S(2)}) async-start(), calls=%async_computation.19 | async-start | bytes 6291456 | tf_op jit(solution)/shard_map/all_gather | solution.py:79
  10.3 62.9 %copy-start.70 = (s32[1,64]{1,0:T(1,128)S(1)}, s32[1,64]{1,0:T(1,128)}, u32[]{:S(2)}) copy-start(s32[1,64]{1,0:T(1,128)} %param.24) | copy-start | bytes 772
  10.3 63.1 %copy-start.10 = (bf16[1,128,1024]{2,1,0:T(8,128)(2,1)S(1)}, bf16[1,128,1024]{2,1,0:T(8,128)(2,1)}, u32[]{:S(2)}) copy-start(bf16[1,128,1024]{2,1,0:T(8,128)(2,1)} %param.22) | copy-start | bytes 786436
  10.3 205.2 %all-gather.29.cloned.1.call-start = ((), (), s32[]{:S(2)}) async-start(), calls=%async_computation.20 | async-start | bytes 3145728 | tf_op jit(solution)/shard_map/all_gather | solution.py:79
  72.2 7.5 collective-permute-start
  72.3 143.3 %all-gather.33.cloned.1.call-start = ((), (), s32[]{:S(2)}) async-start(), calls=%async_computation.22 | async-start | bytes 4718592 | tf_op jit(solution)/shard_map/all_gather | solution.py:79
  73.6 17.8 %copy-start.59 = (f32[128]{0:T(128)}, f32[128]{0:T(128)S(1)}, u32[]{:S(2)}) copy-start(f32[128]{0:T(128)S(1)} %add_rsqrt_fusion.3) | copy-start | bytes 1540
  74.0 29.6 %copy-start.40 = (f32[128,64]{0,1:T(8,128)}, f32[128,64]{0,1:T(8,128)S(1)}, u32[]{:S(2)}) copy-start(f32[128,64]{0,1:T(8,128)S(1)} %get-tuple-element.122) | copy-start | bytes 98308
  74.0 29.6 %copy-start.42 = (f32[128,64]{0,1:T(8,128)}, f32[128,64]{0,1:T(8,128)S(1)}, u32[]{:S(2)}) copy-start(f32[128,64]{0,1:T(8,128)S(1)} %get-tuple-element.123) | copy-start | bytes 98308
  107.1 55.4 %all-to-all-start = ((bf16[32,128,384]{2,1,0:T(8,128)(2,1)}), bf16[32,128,384]{2,1,0:T(8,128)(2,1)S(1)}, u32[]{:S(2)}, u32[]{:S(2)}) async-start(bf16[32,128,384]{2,1,0:T(8,128)(2,1)} %pad_maximum_fusion.5), calls=%async_computation | async-start | bytes 6291456 | tf_op jit(solution)/shard_map/all_to_all | solution.py:160
  116.5 159.9 %all-gather.31.cloned.1.call-start = ((), (), s32[]{:S(2)}) async-start(), calls=%async_computation.21 | async-start | bytes 9437184 | tf_op jit(solution)/shard_map/all_gather | solution.py:79
  120.4 278.4 %all-gather.15.cloned.1.call-start = ((), (), s32[]{:S(2)}) async-start(), calls=%async_computation.9 | async-start | bytes 2621440 | tf_op jit(solution)/shard_map/all_gather | solution.py:256
  120.7 42.4 %copy-start.54 = (s32[4096]{0:T(1024)S(1)}, s32[4096]{0:T(1024)}, u32[]{:S(2)}) copy-start(s32[4096]{0:T(1024)} %copy-done.53) | copy-start | bytes 49156
  120.7 42.4 %dynamic-slice-start = ((s32[4096]{0:T(1024)}, s32[]{:T(128)}), s32[2048]{0:T(1024)S(1)}, s32[]{:S(2)}) async-start(s32[4096]{0:T(1024)} %copy-done.53, s32[]{:T(128)} %select_n.88), calls=%async_computation.25 | async-start | bytes 16896 | tf_op jit(solution)/shard_map/dynamic_slice | solution.py:134
  163.0 13.8 %copy-start.35 = (bf16[32,128,128]{2,1,0:T(8,128)(2,1)}, bf16[32,128,128]{2,1,0:T(8,128)(2,1)S(1)}, u32[]{:S(2)}) copy-start(bf16[32,128,128]{2,1,0:T(8,128)(2,1)S(1)} %get-tuple-element.106) | copy-start | bytes 3145732
  163.1 42.8 %copy-start.15 = (bf16[32,128,128]{2,1,0:T(8,128)(2,1)}, bf16[32,128,128]{2,1,0:T(8,128)(2,1)S(1)}, u32[]{:S(2)}) copy-start(bf16[32,128,128]{2,1,0:T(8,128)(2,1)S(1)} %get-tuple-element.105) | copy-start | bytes 3145732
  163.1 13.7 %copy-start.44 = (bf16[16,128,128]{2,1,0:T(8,128)(2,1)}, bf16[16,128,128]{2,1,0:T(8,128)(2,1)S(1)}, u32[]{:S(2)}) copy-start(bf16[16,128,128]{2,1,0:T(8,128)(2,1)S(1)} %constant_dynamic-slice_fusion.2) | copy-start | bytes 1572868
  176.8 20.2 %copy-start = (f32[2048,4096]{1,0:T(8,128)S(1)}, f32[2048,4096]{1,0:T(8,128)}, u32[]{:S(2)}) copy-start(f32[2048,4096]{1,0:T(8,128)} %get-tuple-element.129) | copy-start | bytes 100663296
  215.4 90.2 %copy-start.17 = (f32[2048,128]{1,0:T(8,128)}, f32[2048,128]{1,0:T(8,128)S(1)}, u32[]{:S(2)}) copy-start(f32[2048,128]{1,0:T(8,128)S(1)} %fusion.49) | copy-start | bytes 3145732
  276.4 38.8 %collective-permute-start.2 = (bf16[2,256,6144]{2,1,0:T(8,128)(2,1)}, bf16[2,256,6144]{2,1,0:T(8,128)(2,1)}, u32[]{:S(2)}, u32[]{:S(2)}) collective-permute-start(bf16[2,256,6144]{2,1,0:T(8,128)(2,1)} %bitcast.214), channel_id=1, source_target_pairs={{0,1},{1,0},{2,3},{3,2},{4,5},{5,4},{6,7},{7,6},{8,9},{9,8},{10,11... | collective-permute-start | bytes 18874376 | tf_op jit(solution)/shard_map/ppermute | solution.py:83
  276.4 29.3 %collective-permute-start.1 = (bf16[2,512,1024]{2,1,0:T(8,128)(2,1)}, bf16[2,512,1024]{2,1,0:T(8,128)(2,1)}, u32[]{:S(2)}, u32[]{:S(2)}) collective-permute-start(bf16[2,512,1024]{2,1,0:T(8,128)(2,1)} %bitcast.246), channel_id=1, source_target_pairs={{0,1},{1,0},{2,3},{3,2},{4,5},{5,4},{6,7},{7,6},{8,9},{9,8},{10,11... | collective-permute-start | bytes 6291464 | tf_op jit(solution)/shard_map/ppermute | solution.py:83
  276.9 34.1 %collective-permute-start.3 = (bf16[2,768,1024]{2,1,0:T(8,128)(2,1)}, bf16[2,768,1024]{2,1,0:T(8,128)(2,1)}, u32[]{:S(2)}, u32[]{:S(2)}) collective-permute-start(bf16[2,768,1024]{2,1,0:T(8,128)(2,1)} %bitcast.236), channel_id=1, source_target_pairs={{0,1},{1,0},{2,3},{3,2},{4,5},{5,4},{6,7},{7,6},{8,9},{9,8},{10,11... | collective-permute-start | bytes 9437192 | tf_op jit(solution)/shard_map/ppermute | solution.py:83
  277.3 28.5 %copy-start.33 = (bf16[1024,1024]{1,0:T(8,128)(2,1)S(1)}, bf16[1024,1024]{1,0:T(8,128)(2,1)}, u32[]{:S(2)}) copy-start(bf16[1024,1024]{1,0:T(8,128)(2,1)} %all-gather.29.cloned.1.call-done) | copy-start | bytes 6291460
  309.4 26.3 %copy-start.57 = (f32[128]{0:T(128)}, f32[128]{0:T(128)S(1)}, u32[]{:S(2)}) copy-start(f32[128]{0:T(128)S(1)} %add_rsqrt_fusion.2) | copy-start | bytes 1540
  315.2 9.2 %copy-start.2 = (bf16[2,2,768,1024]{3,2,1,0:T(8,128)(2,1)}, bf16[2,2,768,1024]{3,2,1,0:T(8,128)(2,1)S(1)}, u32[]{:S(2)}) copy-start(bf16[2,2,768,1024]{3,2,1,0:T(8,128)(2,1)S(1)} %pad_maximum_fusion.2) | copy-start | bytes 18874372
  339.1 108.9 %all-gather.17.cloned.1.call-start = ((), (), s32[]{:S(2)}) async-start(), calls=%async_computation.10 | async-start | bytes 7864320 | tf_op jit(solution)/shard_map/all_gather | solution.py:255
  344.3 7.9 copy-start.14
  345.9 24.3 %all-to-all-start.3 = ((bf16[32,128,128]{1,2,0:T(8,128)(2,1)}), bf16[32,128,128]{1,2,0:T(8,128)(2,1)S(1)}, u32[]{:S(2)}, u32[]{:S(2)}) async-start(bf16[32,128,128]{1,2,0:T(8,128)(2,1)} %bitcast_select_fusion.1), calls=%async_computation.3 | async-start | bytes 2097152 | tf_op jit(solution)/shard_map/all_to_all | solution.py:160
  370.2 28.6 %all-to-all-start.2 = ((bf16[128,4,1792]{2,0,1:T(8,128)(2,1)}), bf16[128,4,1792]{2,0,1:T(8,128)(2,1)}, u32[]{:S(2)}, u32[]{:S(2)}) async-start(bf16[128,4,1792]{2,0,1:T(8,128)(2,1)} %pad_maximum_fusion.10), calls=%async_computation.2 | async-start | bytes 3670016 | tf_op jit(solution)/shard_map/all_to_all | solution.py:248
  374.6 212.9 %reduce-scatter.9.cloned.1.call-start = ((), (), s32[]{:S(2)}) async-start(), calls=%async_computation.15 | async-start | bytes 7208960 | tf_op jit(solution)/shard_map/reduce_scatter | solution.py:94
  456.1 11.7 %copy-start.18 = (f32[2048,128]{1,0:T(8,128)S(1)}, f32[2048,128]{1,0:T(8,128)}, u32[]{:S(2)}) copy-start(f32[2048,128]{1,0:T(8,128)} %copy-done.17) | copy-start | bytes 3145732
  468.2 20.0 %copy-start.45 = (bf16[16,128,128]{2,1,0:T(8,128)(2,1)S(1)}, bf16[16,128,128]{2,1,0:T(8,128)(2,1)}, u32[]{:S(2)}) copy-start(bf16[16,128,128]{2,1,0:T(8,128)(2,1)} %copy-done.44) | copy-start | bytes 1572868
  488.2 9.3 %copy-start.36 = (bf16[32,128,128]{2,1,0:T(8,128)(2,1)S(1)}, bf16[32,128,128]{2,1,0:T(8,128)(2,1)}, u32[]{:S(2)}) copy-start(bf16[32,128,128]{2,1,0:T(8,128)(2,1)} %copy-done.35) | copy-start | bytes 3145732
  511.9 8.2 copy-start.65
  511.9 8.8 %copy-start.52 = (f32[128,8]{0,1:T(8,128)S(1)}, f32[128,8]{0,1:T(8,128)}, u32[]{:S(2)}) copy-start(f32[128,8]{0,1:T(8,128)} %copy-done.51) | copy-start | bytes 12292
  511.9 11.7 %copy-start.49 = (f32[128,16]{0,1:T(8,128)S(1)}, f32[128,16]{0,1:T(8,128)}, u32[]{:S(2)}) copy-start(f32[128,16]{0,1:T(8,128)} %copy-done.48) | copy-start | bytes 24580
  511.9 55.5 %all-to-all-start.4 = ((bf16[32,128,384]{1,2,0:T(8,128)(2,1)}), bf16[32,128,384]{1,2,0:T(8,128)(2,1)S(1)}, u32[]{:S(2)}, u32[]{:S(2)}) async-start(bf16[32,128,384]{1,2,0:T(8,128)(2,1)} %pad_maximum_fusion.7), calls=%async_computation.4 | async-start | bytes 6291456 | tf_op jit(solution)/shard_map/all_to_all | solution.py:160
  519.4 112.8 %all-gather.19.cloned.1.call-start = ((), (), s32[]{:S(2)}) async-start(), calls=%async_computation.11 | async-start | bytes 5242880 | tf_op jit(solution)/shard_map/all_gather | solution.py:319
  586.8 74.2 %reduce-scatter.11.cloned.1.call-start = ((), (), s32[]{:S(2)}) async-start(), calls=%async_computation.16 | async-start | bytes 1802240 | tf_op jit(solution)/shard_map/reduce_scatter | solution.py:95
  587.6 106.5 %reduce-scatter.5.cloned.1.call-start = ((), (), s32[]{:S(2)}) async-start(), calls=%async_computation.12 | async-start | bytes 2703360 | tf_op jit(solution)/shard_map/reduce_scatter | solution.py:94
  637.3 109.7 %copy-start.4 = (f32[128,1024]{1,0:T(8,128)S(1)}, f32[128,1024]{1,0:T(8,128)}, u32[]{:S(2)}) copy-start(f32[128,1024]{1,0:T(8,128)} %copy-done.3) | copy-start | bytes 1572868
  637.3 109.7 %copy-start.27 = (bf16[128,3072]{1,0:T(8,128)(2,1)S(1)}, bf16[128,3072]{1,0:T(8,128)(2,1)}, u32[]{:S(2)}) copy-start(bf16[128,3072]{1,0:T(8,128)(2,1)} %get-tuple-element.104) | copy-start | bytes 2359300
  637.3 80.4 %reduce-scatter.7.cloned.1.call-start = ((), (), s32[]{:S(2)}) async-start(), calls=%async_computation.13 | async-start | bytes 675840 | tf_op jit(solution)/shard_map/reduce_scatter | solution.py:95
  661.0 33.2 %collective-permute-start.5 = (bf16[16,11264]{1,0:T(8,128)(2,1)}, bf16[16,11264]{1,0:T(8,128)(2,1)S(1)}, u32[]{:S(2)}, u32[]{:S(2)}) collective-permute-start(bf16[16,11264]{1,0:T(8,128)(2,1)} %reduce-scatter.11.cloned.1.call-done), channel_id=1, source_target_pairs={{0,64},{64,0},{1,65},{65,1},{2,66},{66,2},{3,67},{67,3},{4,68},{68... | collective-permute-start | bytes 1081352 | tf_op jit(solution)/shard_map/ppermute | solution.py:96
  694.1 52.8 %all-gather.23.cloned.1.call-start = ((), (), s32[]{:S(2)}) async-start(), calls=%async_computation.17 | async-start | bytes 1802240 | tf_op jit(solution)/shard_map/all_gather | solution.py:99
  696.0 84.2 %all-gather.21.cloned.1.call-start = ((), (), s32[]{:S(2)}) async-start(), calls=%async_computation.14 | async-start | bytes 2703360 | tf_op jit(solution)/shard_map/all_gather | solution.py:100
  717.8 6.7 collective-permute-start.4
  740.7 102.5 %all-gather.25.cloned.1.call-start = ((), (), s32[]{:S(2)}) async-start(), calls=%async_computation.18 | async-start | bytes 7208960 | tf_op jit(solution)/shard_map/all_gather | solution.py:100
  (51 other events, 167.4 us)
Sparse Core Ops, SparseCore 0:
  10.4 61.7 all-gather.26
  73.9 36.6 all-gather.28
  112.2 73.0 all-gather.32
  187.3 89.0 all-gather.30
  339.2 36.8 all-gather.14
  378.2 69.6 all-gather.16
  456.3 59.4 reduce-scatter.8
  587.0 45.2 all-gather.18
  634.7 26.3 reduce-scatter.10
  663.9 30.2 reduce-scatter.4
  696.6 21.0 reduce-scatter.6
  719.8 27.0 all-gather.22
  748.6 31.5 all-gather.20
  781.8 61.4 all-gather.24

commit v10 on v9

--- a/solution.py
+++ b/solution.py
@@ -90,14 +90,21 @@
     return gather_cores(gather_across(values), values.shape)
 
 
-def reduce_ctx(packed):
+def scatter_ctx(packed):
     part = lax.psum_scatter(packed, "z", scatter_dimension=0, tiled=True)
     part = lax.psum_scatter(part, "x", scatter_dimension=0, tiled=True)
-    part = (part.astype(jnp.float32) + lax.ppermute(part, "yh", [(0, 1), (1, 0)]).astype(jnp.float32)).astype(
+    return (part.astype(jnp.float32) + lax.ppermute(part, "yh", [(0, 1), (1, 0)]).astype(jnp.float32)).astype(
         part.dtype
     )
+
+
+def gather_ctx(part):
     part = lax.all_gather(part, "x", axis=0, tiled=True)
     return lax.all_gather(part, "z", axis=0, tiled=True).astype(jnp.float32)
+
+
+def reduce_ctx(packed):
+    return gather_ctx(scatter_ctx(packed))
 
 
 def on_device(
@@ -269,7 +276,7 @@
         exchange(to_heads(mixed_gradient.reshape(local_rows, HQ, HEAD_SIZE)))
     )
     mlp_packed, head_out_grad = lax.optimization_barrier((mlp_packed, head_out_grad))
-    mlp_reduced = reduce_ctx(mlp_packed)
+    mlp_part = scatter_ctx(mlp_packed)
     out_grad_f = head_out_grad.astype(jnp.float32)
     delta = jnp.sum(out_grad_f * head_mixed, axis=-1, keepdims=True)
     probabilities = jnp.exp(head_scores() - log_total)
@@ -283,6 +290,8 @@
         jnp.concatenate([key_part, value_part], axis=-1).astype(jnp.bfloat16).reshape(
             ctx_size, local_rows, 2 * HEAD_SIZE),
     ], axis=-1))
+    mlp_part, returned = lax.optimization_barrier((mlp_part, returned))
+    mlp_reduced = gather_ctx(mlp_part)
     query_grad_rows = own_heads(returned[..., :HEAD_SIZE]).astype(jnp.float32)
     kv_parts = returned[..., HEAD_SIZE:].astype(jnp.float32).reshape(
         halves, KEY_VALUE_HEADS, group, local_rows, 2 * HEAD_SIZE)

time: 871 us -> 889 us (1.021)
  waiting for transfers between devices: 471 us -> 481 us
    all_to_all x3, waiting for transfers between devices: 97.4 us -> 57.9 us  [exchange(): return lax.all_to_all(values, CTX, split_axis=0, concat_axis=0, tiled=True)]
    ppermute x2, waiting for transfers between devices: 3.72 us -> 41.7 us  [scatter_ctx(): lax.ppermute(part, 'yh', [(0, 1), (1, 0)]).astype(jnp.float32)]
    reduce_scatter x4, waiting for transfers between devices: 75.4 us -> 93.1 us  [the longest x2 68.7 us: scatter_ctx(): part = lax.psum_scatter(packed, 'z', scatter_dimension=0, tiled=True)]
  transfers between devices with their start and end apart: 24 -> 24, of which waited for: 16 -> 16; matrix products, arithmetic and copies ran while one was open for 26% -> 24% of each run, Pallas kernels for 0% -> 0%
where the time goes in v10:
time: 889 us; the launch traced here: 880 us
  waiting for transfers between devices  481 us (54%)
  matrix products  120 us (13%)
  other arithmetic  98 us (11%)
  local copies, waits for them, and re-layouts  70.6 us (8%)
  blocking collectives  57.3 us (6%)
  starting transfers between devices  35.1 us (4%)
  between operations  17.1 us (2%)
    all_gather x4, waiting for transfers between devices, gather_across(): return lax.all_gather(values, 'yl', axis=0, tiled=False)  121 us
    reduce_scatter x2, waiting for transfers between devices, scatter_ctx(): part = lax.psum_scatter(packed, 'z', scatter_dimension=0, tiled=True)  68.7 us
    all_gather x2, waiting for transfers between devices, gather_ctx(): return lax.all_gather(part, 'z', axis=0, tiled=True).astype(jnp.float32)  58.2 us
    all_to_all x3, waiting for transfers between devices, exchange(): return lax.all_to_all(values, CTX, split_axis=0, concat_axis=0, tiled=True)  57.9 us
    dot_general x5, matrix products, right_dot(): lax.dot_general(left_side, right_side, (((1,), (1,)), ((), ())), preferre...  41.7 us
    ppermute x2, waiting for transfers between devices, scatter_ctx(): lax.ppermute(part, 'yh', [(0, 1), (1, 0)]).astype(jnp.float32)  41.7 us
    all_gather x1, waiting for transfers between devices, on_device(): gate_up_rows = lax.all_gather(gate_up_grad, FSDP, axis=0, tiled=True)  40 us
    dot_general x6, matrix products, left_dot(): lax.dot_general(left_side, right_side, (((0,), (0,)), ((), ())), preferre...  35.3 us
  transfers between devices with their start and end apart: 24, of which 16 were waited for; matrix products, arithmetic and copies ran while one was open for 24% of the time, Pallas kernels for 0%

profile of v10, /device:TPU:0, one launch (start us, length us, event | category | flops | bytes accessed | tf_op | source)
XLA Modules:
  0.0 879.7 jit_solution(10061561753455537186)
XLA Ops:
  10.4 61.8 %all-gather.27.cloned.1.call-done = bf16[512,4096]{1,0:T(8,128)(2,1)} async-done(((bf16[256,4096]{1,0:T(8,128)(2,1)}), bf16[512,4096]{1,0:T(8,128)(2,1)}) %all-gather.27.cloned.1.call-update) | async-done | bytes 4194320 | tf_op jit(solution)/shard_map/all_gather | solution.py:79
  74.0 5.8 collective-permute-done
  79.7 5.2 select_bitcast_fusion.3
  84.9 6.6 pad_maximum_fusion.1
  91.4 4.7 fusion.32
  112.9 9.4 %all-to-all-start = ((bf16[32,128,384]{2,1,0:T(8,128)(2,1)}), bf16[32,128,384]{2,1,0:T(8,128)(2,1)S(1)}, u32[]{:S(2)}, u32[]{:S(2)}) async-start(bf16[32,128,384]{2,1,0:T(8,128)(2,1)} %pad_maximum_fusion.5), calls=%async_computation | async-start | bytes 6291456 | tf_op jit(solution)/shard_map/all_to_all | solution.py:167
  122.3 4.3 pad_maximum_fusion.6
  127.0 42.5 %all-to-all-done = bf16[32,128,384]{2,1,0:T(8,128)(2,1)S(1)} async-done(((bf16[32,128,384]{2,1,0:T(8,128)(2,1)}), bf16[32,128,384]{2,1,0:T(8,128)(2,1)S(1)}, u32[]{:S(2)}, u32[]{:S(2)}) %all-to-all-start) | async-done | bytes 3145760 | tf_op jit(solution)/shard_map/all_to_all | solution.py:167
  170.1 13.7 %fusion.48 = (f32[2048]{0:T(1024)S(1)}, f32[2048,4096]{1,0:T(8,128)}) fusion(bf16[2048,128]{1,0:T(8,128)(2,1)S(1)} %bitcast.256, bf16[4096,128]{1,0:T(8,128)(2,1)S(1)} %bitcast.253, s32[2048]{0:T(1024)S(1)} %dynamic-slice-done, s32[4096]{0:T(1024)S(1)} %copy-done.53), kind=kOutput, calls=%fused_computation.176 | convolution fusion | flops 2181036032 | bytes 35160064 | tf_op jit(solution)/shard_map/qd,kd->qk/dot_general | solution.py:204
  183.8 14.9 %exponential_reduce_fusion = f32[2048]{0:T(1024)S(1)} fusion(f32[2048,4096]{1,0:T(8,128)} %get-tuple-element.133, f32[2048]{0:T(1024)S(1)} %get-tuple-element.132), kind=kLoop, calls=%fused_computation.2 | loop fusion | flops 16775168 | bytes 33570816 | tf_op jit(solution)/shard_map/reduce_sum | solution.py:211
  198.8 5.3 copy-done
  204.1 8.8 %fusion = bf16[2048,4096]{1,0:T(8,128)(2,1)} fusion(f32[2048,4096]{1,0:T(8,128)S(1)} %copy-done, f32[2048]{0:T(1024)S(1)} %log_add_fusion), kind=kLoop, calls=%fused_computation.4 | loop fusion | flops 16777216 | bytes 50339840 | tf_op jit(solution)/shard_map/convert_element_type | solution.py:212
  212.9 9.1 %fusion.49 = f32[2048,128]{1,0:T(8,128)S(1)} fusion(bf16[2048,4096]{1,0:T(8,128)(2,1)} %fusion, bf16[4096,128]{1,0:T(8,128)(2,1)S(1)} %bitcast.225), kind=kOutput, calls=%fused_computation.177 | convolution fusion | flops 2147483648 | bytes 18874368 | tf_op jit(solution)/shard_map/dot_general | solution.py:213
  222.1 59.6 %all-gather.31.cloned.1.call-done = bf16[512,6144]{1,0:T(8,128)(2,1)} async-done(((bf16[256,6144]{1,0:T(8,128)(2,1)}), bf16[512,6144]{1,0:T(8,128)(2,1)}) %all-gather.31.cloned.1.call-update) | async-done | bytes 6291472 | tf_op jit(solution)/shard_map/all_gather | solution.py:79
  282.7 28.2 %all_to_all.35 = bf16[32,128,128]{1,2,0:T(8,128)(2,1)S(1)} all-to-all(bf16[32,128,128]{1,2,0:T(8,128)(2,1)S(1)} %bitcast_select_fusion.2), channel_id=1, replica_groups=mesh['yh'=2,'x'=4,'z'=4,'yl'=2,'c'=2] {'yh','x','z'}, dimensions={0} | all-to-all | bytes 2097152 | tf_op jit(solution)/shard_map/all_to_all | solution.py:167
  321.6 4.9 select_bitcast_fusion.1
  329.6 4.0 multiply_convert_fusion.2
  333.7 7.2 multiply_reduce_fusion.5
  345.8 3.7 fusion.4
  351.3 5.1 all-to-all-start.3
  360.2 15.4 %all-to-all-done.3 = bf16[32,128,128]{1,2,0:T(8,128)(2,1)S(1)} async-done(((bf16[32,128,128]{1,2,0:T(8,128)(2,1)}), bf16[32,128,128]{1,2,0:T(8,128)(2,1)S(1)}, u32[]{:S(2)}, u32[]{:S(2)}) %all-to-all-start.3) | async-done | bytes 1048608 | tf_op jit(solution)/shard_map/all_to_all | solution.py:167
  375.6 4.4 all-to-all-start.2
  380.4 24.2 %all-to-all-done.2 = bf16[128,4,1792]{2,0,1:T(8,128)(2,1)} async-done(((bf16[128,4,1792]{2,0,1:T(8,128)(2,1)}), bf16[128,4,1792]{2,0,1:T(8,128)(2,1)}, u32[]{:S(2)}, u32[]{:S(2)}) %all-to-all-start.2) | async-done | bytes 1835040 | tf_op jit(solution)/shard_map/all_to_all | solution.py:255
  407.1 3.7 convolution_convert_fusion.4
  413.4 40.0 %all-gather.17.cloned.1.call-done = bf16[512,6144]{1,0:T(8,128)(2,1)} async-done(((bf16[128,6144]{1,0:T(8,128)(2,1)}), bf16[512,6144]{1,0:T(8,128)(2,1)}) %all-gather.17.cloned.1.call-update) | async-done | bytes 6291472 | tf_op jit(solution)/shard_map/all_gather | solution.py:262
  453.4 4.7 convolution_convert_fusion
  458.1 3.5 pad_maximum_fusion.3
  463.1 20.2 %multiply_convert_fusion = bf16[2048,4096]{1,0:T(8,128)(2,1)} fusion(f32[2048,4096]{1,0:T(8,128)} %get-tuple-element.133, f32[2048]{0:T(1024)S(1)} %multiply_reduce_fusion.2, f32[2048]{0:T(1024)S(1)} %log_add_fusion, bf16[2048,128]{1,0:T(8,128)(2,1)S(1)} %bitcast.219, bf16[4096,128]{1,0:T(8,128)(2,1)S(1)} %bitcast.226), kind=kOutput, calls=%fused_computation | convolution fusion | flops 2181038080 | bytes 51920896 | tf_op jit(solution)/shard_map/dot_general | solution.py:73
  483.4 37.5 %reduce-scatter.5.cloned.1.call-done = bf16[64,11264]{1,0:T(8,128)(2,1)} async-done(((bf16[256,11264]{1,0:T(8,128)(2,1)}), bf16[64,11264]{1,0:T(8,128)(2,1)}) %reduce-scatter.5.cloned.1.call-update) | async-done | bytes 1441808 | tf_op jit(solution)/shard_map/reduce_scatter | solution.py:94
  520.9 8.2 fusion.2
  529.6 11.7 %fusion.1 = bf16[4096,128]{1,0:T(8,128)(2,1)} fusion(bf16[2048,4096]{1,0:T(8,128)(2,1)} %multiply_convert_fusion, bf16[2048,128]{1,0:T(8,128)(2,1)} %bitcast.257), kind=kOutput, calls=%fused_computation.14 | convolution fusion | flops 2148532224 | bytes 18350080 | tf_op jit(solution)/shard_map/dot_general | solution.py:67
  542.9 9.6 %convolution_convert_fusion.2 = bf16[4096,128]{1,0:T(8,128)(2,1)} fusion(bf16[2048,4096]{1,0:T(8,128)(2,1)} %fusion, bf16[2048,128]{1,0:T(8,128)(2,1)S(1)} %bitcast.220), kind=kOutput, calls=%fused_computation.15 | convolution fusion | flops 2148007936 | bytes 18350080 | tf_op jit(solution)/shard_map/dot_general | solution.py:67
  555.9 8.1 all-to-all-start.4
  564.1 3.4 collective-permute-start.4
  574.5 38.0 %collective-permute-done.4 = bf16[16,11264]{1,0:T(8,128)(2,1)} collective-permute-done((bf16[16,11264]{1,0:T(8,128)(2,1)}, bf16[16,11264]{1,0:T(8,128)(2,1)}, u32[]{:S(2)}, u32[]{:S(2)}) %collective-permute-start.4) | collective-permute-done | bytes 360480 | tf_op jit(solution)/shard_map/ppermute | solution.py:96
  638.2 6.6 fusion.28
  644.7 15.5 %all-reduce.5 = (f32[1024]{0:T(1024)S(1)}, f32[1024]{0:T(1024)S(1)}, bf16[128]{0:T(256)(128)(2,1)S(1)}, bf16[128]{0:T(256)(128)(2,1)S(1)}) all-reduce(f32[1024]{0:T(1024)S(1)} %get-tuple-element.83, f32[1024]{0:T(1024)S(1)} %copy-done.54, ...), channel_id=8, replica_groups=mesh['yh'=2,'x'=4,'z'=4,'yl'=2,'c'=2] {'yl','c'}, use_global_device_ids=true, to_apply=%region_16.17.clone | all-reduce | flops 2304 | bytes 17920
  670.1 10.9 %all-gather.19.cloned.1.call-done = bf16[512,4096]{1,0:T(8,128)(2,1)} async-done(((bf16[128,4096]{1,0:T(8,128)(2,1)}), bf16[512,4096]{1,0:T(8,128)(2,1)}) %all-gather.19.cloned.1.call-update) | async-done | bytes 4194320 | tf_op jit(solution)/shard_map/all_gather | solution.py:328
  681.0 3.6 convolution_convert_fusion.1
  686.9 31.2 %reduce-scatter.9.cloned.1.call-done = bf16[64,4224]{1,0:T(8,128)(2,1)} async-done(((bf16[256,4224]{1,0:T(8,128)(2,1)}), bf16[64,4224]{1,0:T(8,128)(2,1)}) %reduce-scatter.9.cloned.1.call-update) | async-done | bytes 540688 | tf_op jit(solution)/shard_map/reduce_scatter | solution.py:94
  718.2 26.7 %all-gather.23.cloned.1.call-done = bf16[64,11264]{1,0:T(8,128)(2,1)} async-done(((bf16[16,11264]{1,0:T(8,128)(2,1)}), bf16[64,11264]{1,0:T(8,128)(2,1)}) %all-gather.23.cloned.1.call-update) | async-done | bytes 1441808 | tf_op jit(solution)/shard_map/all_gather | solution.py:102
  745.0 24.4 %reduce-scatter.11.cloned.1.call-done = bf16[16,4224]{1,0:T(8,128)(2,1)} async-done(((bf16[64,4224]{1,0:T(8,128)(2,1)}), bf16[16,4224]{1,0:T(8,128)(2,1)}) %reduce-scatter.11.cloned.1.call-update) | async-done | bytes 135184 | tf_op jit(solution)/shard_map/reduce_scatter | solution.py:95
  772.4 3.7 collective-permute-done.5
  777.0 13.6 %all_gather.56 = bf16[64,4224]{1,0:T(8,128)(2,1)} all-gather(bf16[16,4224]{1,0:T(8,128)(2,1)S(1)} %add_convert_fusion.2), channel_id=1, replica_groups=mesh['yh'=2,'x'=4,'z'=4,'yl'=2,'c'=2] {'x'}, dimensions={0}, use_global_device_ids=true | all-gather | bytes 675840 | tf_op jit(solution)/shard_map/all_gather | solution.py:102
  790.7 4.6 fusion.6
  796.4 36.0 %all-gather.25.cloned.1.call-done = bf16[256,11264]{1,0:T(8,128)(2,1)} async-done(((bf16[64,11264]{1,0:T(8,128)(2,1)}), bf16[256,11264]{1,0:T(8,128)(2,1)}) %all-gather.25.cloned.1.call-update) | async-done | bytes 5767184 | tf_op jit(solution)/shard_map/all_gather | solution.py:103
  832.4 6.3 fusion.43
  843.7 22.3 %all-gather.21.cloned.1.call-done = bf16[256,4224]{1,0:T(8,128)(2,1)} async-done(((bf16[64,4224]{1,0:T(8,128)(2,1)}), bf16[256,4224]{1,0:T(8,128)(2,1)}) %all-gather.21.cloned.1.call-update) | async-done | bytes 2162704 | tf_op jit(solution)/shard_map/all_gather | solution.py:103
  (330 shorter events, 120.0 us)
Async XLA Ops:
  7.2 65.0 %all-gather.27.cloned.1.call-start = ((), (), s32[]{:S(2)}) async-start(), calls=%async_computation.19 | async-start | bytes 6291456 | tf_op jit(solution)/shard_map/all_gather | solution.py:79
  10.3 62.9 %copy-start.67 = (s32[1,64]{1,0:T(1,128)S(1)}, s32[1,64]{1,0:T(1,128)}, u32[]{:S(2)}) copy-start(s32[1,64]{1,0:T(1,128)} %param.24) | copy-start | bytes 772
  10.3 63.1 %copy-start.12 = (bf16[1,128,1024]{2,1,0:T(8,128)(2,1)S(1)}, bf16[1,128,1024]{2,1,0:T(8,128)(2,1)}, u32[]{:S(2)}) copy-start(bf16[1,128,1024]{2,1,0:T(8,128)(2,1)} %param.22) | copy-start | bytes 786436
  10.3 211.7 %all-gather.29.cloned.1.call-start = ((), (), s32[]{:S(2)}) async-start(), calls=%async_computation.20 | async-start | bytes 3145728 | tf_op jit(solution)/shard_map/all_gather | solution.py:79
  72.2 7.5 collective-permute-start
  72.3 149.8 %all-gather.33.cloned.1.call-start = ((), (), s32[]{:S(2)}) async-start(), calls=%async_computation.22 | async-start | bytes 4718592 | tf_op jit(solution)/shard_map/all_gather | solution.py:79
  73.6 283.1 %copy-start.58 = (f32[128]{0:T(128)}, f32[128]{0:T(128)S(1)}, u32[]{:S(2)}) copy-start(f32[128]{0:T(128)S(1)} %add_rsqrt_fusion.3) | copy-start | bytes 1540
  74.0 33.2 %copy-start.41 = (f32[128,64]{0,1:T(8,128)}, f32[128,64]{0,1:T(8,128)S(1)}, u32[]{:S(2)}) copy-start(f32[128,64]{0,1:T(8,128)S(1)} %get-tuple-element.126) | copy-start | bytes 98308
  74.0 33.2 %copy-start.43 = (f32[128,64]{0,1:T(8,128)}, f32[128,64]{0,1:T(8,128)S(1)}, u32[]{:S(2)}) copy-start(f32[128,64]{0,1:T(8,128)S(1)} %get-tuple-element.127) | copy-start | bytes 98308
  112.9 56.6 %all-to-all-start = ((bf16[32,128,384]{2,1,0:T(8,128)(2,1)}), bf16[32,128,384]{2,1,0:T(8,128)(2,1)S(1)}, u32[]{:S(2)}, u32[]{:S(2)}) async-start(bf16[32,128,384]{2,1,0:T(8,128)(2,1)} %pad_maximum_fusion.5), calls=%async_computation | async-start | bytes 6291456 | tf_op jit(solution)/shard_map/all_to_all | solution.py:167
  122.3 159.4 %all-gather.31.cloned.1.call-start = ((), (), s32[]{:S(2)}) async-start(), calls=%async_computation.21 | async-start | bytes 9437184 | tf_op jit(solution)/shard_map/all_gather | solution.py:79
  126.7 277.9 %all-gather.15.cloned.1.call-start = ((), (), s32[]{:S(2)}) async-start(), calls=%async_computation.9 | async-start | bytes 2621440 | tf_op jit(solution)/shard_map/all_gather | solution.py:263
  126.9 43.2 %copy-start.53 = (s32[4096]{0:T(1024)S(1)}, s32[4096]{0:T(1024)}, u32[]{:S(2)}) copy-start(s32[4096]{0:T(1024)} %copy-done.52) | copy-start | bytes 49156
  126.9 43.2 %dynamic-slice-start = ((s32[4096]{0:T(1024)}, s32[]{:T(128)}), s32[2048]{0:T(1024)S(1)}, s32[]{:S(2)}) async-start(s32[4096]{0:T(1024)} %copy-done.52, s32[]{:T(128)} %select_n.88), calls=%async_computation.26 | async-start | bytes 16896 | tf_op jit(solution)/shard_map/dynamic_slice | solution.py:141
  170.0 13.8 %copy-start.37 = (bf16[32,128,128]{2,1,0:T(8,128)(2,1)}, bf16[32,128,128]{2,1,0:T(8,128)(2,1)S(1)}, u32[]{:S(2)}) copy-start(bf16[32,128,128]{2,1,0:T(8,128)(2,1)S(1)} %get-tuple-element.110) | copy-start | bytes 3145732
  170.0 42.8 %copy-start.19 = (bf16[32,128,128]{2,1,0:T(8,128)(2,1)}, bf16[32,128,128]{2,1,0:T(8,128)(2,1)S(1)}, u32[]{:S(2)}) copy-start(bf16[32,128,128]{2,1,0:T(8,128)(2,1)S(1)} %get-tuple-element.109) | copy-start | bytes 3145732
  170.1 13.7 %copy-start.45 = (bf16[16,128,128]{2,1,0:T(8,128)(2,1)}, bf16[16,128,128]{2,1,0:T(8,128)(2,1)S(1)}, u32[]{:S(2)}) copy-start(bf16[16,128,128]{2,1,0:T(8,128)(2,1)S(1)} %constant_dynamic-slice_fusion.2) | copy-start | bytes 1572868
  183.8 20.2 %copy-start = (f32[2048,4096]{1,0:T(8,128)S(1)}, f32[2048,4096]{1,0:T(8,128)}, u32[]{:S(2)}) copy-start(f32[2048,4096]{1,0:T(8,128)} %get-tuple-element.133) | copy-start | bytes 100663296
  222.0 88.9 %copy-start.21 = (f32[2048,128]{1,0:T(8,128)}, f32[2048,128]{1,0:T(8,128)S(1)}, u32[]{:S(2)}) copy-start(f32[2048,128]{1,0:T(8,128)S(1)} %fusion.49) | copy-start | bytes 3145732
  281.7 38.8 %collective-permute-start.2 = (bf16[2,256,6144]{2,1,0:T(8,128)(2,1)}, bf16[2,256,6144]{2,1,0:T(8,128)(2,1)}, u32[]{:S(2)}, u32[]{:S(2)}) collective-permute-start(bf16[2,256,6144]{2,1,0:T(8,128)(2,1)} %bitcast.214), channel_id=1, source_target_pairs={{0,1},{1,0},{2,3},{3,2},{4,5},{5,4},{6,7},{7,6},{8,9},{9,8},{10,11... | collective-permute-start | bytes 18874376 | tf_op jit(solution)/shard_map/ppermute | solution.py:83
  281.7 29.3 %collective-permute-start.1 = (bf16[2,512,1024]{2,1,0:T(8,128)(2,1)}, bf16[2,512,1024]{2,1,0:T(8,128)(2,1)}, u32[]{:S(2)}, u32[]{:S(2)}) collective-permute-start(bf16[2,512,1024]{2,1,0:T(8,128)(2,1)} %bitcast.246), channel_id=1, source_target_pairs={{0,1},{1,0},{2,3},{3,2},{4,5},{5,4},{6,7},{7,6},{8,9},{9,8},{10,11... | collective-permute-start | bytes 6291464 | tf_op jit(solution)/shard_map/ppermute | solution.py:83
  282.2 34.1 %collective-permute-start.3 = (bf16[2,768,1024]{2,1,0:T(8,128)(2,1)}, bf16[2,768,1024]{2,1,0:T(8,128)(2,1)}, u32[]{:S(2)}, u32[]{:S(2)}) collective-permute-start(bf16[2,768,1024]{2,1,0:T(8,128)(2,1)} %bitcast.236), channel_id=1, source_target_pairs={{0,1},{1,0},{2,3},{3,2},{4,5},{5,4},{6,7},{7,6},{8,9},{9,8},{10,11... | collective-permute-start | bytes 9437192 | tf_op jit(solution)/shard_map/ppermute | solution.py:83
  282.5 28.5 %copy-start.36 = (bf16[1024,1024]{1,0:T(8,128)(2,1)S(1)}, bf16[1024,1024]{1,0:T(8,128)(2,1)}, u32[]{:S(2)}) copy-start(bf16[1024,1024]{1,0:T(8,128)(2,1)} %all-gather.29.cloned.1.call-done) | copy-start | bytes 6291460
  314.6 26.3 %copy-start.56 = (f32[128]{0:T(128)}, f32[128]{0:T(128)S(1)}, u32[]{:S(2)}) copy-start(f32[128]{0:T(128)S(1)} %add_rsqrt_fusion.2) | copy-start | bytes 1540
  320.5 9.2 %copy-start.2 = (bf16[2,2,768,1024]{3,2,1,0:T(8,128)(2,1)}, bf16[2,2,768,1024]{3,2,1,0:T(8,128)(2,1)S(1)}, u32[]{:S(2)}) copy-start(bf16[2,2,768,1024]{3,2,1,0:T(8,128)(2,1)S(1)} %pad_maximum_fusion.2) | copy-start | bytes 18874372
  344.3 109.1 %all-gather.17.cloned.1.call-start = ((), (), s32[]{:S(2)}) async-start(), calls=%async_computation.10 | async-start | bytes 7864320 | tf_op jit(solution)/shard_map/all_gather | solution.py:262
  349.7 7.9 copy-start.18
  350.1 7.7 copy-start.27
  351.3 24.3 %all-to-all-start.3 = ((bf16[32,128,128]{1,2,0:T(8,128)(2,1)}), bf16[32,128,128]{1,2,0:T(8,128)(2,1)S(1)}, u32[]{:S(2)}, u32[]{:S(2)}) async-start(bf16[32,128,128]{1,2,0:T(8,128)(2,1)} %bitcast_select_fusion.1), calls=%async_computation.3 | async-start | bytes 2097152 | tf_op jit(solution)/shard_map/all_to_all | solution.py:167
  375.6 29.0 %all-to-all-start.2 = ((bf16[128,4,1792]{2,0,1:T(8,128)(2,1)}), bf16[128,4,1792]{2,0,1:T(8,128)(2,1)}, u32[]{:S(2)}, u32[]{:S(2)}) async-start(bf16[128,4,1792]{2,0,1:T(8,128)(2,1)} %pad_maximum_fusion.10), calls=%async_computation.2 | async-start | bytes 3670016 | tf_op jit(solution)/shard_map/all_to_all | solution.py:255
  380.0 140.9 %reduce-scatter.5.cloned.1.call-start = ((), (), s32[]{:S(2)}) async-start(), calls=%async_computation.11 | async-start | bytes 7208960 | tf_op jit(solution)/shard_map/reduce_scatter | solution.py:94
  461.6 102.6 %reduce-scatter.7.cloned.1.call-start = ((), (), s32[]{:S(2)}) async-start(), calls=%async_computation.12 | async-start | bytes 1802240 | tf_op jit(solution)/shard_map/reduce_scatter | solution.py:95
  463.1 57.8 %copy-start.38 = (bf16[32,128,128]{2,1,0:T(8,128)(2,1)S(1)}, bf16[32,128,128]{2,1,0:T(8,128)(2,1)}, u32[]{:S(2)}) copy-start(bf16[32,128,128]{2,1,0:T(8,128)(2,1)} %copy-done.37) | copy-start | bytes 3145732
  555.9 11.6 %copy-start.61 = (f32[128]{0:T(128)S(1)}, f32[128]{0:T(128)}, u32[]{:S(2)}) copy-start(f32[128]{0:T(128)} %param.35) | copy-start | bytes 1540
  555.9 12.2 %copy-start.63 = (f32[128]{0:T(128)S(1)}, f32[128]{0:T(128)}, u32[]{:S(2)}) copy-start(f32[128]{0:T(128)} %param.34) | copy-start | bytes 1540
  555.9 12.2 %copy-start.48 = (f32[128,16]{0,1:T(8,128)S(1)}, f32[128,16]{0,1:T(8,128)}, u32[]{:S(2)}) copy-start(f32[128,16]{0,1:T(8,128)} %copy-done.47) | copy-start | bytes 24580
  555.9 58.5 %all-to-all-start.4 = ((bf16[32,128,384]{1,2,0:T(8,128)(2,1)}), bf16[32,128,384]{1,2,0:T(8,128)(2,1)S(1)}, u32[]{:S(2)}, u32[]{:S(2)}) async-start(bf16[32,128,384]{1,2,0:T(8,128)(2,1)} %pad_maximum_fusion.7), calls=%async_computation.6 | async-start | bytes 6291456 | tf_op jit(solution)/shard_map/all_to_all | solution.py:167
  564.0 117.0 %all-gather.19.cloned.1.call-start = ((), (), s32[]{:S(2)}) async-start(), calls=%async_computation.13 | async-start | bytes 5242880 | tf_op jit(solution)/shard_map/all_gather | solution.py:328
  564.1 48.4 %collective-permute-start.4 = (bf16[16,11264]{1,0:T(8,128)(2,1)}, bf16[16,11264]{1,0:T(8,128)(2,1)}, u32[]{:S(2)}, u32[]{:S(2)}) collective-permute-start(bf16[16,11264]{1,0:T(8,128)(2,1)} %reduce-scatter.7.cloned.1.call-done), channel_id=1, source_target_pairs={{0,64},{64,0},{1,65},{65,1},{2,66},{66,2},{3,67},{67,3},{4,68},{68... | collective-permute-start | bytes 1081352 | tf_op jit(solution)/shard_map/ppermute | solution.py:96
  619.6 10.2 %copy-start.7 = (f32[128,4096]{1,0:T(8,128)S(1)}, f32[128,4096]{1,0:T(8,128)}, u32[]{:S(2)}) copy-start(f32[128,4096]{1,0:T(8,128)} %copy-done.6) | copy-start | bytes 6291460
  633.6 84.5 %reduce-scatter.9.cloned.1.call-start = ((), (), s32[]{:S(2)}) async-start(), calls=%async_computation.14 | async-start | bytes 2703360 | tf_op jit(solution)/shard_map/reduce_scatter | solution.py:94
  686.1 104.5 %copy-start.4 = (f32[128,1024]{1,0:T(8,128)S(1)}, f32[128,1024]{1,0:T(8,128)}, u32[]{:S(2)}) copy-start(f32[128,1024]{1,0:T(8,128)} %copy-done.3) | copy-start | bytes 1572868
  686.1 104.5 %copy-start.28 = (bf16[128,3072]{1,0:T(8,128)(2,1)S(1)}, bf16[128,3072]{1,0:T(8,128)(2,1)}, u32[]{:S(2)}) copy-start(bf16[128,3072]{1,0:T(8,128)(2,1)} %get-tuple-element.108) | copy-start | bytes 2359300
  686.1 58.8 %all-gather.23.cloned.1.call-start = ((), (), s32[]{:S(2)}) async-start(), calls=%async_computation.17 | async-start | bytes 1802240 | tf_op jit(solution)/shard_map/all_gather | solution.py:102
  686.9 82.5 %reduce-scatter.11.cloned.1.call-start = ((), (), s32[]{:S(2)}) async-start(), calls=%async_computation.15 | async-start | bytes 675840 | tf_op jit(solution)/shard_map/reduce_scatter | solution.py:95
  718.1 114.2 %all-gather.25.cloned.1.call-start = ((), (), s32[]{:S(2)}) async-start(), calls=%async_computation.18 | async-start | bytes 7208960 | tf_op jit(solution)/shard_map/all_gather | solution.py:103
  744.9 121.0 %all-gather.21.cloned.1.call-start = ((), (), s32[]{:S(2)}) async-start(), calls=%async_computation.16 | async-start | bytes 2703360 | tf_op jit(solution)/shard_map/all_gather | solution.py:103
  769.4 6.7 collective-permute-start.5
  (49 other events, 164.5 us)
Sparse Core Ops, SparseCore 0:
  10.4 61.7 all-gather.26
  73.9 36.6 all-gather.28
  112.2 78.6 all-gather.32
  193.0 88.6 all-gather.30
  344.4 36.8 all-gather.14
  383.4 69.8 all-gather.16
  461.7 59.1 reduce-scatter.4
  523.3 24.6 reduce-scatter.6
  633.7 47.2 all-gather.18
  686.2 31.8 reduce-scatter.8
  719.9 24.9 all-gather.22
  747.3 22.0 reduce-scatter.10
  771.0 61.3 all-gather.24
  833.9 32.0 all-gather.20

commit v11 on v10

--- a/solution.py
+++ b/solution.py
@@ -290,8 +290,6 @@
         jnp.concatenate([key_part, value_part], axis=-1).astype(jnp.bfloat16).reshape(
             ctx_size, local_rows, 2 * HEAD_SIZE),
     ], axis=-1))
-    mlp_part, returned = lax.optimization_barrier((mlp_part, returned))
-    mlp_reduced = gather_ctx(mlp_part)
     query_grad_rows = own_heads(returned[..., :HEAD_SIZE]).astype(jnp.float32)
     kv_parts = returned[..., HEAD_SIZE:].astype(jnp.float32).reshape(
         halves, KEY_VALUE_HEADS, group, local_rows, 2 * HEAD_SIZE)
@@ -325,6 +323,8 @@
     input_grad = mid_grad + root_mean_square_backward(
         attn_in_grad, first_normed, first_scale, first_gain
     )
+    mlp_part, qkv_grad = lax.optimization_barrier((mlp_part, qkv_grad))
+    mlp_reduced = gather_ctx(mlp_part)
     qkv_rows = lax.all_gather(qkv_grad, FSDP, axis=0, tiled=True)
     first_shard, second_shard, query_gain_shard, key_gain_shard = (
         lax.psum_scatter(first_gain_grad, FSDP, scatter_dimension=0, tiled=True),

time: 889 us -> 863 us (0.971)
  waiting for transfers between devices: 481 us -> 463 us
    all_to_all x3, waiting for transfers between devices: 57.9 us -> 105 us  [exchange(): return lax.all_to_all(values, CTX, split_axis=0, concat_axis=0, tiled=True)]
    reduce_scatter x2, waiting for transfers between devices: 68.7 us -> 31.1 us  [scatter_ctx(): part = lax.psum_scatter(packed, 'z', scatter_dimension=0, tiled=True)]
    ppermute x2, waiting for transfers between devices: 41.7 us -> 11.5 us  [scatter_ctx(): lax.ppermute(part, 'yh', [(0, 1), (1, 0)]).astype(jnp.float32)]
  transfers between devices with their start and end apart: 24 -> 24, of which waited for: 16 -> 16; matrix products, arithmetic and copies ran while one was open for 24% -> 27% of each run, Pallas kernels for 0% -> 0%
where the time goes in v11:
time: 863 us; the launch traced here: 854 us
  waiting for transfers between devices  463 us (54%)
  matrix products  118 us (14%)
  other arithmetic  99.3 us (12%)
  local copies, waits for them, and re-layouts  71.4 us (8%)
  blocking collectives  53 us (6%)
  starting transfers between devices  31.8 us (4%)
  between operations  17 us (2%)
    all_gather x4, waiting for transfers between devices, gather_across(): return lax.all_gather(values, 'yl', axis=0, tiled=False)  122 us
    all_to_all x3, waiting for transfers between devices, exchange(): return lax.all_to_all(values, CTX, split_axis=0, concat_axis=0, tiled=True)  105 us
    all_gather x2, waiting for transfers between devices, gather_ctx(): return lax.all_gather(part, 'z', axis=0, tiled=True).astype(jnp.float32)  58.2 us
    dot_general x5, matrix products, right_dot(): lax.dot_general(left_side, right_side, (((1,), (1,)), ((), ())), preferre...  41.7 us
    all_gather x1, waiting for transfers between devices, on_device(): gate_up_rows = lax.all_gather(gate_up_grad, FSDP, axis=0, tiled=True)  40.1 us
    dot_general x6, matrix products, left_dot(): lax.dot_general(left_side, right_side, (((0,), (0,)), ((), ())), preferre...  32.9 us
    reduce_scatter x2, waiting for transfers between devices, scatter_ctx(): part = lax.psum_scatter(packed, 'z', scatter_dimension=0, tiled=True)  31.1 us
    all_to_all x1, blocking collectives, exchange(): return lax.all_to_all(values, CTX, split_axis=0, concat_axis=0, tiled=True)  28.2 us
  transfers between devices with their start and end apart: 24, of which 16 were waited for; matrix products, arithmetic and copies ran while one was open for 27% of the time, Pallas kernels for 0%

profile of v11, /device:TPU:0, one launch (start us, length us, event | category | flops | bytes accessed | tf_op | source)
XLA Modules:
  0.0 853.9 jit_solution(17656400881290112496)
XLA Ops:
  7.2 3.1 pad_maximum_fusion.9
  10.4 61.8 %all-gather.27.cloned.1.call-done = bf16[512,4096]{1,0:T(8,128)(2,1)} async-done(((bf16[256,4096]{1,0:T(8,128)(2,1)}), bf16[512,4096]{1,0:T(8,128)(2,1)}) %all-gather.27.cloned.1.call-update) | async-done | bytes 4194320 | tf_op jit(solution)/shard_map/all_gather | solution.py:79
  74.0 5.8 collective-permute-done
  79.7 5.2 select_bitcast_fusion.3
  84.9 6.6 pad_maximum_fusion.1
  91.4 4.7 fusion.32
  112.9 9.4 %all-to-all-start = ((bf16[32,128,384]{2,1,0:T(8,128)(2,1)}), bf16[32,128,384]{2,1,0:T(8,128)(2,1)S(1)}, u32[]{:S(2)}, u32[]{:S(2)}) async-start(bf16[32,128,384]{2,1,0:T(8,128)(2,1)} %pad_maximum_fusion.5), calls=%async_computation | async-start | bytes 6291456 | tf_op jit(solution)/shard_map/all_to_all | solution.py:167
  122.3 4.3 pad_maximum_fusion.6
  127.0 42.5 %all-to-all-done = bf16[32,128,384]{2,1,0:T(8,128)(2,1)S(1)} async-done(((bf16[32,128,384]{2,1,0:T(8,128)(2,1)}), bf16[32,128,384]{2,1,0:T(8,128)(2,1)S(1)}, u32[]{:S(2)}, u32[]{:S(2)}) %all-to-all-start) | async-done | bytes 3145760 | tf_op jit(solution)/shard_map/all_to_all | solution.py:167
  170.2 13.7 %fusion.48 = (f32[2048]{0:T(1024)S(1)}, f32[2048,4096]{1,0:T(8,128)}) fusion(bf16[2048,128]{1,0:T(8,128)(2,1)S(1)} %bitcast.256, bf16[4096,128]{1,0:T(8,128)(2,1)S(1)} %bitcast.253, s32[2048]{0:T(1024)S(1)} %dynamic-slice-done, s32[4096]{0:T(1024)S(1)} %copy-done.52), kind=kOutput, calls=%fused_computation.176 | convolution fusion | flops 2181036032 | bytes 35160064 | tf_op jit(solution)/shard_map/qd,kd->qk/dot_general | solution.py:204
  183.8 14.8 %exponential_reduce_fusion = f32[2048]{0:T(1024)S(1)} fusion(f32[2048,4096]{1,0:T(8,128)} %get-tuple-element.133, f32[2048]{0:T(1024)S(1)} %get-tuple-element.132), kind=kLoop, calls=%fused_computation.2 | loop fusion | flops 16775168 | bytes 33570816 | tf_op jit(solution)/shard_map/reduce_sum | solution.py:211
  198.7 5.4 copy-done
  204.1 8.8 %fusion = bf16[2048,4096]{1,0:T(8,128)(2,1)} fusion(f32[2048,4096]{1,0:T(8,128)S(1)} %copy-done, f32[2048]{0:T(1024)S(1)} %log_add_fusion), kind=kLoop, calls=%fused_computation.4 | loop fusion | flops 16777216 | bytes 50339840 | tf_op jit(solution)/shard_map/convert_element_type | solution.py:212
  212.9 9.2 %fusion.49 = f32[2048,128]{1,0:T(8,128)S(1)} fusion(bf16[2048,4096]{1,0:T(8,128)(2,1)} %fusion, bf16[4096,128]{1,0:T(8,128)(2,1)S(1)} %bitcast.225), kind=kOutput, calls=%fused_computation.177 | convolution fusion | flops 2147483648 | bytes 18874368 | tf_op jit(solution)/shard_map/dot_general | solution.py:213
  222.1 59.6 %all-gather.31.cloned.1.call-done = bf16[512,6144]{1,0:T(8,128)(2,1)} async-done(((bf16[256,6144]{1,0:T(8,128)(2,1)}), bf16[512,6144]{1,0:T(8,128)(2,1)}) %all-gather.31.cloned.1.call-update) | async-done | bytes 6291472 | tf_op jit(solution)/shard_map/all_gather | solution.py:79
  282.8 28.2 %all_to_all.35 = bf16[32,128,128]{1,2,0:T(8,128)(2,1)S(1)} all-to-all(bf16[32,128,128]{1,2,0:T(8,128)(2,1)S(1)} %bitcast_select_fusion.2), channel_id=1, replica_groups=mesh['yh'=2,'x'=4,'z'=4,'yl'=2,'c'=2] {'yh','x','z'}, dimensions={0} | all-to-all | bytes 2097152 | tf_op jit(solution)/shard_map/all_to_all | solution.py:167
  321.7 4.9 select_bitcast_fusion.1
  329.7 4.0 multiply_convert_fusion.2
  333.8 7.2 multiply_reduce_fusion.5
  345.8 3.7 fusion.4
  351.2 5.1 all-to-all-start.3
  360.2 15.4 %all-to-all-done.3 = bf16[32,128,128]{1,2,0:T(8,128)(2,1)S(1)} async-done(((bf16[32,128,128]{1,2,0:T(8,128)(2,1)}), bf16[32,128,128]{1,2,0:T(8,128)(2,1)S(1)}, u32[]{:S(2)}, u32[]{:S(2)}) %all-to-all-start.3) | async-done | bytes 1048608 | tf_op jit(solution)/shard_map/all_to_all | solution.py:167
  375.5 4.4 all-to-all-start.2
  380.3 23.8 %all-to-all-done.2 = bf16[128,4,1792]{2,0,1:T(8,128)(2,1)} async-done(((bf16[128,4,1792]{2,0,1:T(8,128)(2,1)}), bf16[128,4,1792]{2,0,1:T(8,128)(2,1)}, u32[]{:S(2)}, u32[]{:S(2)}) %all-to-all-start.2) | async-done | bytes 1835040 | tf_op jit(solution)/shard_map/all_to_all | solution.py:255
  406.8 3.7 convolution_convert_fusion.4
  413.1 40.1 %all-gather.17.cloned.1.call-done = bf16[512,6144]{1,0:T(8,128)(2,1)} async-done(((bf16[128,6144]{1,0:T(8,128)(2,1)}), bf16[512,6144]{1,0:T(8,128)(2,1)}) %all-gather.17.cloned.1.call-update) | async-done | bytes 6291472 | tf_op jit(solution)/shard_map/all_gather | solution.py:262
  453.3 4.7 convolution_convert_fusion
  458.0 3.4 pad_maximum_fusion.3
  463.0 20.3 %multiply_convert_fusion = bf16[2048,4096]{1,0:T(8,128)(2,1)} fusion(f32[2048,4096]{1,0:T(8,128)} %get-tuple-element.133, f32[2048]{0:T(1024)S(1)} %multiply_reduce_fusion.2, f32[2048]{0:T(1024)S(1)} %log_add_fusion, bf16[2048,128]{1,0:T(8,128)(2,1)S(1)} %bitcast.219, bf16[4096,128]{1,0:T(8,128)(2,1)S(1)} %bitcast.226), kind=kOutput, calls=%fused_computation | convolution fusion | flops 2181038080 | bytes 51920896 | tf_op jit(solution)/shard_map/dot_general | solution.py:73
  483.3 8.4 fusion.2
  492.1 9.4 %fusion.1 = bf16[4096,128]{1,0:T(8,128)(2,1)} fusion(bf16[2048,4096]{1,0:T(8,128)(2,1)} %multiply_convert_fusion, bf16[2048,128]{1,0:T(8,128)(2,1)S(1)} %bitcast.257), kind=kOutput, calls=%fused_computation.14 | convolution fusion | flops 2148532224 | bytes 18350080 | tf_op jit(solution)/shard_map/dot_general | solution.py:67
  503.2 9.4 %convolution_convert_fusion.2 = bf16[4096,128]{1,0:T(8,128)(2,1)} fusion(bf16[2048,4096]{1,0:T(8,128)(2,1)} %fusion, bf16[2048,128]{1,0:T(8,128)(2,1)S(1)} %bitcast.220), kind=kOutput, calls=%fused_computation.15 | convolution fusion | flops 2148007936 | bytes 18350080 | tf_op jit(solution)/shard_map/dot_general | solution.py:67
  516.1 7.4 all-to-all-start.4
  531.9 46.7 %all-to-all-done.4 = bf16[32,128,384]{1,2,0:T(8,128)(2,1)S(1)} async-done(((bf16[32,128,384]{1,2,0:T(8,128)(2,1)}), bf16[32,128,384]{1,2,0:T(8,128)(2,1)S(1)}, u32[]{:S(2)}, u32[]{:S(2)}) %all-to-all-start.4) | async-done | bytes 3145760 | tf_op jit(solution)/shard_map/all_to_all | solution.py:167
  600.1 7.8 collective-permute-done.4
  614.3 6.5 fusion.28
  620.9 11.2 %all-reduce.5 = (f32[1024]{0:T(1024)S(1)}, f32[1024]{0:T(1024)S(1)}, bf16[128]{0:T(256)(128)(2,1)S(1)}, bf16[128]{0:T(256)(128)(2,1)S(1)}) all-reduce(f32[1024]{0:T(1024)S(1)} %get-tuple-element.83, f32[1024]{0:T(1024)S(1)} %copy-done.54, ...), channel_id=8, replica_groups=mesh['yh'=2,'x'=4,'z'=4,'yl'=2,'c'=2] {'yl','c'}, use_global_device_ids=true, to_apply=%region_16.17.clone | all-reduce | flops 2304 | bytes 17920
  641.9 12.9 %all-gather.19.cloned.1.call-done = bf16[512,4096]{1,0:T(8,128)(2,1)} async-done(((bf16[128,4096]{1,0:T(8,128)(2,1)}), bf16[512,4096]{1,0:T(8,128)(2,1)}) %all-gather.19.cloned.1.call-update) | async-done | bytes 4194320 | tf_op jit(solution)/shard_map/all_gather | solution.py:328
  654.9 3.6 convolution_convert_fusion.1
  660.8 31.1 %reduce-scatter.9.cloned.1.call-done = bf16[64,4224]{1,0:T(8,128)(2,1)} async-done(((bf16[256,4224]{1,0:T(8,128)(2,1)}), bf16[64,4224]{1,0:T(8,128)(2,1)}) %reduce-scatter.9.cloned.1.call-update) | async-done | bytes 540688 | tf_op jit(solution)/shard_map/reduce_scatter | solution.py:94
  691.9 27.3 %all-gather.23.cloned.1.call-done = bf16[64,11264]{1,0:T(8,128)(2,1)} async-done(((bf16[16,11264]{1,0:T(8,128)(2,1)}), bf16[64,11264]{1,0:T(8,128)(2,1)}) %all-gather.23.cloned.1.call-update) | async-done | bytes 1441808 | tf_op jit(solution)/shard_map/all_gather | solution.py:102
  719.3 24.4 %reduce-scatter.11.cloned.1.call-done = bf16[16,4224]{1,0:T(8,128)(2,1)} async-done(((bf16[64,4224]{1,0:T(8,128)(2,1)}), bf16[16,4224]{1,0:T(8,128)(2,1)}) %reduce-scatter.11.cloned.1.call-update) | async-done | bytes 135184 | tf_op jit(solution)/shard_map/reduce_scatter | solution.py:95
  746.7 3.7 collective-permute-done.5
  751.3 13.6 %all_gather.56 = bf16[64,4224]{1,0:T(8,128)(2,1)} all-gather(bf16[16,4224]{1,0:T(8,128)(2,1)S(1)} %add_convert_fusion.2), channel_id=1, replica_groups=mesh['yh'=2,'x'=4,'z'=4,'yl'=2,'c'=2] {'x'}, dimensions={0}, use_global_device_ids=true | all-gather | bytes 675840 | tf_op jit(solution)/shard_map/all_gather | solution.py:102
  765.0 4.6 fusion.6
  770.7 36.0 %all-gather.25.cloned.1.call-done = bf16[256,11264]{1,0:T(8,128)(2,1)} async-done(((bf16[64,11264]{1,0:T(8,128)(2,1)}), bf16[256,11264]{1,0:T(8,128)(2,1)}) %all-gather.25.cloned.1.call-update) | async-done | bytes 5767184 | tf_op jit(solution)/shard_map/all_gather | solution.py:103
  806.7 6.3 fusion.43
  818.0 22.3 %all-gather.21.cloned.1.call-done = bf16[256,4224]{1,0:T(8,128)(2,1)} async-done(((bf16[64,4224]{1,0:T(8,128)(2,1)}), bf16[256,4224]{1,0:T(8,128)(2,1)}) %all-gather.21.cloned.1.call-update) | async-done | bytes 2162704 | tf_op jit(solution)/shard_map/all_gather | solution.py:103
  (327 shorter events, 120.5 us)
Async XLA Ops:
  7.2 65.0 %all-gather.27.cloned.1.call-start = ((), (), s32[]{:S(2)}) async-start(), calls=%async_computation.19 | async-start | bytes 6291456 | tf_op jit(solution)/shard_map/all_gather | solution.py:79
  10.3 62.9 %copy-start.66 = (s32[1,64]{1,0:T(1,128)S(1)}, s32[1,64]{1,0:T(1,128)}, u32[]{:S(2)}) copy-start(s32[1,64]{1,0:T(1,128)} %param.24) | copy-start | bytes 772
  10.3 63.1 %copy-start.11 = (bf16[1,128,1024]{2,1,0:T(8,128)(2,1)S(1)}, bf16[1,128,1024]{2,1,0:T(8,128)(2,1)}, u32[]{:S(2)}) copy-start(bf16[1,128,1024]{2,1,0:T(8,128)(2,1)} %param.22) | copy-start | bytes 786436
  10.3 211.8 %all-gather.29.cloned.1.call-start = ((), (), s32[]{:S(2)}) async-start(), calls=%async_computation.20 | async-start | bytes 3145728 | tf_op jit(solution)/shard_map/all_gather | solution.py:79
  72.2 7.5 collective-permute-start
  72.3 149.9 %all-gather.33.cloned.1.call-start = ((), (), s32[]{:S(2)}) async-start(), calls=%async_computation.22 | async-start | bytes 4718592 | tf_op jit(solution)/shard_map/all_gather | solution.py:79
  73.6 283.0 %copy-start.57 = (f32[128]{0:T(128)}, f32[128]{0:T(128)S(1)}, u32[]{:S(2)}) copy-start(f32[128]{0:T(128)S(1)} %add_rsqrt_fusion.3) | copy-start | bytes 1540
  74.0 33.2 %copy-start.39 = (f32[128,64]{0,1:T(8,128)}, f32[128,64]{0,1:T(8,128)S(1)}, u32[]{:S(2)}) copy-start(f32[128,64]{0,1:T(8,128)S(1)} %get-tuple-element.126) | copy-start | bytes 98308
  74.0 33.2 %copy-start.41 = (f32[128,64]{0,1:T(8,128)}, f32[128,64]{0,1:T(8,128)S(1)}, u32[]{:S(2)}) copy-start(f32[128,64]{0,1:T(8,128)S(1)} %get-tuple-element.127) | copy-start | bytes 98308
  112.9 56.6 %all-to-all-start = ((bf16[32,128,384]{2,1,0:T(8,128)(2,1)}), bf16[32,128,384]{2,1,0:T(8,128)(2,1)S(1)}, u32[]{:S(2)}, u32[]{:S(2)}) async-start(bf16[32,128,384]{2,1,0:T(8,128)(2,1)} %pad_maximum_fusion.5), calls=%async_computation | async-start | bytes 6291456 | tf_op jit(solution)/shard_map/all_to_all | solution.py:167
  122.3 159.5 %all-gather.31.cloned.1.call-start = ((), (), s32[]{:S(2)}) async-start(), calls=%async_computation.21 | async-start | bytes 9437184 | tf_op jit(solution)/shard_map/all_gather | solution.py:79
  126.7 277.5 %all-gather.15.cloned.1.call-start = ((), (), s32[]{:S(2)}) async-start(), calls=%async_computation.9 | async-start | bytes 2621440 | tf_op jit(solution)/shard_map/all_gather | solution.py:263
  126.9 43.2 %copy-start.52 = (s32[4096]{0:T(1024)S(1)}, s32[4096]{0:T(1024)}, u32[]{:S(2)}) copy-start(s32[4096]{0:T(1024)} %copy-done.51) | copy-start | bytes 49156
  127.0 43.2 %dynamic-slice-start = ((s32[4096]{0:T(1024)}, s32[]{:T(128)}), s32[2048]{0:T(1024)S(1)}, s32[]{:S(2)}) async-start(s32[4096]{0:T(1024)} %copy-done.51, s32[]{:T(128)} %select_n.88), calls=%async_computation.25 | async-start | bytes 16896 | tf_op jit(solution)/shard_map/dynamic_slice | solution.py:141
  170.0 13.8 %copy-start.35 = (bf16[32,128,128]{2,1,0:T(8,128)(2,1)}, bf16[32,128,128]{2,1,0:T(8,128)(2,1)S(1)}, u32[]{:S(2)}) copy-start(bf16[32,128,128]{2,1,0:T(8,128)(2,1)S(1)} %get-tuple-element.110) | copy-start | bytes 3145732
  170.1 42.8 %copy-start.18 = (bf16[32,128,128]{2,1,0:T(8,128)(2,1)}, bf16[32,128,128]{2,1,0:T(8,128)(2,1)S(1)}, u32[]{:S(2)}) copy-start(bf16[32,128,128]{2,1,0:T(8,128)(2,1)S(1)} %get-tuple-element.109) | copy-start | bytes 3145732
  170.1 13.7 %copy-start.43 = (bf16[16,128,128]{2,1,0:T(8,128)(2,1)}, bf16[16,128,128]{2,1,0:T(8,128)(2,1)S(1)}, u32[]{:S(2)}) copy-start(bf16[16,128,128]{2,1,0:T(8,128)(2,1)S(1)} %constant_dynamic-slice_fusion.2) | copy-start | bytes 1572868
  183.8 20.2 %copy-start = (f32[2048,4096]{1,0:T(8,128)S(1)}, f32[2048,4096]{1,0:T(8,128)}, u32[]{:S(2)}) copy-start(f32[2048,4096]{1,0:T(8,128)} %get-tuple-element.133) | copy-start | bytes 100663296
  222.1 89.0 %copy-start.20 = (f32[2048,128]{1,0:T(8,128)}, f32[2048,128]{1,0:T(8,128)S(1)}, u32[]{:S(2)}) copy-start(f32[2048,128]{1,0:T(8,128)S(1)} %fusion.49) | copy-start | bytes 3145732
  281.8 38.8 %collective-permute-start.2 = (bf16[2,256,6144]{2,1,0:T(8,128)(2,1)}, bf16[2,256,6144]{2,1,0:T(8,128)(2,1)}, u32[]{:S(2)}, u32[]{:S(2)}) collective-permute-start(bf16[2,256,6144]{2,1,0:T(8,128)(2,1)} %bitcast.214), channel_id=1, source_target_pairs={{0,1},{1,0},{2,3},{3,2},{4,5},{5,4},{6,7},{7,6},{8,9},{9,8},{10,11... | collective-permute-start | bytes 18874376 | tf_op jit(solution)/shard_map/ppermute | solution.py:83
  281.8 29.3 %collective-permute-start.1 = (bf16[2,512,1024]{2,1,0:T(8,128)(2,1)}, bf16[2,512,1024]{2,1,0:T(8,128)(2,1)}, u32[]{:S(2)}, u32[]{:S(2)}) collective-permute-start(bf16[2,512,1024]{2,1,0:T(8,128)(2,1)} %bitcast.246), channel_id=1, source_target_pairs={{0,1},{1,0},{2,3},{3,2},{4,5},{5,4},{6,7},{7,6},{8,9},{9,8},{10,11... | collective-permute-start | bytes 6291464 | tf_op jit(solution)/shard_map/ppermute | solution.py:83
  282.3 34.1 %collective-permute-start.3 = (bf16[2,768,1024]{2,1,0:T(8,128)(2,1)}, bf16[2,768,1024]{2,1,0:T(8,128)(2,1)}, u32[]{:S(2)}, u32[]{:S(2)}) collective-permute-start(bf16[2,768,1024]{2,1,0:T(8,128)(2,1)} %bitcast.236), channel_id=1, source_target_pairs={{0,1},{1,0},{2,3},{3,2},{4,5},{5,4},{6,7},{7,6},{8,9},{9,8},{10,11... | collective-permute-start | bytes 9437192 | tf_op jit(solution)/shard_map/ppermute | solution.py:83
  282.6 28.5 %copy-start.34 = (bf16[1024,1024]{1,0:T(8,128)(2,1)S(1)}, bf16[1024,1024]{1,0:T(8,128)(2,1)}, u32[]{:S(2)}) copy-start(bf16[1024,1024]{1,0:T(8,128)(2,1)} %all-gather.29.cloned.1.call-done) | copy-start | bytes 6291460
  314.7 26.3 %copy-start.55 = (f32[128]{0:T(128)}, f32[128]{0:T(128)S(1)}, u32[]{:S(2)}) copy-start(f32[128]{0:T(128)S(1)} %add_rsqrt_fusion.2) | copy-start | bytes 1540
  344.4 108.8 %all-gather.17.cloned.1.call-start = ((), (), s32[]{:S(2)}) async-start(), calls=%async_computation.10 | async-start | bytes 7864320 | tf_op jit(solution)/shard_map/all_gather | solution.py:262
  351.2 24.3 %all-to-all-start.3 = ((bf16[32,128,128]{1,2,0:T(8,128)(2,1)}), bf16[32,128,128]{1,2,0:T(8,128)(2,1)S(1)}, u32[]{:S(2)}, u32[]{:S(2)}) async-start(bf16[32,128,128]{1,2,0:T(8,128)(2,1)} %bitcast_select_fusion.1), calls=%async_computation.3 | async-start | bytes 2097152 | tf_op jit(solution)/shard_map/all_to_all | solution.py:167
  375.5 28.6 %all-to-all-start.2 = ((bf16[128,4,1792]{2,0,1:T(8,128)(2,1)}), bf16[128,4,1792]{2,0,1:T(8,128)(2,1)}, u32[]{:S(2)}, u32[]{:S(2)}) async-start(bf16[128,4,1792]{2,0,1:T(8,128)(2,1)} %pad_maximum_fusion.10), calls=%async_computation.2 | async-start | bytes 3670016 | tf_op jit(solution)/shard_map/all_to_all | solution.py:255
  379.9 143.6 %reduce-scatter.5.cloned.1.call-start = ((), (), s32[]{:S(2)}) async-start(), calls=%async_computation.11 | async-start | bytes 7208960 | tf_op jit(solution)/shard_map/reduce_scatter | solution.py:94
  463.0 20.3 %copy-start.36 = (bf16[32,128,128]{2,1,0:T(8,128)(2,1)S(1)}, bf16[32,128,128]{2,1,0:T(8,128)(2,1)}, u32[]{:S(2)}) copy-start(bf16[32,128,128]{2,1,0:T(8,128)(2,1)} %copy-done.35) | copy-start | bytes 3145732
  516.1 62.5 %all-to-all-start.4 = ((bf16[32,128,384]{1,2,0:T(8,128)(2,1)}), bf16[32,128,384]{1,2,0:T(8,128)(2,1)S(1)}, u32[]{:S(2)}, u32[]{:S(2)}) async-start(bf16[32,128,384]{1,2,0:T(8,128)(2,1)} %pad_maximum_fusion.7), calls=%async_computation.4 | async-start | bytes 6291456 | tf_op jit(solution)/shard_map/all_to_all | solution.py:167
  523.5 73.2 %reduce-scatter.7.cloned.1.call-start = ((), (), s32[]{:S(2)}) async-start(), calls=%async_computation.12 | async-start | bytes 1802240 | tf_op jit(solution)/shard_map/reduce_scatter | solution.py:95
  524.3 130.6 %all-gather.19.cloned.1.call-start = ((), (), s32[]{:S(2)}) async-start(), calls=%async_computation.13 | async-start | bytes 5242880 | tf_op jit(solution)/shard_map/all_gather | solution.py:328
  529.1 49.7 %copy-start.40 = (f32[128,64]{0,1:T(8,128)S(1)}, f32[128,64]{0,1:T(8,128)}, u32[]{:S(2)}) copy-start(f32[128,64]{0,1:T(8,128)} %copy-done.39) | copy-start | bytes 98308
  529.1 49.7 %copy-start.42 = (f32[128,64]{0,1:T(8,128)S(1)}, f32[128,64]{0,1:T(8,128)}, u32[]{:S(2)}) copy-start(f32[128,64]{0,1:T(8,128)} %copy-done.41) | copy-start | bytes 98308
  596.7 16.9 %copy-start.65 = (s32[2]{0:T(128)S(1)}, s32[2]{0:T(128)}, u32[]{:S(2)}) copy-start(s32[2]{0:T(128)} %constant.178.clone.1) | copy-start | bytes 28
  596.7 17.7 %copy-start.33 = (bf16[128,2048]{1,0:T(8,128)(2,1)S(1)}, bf16[128,2048]{1,0:T(8,128)(2,1)}, u32[]{:S(2)}) copy-start(bf16[128,2048]{1,0:T(8,128)(2,1)} %get-tuple-element.103) | copy-start | bytes 1572868
  596.7 17.7 %copy-start.37 = (bf16[128,1024]{1,0:T(8,128)(2,1)S(1)}, bf16[128,1024]{1,0:T(8,128)(2,1)}, u32[]{:S(2)}) copy-start(bf16[128,1024]{1,0:T(8,128)(2,1)} %get-tuple-element.107) | copy-start | bytes 786436
  596.7 17.7 %copy-start.38 = (bf16[128,1024]{1,0:T(8,128)(2,1)S(1)}, bf16[128,1024]{1,0:T(8,128)(2,1)}, u32[]{:S(2)}) copy-start(bf16[128,1024]{1,0:T(8,128)(2,1)} %copy.260) | copy-start | bytes 786436
  596.7 17.7 %copy-start.58 = (f32[128]{0:T(128)S(1)}, f32[128]{0:T(128)}, u32[]{:S(2)}) copy-start(f32[128]{0:T(128)} %copy-done.57) | copy-start | bytes 1540
  596.7 11.3 %collective-permute-start.4 = (bf16[16,11264]{1,0:T(8,128)(2,1)}, bf16[16,11264]{1,0:T(8,128)(2,1)S(1)}, u32[]{:S(2)}, u32[]{:S(2)}) collective-permute-start(bf16[16,11264]{1,0:T(8,128)(2,1)} %reduce-scatter.7.cloned.1.call-done), channel_id=1, source_target_pairs={{0,64},{64,0},{1,65},{65,1},{2,66},{66,2},{3,67},{67,3},{4,68},{68... | collective-permute-start | bytes 1081352 | tf_op jit(solution)/shard_map/ppermute | solution.py:96
  609.8 82.0 %reduce-scatter.9.cloned.1.call-start = ((), (), s32[]{:S(2)}) async-start(), calls=%async_computation.14 | async-start | bytes 2703360 | tf_op jit(solution)/shard_map/reduce_scatter | solution.py:94
  659.9 105.0 %copy-start.4 = (f32[128,1024]{1,0:T(8,128)S(1)}, f32[128,1024]{1,0:T(8,128)}, u32[]{:S(2)}) copy-start(f32[128,1024]{1,0:T(8,128)} %copy-done.3) | copy-start | bytes 1572868
  660.0 105.0 %copy-start.28 = (bf16[128,3072]{1,0:T(8,128)(2,1)S(1)}, bf16[128,3072]{1,0:T(8,128)(2,1)}, u32[]{:S(2)}) copy-start(bf16[128,3072]{1,0:T(8,128)(2,1)} %get-tuple-element.108) | copy-start | bytes 2359300
  660.0 59.2 %all-gather.23.cloned.1.call-start = ((), (), s32[]{:S(2)}) async-start(), calls=%async_computation.17 | async-start | bytes 1802240 | tf_op jit(solution)/shard_map/all_gather | solution.py:102
  660.7 82.9 %reduce-scatter.11.cloned.1.call-start = ((), (), s32[]{:S(2)}) async-start(), calls=%async_computation.15 | async-start | bytes 675840 | tf_op jit(solution)/shard_map/reduce_scatter | solution.py:95
  691.9 114.8 %all-gather.25.cloned.1.call-start = ((), (), s32[]{:S(2)}) async-start(), calls=%async_computation.18 | async-start | bytes 7208960 | tf_op jit(solution)/shard_map/all_gather | solution.py:103
  719.2 121.0 %all-gather.21.cloned.1.call-start = ((), (), s32[]{:S(2)}) async-start(), calls=%async_computation.16 | async-start | bytes 2703360 | tf_op jit(solution)/shard_map/all_gather | solution.py:103
  743.7 6.7 collective-permute-start.5
  (47 other events, 213.2 us)
Sparse Core Ops, SparseCore 0:
  10.4 61.7 all-gather.26
  73.9 36.6 all-gather.28
  112.2 78.7 all-gather.32
  193.1 88.6 all-gather.30
  344.5 36.8 all-gather.14
  383.5 69.6 all-gather.16
  461.5 59.4 reduce-scatter.4
  526.8 41.6 reduce-scatter.6
  609.9 44.8 all-gather.18
  660.1 31.6 reduce-scatter.8
  694.2 24.9 all-gather.22
  721.6 22.0 reduce-scatter.10
  745.3 61.3 all-gather.24
  808.2 32.0 all-gather.20

commit v12 on v11

--- a/solution.py
+++ b/solution.py
@@ -91,16 +91,15 @@
 
 
 def scatter_ctx(packed):
-    part = lax.psum_scatter(packed, "z", scatter_dimension=0, tiled=True)
-    part = lax.psum_scatter(part, "x", scatter_dimension=0, tiled=True)
+    part = lax.psum_scatter(packed, "x", scatter_dimension=0, tiled=True)
+    part = lax.psum_scatter(part, "z", scatter_dimension=0, tiled=True)
     return (part.astype(jnp.float32) + lax.ppermute(part, "yh", [(0, 1), (1, 0)]).astype(jnp.float32)).astype(
         part.dtype
     )
 
 
 def gather_ctx(part):
-    part = lax.all_gather(part, "x", axis=0, tiled=True)
-    return lax.all_gather(part, "z", axis=0, tiled=True).astype(jnp.float32)
+    return lax.all_gather(part, ("x", "z"), axis=0, tiled=True).astype(jnp.float32)
 
 
 def reduce_ctx(packed):

time: 863 us -> 840 us (0.973)
  blocking collectives: 53 us -> 39.4 us
    all_gather x1 -> x0, blocking collectives: 13.6 us -> none  [gather_ctx(): part = lax.all_gather(part, 'x', axis=0, tiled=True)]
    all_gather x3 -> x2, waiting for transfers between devices: 85.5 us -> 83.6 us  [gather_ctx(): lax.all_gather(part, ('x', 'z'), axis=0, tiled=True).astype(jnp.float32)]
  transfers between devices with their start and end apart: 24 -> 23, of which waited for: 16 -> 15; matrix products, arithmetic and copies ran while one was open for 27% -> 27% of each run, Pallas kernels for 0% -> 0%
where the time goes in v12:
time: 840 us; the launch traced here: 832 us
  waiting for transfers between devices  455 us (54%)
  matrix products  118 us (14%)
  other arithmetic  99.9 us (12%)
  local copies, waits for them, and re-layouts  71.3 us (8%)
  blocking collectives  39.4 us (5%)
  starting transfers between devices  31.7 us (4%)
  between operations  17 us (2%)
    all_gather x4, waiting for transfers between devices, gather_across(): return lax.all_gather(values, 'yl', axis=0, tiled=False)  121 us
    all_to_all x3, waiting for transfers between devices, exchange(): return lax.all_to_all(values, CTX, split_axis=0, concat_axis=0, tiled=True)  96.2 us
    all_gather x2, waiting for transfers between devices, gather_ctx(): lax.all_gather(part, ('x', 'z'), axis=0, tiled=True).astype(jnp.float32)  83.6 us
    dot_general x5, matrix products, right_dot(): lax.dot_general(left_side, right_side, (((1,), (1,)), ((), ())), preferre...  41.6 us
    all_gather x1, waiting for transfers between devices, on_device(): gate_up_rows = lax.all_gather(gate_up_grad, FSDP, axis=0, tiled=True)  40.1 us
    dot_general x6, matrix products, left_dot(): lax.dot_general(left_side, right_side, (((0,), (0,)), ((), ())), preferre...  32.9 us
    reduce_scatter x2, waiting for transfers between devices, scatter_ctx(): part = lax.psum_scatter(packed, 'x', scatter_dimension=0, tiled=True)  31.6 us
    all_to_all x1, blocking collectives, exchange(): return lax.all_to_all(values, CTX, split_axis=0, concat_axis=0, tiled=True)  28.2 us
  transfers between devices with their start and end apart: 23, of which 15 were waited for; matrix products, arithmetic and copies ran while one was open for 27% of the time, Pallas kernels for 0%

profile of v12, /device:TPU:0, one launch (start us, length us, event | category | flops | bytes accessed | tf_op | source)
XLA Modules:
  0.0 831.8 jit_solution(9479264936570820364)
XLA Ops:
  7.2 3.1 pad_maximum_fusion.9
  10.4 61.8 %all-gather.24.cloned.1.call-done = bf16[512,4096]{1,0:T(8,128)(2,1)} async-done(((bf16[256,4096]{1,0:T(8,128)(2,1)}), bf16[512,4096]{1,0:T(8,128)(2,1)}) %all-gather.24.cloned.1.call-update) | async-done | bytes 4194320 | tf_op jit(solution)/shard_map/all_gather | solution.py:79
  74.0 5.8 collective-permute-done
  79.7 5.2 select_bitcast_fusion.3
  84.9 6.5 pad_maximum_fusion.1
  91.4 4.7 fusion.32
  112.9 9.4 %all-to-all-start = ((bf16[32,128,384]{2,1,0:T(8,128)(2,1)}), bf16[32,128,384]{2,1,0:T(8,128)(2,1)S(1)}, u32[]{:S(2)}, u32[]{:S(2)}) async-start(bf16[32,128,384]{2,1,0:T(8,128)(2,1)} %pad_maximum_fusion.5), calls=%async_computation | async-start | bytes 6291456 | tf_op jit(solution)/shard_map/all_to_all | solution.py:166
  122.4 4.3 pad_maximum_fusion.6
  127.0 42.5 %all-to-all-done = bf16[32,128,384]{2,1,0:T(8,128)(2,1)S(1)} async-done(((bf16[32,128,384]{2,1,0:T(8,128)(2,1)}), bf16[32,128,384]{2,1,0:T(8,128)(2,1)S(1)}, u32[]{:S(2)}, u32[]{:S(2)}) %all-to-all-start) | async-done | bytes 3145760 | tf_op jit(solution)/shard_map/all_to_all | solution.py:166
  170.2 13.7 %fusion.48 = (f32[2048]{0:T(1024)S(1)}, f32[2048,4096]{1,0:T(8,128)}) fusion(bf16[2048,128]{1,0:T(8,128)(2,1)S(1)} %bitcast.256, bf16[4096,128]{1,0:T(8,128)(2,1)S(1)} %bitcast.253, s32[2048]{0:T(1024)S(1)} %dynamic-slice-done, s32[4096]{0:T(1024)S(1)} %copy-done.52), kind=kOutput, calls=%fused_computation.176 | convolution fusion | flops 2181036032 | bytes 35160064 | tf_op jit(solution)/shard_map/qd,kd->qk/dot_general | solution.py:203
  183.9 14.8 %exponential_reduce_fusion = f32[2048]{0:T(1024)S(1)} fusion(f32[2048,4096]{1,0:T(8,128)} %get-tuple-element.133, f32[2048]{0:T(1024)S(1)} %get-tuple-element.132), kind=kLoop, calls=%fused_computation.2 | loop fusion | flops 16775168 | bytes 33570816 | tf_op jit(solution)/shard_map/reduce_sum | solution.py:210
  198.8 5.4 copy-done
  204.1 8.9 %fusion = bf16[2048,4096]{1,0:T(8,128)(2,1)} fusion(f32[2048,4096]{1,0:T(8,128)S(1)} %copy-done, f32[2048]{0:T(1024)S(1)} %log_add_fusion), kind=kLoop, calls=%fused_computation.4 | loop fusion | flops 16777216 | bytes 50339840 | tf_op jit(solution)/shard_map/convert_element_type | solution.py:211
  213.0 9.1 %fusion.49 = f32[2048,128]{1,0:T(8,128)S(1)} fusion(bf16[2048,4096]{1,0:T(8,128)(2,1)} %fusion, bf16[4096,128]{1,0:T(8,128)(2,1)S(1)} %bitcast.225), kind=kOutput, calls=%fused_computation.177 | convolution fusion | flops 2147483648 | bytes 18874368 | tf_op jit(solution)/shard_map/dot_general | solution.py:212
  222.2 59.5 %all-gather.28.cloned.1.call-done = bf16[512,6144]{1,0:T(8,128)(2,1)} async-done(((bf16[256,6144]{1,0:T(8,128)(2,1)}), bf16[512,6144]{1,0:T(8,128)(2,1)}) %all-gather.28.cloned.1.call-update) | async-done | bytes 6291472 | tf_op jit(solution)/shard_map/all_gather | solution.py:79
  282.7 28.2 %all_to_all.35 = bf16[32,128,128]{1,2,0:T(8,128)(2,1)S(1)} all-to-all(bf16[32,128,128]{1,2,0:T(8,128)(2,1)S(1)} %bitcast_select_fusion.2), channel_id=1, replica_groups=mesh['yh'=2,'x'=4,'z'=4,'yl'=2,'c'=2] {'yh','x','z'}, dimensions={0} | all-to-all | bytes 2097152 | tf_op jit(solution)/shard_map/all_to_all | solution.py:166
  321.7 4.9 select_bitcast_fusion.1
  329.7 4.0 multiply_convert_fusion.2
  333.7 7.2 multiply_reduce_fusion.5
  345.7 3.7 fusion.4
  351.1 5.1 all-to-all-start.3
  360.1 15.4 %all-to-all-done.3 = bf16[32,128,128]{1,2,0:T(8,128)(2,1)S(1)} async-done(((bf16[32,128,128]{1,2,0:T(8,128)(2,1)}), bf16[32,128,128]{1,2,0:T(8,128)(2,1)S(1)}, u32[]{:S(2)}, u32[]{:S(2)}) %all-to-all-start.3) | async-done | bytes 1048608 | tf_op jit(solution)/shard_map/all_to_all | solution.py:166
  375.4 4.4 all-to-all-start.2
  380.2 23.8 %all-to-all-done.2 = bf16[128,4,1792]{2,0,1:T(8,128)(2,1)} async-done(((bf16[128,4,1792]{2,0,1:T(8,128)(2,1)}), bf16[128,4,1792]{2,0,1:T(8,128)(2,1)}, u32[]{:S(2)}, u32[]{:S(2)}) %all-to-all-start.2) | async-done | bytes 1835040 | tf_op jit(solution)/shard_map/all_to_all | solution.py:254
  406.8 3.7 convolution_convert_fusion.4
  410.5 2.6 reshape.454
  413.1 40.1 %all-gather.16.cloned.1.call-done = bf16[512,6144]{1,0:T(8,128)(2,1)} async-done(((bf16[128,6144]{1,0:T(8,128)(2,1)}), bf16[512,6144]{1,0:T(8,128)(2,1)}) %all-gather.16.cloned.1.call-update) | async-done | bytes 6291472 | tf_op jit(solution)/shard_map/all_gather | solution.py:261
  453.2 4.7 convolution_convert_fusion
  457.9 3.4 pad_maximum_fusion.3
  462.9 20.2 %multiply_convert_fusion = bf16[2048,4096]{1,0:T(8,128)(2,1)} fusion(f32[2048,4096]{1,0:T(8,128)} %get-tuple-element.133, f32[2048]{0:T(1024)S(1)} %multiply_reduce_fusion.2, f32[2048]{0:T(1024)S(1)} %log_add_fusion, bf16[2048,128]{1,0:T(8,128)(2,1)S(1)} %bitcast.219, bf16[4096,128]{1,0:T(8,128)(2,1)S(1)} %bitcast.226), kind=kOutput, calls=%fused_computation | convolution fusion | flops 2181038080 | bytes 51920896 | tf_op jit(solution)/shard_map/dot_general | solution.py:73
  483.2 8.4 %fusion.2 = bf16[2048,128]{1,0:T(8,128)(2,1)S(1)} fusion(bf16[2048,4096]{1,0:T(8,128)(2,1)} %multiply_convert_fusion, bf16[4096,128]{1,0:T(8,128)(2,1)S(1)} %bitcast.254), kind=kOutput, calls=%fused_computation.27 | convolution fusion | flops 2148007936 | bytes 18350080 | tf_op jit(solution)/shard_map/dot_general | solution.py:285
  492.0 9.4 %fusion.1 = bf16[4096,128]{1,0:T(8,128)(2,1)} fusion(bf16[2048,4096]{1,0:T(8,128)(2,1)} %multiply_convert_fusion, bf16[2048,128]{1,0:T(8,128)(2,1)S(1)} %bitcast.257), kind=kOutput, calls=%fused_computation.14 | convolution fusion | flops 2148532224 | bytes 18350080 | tf_op jit(solution)/shard_map/dot_general | solution.py:67
  503.1 9.4 %convolution_convert_fusion.2 = bf16[4096,128]{1,0:T(8,128)(2,1)} fusion(bf16[2048,4096]{1,0:T(8,128)(2,1)} %fusion, bf16[2048,128]{1,0:T(8,128)(2,1)S(1)} %bitcast.220), kind=kOutput, calls=%fused_computation.15 | convolution fusion | flops 2148007936 | bytes 18350080 | tf_op jit(solution)/shard_map/dot_general | solution.py:67
  516.0 7.4 all-to-all-start.4
  531.9 38.4 %all-to-all-done.4 = bf16[32,128,384]{1,2,0:T(8,128)(2,1)S(1)} async-done(((bf16[32,128,384]{1,2,0:T(8,128)(2,1)}), bf16[32,128,384]{1,2,0:T(8,128)(2,1)S(1)}, u32[]{:S(2)}, u32[]{:S(2)}) %all-to-all-start.4) | async-done | bytes 3145760 | tf_op jit(solution)/shard_map/all_to_all | solution.py:166
  591.7 8.2 collective-permute-done.4
  606.3 6.4 fusion.28
  612.7 11.2 %all-reduce.5 = (f32[1024]{0:T(1024)S(1)}, f32[1024]{0:T(1024)S(1)}, bf16[128]{0:T(256)(128)(2,1)S(1)}, bf16[128]{0:T(256)(128)(2,1)S(1)}) all-reduce(f32[1024]{0:T(1024)S(1)} %get-tuple-element.83, f32[1024]{0:T(1024)S(1)} %copy-done.54, ...), channel_id=8, replica_groups=mesh['yh'=2,'x'=4,'z'=4,'yl'=2,'c'=2] {'yl','c'}, use_global_device_ids=true, to_apply=%region_16.17.clone | all-reduce | flops 2304 | bytes 17920
  633.4 15.0 %all-gather.18.cloned.1.call-done = bf16[512,4096]{1,0:T(8,128)(2,1)} async-done(((bf16[128,4096]{1,0:T(8,128)(2,1)}), bf16[512,4096]{1,0:T(8,128)(2,1)}) %all-gather.18.cloned.1.call-update) | async-done | bytes 4194320 | tf_op jit(solution)/shard_map/all_gather | solution.py:327
  648.4 3.6 convolution_convert_fusion.1
  653.6 31.6 %reduce-scatter.9.cloned.1.call-done = bf16[64,4224]{1,0:T(8,128)(2,1)} async-done(((bf16[256,4224]{1,0:T(8,128)(2,1)}), bf16[64,4224]{1,0:T(8,128)(2,1)}) %reduce-scatter.9.cloned.1.call-update) | async-done | bytes 540688 | tf_op jit(solution)/shard_map/reduce_scatter | solution.py:94
  685.8 23.4 %reduce-scatter.11.cloned.1.call-done = bf16[16,4224]{1,0:T(8,128)(2,1)} async-done(((bf16[64,4224]{1,0:T(8,128)(2,1)}), bf16[16,4224]{1,0:T(8,128)(2,1)}) %reduce-scatter.11.cloned.1.call-update) | async-done | bytes 135184 | tf_op jit(solution)/shard_map/reduce_scatter | solution.py:95
  709.2 3.0 collective-permute-start.5
  712.2 3.7 collective-permute-done.5
  717.6 4.5 fusion.6
  723.3 47.2 %all-gather.22.cloned.1.call-done = bf16[256,11264]{1,0:T(8,128)(2,1)} async-done(((bf16[16,11264]{1,0:T(8,128)(2,1)}), bf16[256,11264]{1,0:T(8,128)(2,1)}) %all-gather.22.cloned.1.call-update) | async-done | bytes 5767184 | tf_op jit(solution)/shard_map/all_gather | solution.py:102
  770.4 6.3 fusion.43
  781.7 36.4 %all-gather.20.cloned.1.call-done = bf16[256,4224]{1,0:T(8,128)(2,1)} async-done(((bf16[16,4224]{1,0:T(8,128)(2,1)}), bf16[256,4224]{1,0:T(8,128)(2,1)}) %all-gather.20.cloned.1.call-update) | async-done | bytes 2162704 | tf_op jit(solution)/shard_map/all_gather | solution.py:102
  (323 shorter events, 115.0 us)
Async XLA Ops:
  7.2 65.0 %all-gather.24.cloned.1.call-start = ((), (), s32[]{:S(2)}) async-start(), calls=%async_computation.18 | async-start | bytes 6291456 | tf_op jit(solution)/shard_map/all_gather | solution.py:79
  10.3 62.9 %copy-start.66 = (s32[1,64]{1,0:T(1,128)S(1)}, s32[1,64]{1,0:T(1,128)}, u32[]{:S(2)}) copy-start(s32[1,64]{1,0:T(1,128)} %param.24) | copy-start | bytes 772
  10.3 63.1 %copy-start.11 = (bf16[1,128,1024]{2,1,0:T(8,128)(2,1)S(1)}, bf16[1,128,1024]{2,1,0:T(8,128)(2,1)}, u32[]{:S(2)}) copy-start(bf16[1,128,1024]{2,1,0:T(8,128)(2,1)} %param.22) | copy-start | bytes 786436
  10.3 211.8 %all-gather.26.cloned.1.call-start = ((), (), s32[]{:S(2)}) async-start(), calls=%async_computation.19 | async-start | bytes 3145728 | tf_op jit(solution)/shard_map/all_gather | solution.py:79
  72.2 7.5 collective-permute-start
  72.3 149.9 %all-gather.30.cloned.1.call-start = ((), (), s32[]{:S(2)}) async-start(), calls=%async_computation.21 | async-start | bytes 4718592 | tf_op jit(solution)/shard_map/all_gather | solution.py:79
  73.6 282.9 %copy-start.57 = (f32[128]{0:T(128)}, f32[128]{0:T(128)S(1)}, u32[]{:S(2)}) copy-start(f32[128]{0:T(128)S(1)} %add_rsqrt_fusion.3) | copy-start | bytes 1540
  74.0 33.2 %copy-start.39 = (f32[128,64]{0,1:T(8,128)}, f32[128,64]{0,1:T(8,128)S(1)}, u32[]{:S(2)}) copy-start(f32[128,64]{0,1:T(8,128)S(1)} %get-tuple-element.126) | copy-start | bytes 98308
  74.0 33.2 %copy-start.41 = (f32[128,64]{0,1:T(8,128)}, f32[128,64]{0,1:T(8,128)S(1)}, u32[]{:S(2)}) copy-start(f32[128,64]{0,1:T(8,128)S(1)} %get-tuple-element.127) | copy-start | bytes 98308
  112.9 56.6 %all-to-all-start = ((bf16[32,128,384]{2,1,0:T(8,128)(2,1)}), bf16[32,128,384]{2,1,0:T(8,128)(2,1)S(1)}, u32[]{:S(2)}, u32[]{:S(2)}) async-start(bf16[32,128,384]{2,1,0:T(8,128)(2,1)} %pad_maximum_fusion.5), calls=%async_computation | async-start | bytes 6291456 | tf_op jit(solution)/shard_map/all_to_all | solution.py:166
  122.3 159.4 %all-gather.28.cloned.1.call-start = ((), (), s32[]{:S(2)}) async-start(), calls=%async_computation.20 | async-start | bytes 9437184 | tf_op jit(solution)/shard_map/all_gather | solution.py:79
  126.7 277.4 %all-gather.14.cloned.1.call-start = ((), (), s32[]{:S(2)}) async-start(), calls=%async_computation.9 | async-start | bytes 2621440 | tf_op jit(solution)/shard_map/all_gather | solution.py:262
  127.0 43.2 %copy-start.52 = (s32[4096]{0:T(1024)S(1)}, s32[4096]{0:T(1024)}, u32[]{:S(2)}) copy-start(s32[4096]{0:T(1024)} %copy-done.51) | copy-start | bytes 49156
  127.0 43.2 %dynamic-slice-start = ((s32[4096]{0:T(1024)}, s32[]{:T(128)}), s32[2048]{0:T(1024)S(1)}, s32[]{:S(2)}) async-start(s32[4096]{0:T(1024)} %copy-done.51, s32[]{:T(128)} %select_n.88), calls=%async_computation.24 | async-start | bytes 16896 | tf_op jit(solution)/shard_map/dynamic_slice | solution.py:140
  170.1 13.8 %copy-start.35 = (bf16[32,128,128]{2,1,0:T(8,128)(2,1)}, bf16[32,128,128]{2,1,0:T(8,128)(2,1)S(1)}, u32[]{:S(2)}) copy-start(bf16[32,128,128]{2,1,0:T(8,128)(2,1)S(1)} %get-tuple-element.110) | copy-start | bytes 3145732
  170.1 42.9 %copy-start.18 = (bf16[32,128,128]{2,1,0:T(8,128)(2,1)}, bf16[32,128,128]{2,1,0:T(8,128)(2,1)S(1)}, u32[]{:S(2)}) copy-start(bf16[32,128,128]{2,1,0:T(8,128)(2,1)S(1)} %get-tuple-element.109) | copy-start | bytes 3145732
  170.2 13.7 %copy-start.43 = (bf16[16,128,128]{2,1,0:T(8,128)(2,1)}, bf16[16,128,128]{2,1,0:T(8,128)(2,1)S(1)}, u32[]{:S(2)}) copy-start(bf16[16,128,128]{2,1,0:T(8,128)(2,1)S(1)} %constant_dynamic-slice_fusion.2) | copy-start | bytes 1572868
  183.9 20.2 %copy-start = (f32[2048,4096]{1,0:T(8,128)S(1)}, f32[2048,4096]{1,0:T(8,128)}, u32[]{:S(2)}) copy-start(f32[2048,4096]{1,0:T(8,128)} %get-tuple-element.133) | copy-start | bytes 100663296
  222.1 88.8 %copy-start.20 = (f32[2048,128]{1,0:T(8,128)}, f32[2048,128]{1,0:T(8,128)S(1)}, u32[]{:S(2)}) copy-start(f32[2048,128]{1,0:T(8,128)S(1)} %fusion.49) | copy-start | bytes 3145732
  281.7 38.8 %collective-permute-start.2 = (bf16[2,256,6144]{2,1,0:T(8,128)(2,1)}, bf16[2,256,6144]{2,1,0:T(8,128)(2,1)}, u32[]{:S(2)}, u32[]{:S(2)}) collective-permute-start(bf16[2,256,6144]{2,1,0:T(8,128)(2,1)} %bitcast.214), channel_id=1, source_target_pairs={{0,1},{1,0},{2,3},{3,2},{4,5},{5,4},{6,7},{7,6},{8,9},{9,8},{10,11... | collective-permute-start | bytes 18874376 | tf_op jit(solution)/shard_map/ppermute | solution.py:83
  281.7 29.3 %collective-permute-start.1 = (bf16[2,512,1024]{2,1,0:T(8,128)(2,1)}, bf16[2,512,1024]{2,1,0:T(8,128)(2,1)}, u32[]{:S(2)}, u32[]{:S(2)}) collective-permute-start(bf16[2,512,1024]{2,1,0:T(8,128)(2,1)} %bitcast.246), channel_id=1, source_target_pairs={{0,1},{1,0},{2,3},{3,2},{4,5},{5,4},{6,7},{7,6},{8,9},{9,8},{10,11... | collective-permute-start | bytes 6291464 | tf_op jit(solution)/shard_map/ppermute | solution.py:83
  282.2 34.1 %collective-permute-start.3 = (bf16[2,768,1024]{2,1,0:T(8,128)(2,1)}, bf16[2,768,1024]{2,1,0:T(8,128)(2,1)}, u32[]{:S(2)}, u32[]{:S(2)}) collective-permute-start(bf16[2,768,1024]{2,1,0:T(8,128)(2,1)} %bitcast.236), channel_id=1, source_target_pairs={{0,1},{1,0},{2,3},{3,2},{4,5},{5,4},{6,7},{7,6},{8,9},{9,8},{10,11... | collective-permute-start | bytes 9437192 | tf_op jit(solution)/shard_map/ppermute | solution.py:83
  282.5 28.5 %copy-start.34 = (bf16[1024,1024]{1,0:T(8,128)(2,1)S(1)}, bf16[1024,1024]{1,0:T(8,128)(2,1)}, u32[]{:S(2)}) copy-start(bf16[1024,1024]{1,0:T(8,128)(2,1)} %all-gather.26.cloned.1.call-done) | copy-start | bytes 6291460
  314.6 26.3 %copy-start.55 = (f32[128]{0:T(128)}, f32[128]{0:T(128)S(1)}, u32[]{:S(2)}) copy-start(f32[128]{0:T(128)S(1)} %add_rsqrt_fusion.2) | copy-start | bytes 1540
  344.3 108.8 %all-gather.16.cloned.1.call-start = ((), (), s32[]{:S(2)}) async-start(), calls=%async_computation.10 | async-start | bytes 7864320 | tf_op jit(solution)/shard_map/all_gather | solution.py:261
  351.1 24.3 %all-to-all-start.3 = ((bf16[32,128,128]{1,2,0:T(8,128)(2,1)}), bf16[32,128,128]{1,2,0:T(8,128)(2,1)S(1)}, u32[]{:S(2)}, u32[]{:S(2)}) async-start(bf16[32,128,128]{1,2,0:T(8,128)(2,1)} %bitcast_select_fusion.1), calls=%async_computation.3 | async-start | bytes 2097152 | tf_op jit(solution)/shard_map/all_to_all | solution.py:166
  375.4 28.6 %all-to-all-start.2 = ((bf16[128,4,1792]{2,0,1:T(8,128)(2,1)}), bf16[128,4,1792]{2,0,1:T(8,128)(2,1)}, u32[]{:S(2)}, u32[]{:S(2)}) async-start(bf16[128,4,1792]{2,0,1:T(8,128)(2,1)} %pad_maximum_fusion.10), calls=%async_computation.2 | async-start | bytes 3670016 | tf_op jit(solution)/shard_map/all_to_all | solution.py:254
  379.9 143.6 %reduce-scatter.5.cloned.1.call-start = ((), (), s32[]{:S(2)}) async-start(), calls=%async_computation.11 | async-start | bytes 7208960 | tf_op jit(solution)/shard_map/reduce_scatter | solution.py:94
  462.9 20.3 %copy-start.36 = (bf16[32,128,128]{2,1,0:T(8,128)(2,1)S(1)}, bf16[32,128,128]{2,1,0:T(8,128)(2,1)}, u32[]{:S(2)}) copy-start(bf16[32,128,128]{2,1,0:T(8,128)(2,1)} %copy-done.35) | copy-start | bytes 3145732
  516.0 54.2 %all-to-all-start.4 = ((bf16[32,128,384]{1,2,0:T(8,128)(2,1)}), bf16[32,128,384]{1,2,0:T(8,128)(2,1)S(1)}, u32[]{:S(2)}, u32[]{:S(2)}) async-start(bf16[32,128,384]{1,2,0:T(8,128)(2,1)} %pad_maximum_fusion.7), calls=%async_computation.4 | async-start | bytes 6291456 | tf_op jit(solution)/shard_map/all_to_all | solution.py:166
  523.4 64.9 %reduce-scatter.7.cloned.1.call-start = ((), (), s32[]{:S(2)}) async-start(), calls=%async_computation.12 | async-start | bytes 1802240 | tf_op jit(solution)/shard_map/reduce_scatter | solution.py:95
  524.2 124.2 %all-gather.18.cloned.1.call-start = ((), (), s32[]{:S(2)}) async-start(), calls=%async_computation.13 | async-start | bytes 5242880 | tf_op jit(solution)/shard_map/all_gather | solution.py:327
  529.0 41.5 %copy-start.40 = (f32[128,64]{0,1:T(8,128)S(1)}, f32[128,64]{0,1:T(8,128)}, u32[]{:S(2)}) copy-start(f32[128,64]{0,1:T(8,128)} %copy-done.39) | copy-start | bytes 98308
  529.0 41.5 %copy-start.42 = (f32[128,64]{0,1:T(8,128)S(1)}, f32[128,64]{0,1:T(8,128)}, u32[]{:S(2)}) copy-start(f32[128,64]{0,1:T(8,128)} %copy-done.41) | copy-start | bytes 98308
  588.3 13.5 %copy-start.67 = (u32[128]{0:T(128)S(1)}, u32[128]{0:T(128)}, u32[]{:S(2)}) copy-start(u32[128]{0:T(128)} %constant.187) | copy-start | bytes 1540
  588.3 17.3 %copy-start.65 = (s32[2]{0:T(128)S(1)}, s32[2]{0:T(128)}, u32[]{:S(2)}) copy-start(s32[2]{0:T(128)} %constant.178.clone.1) | copy-start | bytes 28
  588.3 18.0 %copy-start.33 = (bf16[128,2048]{1,0:T(8,128)(2,1)S(1)}, bf16[128,2048]{1,0:T(8,128)(2,1)}, u32[]{:S(2)}) copy-start(bf16[128,2048]{1,0:T(8,128)(2,1)} %get-tuple-element.103) | copy-start | bytes 1572868
  588.3 18.0 %copy-start.37 = (bf16[128,1024]{1,0:T(8,128)(2,1)S(1)}, bf16[128,1024]{1,0:T(8,128)(2,1)}, u32[]{:S(2)}) copy-start(bf16[128,1024]{1,0:T(8,128)(2,1)} %get-tuple-element.107) | copy-start | bytes 786436
  588.3 18.0 %copy-start.38 = (bf16[128,1024]{1,0:T(8,128)(2,1)S(1)}, bf16[128,1024]{1,0:T(8,128)(2,1)}, u32[]{:S(2)}) copy-start(bf16[128,1024]{1,0:T(8,128)(2,1)} %copy.260) | copy-start | bytes 786436
  588.3 18.0 %copy-start.58 = (f32[128]{0:T(128)S(1)}, f32[128]{0:T(128)}, u32[]{:S(2)}) copy-start(f32[128]{0:T(128)} %copy-done.57) | copy-start | bytes 1540
  588.3 11.6 %collective-permute-start.4 = (bf16[16,11264]{1,0:T(8,128)(2,1)}, bf16[16,11264]{1,0:T(8,128)(2,1)S(1)}, u32[]{:S(2)}, u32[]{:S(2)}) collective-permute-start(bf16[16,11264]{1,0:T(8,128)(2,1)} %reduce-scatter.7.cloned.1.call-done), channel_id=1, source_target_pairs={{0,64},{64,0},{1,65},{65,1},{2,66},{66,2},{3,67},{67,3},{4,68},{68... | collective-permute-start | bytes 1081352 | tf_op jit(solution)/shard_map/ppermute | solution.py:96
  601.7 83.4 %reduce-scatter.9.cloned.1.call-start = ((), (), s32[]{:S(2)}) async-start(), calls=%async_computation.14 | async-start | bytes 2703360 | tf_op jit(solution)/shard_map/reduce_scatter | solution.py:94
  652.0 65.6 %copy-start.4 = (f32[128,1024]{1,0:T(8,128)S(1)}, f32[128,1024]{1,0:T(8,128)}, u32[]{:S(2)}) copy-start(f32[128,1024]{1,0:T(8,128)} %copy-done.3) | copy-start | bytes 1572868
  652.0 65.6 %copy-start.28 = (bf16[128,3072]{1,0:T(8,128)(2,1)S(1)}, bf16[128,3072]{1,0:T(8,128)(2,1)}, u32[]{:S(2)}) copy-start(bf16[128,3072]{1,0:T(8,128)(2,1)} %get-tuple-element.108) | copy-start | bytes 2359300
  653.5 55.7 %reduce-scatter.11.cloned.1.call-start = ((), (), s32[]{:S(2)}) async-start(), calls=%async_computation.15 | async-start | bytes 675840 | tf_op jit(solution)/shard_map/reduce_scatter | solution.py:95
  685.2 85.3 %all-gather.22.cloned.1.call-start = ((), (), s32[]{:S(2)}) async-start(), calls=%async_computation.17 | async-start | bytes 6127616 | tf_op jit(solution)/shard_map/all_gather | solution.py:102
  685.8 132.4 %all-gather.20.cloned.1.call-start = ((), (), s32[]{:S(2)}) async-start(), calls=%async_computation.16 | async-start | bytes 2297856 | tf_op jit(solution)/shard_map/all_gather | solution.py:102
  709.2 6.7 collective-permute-start.5
  (46 other events, 199.4 us)
Sparse Core Ops, SparseCore 0:
  10.4 61.7 all-gather.23
  73.9 36.6 all-gather.25
  112.2 78.7 all-gather.29
  193.0 88.6 all-gather.27
  344.4 36.8 all-gather.13
  383.5 69.6 all-gather.15
  461.5 59.1 reduce-scatter.4
  526.7 51.2 reduce-scatter.6
  601.9 46.4 all-gather.17
  653.7 31.4 reduce-scatter.8
  687.7 21.4 reduce-scatter.10
  711.8 58.5 all-gather.21
  773.2 44.8 all-gather.19
